TPU v7x, 128 devices: a whole 4x4x4 slice. The times are simulated.
128 devices in a mesh: grp: 4 (over y_hi, core), req: 32 (over x, z, y_lo).
Axes of the slice: x: 4, y: 4 (y_hi: 2, y_lo: 2; y = y_hi * 2 + y_lo), z: 4, core: 2. Of those that a mesh axis runs over, the one named last changes fastest.
Arguments:
- tokens: bfloat16 [16384, 1024], P(('grp', 'req')), may hold values from -6 to 6
- attn_gain: float32 [1024], replicated, may hold values from 0.1 to 1.9
- w_query: bfloat16 [1024, 1024], replicated, may hold values from -0.0234375 to 0.0234375
- w_key: bfloat16 [1024, 1024], replicated, may hold values from -0.1875 to 0.1875
- w_value: bfloat16 [1024, 1024], replicated, may hold values from -0.1875 to 0.1875
- w_attn_out: bfloat16 [1024, 1024], replicated, may hold values from -0.1875 to 0.1875
- rel_bias: float32 [32, 16], replicated, may hold values from -4 to 4
- prefix_cache: bfloat16 [8, 512, 2048], P('grp', 'req'), may hold values from -6 to 6
- lengths: int32 [4, 64], P('grp'), may hold values from 1 to 128, 4096 in all within a row
- prefix_map: int32 [4, 64], P('grp'), may hold values from 0 to 1
- mlp_gain: float32 [1024], replicated, may hold values from 0.1 to 1.9
- w_in: bfloat16 [4096, 1024], P('grp'), may hold values from -0.1875 to 0.1875
- w_out: bfloat16 [4096, 1024], P('grp'), may hold values from -0.09375 to 0.09375
Outputs:
- layer_out: bfloat16 [16384, 1024], P(('grp', 'req'))
Inputs may be any that keep to these rules, and one draw needn't show every extreme that they name: In each group the lengths sum to 4096 and the longest is exactly 128.
All inputs are finite; a program needn't handle non-finite values.
Results may differ from a plain program's by a relative error of at most 0.017.
Values may be sent and summed in bfloat16 or wider, within the bound.
No kernel may reach another device: no remote copies, remote signals or barrier semaphores. Data moves between devices by JAX's collectives and lax.ppermute only.
A program may use at most 128 MiB of HBM per device.

v0:
```python
import jax
import jax.numpy as jnp
from jax import lax
from jax.sharding import PartitionSpec as P

D = 1024
H = 16
DK = 64
PLEN = 512
PREF_GRP = 2


epsilon = 1e-06
far_marks = (12, 16, 23, 32, 46, 64, 91)
masked_score = -1e30


def padded(value, sides, width):
    for axis, dim in sides:
        count, length = (lax.axis_size(axis), value.shape[dim])
        up = [(i, (i + 1) % count) for i in range(count - 1)]
        down = [(j, i) for i, j in up]
        last = lax.slice_in_dim(value, length - width, length, axis=dim)
        leading = lax.slice_in_dim(value, 0, width, axis=dim)
        before = lax.ppermute(last, axis, up)
        after = lax.ppermute(leading, axis, down)
        value = jnp.concatenate([before, value, after], axis=dim)
    return value


def bucket_of(relative):
    distance = jnp.abs(relative)
    far_bucket = 8 + sum([(distance >= threshold).astype(jnp.int32) for threshold in far_marks])
    bucket = jnp.where(distance < 8, distance, far_bucket)
    return bucket + jnp.where(relative > 0, 16, 0)


def bias_lookup(relative, rel_bias):
    buckets = bucket_of(relative)
    marks = jnp.arange(rel_bias.shape[0], dtype=jnp.int32)
    one_hot = (buckets[:, :, None] == marks[None, None, :]).astype(jnp.float32)
    return jnp.einsum(
        "qkb,bh->hqk",
        one_hot,
        rel_bias,
        precision=lax.Precision.HIGHEST,
        preferred_element_type=jnp.float32,
    )


def norm_rows(values_in, gain):
    widened = values_in.astype(jnp.float32)
    scale = lax.rsqrt(jnp.mean(widened * widened, axis=-1, keepdims=True) + epsilon)
    return (widened * scale * gain).astype(jnp.bfloat16)


def layout(lengths_row, prefix_row, row_ids):
    req_ends = jnp.cumsum(lengths_row)
    req_starts = req_ends - lengths_row
    member = (
        (row_ids[:, None] >= req_starts[None, :]) & (row_ids[:, None] < req_ends[None, :])
    ).astype(jnp.int32)
    numbers = jnp.arange(lengths_row.shape[0], dtype=jnp.int32)
    req_index = jnp.sum(member * numbers[None, :], axis=1) + jnp.sum(member, axis=1) - 1
    offset = row_ids - jnp.sum(member * req_starts[None, :], axis=1)
    chosen = jnp.sum(member * prefix_row[None, :], axis=1)
    return (req_index, offset, chosen)


def softmax_part(scores, value_rows, allowed):
    scores = jnp.where(allowed[None], scores, masked_score)
    row_max = jnp.max(scores, axis=2)
    exp_terms = jnp.where(allowed[None], jnp.exp(scores - row_max[:, :, None]), 0.0)
    row_sum = jnp.sum(exp_terms, axis=2)
    weighted = jnp.einsum(
        "hqk,khd->hqd",
        exp_terms.astype(jnp.bfloat16),
        value_rows,
        preferred_element_type=jnp.float32,
    )
    return (row_max, row_sum, weighted)


def combine(first_part, second_part):
    row_max = jnp.maximum(first_part[0], second_part[0])
    scale_one = jnp.exp(first_part[0] - row_max)
    scale_two = jnp.exp(second_part[0] - row_max)
    row_sum = first_part[1] * scale_one + second_part[1] * scale_two
    weighted = first_part[2] * scale_one[:, :, None] + second_part[2] * scale_two[:, :, None]
    return (row_max, row_sum, weighted)


def feed_forward(rows_in, in_part, out_part):
    units = lax.dot_general(
        rows_in, in_part, (((1,), (1,)), ((), ())), preferred_element_type=jnp.float32
    )
    units = jnp.maximum(units, 0.0).astype(jnp.bfloat16)
    return jnp.dot(units, out_part, preferred_element_type=jnp.float32)


def body(
    tokens,
    attn_gain,
    w_query,
    w_key,
    w_value,
    w_attn_out,
    rel_bias,
    prefix_cache,
    lengths,
    prefix_map,
    mlp_gain,
    w_in,
    w_out,
):
    rows_here = tokens.shape[0]
    device_pos = lax.axis_index("req")
    group_lengths = lengths[0]
    group_map = prefix_map[0]
    normed = norm_rows(tokens, attn_gain)
    query = (
        jnp.dot(normed, w_query, preferred_element_type=jnp.float32)
        .astype(jnp.bfloat16)
        .reshape(rows_here, H, DK)
    )
    key_value = jnp.concatenate(
        [
            jnp.dot(normed, w_key, preferred_element_type=jnp.float32).astype(jnp.bfloat16),
            jnp.dot(normed, w_value, preferred_element_type=jnp.float32).astype(jnp.bfloat16),
        ],
        axis=1,
    )
    query_ids = device_pos * rows_here + jnp.arange(rows_here, dtype=jnp.int32)
    query_req, query_offset, query_prefix = layout(group_lengths, group_map, query_ids)
    all_positions = jnp.arange(PLEN, dtype=jnp.int32)
    prefix_bias = bias_lookup(all_positions[None, :] - PLEN - query_offset[:, None], rel_bias)
    empty_state = (
        jnp.full((H, rows_here), masked_score, jnp.float32),
        jnp.zeros((H, rows_here), jnp.float32),
        jnp.zeros((H, rows_here, DK), jnp.float32),
    )
    running = empty_state
    shard_kv = lax.all_gather(prefix_cache, "req", axis=1, tiled=True)
    prefix_ids = jnp.arange(PREF_GRP, dtype=jnp.int32)
    slices = shard_kv.shape[0]
    piece_len = shard_kv.shape[1]
    step_len = max(min(piece_len, 512 // slices), 1)
    for begin in range(0, piece_len, step_len):
        width = min(step_len, piece_len - begin)
        block = shard_kv[:, begin : begin + width]
        key_rows = block[:, :, :D].reshape(slices, width, H, DK)
        value_rows = block[:, :, D:].reshape(-1, H, DK)
        rel_terms = lax.dynamic_slice_in_dim(prefix_bias, begin, width, 2)
        prefix_scores = jnp.einsum(
            "qhd,swhd->hqsw", query, key_rows, preferred_element_type=jnp.float32
        )
        prefix_scores = (prefix_scores + rel_terms[:, :, None, :]).reshape(
            H, rows_here, slices * width
        )
        allowed = jnp.repeat(query_prefix[:, None] == prefix_ids[None, :], width, axis=1)
        running = combine(running, softmax_part(prefix_scores, value_rows, allowed))
    state = running
    window = padded(key_value, (("req", 0),), rows_here)
    window_ids = device_pos * rows_here - rows_here + jnp.arange(3 * rows_here, dtype=jnp.int32)
    window_req = layout(group_lengths, group_map, window_ids)[0]
    for part_idx in range(3):
        part_rows = window[part_idx * rows_here : (part_idx + 1) * rows_here]
        part_ids = window_ids[part_idx * rows_here : (part_idx + 1) * rows_here]
        part_req = window_req[part_idx * rows_here : (part_idx + 1) * rows_here]
        suffix_terms = bias_lookup(part_ids[None, :] - query_ids[:, None], rel_bias)
        suffix_allowed = part_req[None, :] == query_req[:, None]
        scores = (
            jnp.einsum(
                "qhd,khd->hqk",
                query,
                part_rows[:, :D].reshape(-1, H, DK),
                preferred_element_type=jnp.float32,
            )
            + suffix_terms
        )
        suffix_state = softmax_part(scores, part_rows[:, D:].reshape(-1, H, DK), suffix_allowed)
        state = combine(state, suffix_state)
    attended = (
        (state[2] / state[1][:, :, None])
        .transpose(1, 0, 2)
        .reshape(rows_here, D)
        .astype(jnp.bfloat16)
    )
    hidden_one = (
        tokens.astype(jnp.float32)
        + jnp.dot(attended, w_attn_out, preferred_element_type=jnp.float32)
    ).astype(jnp.bfloat16)
    normed_two = norm_rows(hidden_one, mlp_gain)
    gathered = lax.all_gather(normed_two, "grp", axis=0, tiled=True)
    mlp_total = lax.psum_scatter(
        feed_forward(gathered, w_in, w_out).astype(jnp.bfloat16),
        "grp",
        scatter_dimension=0,
        tiled=True,
    ).astype(jnp.float32)
    return (hidden_one.astype(jnp.float32) + mlp_total).astype(jnp.bfloat16)


def solution(mesh):
    return jax.shard_map(
        body,
        mesh=mesh,
        in_specs=(
            P(("grp", "req"), None),
            P(),
            P(),
            P(),
            P(),
            P(),
            P(),
            P("grp", "req", None),
            P("grp", None),
            P("grp", None),
            P(),
            P("grp", None),
            P("grp", None),
        ),
        out_specs=P(("grp", "req"), None),
        check_vma=False,
    )
```

profile of v0, /device:TPU:0, one launch (start us, length us, event | category | flops | bytes accessed | tf_op | source)
XLA Modules:
  0.0 307.3 jit_solution(4124527477737952821)
XLA Ops:
  6.5 1.8 copy.91
  8.5 1.2 fusion.46
  9.7 2.2 convolution_convert_fusion.1
  13.5 1.4 collective-permute-start.1
  14.9 5.4 %collective-permute-start = (bf16[128,2048]{1,0:T(8,128)(2,1)}, bf16[128,2048]{1,0:T(8,128)(2,1)}, u32[]{:S(2)}, u32[]{:S(2)}) collective-permute-start(bf16[128,2048]{1,0:T(8,128)(2,1)} %pad_maximum_fusion), channel_id=1, source_target_pairs={{0,1},{1,2},{2,3},{3,4},{4,5},{5,6},{6,7},{7,8},{8,9},{9,10},{10,1... | collective-permute-start | bytes 1572872 | tf_op jit(solution)/shard_map/ppermute | solution.py:25
  20.3 0.8 copy.108
  21.1 2.1 convolution_convert_fusion.3
  23.7 0.9 fusion.90
  25.4 1.4 copy.109
  27.5 2.6 fusion.13
  30.1 1.3 fusion.137
  31.4 3.0 fusion.10
  34.4 2.7 fusion.131
  37.1 1.8 fusion.11
  39.1 1.8 copy.110
  40.9 2.6 copy.113
  43.4 4.1 %copy.94 = f32[16,128,256]{2,1,0:T(8,128)} copy(f32[16,128,256]{2,0,1:T(8,128)} %get-tuple-element.28) | data formatting | bytes 4194304 | tf_op jit(solution)/shard_map/dynamic_slice | solution.py:153
  47.6 2.6 copy.105
  50.1 4.2 %copy.100 = f32[16,128,256]{2,1,0:T(8,128)} copy(f32[16,128,256]{2,0,1:T(8,128)} %get-tuple-element.29) | data formatting | bytes 4194304 | tf_op jit(solution)/shard_map/dynamic_slice | solution.py:153
  54.3 1.8 fusion.133
  56.2 1.8 copy.114
  58.0 1.8 copy.112
  59.8 1.8 fusion.132
  61.6 1.8 copy.104
  63.4 1.8 copy.106
  65.2 2.0 fusion.136
  67.2 1.0 copy-done.3
  68.7 1.0 copy-done.7
  70.0 114.0 %all-gather.3.cloned.1.call-done = bf16[2,512,2048]{2,0,1:T(2,128)(2,1)} async-done(((bf16[2,16,2048]{2,0,1:T(2,128)(2,1)}), bf16[2,512,2048]{2,0,1:T(2,128)(2,1)}) %all-gather.3.cloned.1.call-update) | async-done | bytes 4194320 | tf_op jit(solution)/shard_map/all_gather | solution.py:143
  184.0 5.7 %fusion.130 = (bf16[2,256,1024]{2,0,1:T(2,128)(2,1)}, bf16[2,256,1024]{2,0,1:T(2,128)(2,1)}, bf16[2,256,1024]{2,0,1:T(2,128)(2,1)}, bf16[2,256,1024]{2,0,1:T(2,128)(2,1)}) fusion(bf16[2,512,2048]{2,0,1:T(2,128)(2,1)} %all-gather.3.cloned.1.call-done), kind=kLoop, calls=%fused_computation.203 | loop fusion | bytes 8388608 | tf_op jit(solution)/shard_map/slice | solution.py:152
  189.7 3.6 %copy.122 = bf16[2,256,1024]{1,2,0:T(8,128)(2,1)} copy(bf16[2,256,1024]{2,0,1:T(2,128)(2,1)} %get-tuple-element.25) | data formatting | bytes 2097152
  193.4 3.7 %copy.123 = bf16[2,256,1024]{1,2,0:T(8,128)(2,1)} copy(bf16[2,256,1024]{2,0,1:T(2,128)(2,1)} %get-tuple-element.27) | data formatting | bytes 2097152
  197.0 2.9 select_reduce_fusion.3
  199.9 2.4 select_reduce_fusion.1
  202.4 2.0 copy-done.2
  204.4 1.2 select_reduce_fusion
  205.6 5.3 %copy.101 = f32[16,128,2,256]{1,3,2,0:T(8,128)} copy(f32[16,128,2,256]{3,1,2,0:T(8,128)} %copy-done.2) | data formatting | bytes 8388608 | tf_op jit(solution)/shard_map/add | solution.py:157
  210.9 5.3 %copy.95 = f32[16,128,2,256]{1,3,2,0:T(8,128)} copy(f32[16,128,2,256]{3,1,2,0:T(8,128)} %copy-done.1) | data formatting | bytes 8388608 | tf_op jit(solution)/shard_map/add | solution.py:157
  216.2 4.9 %copy.96 = bf16[2,256,1024]{1,0,2:T(2,128)(2,1)} copy(bf16[2,256,1024]{2,0,1:T(2,128)(2,1)} %get-tuple-element.26) | data formatting | bytes 2097152 | tf_op jit(solution)/shard_map/slice | solution.py:152
  221.1 2.6 reshape.536
  223.7 4.9 %copy.102 = bf16[2,256,1024]{1,0,2:T(2,128)(2,1)} copy(bf16[2,256,1024]{2,0,1:T(2,128)(2,1)} %get-tuple-element.24) | data formatting | bytes 2097152 | tf_op jit(solution)/shard_map/slice | solution.py:152
  228.5 2.6 reshape.539
  231.8 1.6 fusion.31
  233.8 5.3 %fusion.4 = (bf16[16,128,512]{1,2,0:T(8,128)(2,1)S(1)}, bf16[16,128,512]{1,2,0:T(8,128)(2,1)S(1)}) fusion(f32[16,128,2,256]{1,3,2,0:T(8,128)} %copy.101, f32[16,128]{1,0:T(8,128)S(1)} %get-tuple-element.12, pred[128,512]{0,1:T(8,128)(4,1)S(1)} %bitcast.222, f32[16,128]{1,0:T(8,128)S(1)} %get-tuple-element.61, f32[16,128,2,256]{1,3,2,0:T(8,128)} %copy.95), kind=kLoop, calls=%fused_computation.6 | loop fusion | flops 8388608 | bytes 12664832 | tf_op jit(solution)/shard_map/convert_element_type | solution.py:77
  244.1 18.3 %all-gather.5.cloned.1.call-done = bf16[512,1024]{1,0:T(8,128)(2,1)} async-done(((bf16[128,1024]{1,0:T(8,128)(2,1)}), bf16[512,1024]{1,0:T(8,128)(2,1)}) %all-gather.5.cloned.1.call-update) | async-done | bytes 1048592 | tf_op jit(solution)/shard_map/all_gather | solution.py:194
  262.4 5.3 %convolution_convert_fusion = bf16[512,1024]{1,0:T(8,128)(2,1)} fusion(bf16[1024,1024]{1,0:T(8,128)(2,1)S(1)} %copy-done, bf16[512,1024]{1,0:T(8,128)(2,1)} %all-gather.5.cloned.1.call-done, bf16[1024,1024]{1,0:T(8,128)(2,1)} %param.24), kind=kOutput, calls=%fused_computation.27 | convolution fusion | flops 2149056512 | bytes 6291456 | tf_op jit(solution)/shard_map/dot_general | solution.py:98
  267.7 31.4 %reduce-scatter.2.cloned.1.call-done = bf16[128,1024]{1,0:T(8,128)(2,1)} async-done(((bf16[512,1024]{1,0:T(8,128)(2,1)}), bf16[128,1024]{1,0:T(8,128)(2,1)}) %reduce-scatter.2.cloned.1.call-update) | async-done | bytes 262160 | tf_op jit(solution)/shard_map/reduce_scatter | solution.py:195
  299.1 1.7 add_convert_fusion
  (94 shorter events, 10.5 us)
Async XLA Ops:
  6.5 255.9 %copy-start = (bf16[1024,1024]{1,0:T(8,128)(2,1)S(1)}, bf16[1024,1024]{1,0:T(8,128)(2,1)}, u32[]{:S(2)}) copy-start(bf16[1024,1024]{1,0:T(8,128)(2,1)} %param.25) | copy-start | bytes 6291460
  6.5 5.4 %copy-start.4 = (bf16[128,1024]{1,0:T(8,128)(2,1)S(1)}, bf16[128,1024]{1,0:T(8,128)(2,1)}, u32[]{:S(2)}) copy-start(bf16[128,1024]{1,0:T(8,128)(2,1)} %param.13) | copy-start | bytes 786436
  6.5 5.4 %copy-start.21 = (f32[1024]{0:T(1024)S(1)}, f32[1024]{0:T(1024)}, u32[]{:S(2)}) copy-start(f32[1024]{0:T(1024)} %param.14) | copy-start | bytes 12292
  6.5 177.5 %all-gather.3.cloned.1.call-start = ((), (), s32[]{:S(2)}) async-start(), calls=%async_computation.1 | async-start | bytes 4325376 | tf_op jit(solution)/shard_map/all_gather | solution.py:143
  8.4 254.0 %all-gather.5.cloned.1.call-start = ((), (), s32[]{:S(2)}) async-start(), calls=%async_computation.2 | async-start | bytes 1310720 | tf_op jit(solution)/shard_map/all_gather | solution.py:194
  8.5 3.5 %copy-start.13 = (bf16[1024,1024]{1,0:T(8,128)(2,1)S(1)}, bf16[1024,1024]{1,0:T(8,128)(2,1)}, u32[]{:S(2)}) copy-start(bf16[1024,1024]{1,0:T(8,128)(2,1)} %param.16) | copy-start | bytes 6291460
  11.9 0.7 copy-start.12
  13.5 9.9 %copy-start.25 = (s32[1,64]{1,0:T(1,128)S(1)}, s32[1,64]{1,0:T(1,128)}, u32[]{:S(2)}) copy-start(s32[1,64]{1,0:T(1,128)} %param.21) | copy-start | bytes 772
  13.5 11.1 %copy-start.20 = (f32[32,16]{0,1:T(8,128)S(1)}, f32[32,16]{0,1:T(8,128)}, u32[]{:S(2)}) copy-start(f32[32,16]{0,1:T(8,128)} %param.19) | copy-start | bytes 6148
  13.5 40.8 %collective-permute-start.1 = (bf16[128,2048]{1,0:T(8,128)(2,1)}, bf16[128,2048]{1,0:T(8,128)(2,1)}, u32[]{:S(2)}, u32[]{:S(2)}) collective-permute-start(bf16[128,2048]{1,0:T(8,128)(2,1)} %pad_maximum_fusion), channel_id=1, source_target_pairs={{1,0},{2,1},{3,2},{4,3},{5,4},{6,5},{7,6},{8,7},{9,8},{10,9},{11,1... | collective-permute-start | bytes 1572872 | tf_op jit(solution)/shard_map/ppermute | solution.py:26
  14.9 44.9 %collective-permute-start = (bf16[128,2048]{1,0:T(8,128)(2,1)}, bf16[128,2048]{1,0:T(8,128)(2,1)}, u32[]{:S(2)}, u32[]{:S(2)}) collective-permute-start(bf16[128,2048]{1,0:T(8,128)(2,1)} %pad_maximum_fusion), channel_id=1, source_target_pairs={{0,1},{1,2},{2,3},{3,4},{4,5},{5,6},{6,7},{7,8},{8,9},{9,10},{10,1... | collective-permute-start | bytes 1572872 | tf_op jit(solution)/shard_map/ppermute | solution.py:25
  23.2 3.6 %copy-start.26 = (s32[1,64]{1,0:T(1,128)S(1)}, s32[1,64]{1,0:T(1,128)}, u32[]{:S(2)}) copy-start(s32[1,64]{1,0:T(1,128)} %param.22) | copy-start | bytes 772
  26.8 3.3 %copy-start.9 = (f32[128,128,16]{0,1,2:T(8,128)S(1)}, f32[128,128,16]{0,1,2:T(8,128)}, u32[]{:S(2)}) copy-start(f32[128,128,16]{0,1,2:T(8,128)} %copy.109) | copy-start | bytes 3145732
  54.3 148.1 %copy-start.22 = (pred[128,2]{0,1:T(4,128)(4,1)}, pred[128,2]{0,1:T(4,128)(4,1)S(1)}, u32[]{:S(2)}) copy-start(pred[128,2]{0,1:T(4,128)(4,1)S(1)} %iota_compare_fusion.10) | copy-start | bytes 772
  65.2 3.2 %copy-start.10 = (f32[128,128,16]{0,1,2:T(8,128)S(1)}, f32[128,128,16]{0,1,2:T(8,128)}, u32[]{:S(2)}) copy-start(f32[128,128,16]{0,1,2:T(8,128)} %copy.105) | copy-start | bytes 3145732
  65.2 3.2 %copy-start.17 = (bf16[128,1024]{0,1:T(8,128)(2,1)S(1)}, bf16[128,1024]{0,1:T(8,128)(2,1)}, u32[]{:S(2)}) copy-start(bf16[128,1024]{0,1:T(8,128)(2,1)} %copy.104) | copy-start | bytes 786436
  67.2 1.0 copy-start.3
  68.7 1.1 copy-start.7
  197.0 2.9 copy-start.15
  197.0 2.9 copy-start.18
  199.9 2.5 copy-start.1
  202.4 2.0 copy-start.2
  228.5 4.9 %copy-start.16 = (bf16[128,1024]{0,1:T(8,128)(2,1)S(1)}, bf16[128,1024]{0,1:T(8,128)(2,1)}, u32[]{:S(2)}) copy-start(bf16[128,1024]{0,1:T(8,128)(2,1)} %copy.110) | copy-start | bytes 786436
  231.1 2.6 copy-start.23
  233.8 5.4 %copy-start.6 = (bf16[512,16,64]{0,2,1:T(8,128)(2,1)S(1)}, bf16[512,16,64]{0,2,1:T(8,128)(2,1)}, u32[]{:S(2)}) copy-start(bf16[512,16,64]{0,2,1:T(8,128)(2,1)} %reshape.536) | copy-start | bytes 3145732
  239.1 1.2 copy-start.11
  240.3 1.2 copy-start.8
  240.3 1.3 copy-start.19
  240.9 1.1 copy-start.5
  240.9 1.8 copy-start.14
  241.9 1.3 copy-start.24
  244.1 55.0 %reduce-scatter.2.cloned.1.call-start = ((), (), s32[]{:S(2)}) async-start(), calls=%async_computation.3 | async-start | bytes 1310720 | tf_op jit(solution)/shard_map/reduce_scatter | solution.py:195
Sparse Core Ops, SparseCore 0:
  9.0 174.9 all-gather.2
  244.2 18.1 all-gather.4
  267.8 31.2 reduce-scatter.1
where the time goes:
time: 309 us; the launch traced here: 307 us
  waiting for transfers between devices  164 us (53%)
  local copies, waits for them, and re-layouts  78 us (25%)
  matrix products  31 us (10%)
  other arithmetic  14.2 us (5%)
  between operations  13.5 us (4%)
  starting transfers between devices  6.85 us (2%)
    all_gather x1, waiting for transfers between devices, body(): shard_kv = lax.all_gather(prefix_cache, 'req', axis=1, tiled=True)  114 us
    reduce_scatter x1, waiting for transfers between devices, body(): lax.psum_scatter(feed_forward(gathered, w_in, w_out).astype(jnp.bfloat16)...  31.4 us
    all_gather x1, waiting for transfers between devices, body(): gathered = lax.all_gather(normed_two, 'grp', axis=0, tiled=True)  18.3 us
    unnamed x57, local copies, waits for them, and re-layouts  15.5 us
    slice x3, local copies, waits for them, and re-layouts, body(): value_rows = block[:, :, D:].reshape(-1, H, DK)  15.4 us
    dynamic_slice x3, local copies, waits for them, and re-layouts, body(): rel_terms = lax.dynamic_slice_in_dim(prefix_bias, begin, width, 2)  11 us
    add x2, local copies, waits for them, and re-layouts, body(): prefix_scores + rel_terms[:, :, None, :]  10.6 us
    dot_general x4, matrix products, bias_lookup(): jnp.einsum('qkb,bh->hqk', one_hot, rel_bias, precision=lax.Precision.HIGH...  8.1 us
  transfers between devices with their start and end apart: 5, of which 3 were waited for; matrix products, arithmetic and copies ran while one was open for 17% of the time, Pallas kernels for 0%

commit v1 on v0

v1 whole, which is shorter than its diff:
```python
import functools

import jax
import jax.numpy as jnp
from jax import lax
from jax.experimental import pallas as pl
from jax.experimental.pallas import tpu as pltpu
from jax.sharding import Mesh, PartitionSpec as P

D = 1024
H = 16
DK = 64
PLEN = 512
PREF_GRP = 2
ROWS = 128
PAIRS = 8
LANES = 128

epsilon = 1e-06
far_marks = (12, 16, 23, 32, 46, 64, 91)
masked_score = -1e30
VMEM_LIMIT = 56 * 1024 * 1024

AXES = ("yhi", "core", "x", "z", "ylo")
REQ = ("x", "z", "ylo")
PLANE = ("z", "ylo")
MIRROR = [(0, 3), (3, 0), (1, 2), (2, 1)]
SWAP = [(0, 1), (1, 0)]


def norm_rows(values_in, gain):
    widened = values_in.astype(jnp.float32)
    scale = lax.rsqrt(jnp.mean(widened * widened, axis=-1, keepdims=True) + epsilon)
    return (widened * scale * gain).astype(jnp.bfloat16)


def project_kernel(tok_ref, gain_ref, wq_ref, wk_ref, wv_ref, out_ref, normed_ref):
    @pl.when(pl.program_id(0) == 0)
    def _():
        normed_ref[...] = norm_rows(tok_ref[...], gain_ref[...])

    normed = normed_ref[...]
    for kind, w_ref in enumerate((wq_ref, wk_ref, wv_ref)):
        got = jnp.dot(normed, w_ref[...], preferred_element_type=jnp.float32)
        got = got.astype(jnp.bfloat16)
        for part in range(got.shape[1] // LANES):
            out_ref[part, kind] = got[:, part * LANES : (part + 1) * LANES]


def project(tokens, gain, w_query, w_key, w_value):
    width = 256
    per = width // LANES
    w_spec = pl.BlockSpec((D, width), lambda j: (0, j))
    return pl.pallas_call(
        project_kernel,
        grid=(D // width,),
        in_specs=[
            pl.BlockSpec((ROWS, D), lambda j: (0, 0)),
            pl.BlockSpec((1, D), lambda j: (0, 0)),
            w_spec,
            w_spec,
            w_spec,
        ],
        out_specs=pl.BlockSpec((per, 3, ROWS, LANES), lambda j: (j, 0, 0, 0)),
        out_shape=jax.ShapeDtypeStruct((PAIRS, 3, ROWS, LANES), jnp.bfloat16),
        scratch_shapes=[pltpu.VMEM((ROWS, D), jnp.bfloat16)],
        compiler_params=pltpu.CompilerParams(vmem_limit_bytes=VMEM_LIMIT),
        name="project",
    )(tokens, gain.reshape(1, D), w_query, w_key, w_value)


def bias_line(rel_ref, head, first_bucket):
    lane = lax.broadcasted_iota(jnp.int32, (ROWS, LANES), 1)
    line = jnp.full((ROWS, LANES), rel_ref[first_bucket, head], jnp.float32)
    for bucket in range(1, 16):
        mark = bucket if bucket <= 8 else far_marks[bucket - 9]
        line = jnp.where(lane >= mark, rel_ref[first_bucket + bucket, head], line)
    return line


def attend_kernel(
    pair_ref, rel_ref, qkv_ref, halo_ref, pref_ref, meta_ref, out_ref, kcat, vcat, kwin, vwin, near
):
    step = pl.program_id(0)
    pair = pair_ref[0]
    row = lax.broadcasted_iota(jnp.int32, (ROWS, LANES), 0)
    lane = lax.broadcasted_iota(jnp.int32, (ROWS, LANES), 1)

    @pl.when(step == 0)
    def _():
        for p in range(PREF_GRP):
            kcat[:, p * LANES : (p + 1) * LANES] = pref_ref[:, 0, p].reshape(PLEN, LANES)
            vcat[:, p * LANES : (p + 1) * LANES] = pref_ref[:, 1, p].reshape(PLEN, LANES)
        for dst, kind in ((kwin, 0), (vwin, 1)):
            dst[0:ROWS] = halo_ref[0, kind]
            for b in range(PAIRS):
                dst[(b + 1) * ROWS : (b + 2) * ROWS] = qkv_ref[b, kind + 1]
            dst[(PAIRS + 1) * ROWS : (PAIRS + 2) * ROWS] = halo_ref[1, kind]
        for h in range(2):
            before = bias_line(rel_ref, pair * 2 + h, 0)
            after = bias_line(rel_ref, pair * 2 + h, 16)

            def pick(line, distance):
                at = jnp.clip(distance, 0, LANES - 1)
                return jnp.take_along_axis(line, at, axis=1)

            rows = slice(h * ROWS, (h + 1) * ROWS)
            near[rows, 0:LANES] = pick(before, row + LANES - lane)
            near[rows, LANES : 2 * LANES] = jnp.where(
                lane > row, pick(after, lane - row), pick(before, row - lane)
            )
            near[rows, 2 * LANES : 3 * LANES] = pick(after, lane + LANES - row)

    query = qkv_ref[step, 0]
    own = jnp.transpose(meta_ref[step + 1])
    request, offset, chosen = own[:, 0:1], own[:, 1:2], own[:, 2:3]
    zero = jnp.zeros_like(query)
    low = lane < DK
    halves = [jnp.where(low, query, zero), jnp.where(low, zero, query)]
    stacked = jnp.concatenate(halves, axis=0)
    second = jnp.concatenate([chosen, chosen], axis=0) > 0.5
    zeros = jnp.zeros_like(stacked)
    split = jnp.concatenate(
        [jnp.where(second, zeros, stacked), jnp.where(second, stacked, zeros)], axis=1
    )
    contract = (((1,), (1,)), ((), ()))
    far_scores = lax.dot_general(split, kcat[...], contract, preferred_element_type=jnp.float32)
    begin = pl.multiple_of(step * ROWS, ROWS)
    near_scores = lax.dot_general(
        stacked, kwin[pl.ds(begin, 3 * ROWS)], contract, preferred_element_type=jnp.float32
    )
    tail_at = jnp.minimum(LANES - lane + offset.astype(jnp.int32), LANES - 1)
    tails, fulls = [], []
    for h in range(2):
        line = bias_line(rel_ref, pair * 2 + h, 0)
        tails.append(jnp.take_along_axis(line, tail_at, axis=1))
        fulls.append(jnp.full((ROWS, 1), rel_ref[15, pair * 2 + h], jnp.float32))
    far_head = far_scores[:, : PLEN - LANES] + jnp.concatenate(fulls, axis=0)
    far_tail = far_scores[:, PLEN - LANES :] + jnp.concatenate(tails, axis=0)
    same = []
    for b in range(3):
        mine = meta_ref[step + b, 0:1, :] == request
        same.append(jnp.concatenate([mine, mine], axis=0))
    near_scores = near_scores + near[...]
    near_parts = [
        jnp.where(same[b], near_scores[:, b * LANES : (b + 1) * LANES], masked_score)
        for b in range(3)
    ]
    parts = [far_head[:, b * LANES : (b + 1) * LANES] for b in range(3)] + [far_tail] + near_parts
    tallest = functools.reduce(jnp.maximum, parts)
    row_max = jnp.max(tallest, axis=1, keepdims=True)
    terms = [jnp.exp(part - row_max) for part in parts]
    row_sum = jnp.sum(functools.reduce(jnp.add, terms), axis=1, keepdims=True)
    weights = [t.astype(jnp.bfloat16) for t in terms]
    far_out = jnp.dot(
        jnp.concatenate(weights[:4], axis=1), vcat[...], preferred_element_type=jnp.float32
    )
    near_out = jnp.dot(
        jnp.concatenate(weights[4:], axis=1),
        vwin[pl.ds(begin, 3 * ROWS)],
        preferred_element_type=jnp.float32,
    )
    total = jnp.where(second, far_out[:, LANES:], far_out[:, :LANES]) + near_out
    total = total / row_sum
    out_ref[0] = jnp.where(low, total[:ROWS], total[ROWS:]).astype(jnp.bfloat16)


def attend(pair, rel_bias, qkv, halo, pref, meta):
    whole = lambda shape: pl.BlockSpec(shape, lambda i: (0,) * len(shape))
    smem = pl.BlockSpec(memory_space=pltpu.SMEM)
    window = (PAIRS + 2) * ROWS
    return pl.pallas_call(
        attend_kernel,
        grid=(PAIRS,),
        in_specs=[smem, smem, whole(qkv.shape), whole(halo.shape), whole(pref.shape), whole(meta.shape)],
        out_specs=pl.BlockSpec((1, ROWS, LANES), lambda i: (i, 0, 0)),
        out_shape=jax.ShapeDtypeStruct((PAIRS, ROWS, LANES), jnp.bfloat16),
        scratch_shapes=[
            pltpu.VMEM((PLEN, 2 * LANES), jnp.bfloat16),
            pltpu.VMEM((PLEN, 2 * LANES), jnp.bfloat16),
            pltpu.VMEM((window, LANES), jnp.bfloat16),
            pltpu.VMEM((window, LANES), jnp.bfloat16),
            pltpu.VMEM((2 * ROWS, 3 * LANES), jnp.float32),
        ],
        compiler_params=pltpu.CompilerParams(vmem_limit_bytes=VMEM_LIMIT),
        name="attend",
    )(pair, rel_bias, qkv, halo, pref, meta)


def token_table(lengths_row, prefix_row, first):
    count = (PAIRS + 2) * ROWS
    ends = jnp.cumsum(lengths_row)
    starts = ends - lengths_row
    ids = first + jnp.arange(count, dtype=jnp.int32)
    member = ((ids[None, :] >= starts[:, None]) & (ids[None, :] < ends[:, None])).astype(jnp.int32)
    numbers = jnp.arange(1, lengths_row.shape[0] + 1, dtype=jnp.int32)
    request = jnp.sum(member * numbers[:, None], axis=0) - 1
    offset = ids - jnp.sum(member * starts[:, None], axis=0)
    chosen = jnp.sum(member * prefix_row[:, None], axis=0)
    table = jnp.stack([request, offset, chosen] + [request] * 5, axis=0).astype(jnp.float32)
    return table.reshape(8, PAIRS + 2, ROWS).transpose(1, 0, 2)


def join_kernel(att_ref, w_ref, tok_ref, gain_ref, hidden_ref, normed_ref):
    attended = jnp.concatenate([att_ref[j] for j in range(PAIRS)], axis=1)
    got = jnp.dot(attended, w_ref[...], preferred_element_type=jnp.float32)
    hidden = (tok_ref[...].astype(jnp.float32) + got).astype(jnp.bfloat16)
    hidden_ref[...] = hidden
    normed_ref[...] = norm_rows(hidden, gain_ref[...])


def join(att, w_attn_out, tokens, gain):
    shape = jax.ShapeDtypeStruct((ROWS, D), jnp.bfloat16)
    return pl.pallas_call(
        join_kernel,
        out_shape=(shape, shape),
        compiler_params=pltpu.CompilerParams(vmem_limit_bytes=VMEM_LIMIT),
        name="join",
    )(att, w_attn_out, tokens, gain.reshape(1, D))


def feed_kernel(one_ref, two_ref, in_ref, out_ref, first_ref, second_ref):
    rows = jnp.concatenate([one_ref[...], two_ref[...]], axis=0)
    units = lax.dot_general(
        rows, in_ref[...], (((1,), (1,)), ((), ())), preferred_element_type=jnp.float32
    )
    units = jnp.maximum(units, 0.0).astype(jnp.bfloat16)
    got = jnp.dot(units, out_ref[...], preferred_element_type=jnp.float32).astype(jnp.bfloat16)
    first_ref[...] = got[:ROWS]
    second_ref[...] = got[ROWS:]


def feed(one, two, w_in, w_out):
    shape = jax.ShapeDtypeStruct((ROWS, D), jnp.bfloat16)
    return pl.pallas_call(
        feed_kernel,
        out_shape=(shape, shape),
        compiler_params=pltpu.CompilerParams(vmem_limit_bytes=VMEM_LIMIT),
        name="feed",
    )(one, two, w_in, w_out)


def body(
    tokens,
    attn_gain,
    w_query,
    w_key,
    w_value,
    w_attn_out,
    rel_bias,
    prefix_cache,
    lengths,
    prefix_map,
    mlp_gain,
    w_in,
    w_out,
):
    plane_x = lax.axis_index("x")
    count_x = lax.axis_size("x")
    pair = (lax.axis_index("z") * 2 + lax.axis_index("ylo")).astype(jnp.int32).reshape(1)

    held = prefix_cache.reshape(PREF_GRP, -1, 2, PAIRS, LANES).transpose(3, 2, 0, 1, 4)
    sent = jnp.broadcast_to(held[None], (count_x,) + held.shape).reshape((-1,) + held.shape[1:])
    pref = lax.all_to_all(sent, REQ, 0, 0, tiled=True)

    meta = token_table(lengths[0], prefix_map[0], plane_x * (PAIRS * ROWS) - ROWS)
    blocks = project(tokens, attn_gain, w_query, w_key, w_value)
    qkv = lax.all_to_all(blocks, PLANE, 0, 0, tiled=True)
    up = [(i, (i + 1) % count_x) for i in range(count_x)]
    down = [(j, i) for i, j in up]
    before = lax.ppermute(qkv[PAIRS - 1, 1:], "x", up)
    after = lax.ppermute(qkv[0, 1:], "x", down)
    mixed = attend(pair, rel_bias, qkv, jnp.stack([before, after]), pref, meta)
    att = lax.all_to_all(mixed, PLANE, 0, 0, tiled=True)
    hidden, normed = join(att, w_attn_out, tokens, mlp_gain)

    other = lax.ppermute(normed, "core", SWAP)
    far = lax.ppermute(normed, ("yhi", "ylo"), MIRROR)
    far_other = lax.ppermute(far, "core", SWAP)
    mine, theirs = feed(normed, other, w_in, w_out)
    far_mine, far_theirs = feed(far, far_other, w_in, w_out)
    far_sum = far_mine.astype(jnp.float32) + lax.ppermute(far_theirs, "core", SWAP).astype(jnp.float32)
    back = lax.ppermute(far_sum.astype(jnp.bfloat16), ("yhi", "ylo"), MIRROR)
    local = mine.astype(jnp.float32) + lax.ppermute(theirs, "core", SWAP).astype(jnp.float32)
    return (hidden.astype(jnp.float32) + (local + back.astype(jnp.float32))).astype(jnp.bfloat16)


def solution(mesh):
    split = Mesh(mesh.devices.reshape(2, 2, 4, 4, 2), AXES)
    grp, req = ("yhi", "core"), REQ
    return jax.shard_map(
        body,
        mesh=split,
        in_specs=(
            P(grp + req, None),
            P(),
            P(),
            P(),
            P(),
            P(),
            P(),
            P(grp, req, None),
            P(grp, None),
            P(grp, None),
            P(),
            P(grp, None),
            P(grp, None),
        ),
        out_specs=P(grp + req, None),
        check_vma=False,
    )
```

time: 309 us -> 101 us (0.33)
  waiting for transfers between devices: 164 us -> 33.8 us
  local copies, waits for them, and re-layouts: 78 us -> 4.25 us
  matrix products: 31 us -> 0 us
  Pallas kernels: 0 us -> 26.6 us
  starting transfers between devices: 6.85 us -> 20.9 us
  between operations: 13.5 us -> 0.15 us
  blocking collectives: 0 us -> 11.3 us
  other arithmetic: 14.2 us -> 3.58 us
    all_gather x2 -> x0, waiting for transfers between devices: 132 us -> none  [the longest x1 114 us: body(): shard_kv = lax.all_gather(prefix_cache, 'req', axis=1, tiled=True)]
    reduce_scatter x1 -> x0, waiting for transfers between devices: 31.4 us -> none  [body(): lax.psum_scatter(feed_forward(gathered, w_in, w_out).astype(jnp.bfloat16)...]
    dot_general x19 -> x0, matrix products: 31 us -> none  [the longest x4 8.1 us: bias_lookup(): jnp.einsum('qkb,bh->hqk', one_hot, rel_bias, precision=lax.Precision.HIGH...]
    pallas_call x0 -> x5, Pallas kernels: none -> 26.6 us  [the longest x1 9.23 us: attend(): pl.pallas_call(attend_kernel, grid=(PAIRS,), in_specs=[smem, smem, whole(...]
    slice x11 -> x0, local copies, waits for them, and re-layouts: 26.3 us -> none  [the longest x3 15.4 us: body(): value_rows = block[:, :, D:].reshape(-1, H, DK)]
    ppermute x2 -> x8, waiting for transfers between devices: 0.01 us -> 19.9 us  [the longest x1 7.26 us: body(): back = lax.ppermute(far_sum.astype(jnp.bfloat16), ('yhi', 'ylo'), MIRROR)]
    all_to_all x0 -> x2, waiting for transfers between devices: none -> 13.9 us  [the longest x1 12.1 us: body(): qkv = lax.all_to_all(blocks, PLANE, 0, 0, tiled=True)]
    unnamed x57 -> x24, local copies, waits for them, and re-layouts: 15.5 us -> 2.95 us
  transfers between devices with their start and end apart: 5 -> 10, of which waited for: 3 -> 7; matrix products, arithmetic and copies ran while one was open for 17% -> 3% of each run, Pallas kernels for 0% -> 9%
where the time goes in v1:
time: 101 us
  waiting for transfers between devices  33.8 us (33%)
  Pallas kernels  26.6 us (26%)
  starting transfers between devices  20.9 us (21%)
  blocking collectives  11.3 us (11%)
  local copies, waits for them, and re-layouts  4.25 us (4%)
  other arithmetic  3.58 us (4%)
    all_to_all x1, waiting for transfers between devices, body(): qkv = lax.all_to_all(blocks, PLANE, 0, 0, tiled=True)  12.1 us
    all_to_all x1, blocking collectives, body(): att = lax.all_to_all(mixed, PLANE, 0, 0, tiled=True)  11.3 us
    pallas_call x1, Pallas kernels, attend(): pl.pallas_call(attend_kernel, grid=(PAIRS,), in_specs=[smem, smem, whole(...  9.23 us
    pallas_call x2, Pallas kernels, feed(): pl.pallas_call(feed_kernel, out_shape=(shape, shape), compiler_params=plt...  8.94 us
    ppermute x1, waiting for transfers between devices, body(): back = lax.ppermute(far_sum.astype(jnp.bfloat16), ('yhi', 'ylo'), MIRROR)  7.26 us
    all_to_all x1, starting transfers between devices, body(): qkv = lax.all_to_all(blocks, PLANE, 0, 0, tiled=True)  6.56 us
    all_to_all x1, starting transfers between devices, body(): pref = lax.all_to_all(sent, REQ, 0, 0, tiled=True)  5.58 us
    ppermute x1, waiting for transfers between devices, body(): far = lax.ppermute(normed, ('yhi', 'ylo'), MIRROR)  5.5 us
  transfers between devices with their start and end apart: 10, of which 7 were waited for; matrix products, arithmetic and copies ran while one was open for 3% of the time, Pallas kernels for 9%

profile of v1, /device:TPU:0, one launch (start us, length us, event | category | flops | bytes accessed | tf_op | source)
XLA Modules:
  0.0 100.6 jit_solution(8930120003307312684)
XLA Ops:
  0.0 5.4 %project.1 = bf16[8,3,128,128]{3,2,1,0:T(8,128)(2,1)} custom-call(bf16[128,1024]{1,0:T(8,128)(2,1)} %tok_ref.3, f32[1,1024]{1,0:T(1,128)} %bitcast.26, bf16[1024,1024]{1,0:T(8,128)(2,1)} %wq_ref.1, bf16[1024,1024]{1,0:T(8,128)(2,1)} %wk_ref.1, bf16[1024,1024]{1,0:T(8,128)(2,1)} %wv_ref.1), custom_call_target="tpu_custom_call" | custom-call | tf_op jit(solution)/shard_map/project/pallas_call | solution.py:54
  5.5 6.6 %all-to-all-start = ((bf16[8,3,128,128]{3,2,1,0:T(8,128)(2,1)}), bf16[8,3,128,128]{3,2,1,0:T(8,128)(2,1)S(1)}, u32[]{:S(2)}, u32[]{:S(2)}) async-start(bf16[8,3,128,128]{3,2,1,0:T(8,128)(2,1)} %project.1), calls=%async_computation | async-start | bytes 1572864 | tf_op jit(solution)/shard_map/all_to_all | solution.py:268
  12.0 0.0 copy-done.7
  12.1 0.0 copy-done.9
  12.1 0.1 copy.21
  12.2 0.1 reduce-window.7
  12.3 0.1 reduce
  12.4 0.0 copy-done.10
  12.4 0.2 select_reduce_fusion
  12.7 0.1 stack.26
  12.8 12.1 %all-to-all-done.qkv_ref = bf16[8,3,128,128]{3,2,1,0:T(8,128)(2,1)S(1)} async-done(((bf16[8,3,128,128]{3,2,1,0:T(8,128)(2,1)}), bf16[8,3,128,128]{3,2,1,0:T(8,128)(2,1)S(1)}, u32[]{:S(2)}, u32[]{:S(2)}) %all-to-all-start) | async-done | bytes 786464 | tf_op jit(solution)/shard_map/all_to_all | solution.py:268
  24.9 1.0 %broadcast_in_dim.2 = bf16[4,8,2,2,16,128]{5,4,3,2,1,0:T(8,128)(2,1)} broadcast(bf16[8,2,2,16,128]{4,3,2,1,0:T(8,128)(2,1)S(1)} %copy.20), dimensions={1,2,3,4,5} | broadcast | bytes 655360 | tf_op jit(solution)/shard_map/broadcast_in_dim | solution.py:263
  26.0 5.6 %all-to-all-start.1 = ((bf16[32,2,2,16,128]{4,3,2,1,0:T(8,128)(2,1)}), bf16[32,2,2,16,128]{4,3,2,1,0:T(8,128)(2,1)S(1)}, u32[]{:S(2)}, u32[]{:S(2)}) async-start(bf16[32,2,2,16,128]{4,3,2,1,0:T(8,128)(2,1)} %bitcast.7), calls=%async_computation.1 | async-start | bytes 1048576 | tf_op jit(solution)/shard_map/all_to_all | solution.py:264
  31.6 3.1 %collective-permute-start.1 = (bf16[2,128,128]{2,1,0:T(8,128)(2,1)S(1)}, bf16[2,128,128]{2,1,0:T(8,128)(2,1)S(1)}, u32[]{:S(2)}, u32[]{:S(2)}) collective-permute-start(bf16[2,128,128]{2,1,0:T(8,128)(2,1)S(1)} %get-tuple-element.21), channel_id=1, source_target_pairs={{8,0},{16,8},{24,16},{0,24},{9,1},{17,9},{25,17},{1,25},{10,2},{18... | collective-permute-start | bytes 196616 | tf_op jit(solution)/shard_map/ppermute | solution.py:272
  34.7 0.0 collective-permute-start
  34.7 0.6 convert_bitcast_fusion.meta_ref
  35.3 0.0 copy-done.8
  35.3 0.7 copy.22.rel_ref
  36.0 4.5 %collective-permute-done.1 = bf16[2,128,128]{2,1,0:T(8,128)(2,1)S(1)} collective-permute-done((bf16[2,128,128]{2,1,0:T(8,128)(2,1)S(1)}, bf16[2,128,128]{2,1,0:T(8,128)(2,1)S(1)}, u32[]{:S(2)}, u32[]{:S(2)}) %collective-permute-start.1) | collective-permute-done | bytes 65568 | tf_op jit(solution)/shard_map/ppermute | solution.py:272
  40.4 1.3 %collective-permute-done = bf16[2,128,128]{2,1,0:T(8,128)(2,1)S(1)} collective-permute-done((bf16[2,128,128]{2,1,0:T(8,128)(2,1)S(1)}, bf16[2,128,128]{2,1,0:T(8,128)(2,1)S(1)}, u32[]{:S(2)}, u32[]{:S(2)}) %collective-permute-start) | collective-permute-done | bytes 65568 | tf_op jit(solution)/shard_map/ppermute | solution.py:271
  41.7 0.7 pad_maximum_fusion.halo_ref
  42.4 1.8 %all-to-all-done.1.pref_ref = bf16[32,2,2,16,128]{4,3,2,1,0:T(8,128)(2,1)S(1)} async-done(((bf16[32,2,2,16,128]{4,3,2,1,0:T(8,128)(2,1)}), bf16[32,2,2,16,128]{4,3,2,1,0:T(8,128)(2,1)S(1)}, u32[]{:S(2)}, u32[]{:S(2)}) %all-to-all-start.1) | async-done | bytes 524320 | tf_op jit(solution)/shard_map/all_to_all | solution.py:264
  44.1 0.0 copy-done
  44.2 0.8 copy-done.1
  45.0 9.2 %attend.1 = bf16[8,128,128]{2,1,0:T(8,128)(2,1)} custom-call(s32[1]{0:T(128)} %bitcast.pair_ref, f32[32,16]{1,0:T(8,128)} %copy.22.rel_ref, bf16[8,3,128,128]{3,2,1,0:T(8,128)(2,1)} %copy-done, bf16[2,2,128,128]{3,2,1,0:T(8,128)(2,1)} %pad_maximum_fusion.halo_ref, bf16[32,2,2,16,128]{4,3,2,1,0:T(8,128)(2,1)} %copy-done.1, ...), custom_call_target="tpu_custom_call" | custom-call | tf_op jit(solution)/shard_map/attend/pallas_call | solution.py:172
  54.2 11.3 %all_to_all.15.att_ref = bf16[8,128,128]{2,1,0:T(8,128)(2,1)} all-to-all(bf16[8,128,128]{2,1,0:T(8,128)(2,1)} %attend.1), channel_id=1, replica_groups=mesh['yhi'=2,'core'=2,'x'=4,'z'=4,'ylo'=2] {'z','ylo'}, dimensions={0} | all-to-all | bytes 524288 | tf_op jit(solution)/shard_map/all_to_all | solution.py:274
  65.5 3.0 %join.1 = (bf16[128,1024]{1,0:T(8,128)(2,1)}, bf16[128,1024]{1,0:T(8,128)(2,1)}) custom-call(bf16[8,128,128]{2,1,0:T(8,128)(2,1)} %all_to_all.15.att_ref, bf16[1024,1024]{1,0:T(8,128)(2,1)} %w_ref.1, bf16[128,1024]{1,0:T(8,128)(2,1)} %tok_ref.3, f32[1,1024]{1,0:T(1,128)} %bitcast.27), custom_call_target="tpu_custom_call" | custom-call | tf_op jit(solution)/shard_map/join/pallas_call | solution.py:214
  68.5 2.3 %collective-permute-start.4 = (bf16[128,1024]{1,0:T(8,128)(2,1)}, bf16[128,1024]{1,0:T(8,128)(2,1)S(1)}, u32[]{:S(2)}, u32[]{:S(2)}) collective-permute-start(bf16[128,1024]{1,0:T(8,128)(2,1)} %get-tuple-element.12.one_ref), channel_id=1, source_target_pairs={{0,65},{65,0},{1,64},{64,1},{2,67},{67,2},{3,66},{66,3},{4,69},{69... | collective-permute-start | bytes 786440 | tf_op jit(solution)/shard_map/ppermute | solution.py:278
  70.8 5.5 %collective-permute-done.4.one_ref = bf16[128,1024]{1,0:T(8,128)(2,1)S(1)} collective-permute-done((bf16[128,1024]{1,0:T(8,128)(2,1)}, bf16[128,1024]{1,0:T(8,128)(2,1)S(1)}, u32[]{:S(2)}, u32[]{:S(2)}) %collective-permute-start.4) | collective-permute-done | bytes 262176 | tf_op jit(solution)/shard_map/ppermute | solution.py:278
  76.3 0.0 collective-permute-start.5
  76.3 0.5 collective-permute-start.2
  76.8 1.4 %collective-permute-done.5.two_ref = bf16[128,1024]{1,0:T(8,128)(2,1)S(1)} collective-permute-done((bf16[128,1024]{1,0:T(8,128)(2,1)S(1)}, bf16[128,1024]{1,0:T(8,128)(2,1)S(1)}, u32[]{:S(2)}, u32[]{:S(2)}) %collective-permute-start.5) | collective-permute-done | bytes 262176 | tf_op jit(solution)/shard_map/ppermute | solution.py:279
  78.1 0.0 copy-done.5
  78.1 0.7 copy-done.6
  78.9 4.5 %feed.3 = (bf16[128,1024]{1,0:T(8,128)(2,1)}, bf16[128,1024]{1,0:T(8,128)(2,1)}) custom-call(bf16[128,1024]{1,0:T(8,128)(2,1)} %copy-done.5, bf16[128,1024]{1,0:T(8,128)(2,1)} %copy-done.6, bf16[1024,1024]{1,0:T(8,128)(2,1)} %in_ref.3, bf16[1024,1024]{1,0:T(8,128)(2,1)} %out_ref.3), custom_call_target="tpu_custom_call" | custom-call | tf_op jit(solution)/shard_map/feed/pallas_call | solution.py:235
  83.3 0.1 collective-permute-start.6
  83.5 0.0 collective-permute-done.2.two_ref
  83.5 0.7 copy-done.4
  84.2 4.5 %feed.2 = (bf16[128,1024]{1,0:T(8,128)(2,1)}, bf16[128,1024]{1,0:T(8,128)(2,1)}) custom-call(bf16[128,1024]{1,0:T(8,128)(2,1)} %get-tuple-element.12.one_ref, bf16[128,1024]{1,0:T(8,128)(2,1)} %copy-done.4, bf16[1024,1024]{1,0:T(8,128)(2,1)} %in_ref.3, bf16[1024,1024]{1,0:T(8,128)(2,1)} %out_ref.3), custom_call_target="tpu_custom_call" | custom-call | tf_op jit(solution)/shard_map/feed/pallas_call | solution.py:235
  88.7 0.4 collective-permute-start.3
  89.0 0.0 collective-permute-done.6
  89.0 0.0 copy-done.3
  89.0 0.1 add_convert_fusion.1
  89.1 2.4 %collective-permute-start.7 = (bf16[128,1024]{1,0:T(8,128)(2,1)S(1)}, bf16[128,1024]{1,0:T(8,128)(2,1)S(1)}, u32[]{:S(2)}, u32[]{:S(2)}) collective-permute-start(bf16[128,1024]{1,0:T(8,128)(2,1)S(1)} %add_convert_fusion.1), channel_id=1, source_target_pairs={{0,65},{65,0},{1,64},{64,1},{2,67},{67,2},{3,66},{66,3},{4,69},{69... | collective-permute-start | bytes 786440 | tf_op jit(solution)/shard_map/ppermute | solution.py:283
  91.5 0.0 collective-permute-done.3
  91.5 7.3 %collective-permute-done.7 = bf16[128,1024]{1,0:T(8,128)(2,1)S(1)} collective-permute-done((bf16[128,1024]{1,0:T(8,128)(2,1)S(1)}, bf16[128,1024]{1,0:T(8,128)(2,1)S(1)}, u32[]{:S(2)}, u32[]{:S(2)}) %collective-permute-start.7) | collective-permute-done | bytes 262176 | tf_op jit(solution)/shard_map/ppermute | solution.py:283
  98.7 0.0 copy-done.2
  98.7 1.8 %add_convert_fusion = bf16[128,1024]{1,0:T(8,128)(2,1)} fusion(bf16[128,1024]{1,0:T(8,128)(2,1)S(1)} %collective-permute-done.7, bf16[128,1024]{1,0:T(8,128)(2,1)S(1)} %collective-permute-done.3, bf16[128,1024]{1,0:T(8,128)(2,1)} %get-tuple-element.13, bf16[128,1024]{1,0:T(8,128)(2,1)S(1)} %copy-done.2), kind=kLoop, calls=%fused_computation | loop fusion | flops 1048576 | bytes 1310720 | tf_op jit(solution)/shard_map/convert_element_type | solution.py:285
  (21 shorter events, 0.1 us)
Async XLA Ops:
  0.0 12.0 %copy-start.7 = (bf16[2,16,2048]{2,1,0:T(8,128)(2,1)S(1)}, bf16[2,16,2048]{2,1,0:T(8,128)(2,1)}, u32[]{:S(2)}) copy-start(bf16[2,16,2048]{2,1,0:T(8,128)(2,1)} %param.20) | copy-start | bytes 393220
  5.4 6.7 %copy-start.9 = (s32[1,64]{1,0:T(1,128)S(1)}, s32[1,64]{1,0:T(1,128)}, u32[]{:S(2)}) copy-start(s32[1,64]{1,0:T(1,128)} %param.21) | copy-start | bytes 772
  5.4 7.0 %copy-start.10 = (s32[1,64]{1,0:T(1,128)S(1)}, s32[1,64]{1,0:T(1,128)}, u32[]{:S(2)}) copy-start(s32[1,64]{1,0:T(1,128)} %param.22) | copy-start | bytes 772
  5.5 29.8 %copy-start.8 = (f32[32,16]{0,1:T(8,128)S(1)}, f32[32,16]{0,1:T(8,128)}, u32[]{:S(2)}) copy-start(f32[32,16]{0,1:T(8,128)} %param.19) | copy-start | bytes 6148
  5.5 19.4 %all-to-all-start = ((bf16[8,3,128,128]{3,2,1,0:T(8,128)(2,1)}), bf16[8,3,128,128]{3,2,1,0:T(8,128)(2,1)S(1)}, u32[]{:S(2)}, u32[]{:S(2)}) async-start(bf16[8,3,128,128]{3,2,1,0:T(8,128)(2,1)} %project.1), calls=%async_computation | async-start | bytes 1572864 | tf_op jit(solution)/shard_map/all_to_all | solution.py:268
  24.9 19.2 %copy-start = (bf16[8,3,128,128]{3,2,1,0:T(8,128)(2,1)}, bf16[8,3,128,128]{3,2,1,0:T(8,128)(2,1)S(1)}, u32[]{:S(2)}) copy-start(bf16[8,3,128,128]{3,2,1,0:T(8,128)(2,1)S(1)} %all-to-all-done.qkv_ref) | copy-start | bytes 2359300
  26.0 18.2 %all-to-all-start.1 = ((bf16[32,2,2,16,128]{4,3,2,1,0:T(8,128)(2,1)}), bf16[32,2,2,16,128]{4,3,2,1,0:T(8,128)(2,1)S(1)}, u32[]{:S(2)}, u32[]{:S(2)}) async-start(bf16[32,2,2,16,128]{4,3,2,1,0:T(8,128)(2,1)} %bitcast.7), calls=%async_computation.1 | async-start | bytes 1048576 | tf_op jit(solution)/shard_map/all_to_all | solution.py:264
  31.6 8.9 %collective-permute-start.1 = (bf16[2,128,128]{2,1,0:T(8,128)(2,1)S(1)}, bf16[2,128,128]{2,1,0:T(8,128)(2,1)S(1)}, u32[]{:S(2)}, u32[]{:S(2)}) collective-permute-start(bf16[2,128,128]{2,1,0:T(8,128)(2,1)S(1)} %get-tuple-element.21), channel_id=1, source_target_pairs={{8,0},{16,8},{24,16},{0,24},{9,1},{17,9},{25,17},{1,25},{10,2},{18... | collective-permute-start | bytes 196616 | tf_op jit(solution)/shard_map/ppermute | solution.py:272
  34.7 7.0 %collective-permute-start = (bf16[2,128,128]{2,1,0:T(8,128)(2,1)S(1)}, bf16[2,128,128]{2,1,0:T(8,128)(2,1)S(1)}, u32[]{:S(2)}, u32[]{:S(2)}) collective-permute-start(bf16[2,128,128]{2,1,0:T(8,128)(2,1)S(1)} %get-tuple-element.20), channel_id=1, source_target_pairs={{0,8},{8,16},{16,24},{24,0},{1,9},{9,17},{17,25},{25,1},{2,10},{10... | collective-permute-start | bytes 196616 | tf_op jit(solution)/shard_map/ppermute | solution.py:271
  44.1 0.8 copy-start.1
  68.5 7.8 %collective-permute-start.4 = (bf16[128,1024]{1,0:T(8,128)(2,1)}, bf16[128,1024]{1,0:T(8,128)(2,1)S(1)}, u32[]{:S(2)}, u32[]{:S(2)}) collective-permute-start(bf16[128,1024]{1,0:T(8,128)(2,1)} %get-tuple-element.12.one_ref), channel_id=1, source_target_pairs={{0,65},{65,0},{1,64},{64,1},{2,67},{67,2},{3,66},{66,3},{4,69},{69... | collective-permute-start | bytes 786440 | tf_op jit(solution)/shard_map/ppermute | solution.py:278
  76.3 1.9 %copy-start.5 = (bf16[128,1024]{1,0:T(8,128)(2,1)}, bf16[128,1024]{1,0:T(8,128)(2,1)S(1)}, u32[]{:S(2)}) copy-start(bf16[128,1024]{1,0:T(8,128)(2,1)S(1)} %collective-permute-done.4.one_ref) | copy-start | bytes 786436
  76.3 1.9 %collective-permute-start.5 = (bf16[128,1024]{1,0:T(8,128)(2,1)S(1)}, bf16[128,1024]{1,0:T(8,128)(2,1)S(1)}, u32[]{:S(2)}, u32[]{:S(2)}) collective-permute-start(bf16[128,1024]{1,0:T(8,128)(2,1)S(1)} %collective-permute-done.4.one_ref), channel_id=1, source_target_pairs={{0,32},{32,0},{1,33},{33,1},{2,34},{34,2},{3,35},{35,3},{4,36},{36... | collective-permute-start | bytes 786440 | tf_op jit(solution)/shard_map/ppermute | solution.py:279
  76.3 7.2 %collective-permute-start.2 = (bf16[128,1024]{1,0:T(8,128)(2,1)}, bf16[128,1024]{1,0:T(8,128)(2,1)S(1)}, u32[]{:S(2)}, u32[]{:S(2)}) collective-permute-start(bf16[128,1024]{1,0:T(8,128)(2,1)} %get-tuple-element.12.one_ref), channel_id=1, source_target_pairs={{0,32},{32,0},{1,33},{33,1},{2,34},{34,2},{3,35},{35,3},{4,36},{36... | collective-permute-start | bytes 786440 | tf_op jit(solution)/shard_map/ppermute | solution.py:277
  78.1 0.7 copy-start.6
  83.3 5.7 %copy-start.3 = (bf16[128,1024]{1,0:T(8,128)(2,1)S(1)}, bf16[128,1024]{1,0:T(8,128)(2,1)}, u32[]{:S(2)}) copy-start(bf16[128,1024]{1,0:T(8,128)(2,1)} %get-tuple-element.15) | copy-start | bytes 786436
  83.3 15.4 %copy-start.2 = (bf16[128,1024]{1,0:T(8,128)(2,1)S(1)}, bf16[128,1024]{1,0:T(8,128)(2,1)}, u32[]{:S(2)}) copy-start(bf16[128,1024]{1,0:T(8,128)(2,1)} %get-tuple-element.11) | copy-start | bytes 786436
  83.3 5.7 %collective-permute-start.6 = (bf16[128,1024]{1,0:T(8,128)(2,1)}, bf16[128,1024]{1,0:T(8,128)(2,1)S(1)}, u32[]{:S(2)}, u32[]{:S(2)}) collective-permute-start(bf16[128,1024]{1,0:T(8,128)(2,1)} %get-tuple-element.16), channel_id=1, source_target_pairs={{0,32},{32,0},{1,33},{33,1},{2,34},{34,2},{3,35},{35,3},{4,36},{36... | collective-permute-start | bytes 786440 | tf_op jit(solution)/shard_map/ppermute | solution.py:282
  83.5 0.7 copy-start.4
  88.7 2.8 %collective-permute-start.3 = (bf16[128,1024]{1,0:T(8,128)(2,1)}, bf16[128,1024]{1,0:T(8,128)(2,1)S(1)}, u32[]{:S(2)}, u32[]{:S(2)}) collective-permute-start(bf16[128,1024]{1,0:T(8,128)(2,1)} %get-tuple-element.14), channel_id=1, source_target_pairs={{0,32},{32,0},{1,33},{33,1},{2,34},{34,2},{3,35},{35,3},{4,36},{36... | collective-permute-start | bytes 786440 | tf_op jit(solution)/shard_map/ppermute | solution.py:284
  89.1 9.6 %collective-permute-start.7 = (bf16[128,1024]{1,0:T(8,128)(2,1)S(1)}, bf16[128,1024]{1,0:T(8,128)(2,1)S(1)}, u32[]{:S(2)}, u32[]{:S(2)}) collective-permute-start(bf16[128,1024]{1,0:T(8,128)(2,1)S(1)} %add_convert_fusion.1), channel_id=1, source_target_pairs={{0,65},{65,0},{1,64},{64,1},{2,67},{67,2},{3,66},{66,3},{4,69},{69... | collective-permute-start | bytes 786440 | tf_op jit(solution)/shard_map/ppermute | solution.py:283

commit v2 on v1

v2 whole, which is shorter than its diff:
```python
import functools

import jax
import jax.numpy as jnp
from jax import lax
from jax.experimental import pallas as pl
from jax.experimental.pallas import tpu as pltpu
from jax.sharding import Mesh, PartitionSpec as P

D = 1024
H = 16
DK = 64
PLEN = 512
PREF_GRP = 2
ROWS = 128
PAIRS = 8
LANES = 128

epsilon = 1e-06
far_marks = (12, 16, 23, 32, 46, 64, 91)
masked_score = -1e30
VMEM_LIMIT = 16 * 1024 * 1024

AXES = ("yhi", "core", "x", "z", "ylo")
REQ = ("x", "z", "ylo")
PLANE = ("z", "ylo")
MIRROR = [(0, 3), (3, 0), (1, 2), (2, 1)]
SWAP = [(0, 1), (1, 0)]


def norm_rows(values_in, gain):
    widened = values_in.astype(jnp.float32)
    scale = lax.rsqrt(jnp.mean(widened * widened, axis=-1, keepdims=True) + epsilon)
    return (widened * scale * gain).astype(jnp.bfloat16)


def on_chip(*arrays):
    return tuple(pltpu.with_memory_space_constraint(a, pltpu.VMEM) for a in arrays)


VMEM_SPEC = pl.BlockSpec(memory_space=pltpu.VMEM)
SMEM_SPEC = pl.BlockSpec(memory_space=pltpu.SMEM)


def project_kernel(tok_ref, gain_ref, wq_ref, wk_ref, wv_ref, out_ref):
    normed = norm_rows(tok_ref[...], gain_ref[...])
    for kind, w_ref in enumerate((wq_ref, wk_ref, wv_ref)):
        got = jnp.dot(normed, w_ref[...], preferred_element_type=jnp.float32)
        got = got.astype(jnp.bfloat16)
        for part in range(PAIRS):
            out_ref[part, kind] = got[:, part * LANES : (part + 1) * LANES]


def project(tokens, gain, w_query, w_key, w_value):
    return pl.pallas_call(
        project_kernel,
        in_specs=[VMEM_SPEC] * 5,
        out_specs=VMEM_SPEC,
        out_shape=jax.ShapeDtypeStruct((PAIRS, 3, ROWS, LANES), jnp.bfloat16),
        compiler_params=pltpu.CompilerParams(vmem_limit_bytes=VMEM_LIMIT),
        name="project",
    )(*on_chip(tokens, gain.reshape(1, D), w_query, w_key, w_value))


def after(value, other):
    anywhere = pl.BlockSpec(memory_space=pl.ANY)
    return pl.pallas_call(
        lambda value_ref, other_ref, out_ref: None,
        in_specs=[anywhere, anywhere],
        out_specs=anywhere,
        out_shape=jax.ShapeDtypeStruct(value.shape, value.dtype),
        input_output_aliases={0: 0},
        name="after",
    )(value, other)


def bias_line(rel_ref, head, first_bucket):
    lane = lax.broadcasted_iota(jnp.int32, (ROWS, LANES), 1)
    line = jnp.full((ROWS, LANES), rel_ref[first_bucket, head], jnp.float32)
    for bucket in range(1, 16):
        mark = bucket if bucket <= 8 else far_marks[bucket - 9]
        line = jnp.where(lane >= mark, rel_ref[first_bucket + bucket, head], line)
    return line


def prepare_kernel(pair_ref, rel_ref, pref_ref, keys_ref, values_ref, near_ref, line_ref):
    row = lax.broadcasted_iota(jnp.int32, (ROWS, LANES), 0)
    lane = lax.broadcasted_iota(jnp.int32, (ROWS, LANES), 1)
    for p in range(PREF_GRP):
        keys_ref[p * LANES : (p + 1) * LANES, :] = jnp.transpose(pref_ref[:, 0, p].reshape(PLEN, LANES))
        values_ref[:, p * LANES : (p + 1) * LANES] = pref_ref[:, 1, p].reshape(PLEN, LANES)
    for h in range(2):
        head = pair_ref[0] * 2 + h
        before = bias_line(rel_ref, head, 0)
        after_it = bias_line(rel_ref, head, 16)

        def pick(line, distance):
            return jnp.take_along_axis(line, jnp.clip(distance, 0, LANES - 1), axis=1)

        rows = slice(h * ROWS, (h + 1) * ROWS)
        near_ref[rows, 0:LANES] = pick(before, row + LANES - lane)
        near_ref[rows, LANES : 2 * LANES] = jnp.where(
            lane > row, pick(after_it, lane - row), pick(before, row - lane)
        )
        near_ref[rows, 2 * LANES : 3 * LANES] = pick(after_it, lane + LANES - row)
        line_ref[rows, :] = before


def prepare(pair, rel_bias, pref):
    return pl.pallas_call(
        prepare_kernel,
        in_specs=[SMEM_SPEC, SMEM_SPEC, VMEM_SPEC],
        out_specs=(VMEM_SPEC,) * 4,
        out_shape=(
            pltpu.VMEM((PREF_GRP * LANES, PLEN), jnp.bfloat16),
            pltpu.VMEM((PLEN, PREF_GRP * LANES), jnp.bfloat16),
            pltpu.VMEM((2 * ROWS, 3 * LANES), jnp.float32),
            pltpu.VMEM((2 * ROWS, LANES), jnp.float32),
        ),
        compiler_params=pltpu.CompilerParams(vmem_limit_bytes=VMEM_LIMIT),
        name="prepare",
    )(pair, rel_bias, *on_chip(pref))


def attend_kernel(
    qkv_ref, prev_ref, next_ref, keys_ref, values_ref, near_ref, line_ref, meta_ref, out_ref, kwin, vwin
):
    lane = lax.broadcasted_iota(jnp.int32, (ROWS, LANES), 1)
    low = lane < DK
    for b in range(PAIRS + 2):
        for dst, kind in ((kwin, 0), (vwin, 1)):
            if b == 0:
                block = prev_ref[kind]
            elif b == PAIRS + 1:
                block = next_ref[kind]
            else:
                block = qkv_ref[b - 1, kind + 1]
            dst[b] = jnp.transpose(block) if kind == 0 else block

    def one(step, _):
        query = qkv_ref[step, 0]
        own = jnp.transpose(meta_ref[step + 1])
        request, offset, chosen = own[:, 0:1], own[:, 1:2], own[:, 2:3]
        zero = jnp.zeros_like(query)
        stacked = jnp.concatenate([jnp.where(low, query, zero), jnp.where(low, zero, query)], axis=0)
        second = jnp.concatenate([chosen, chosen], axis=0) > 0.5
        zeros = jnp.zeros_like(stacked)
        split = jnp.concatenate(
            [jnp.where(second, zeros, stacked), jnp.where(second, stacked, zeros)], axis=1
        )
        far_scores = jnp.dot(split, keys_ref[...], preferred_element_type=jnp.float32)
        near_keys = jnp.concatenate([kwin[step + b] for b in range(3)], axis=1)
        near_scores = jnp.dot(stacked, near_keys, preferred_element_type=jnp.float32)
        tail_at = jnp.minimum(LANES - lane + offset.astype(jnp.int32), LANES - 1)
        line = line_ref[...]
        tail = jnp.take_along_axis(line, jnp.concatenate([tail_at, tail_at], axis=0), axis=1)
        full = line[:, LANES - 1 :]
        parts = [far_scores[:, b * LANES : (b + 1) * LANES] + full for b in range(3)]
        parts.append(far_scores[:, 3 * LANES :] + tail)
        for b in range(3):
            mine = meta_ref[step + b, 0:1, :] == request
            mine = jnp.concatenate([mine, mine], axis=0)
            at = slice(b * LANES, (b + 1) * LANES)
            parts.append(jnp.where(mine, near_scores[:, at] + near_ref[:, at], masked_score))
        row_max = jnp.max(functools.reduce(jnp.maximum, parts), axis=1, keepdims=True)
        terms = [jnp.exp(part - row_max) for part in parts]
        row_sum = jnp.sum(functools.reduce(jnp.add, terms), axis=1, keepdims=True)
        weights = [t.astype(jnp.bfloat16) for t in terms]
        far_out = jnp.dot(
            jnp.concatenate(weights[:4], axis=1), values_ref[...], preferred_element_type=jnp.float32
        )
        near_values = jnp.concatenate([vwin[step + b] for b in range(3)], axis=0)
        near_out = jnp.dot(
            jnp.concatenate(weights[4:], axis=1), near_values, preferred_element_type=jnp.float32
        )
        total = jnp.where(second, far_out[:, LANES:], far_out[:, :LANES]) + near_out
        total = total / row_sum
        out_ref[step] = jnp.where(low, total[:ROWS], total[ROWS:]).astype(jnp.bfloat16)
        return 0

    lax.fori_loop(0, PAIRS, one, 0)


def attend(qkv, prev, after_it, prepared, meta):
    return pl.pallas_call(
        attend_kernel,
        in_specs=[VMEM_SPEC] * 8,
        out_specs=VMEM_SPEC,
        out_shape=pltpu.VMEM((PAIRS, ROWS, LANES), jnp.bfloat16),
        scratch_shapes=[
            pltpu.VMEM((PAIRS + 2, LANES, ROWS), jnp.bfloat16),
            pltpu.VMEM((PAIRS + 2, ROWS, LANES), jnp.bfloat16),
        ],
        compiler_params=pltpu.CompilerParams(vmem_limit_bytes=VMEM_LIMIT),
        name="attend",
    )(*on_chip(qkv, prev, after_it, *prepared, meta))


def token_table(lengths_row, prefix_row, first):
    count = (PAIRS + 2) * ROWS
    ends = jnp.cumsum(lengths_row)
    starts = ends - lengths_row
    ids = first + jnp.arange(count, dtype=jnp.int32)
    member = ((ids[None, :] >= starts[:, None]) & (ids[None, :] < ends[:, None])).astype(jnp.int32)
    numbers = jnp.arange(1, lengths_row.shape[0] + 1, dtype=jnp.int32)
    request = jnp.sum(member * numbers[:, None], axis=0) - 1
    offset = ids - jnp.sum(member * starts[:, None], axis=0)
    chosen = jnp.sum(member * prefix_row[:, None], axis=0)
    table = jnp.stack([request, offset, chosen] + [request] * 5, axis=0).astype(jnp.float32)
    return table.reshape(8, PAIRS + 2, ROWS).transpose(1, 0, 2)


def join_kernel(att_ref, w_ref, tok_ref, gain_ref, hidden_ref, normed_ref):
    attended = jnp.concatenate([att_ref[j] for j in range(PAIRS)], axis=1)
    got = jnp.dot(attended, w_ref[...], preferred_element_type=jnp.float32)
    hidden = (tok_ref[...].astype(jnp.float32) + got).astype(jnp.bfloat16)
    hidden_ref[...] = hidden
    normed_ref[...] = norm_rows(hidden, gain_ref[...])


def join(att, w_attn_out, tokens, gain):
    shape = pltpu.VMEM((ROWS, D), jnp.bfloat16)
    return pl.pallas_call(
        join_kernel,
        in_specs=[VMEM_SPEC] * 4,
        out_specs=(VMEM_SPEC,) * 2,
        out_shape=(shape, shape),
        compiler_params=pltpu.CompilerParams(vmem_limit_bytes=VMEM_LIMIT),
        name="join",
    )(*on_chip(att, w_attn_out, tokens, gain.reshape(1, D)))


def feed_kernel(one_ref, two_ref, in_ref, out_ref, first_ref, second_ref):
    two = two_ref[...] if len(two_ref.shape) == 2 else two_ref[0]
    rows = jnp.concatenate([one_ref[...], two], axis=0)
    units = lax.dot_general(
        rows, in_ref[...], (((1,), (1,)), ((), ())), preferred_element_type=jnp.float32
    )
    units = jnp.maximum(units, 0.0).astype(jnp.bfloat16)
    got = jnp.dot(units, out_ref[...], preferred_element_type=jnp.float32).astype(jnp.bfloat16)
    first_ref[...] = got[:ROWS]
    second_ref[...] = got[ROWS:]


def feed(one, two, w_in, w_out):
    shape = pltpu.VMEM((ROWS, D), jnp.bfloat16)
    return pl.pallas_call(
        feed_kernel,
        in_specs=[VMEM_SPEC] * 4,
        out_specs=(VMEM_SPEC,) * 2,
        out_shape=(shape, shape),
        compiler_params=pltpu.CompilerParams(vmem_limit_bytes=VMEM_LIMIT),
        name="feed",
    )(*on_chip(one, two, w_in, w_out))


def pack_kernel(one_ref, two_ref, out_ref):
    out_ref[0] = one_ref[...]
    out_ref[1] = two_ref[...]


def pack(one, two):
    return pl.pallas_call(
        pack_kernel,
        in_specs=[VMEM_SPEC] * 2,
        out_specs=VMEM_SPEC,
        out_shape=pltpu.VMEM((2,) + one.shape, one.dtype),
        compiler_params=pltpu.CompilerParams(vmem_limit_bytes=VMEM_LIMIT),
        name="pack",
    )(*on_chip(one, two))


def total_kernel(*refs):
    out_ref = refs[-1]
    values = [ref[...] if len(ref.shape) == 2 else ref[1] for ref in refs[:-1]]
    total = functools.reduce(jnp.add, [value.astype(jnp.float32) for value in values])
    out_ref[...] = total.astype(out_ref.dtype)


def total(dtype, *arrays, last=False):
    return pl.pallas_call(
        total_kernel,
        in_specs=[VMEM_SPEC] * len(arrays),
        out_specs=VMEM_SPEC,
        out_shape=(jax.ShapeDtypeStruct if last else pltpu.VMEM)(arrays[0].shape, dtype),
        compiler_params=pltpu.CompilerParams(vmem_limit_bytes=VMEM_LIMIT),
        name="total",
    )(*on_chip(*arrays))


def body(
    tokens,
    attn_gain,
    w_query,
    w_key,
    w_value,
    w_attn_out,
    rel_bias,
    prefix_cache,
    lengths,
    prefix_map,
    mlp_gain,
    w_in,
    w_out,
):
    plane_x = lax.axis_index("x")
    count_x = lax.axis_size("x")
    pair = (lax.axis_index("z") * 2 + lax.axis_index("ylo")).astype(jnp.int32).reshape(1)

    held = prefix_cache.reshape(PREF_GRP, -1, 2, PAIRS, LANES).transpose(3, 2, 0, 1, 4)
    sent = jnp.broadcast_to(held[None], (count_x,) + held.shape).reshape((-1,) + held.shape[1:])
    pref = lax.all_to_all(sent, REQ, 0, 0, tiled=True)

    meta = token_table(lengths[0], prefix_map[0], plane_x * (PAIRS * ROWS) - ROWS)
    blocks = after(project(tokens, attn_gain, w_query, w_key, w_value), pref[0, 0, 0])
    qkv = lax.all_to_all(blocks, PLANE, 0, 0, tiled=True)
    prepared = prepare(pair, rel_bias, pref)
    up = [(i, (i + 1) % count_x) for i in range(count_x)]
    down = [(j, i) for i, j in up]
    before = lax.ppermute(qkv[PAIRS - 1, 1:], "x", up)
    later = lax.ppermute(qkv[0, 1:], "x", down)
    mixed = attend(qkv, before, later, prepared, meta)
    att = lax.all_to_all(mixed, PLANE, 0, 0, tiled=True)
    hidden, normed = join(att, w_attn_out, tokens, mlp_gain)

    mirrored = ("yhi", "ylo")
    far = lax.ppermute(normed, mirrored, MIRROR)
    other = lax.ppermute(normed, "core", SWAP)
    mine, theirs = feed(normed, other, w_in, w_out)
    pair_swap = lax.ppermute(pack(far, theirs), "core", SWAP)
    far_mine, far_theirs = feed(far, pair_swap, w_in, w_out)
    far_sum = total(jnp.bfloat16, far_mine, lax.ppermute(far_theirs, "core", SWAP))
    back = lax.ppermute(far_sum, mirrored, MIRROR)
    local = total(jnp.float32, hidden, mine, pair_swap)
    return total(jnp.bfloat16, local, back, last=True)


def solution(mesh):
    split = Mesh(mesh.devices.reshape(2, 2, 4, 4, 2), AXES)
    grp, req = ("yhi", "core"), REQ
    return jax.shard_map(
        body,
        mesh=split,
        in_specs=(
            P(grp + req, None),
            P(),
            P(),
            P(),
            P(),
            P(),
            P(),
            P(grp, req, None),
            P(grp, None),
            P(grp, None),
            P(),
            P(grp, None),
            P(grp, None),
        ),
        out_specs=P(grp + req, None),
        check_vma=False,
    )
```

time: 101 us -> 89.9 us (0.89)
  Pallas kernels: 26.6 us -> 14 us
  local copies, waits for them, and re-layouts: 4.25 us -> 8.3 us
  other arithmetic: 3.58 us -> 1.2 us
  blocking collectives: 11.3 us -> 9.83 us
    pallas_call x5 -> x11, Pallas kernels: 26.6 us -> 14 us  [the longest x1 7.58 us: attend(): pl.pallas_call(attend_kernel, in_specs=[VMEM_SPEC] * 8, out_specs=VMEM_SP...]
    all_to_all x1, waiting for transfers between devices: 1.79 us -> 6.52 us  [body(): pref = lax.all_to_all(sent, REQ, 0, 0, tiled=True)]
    all_to_all x1, starting transfers between devices: 5.58 us -> 9.27 us  [body(): pref = lax.all_to_all(sent, REQ, 0, 0, tiled=True)]
    all_to_all x1, starting transfers between devices: 6.56 us -> 3.55 us  [body(): qkv = lax.all_to_all(blocks, PLANE, 0, 0, tiled=True)]
    unnamed x24 -> x30, local copies, waits for them, and re-layouts: 2.95 us -> 5.26 us
    convert_element_type x2 -> x0, other arithmetic: 1.88 us -> none  [the longest x1 1.82 us: body(): (hidden.astype(jnp.float32) + (local + back.astype(jnp.float32))).astype(...]
    ppermute x6 -> x5, waiting for transfers between devices: 18.6 us -> 16.7 us  [the longest x1 7.17 us: body(): back = lax.ppermute(far_sum, mirrored, MIRROR)]
    all_to_all x1, waiting for transfers between devices: 12.1 us -> 10.6 us  [body(): qkv = lax.all_to_all(blocks, PLANE, 0, 0, tiled=True)]
  transfers between devices with their start and end apart: 10 -> 9, of which waited for: 7 -> 7; matrix products, arithmetic and copies ran while one was open for 3% -> 2% of each run, Pallas kernels for 9% -> 4%
where the time goes in v2:
time: 89.9 us; the launch traced here: 88.9 us
  waiting for transfers between devices  34.1 us (38%)
  starting transfers between devices  21.2 us (24%)
  Pallas kernels  14 us (16%)
  blocking collectives  9.83 us (11%)
  local copies, waits for them, and re-layouts  8.3 us (9%)
  other arithmetic  1.2 us (1%)
    all_to_all x1, waiting for transfers between devices, body(): qkv = lax.all_to_all(blocks, PLANE, 0, 0, tiled=True)  10.6 us
    all_to_all x1, blocking collectives, body(): att = lax.all_to_all(mixed, PLANE, 0, 0, tiled=True)  9.83 us
    all_to_all x1, starting transfers between devices, body(): pref = lax.all_to_all(sent, REQ, 0, 0, tiled=True)  9.27 us
    pallas_call x1, Pallas kernels, attend(): pl.pallas_call(attend_kernel, in_specs=[VMEM_SPEC] * 8, out_specs=VMEM_SP...  7.58 us
    ppermute x1, waiting for transfers between devices, body(): back = lax.ppermute(far_sum, mirrored, MIRROR)  7.17 us
    all_to_all x1, waiting for transfers between devices, body(): pref = lax.all_to_all(sent, REQ, 0, 0, tiled=True)  6.52 us
    ppermute x1, waiting for transfers between devices, body(): far = lax.ppermute(normed, mirrored, MIRROR)  6.25 us
    unnamed x30, local copies, waits for them, and re-layouts  5.26 us
  transfers between devices with their start and end apart: 9, of which 7 were waited for; matrix products, arithmetic and copies ran while one was open for 2% of the time, Pallas kernels for 4%

profile of v2, /device:TPU:0, one launch (start us, length us, event | category | flops | bytes accessed | tf_op | source)
XLA Modules:
  0.0 88.9 jit_solution(11430847826693648606)
XLA Ops:
  0.0 1.1 %copy.24 = bf16[4,8,16,128]{3,2,1,0:T(8,128)(2,1)S(1)} copy(bf16[4,8,16,128]{3,1,2,0:T(8,128)(2,1)} %bitcast.25) | data formatting | bytes 262144
  1.1 0.9 %broadcast_in_dim.2 = bf16[4,8,2,2,16,128]{5,4,3,2,1,0:T(8,128)(2,1)} broadcast(bf16[8,2,2,16,128]{4,3,2,1,0:T(8,128)(2,1)S(1)} %copy.21), dimensions={1,2,3,4,5} | broadcast | bytes 655360 | tf_op jit(solution)/shard_map/broadcast_in_dim | solution.py:311
  2.1 9.3 %all-to-all-start = ((bf16[32,2,2,16,128]{4,3,2,1,0:T(8,128)(2,1)}), bf16[32,2,2,16,128]{4,3,2,1,0:T(8,128)(2,1)S(1)}, u32[]{:S(2)}, u32[]{:S(2)}) async-start(bf16[32,2,2,16,128]{4,3,2,1,0:T(8,128)(2,1)} %bitcast.2), calls=%async_computation | async-start | bytes 1048576 | tf_op jit(solution)/shard_map/all_to_all | solution.py:312
  11.4 0.1 copy.23
  11.4 0.1 reduce-window.7
  11.5 0.1 reduce
  11.7 0.0 copy-done.7
  11.7 0.0 copy-done.9
  11.7 0.0 copy-start.4
  11.7 1.6 %copy-done.4 = bf16[1024,1024]{1,0:T(8,128)(2,1)S(1)} copy-done((bf16[1024,1024]{1,0:T(8,128)(2,1)S(1)}, bf16[1024,1024]{1,0:T(8,128)(2,1)}, u32[]{:S(2)}) %copy-start.4) | copy-done | bytes 2097176
  13.3 1.6 %copy-done.5 = bf16[1024,1024]{1,0:T(8,128)(2,1)S(1)} copy-done((bf16[1024,1024]{1,0:T(8,128)(2,1)S(1)}, bf16[1024,1024]{1,0:T(8,128)(2,1)}, u32[]{:S(2)}) %copy-start.5) | copy-done | bytes 2097176
  14.9 1.1 %project.1.value_ref = bf16[8,3,128,128]{3,2,1,0:T(8,128)(2,1)S(1)} custom-call(bf16[128,1024]{1,0:T(8,128)(2,1)S(1)} %copy-done.7, f32[1,1024]{1,0:T(1,128)S(1)} %bitcast.22, bf16[1024,1024]{1,0:T(8,128)(2,1)S(1)} %copy-done.3, bf16[1024,1024]{1,0:T(8,128)(2,1)S(1)} %copy-done.4, bf16[1024,1024]{1,0:T(8,128)(2,1)S(1)} %copy-done.5), custom_call_target="tpu_custom_call" | custom-call | tf_op jit(solution)/shard_map/project/pallas_call | solution.py:55
  16.0 0.9 copy-done.2
  16.9 6.5 %all-to-all-done.pref_ref = bf16[32,2,2,16,128]{4,3,2,1,0:T(8,128)(2,1)S(1)} async-done(((bf16[32,2,2,16,128]{4,3,2,1,0:T(8,128)(2,1)}), bf16[32,2,2,16,128]{4,3,2,1,0:T(8,128)(2,1)S(1)}, u32[]{:S(2)}, u32[]{:S(2)}) %all-to-all-start) | async-done | bytes 524320 | tf_op jit(solution)/shard_map/all_to_all | solution.py:312
  23.4 0.6 slice_bitcast_fusion.2.other_ref
  24.0 3.5 %all-to-all-start.1 = ((bf16[8,3,128,128]{3,2,1,0:T(8,128)(2,1)}), bf16[8,3,128,128]{3,2,1,0:T(8,128)(2,1)S(1)}, u32[]{:S(2)}, u32[]{:S(2)}) async-start(bf16[8,3,128,128]{3,2,1,0:T(8,128)(2,1)} %after.1), calls=%async_computation.1 | async-start | bytes 1572864 | tf_op jit(solution)/shard_map/all_to_all | solution.py:316
  27.5 0.0 copy-start.6
  27.5 0.0 copy-start.10
  27.6 0.2 select_reduce_fusion
  27.8 0.7 stack.5
  28.5 10.6 %all-to-all-done.1.qkv_ref = bf16[8,3,128,128]{3,2,1,0:T(8,128)(2,1)S(1)} async-done(((bf16[8,3,128,128]{3,2,1,0:T(8,128)(2,1)}), bf16[8,3,128,128]{3,2,1,0:T(8,128)(2,1)S(1)}, u32[]{:S(2)}, u32[]{:S(2)}) %all-to-all-start.1) | async-done | bytes 786464 | tf_op jit(solution)/shard_map/all_to_all | solution.py:316
  39.1 0.7 slice_bitcast_fusion
  39.8 0.0 collective-permute-start
  39.8 3.2 %collective-permute-start.1 = (bf16[2,128,128]{2,1,0:T(8,128)(2,1)}, bf16[2,128,128]{2,1,0:T(8,128)(2,1)}, u32[]{:S(2)}, u32[]{:S(2)}) collective-permute-start(bf16[2,128,128]{2,1,0:T(8,128)(2,1)} %get-tuple-element.28), channel_id=1, source_target_pairs={{8,0},{16,8},{24,16},{0,24},{9,1},{17,9},{25,17},{1,25},{10,2},{18... | collective-permute-start | bytes 196616 | tf_op jit(solution)/shard_map/ppermute | solution.py:321
  43.0 0.8 convert_bitcast_fusion.meta_ref
  43.8 0.1 copy.22.rel_ref
  43.9 1.3 %prepare.1 = (bf16[256,512]{1,0:T(8,128)(2,1)S(1)}, bf16[512,256]{1,0:T(8,128)(2,1)S(1)}, f32[256,384]{1,0:T(8,128)S(1)}, f32[256,128]{1,0:T(8,128)S(1)}) custom-call(s32[1]{0:T(128)} %bitcast.6.pair_ref, f32[32,16]{1,0:T(8,128)S(1)} %copy.22.rel_ref, bf16[32,2,2,16,128]{4,3,2,1,0:T(8,128)(2,1)S(1)} %all-to-all-done.pref_ref), custom_call_target="tpu_custom_call" | custom-call | tf_op jit(solution)/shard_map/prepare/pallas_call | solution.py:110
  45.2 0.3 collective-permute-done.prev_ref
  45.5 0.0 collective-permute-done.1.next_ref
  45.5 7.6 %attend.1 = bf16[8,128,128]{2,1,0:T(8,128)(2,1)S(1)} custom-call(bf16[8,3,128,128]{3,2,1,0:T(8,128)(2,1)S(1)} %all-to-all-done.1.qkv_ref, bf16[2,128,128]{2,1,0:T(8,128)(2,1)S(1)} %collective-permute-done.prev_ref, bf16[2,128,128]{2,1,0:T(8,128)(2,1)} %collective-permute-done.1.next_ref, bf16[256,512]{1,0:T(8,128)(2,1)S(1)} %get-tuple-element.15.keys_ref, ...), custom_call_target="tpu_custom_call" | custom-call | tf_op jit(solution)/shard_map/attend/pallas_call | solution.py:185
  53.0 0.0 copy-start
  53.1 9.8 %all_to_all.15.att_ref = bf16[8,128,128]{2,1,0:T(8,128)(2,1)S(1)} all-to-all(bf16[8,128,128]{2,1,0:T(8,128)(2,1)S(1)} %attend.1), channel_id=1, replica_groups=mesh['yhi'=2,'core'=2,'x'=4,'z'=4,'ylo'=2] {'z','ylo'}, dimensions={0} | all-to-all | bytes 524288 | tf_op jit(solution)/shard_map/all_to_all | solution.py:323
  62.9 0.6 join.1
  63.5 0.1 collective-permute-start.2
  63.6 2.4 %collective-permute-start.3 = (bf16[128,1024]{1,0:T(8,128)(2,1)S(1)}, bf16[128,1024]{1,0:T(8,128)(2,1)S(1)}, u32[]{:S(2)}, u32[]{:S(2)}) collective-permute-start(bf16[128,1024]{1,0:T(8,128)(2,1)S(1)} %get-tuple-element.20.one_ref), channel_id=1, source_target_pairs={{0,65},{65,0},{1,64},{64,1},{2,67},{67,2},{3,66},{66,3},{4,69},{69... | collective-permute-start | bytes 786440 | tf_op jit(solution)/shard_map/ppermute | solution.py:327
  66.0 0.0 collective-permute-done.2.two_ref
  66.0 1.3 %feed.2 = (bf16[128,1024]{1,0:T(8,128)(2,1)S(1)}, bf16[128,1024]{1,0:T(8,128)(2,1)S(1)}) custom-call(bf16[128,1024]{1,0:T(8,128)(2,1)S(1)} %get-tuple-element.20.one_ref, bf16[128,1024]{1,0:T(8,128)(2,1)S(1)} %collective-permute-done.2.two_ref, bf16[1024,1024]{1,0:T(8,128)(2,1)S(1)} %copy-done, bf16[1024,1024]{1,0:T(8,128)(2,1)S(1)} %copy-done.1), custom_call_target="tpu_custom_call" | custom-call | tf_op jit(solution)/shard_map/feed/pallas_call | solution.py:247
  67.3 6.3 %collective-permute-done.3.one_ref = bf16[128,1024]{1,0:T(8,128)(2,1)S(1)} collective-permute-done((bf16[128,1024]{1,0:T(8,128)(2,1)S(1)}, bf16[128,1024]{1,0:T(8,128)(2,1)S(1)}, u32[]{:S(2)}, u32[]{:S(2)}) %collective-permute-start.3) | collective-permute-done | bytes 262176 | tf_op jit(solution)/shard_map/ppermute | solution.py:327
  73.6 0.1 collective-permute-start.4
  73.7 1.9 %collective-permute-done.4.refs_2_.two_ref = bf16[2,128,1024]{2,1,0:T(8,128)(2,1)S(1)} collective-permute-done((bf16[2,128,1024]{2,1,0:T(8,128)(2,1)S(1)}, bf16[2,128,1024]{2,1,0:T(8,128)(2,1)S(1)}, u32[]{:S(2)}, u32[]{:S(2)}) %collective-permute-start.4) | collective-permute-done | bytes 524320 | tf_op jit(solution)/shard_map/ppermute | solution.py:330
  75.6 1.3 %feed.3 = (bf16[128,1024]{1,0:T(8,128)(2,1)S(1)}, bf16[128,1024]{1,0:T(8,128)(2,1)S(1)}) custom-call(bf16[128,1024]{1,0:T(8,128)(2,1)S(1)} %collective-permute-done.3.one_ref, bf16[2,128,1024]{2,1,0:T(8,128)(2,1)S(1)} %collective-permute-done.4.refs_2_.two_ref, bf16[1024,1024]{1,0:T(8,128)(2,1)S(1)} %copy-done, bf16[1024,1024]{1,0:T(8,128)(2,1)S(1)} %copy-done.1), custom_call_target="tpu_custom_call" | custom-call | tf_op jit(solution)/shard_map/feed/pallas_call | solution.py:247
  76.8 0.2 collective-permute-start.5
  77.1 1.4 %collective-permute-done.5.refs_1_ = bf16[128,1024]{1,0:T(8,128)(2,1)S(1)} collective-permute-done((bf16[128,1024]{1,0:T(8,128)(2,1)S(1)}, bf16[128,1024]{1,0:T(8,128)(2,1)S(1)}, u32[]{:S(2)}, u32[]{:S(2)}) %collective-permute-start.5) | collective-permute-done | bytes 262176 | tf_op jit(solution)/shard_map/ppermute | solution.py:332
  78.5 0.1 total.4
  78.5 2.4 %collective-permute-start.6 = (bf16[128,1024]{1,0:T(8,128)(2,1)S(1)}, bf16[128,1024]{1,0:T(8,128)(2,1)S(1)}, u32[]{:S(2)}, u32[]{:S(2)}) collective-permute-start(bf16[128,1024]{1,0:T(8,128)(2,1)S(1)} %total.4), channel_id=1, source_target_pairs={{0,65},{65,0},{1,64},{64,1},{2,67},{67,2},{3,66},{66,3},{4,69},{69... | collective-permute-start | bytes 786440 | tf_op jit(solution)/shard_map/ppermute | solution.py:333
  80.9 0.1 total.3.refs_0_
  81.0 7.2 %collective-permute-done.6.refs_1_ = bf16[128,1024]{1,0:T(8,128)(2,1)S(1)} collective-permute-done((bf16[128,1024]{1,0:T(8,128)(2,1)S(1)}, bf16[128,1024]{1,0:T(8,128)(2,1)S(1)}, u32[]{:S(2)}, u32[]{:S(2)}) %collective-permute-start.6) | collective-permute-done | bytes 262176 | tf_op jit(solution)/shard_map/ppermute | solution.py:333
  88.2 0.7 total.5
  (29 shorter events, 0.2 us)
Async XLA Ops:
  0.0 11.3 %copy-start.12 = (s32[1,64]{1,0:T(1,128)S(1)}, s32[1,64]{1,0:T(1,128)}, u32[]{:S(2)}) copy-start(s32[1,64]{1,0:T(1,128)} %param.21) | copy-start | bytes 772
  0.0 11.7 %copy-start.7 = (bf16[128,1024]{1,0:T(8,128)(2,1)S(1)}, bf16[128,1024]{1,0:T(8,128)(2,1)}, u32[]{:S(2)}) copy-start(bf16[128,1024]{1,0:T(8,128)(2,1)} %tok_ref.3) | copy-start | bytes 786436
  0.0 11.7 %copy-start.9 = (f32[1024]{0:T(1024)S(1)}, f32[1024]{0:T(1024)}, u32[]{:S(2)}) copy-start(f32[1024]{0:T(1024)} %param.14) | copy-start | bytes 12292
  0.0 11.7 %copy-start.3 = (bf16[1024,1024]{1,0:T(8,128)(2,1)S(1)}, bf16[1024,1024]{1,0:T(8,128)(2,1)}, u32[]{:S(2)}) copy-start(bf16[1024,1024]{1,0:T(8,128)(2,1)} %wq_ref.1) | copy-start | bytes 6291460
  2.1 21.3 %all-to-all-start = ((bf16[32,2,2,16,128]{4,3,2,1,0:T(8,128)(2,1)}), bf16[32,2,2,16,128]{4,3,2,1,0:T(8,128)(2,1)S(1)}, u32[]{:S(2)}, u32[]{:S(2)}) async-start(bf16[32,2,2,16,128]{4,3,2,1,0:T(8,128)(2,1)} %bitcast.2), calls=%async_computation | async-start | bytes 1048576 | tf_op jit(solution)/shard_map/all_to_all | solution.py:312
  11.7 1.6 %copy-start.4 = (bf16[1024,1024]{1,0:T(8,128)(2,1)S(1)}, bf16[1024,1024]{1,0:T(8,128)(2,1)}, u32[]{:S(2)}) copy-start(bf16[1024,1024]{1,0:T(8,128)(2,1)} %wk_ref.1) | copy-start | bytes 6291460
  13.3 1.6 %copy-start.5 = (bf16[1024,1024]{1,0:T(8,128)(2,1)S(1)}, bf16[1024,1024]{1,0:T(8,128)(2,1)}, u32[]{:S(2)}) copy-start(bf16[1024,1024]{1,0:T(8,128)(2,1)} %wv_ref.1) | copy-start | bytes 6291460
  15.9 0.9 %copy-start.2 = (bf16[8,3,128,128]{3,2,1,0:T(8,128)(2,1)}, bf16[8,3,128,128]{3,2,1,0:T(8,128)(2,1)S(1)}, u32[]{:S(2)}) copy-start(bf16[8,3,128,128]{3,2,1,0:T(8,128)(2,1)S(1)} %project.1.value_ref) | copy-start | bytes 2359300
  16.8 10.7 %copy-start.13 = (s32[1,64]{1,0:T(1,128)S(1)}, s32[1,64]{1,0:T(1,128)}, u32[]{:S(2)}) copy-start(s32[1,64]{1,0:T(1,128)} %param.22) | copy-start | bytes 772
  16.8 26.9 %copy-start.11 = (f32[32,16]{0,1:T(8,128)S(1)}, f32[32,16]{0,1:T(8,128)}, u32[]{:S(2)}) copy-start(f32[32,16]{0,1:T(8,128)} %param.19) | copy-start | bytes 6148
  24.0 15.1 %all-to-all-start.1 = ((bf16[8,3,128,128]{3,2,1,0:T(8,128)(2,1)}), bf16[8,3,128,128]{3,2,1,0:T(8,128)(2,1)S(1)}, u32[]{:S(2)}, u32[]{:S(2)}) async-start(bf16[8,3,128,128]{3,2,1,0:T(8,128)(2,1)} %after.1), calls=%async_computation.1 | async-start | bytes 1572864 | tf_op jit(solution)/shard_map/all_to_all | solution.py:316
  27.5 35.4 %copy-start.6 = (bf16[1024,1024]{1,0:T(8,128)(2,1)S(1)}, bf16[1024,1024]{1,0:T(8,128)(2,1)}, u32[]{:S(2)}) copy-start(bf16[1024,1024]{1,0:T(8,128)(2,1)} %w_ref.1) | copy-start | bytes 6291460
  27.5 35.4 %copy-start.10 = (f32[1024]{0:T(1024)S(1)}, f32[1024]{0:T(1024)}, u32[]{:S(2)}) copy-start(f32[1024]{0:T(1024)} %param.23) | copy-start | bytes 12292
  39.8 5.7 %collective-permute-start = (bf16[2,128,128]{2,1,0:T(8,128)(2,1)}, bf16[2,128,128]{2,1,0:T(8,128)(2,1)S(1)}, u32[]{:S(2)}, u32[]{:S(2)}) collective-permute-start(bf16[2,128,128]{2,1,0:T(8,128)(2,1)} %get-tuple-element.29), channel_id=1, source_target_pairs={{0,8},{8,16},{16,24},{24,0},{1,9},{9,17},{17,25},{25,1},{2,10},{10... | collective-permute-start | bytes 196616 | tf_op jit(solution)/shard_map/ppermute | solution.py:320
  39.8 5.7 %collective-permute-start.1 = (bf16[2,128,128]{2,1,0:T(8,128)(2,1)}, bf16[2,128,128]{2,1,0:T(8,128)(2,1)}, u32[]{:S(2)}, u32[]{:S(2)}) collective-permute-start(bf16[2,128,128]{2,1,0:T(8,128)(2,1)} %get-tuple-element.28), channel_id=1, source_target_pairs={{8,0},{16,8},{24,16},{0,24},{9,1},{17,9},{25,17},{1,25},{10,2},{18... | collective-permute-start | bytes 196616 | tf_op jit(solution)/shard_map/ppermute | solution.py:321
  43.9 19.0 %copy-start.8 = (bf16[128,1024]{1,0:T(8,128)(2,1)S(1)}, bf16[128,1024]{1,0:T(8,128)(2,1)}, u32[]{:S(2)}) copy-start(bf16[128,1024]{1,0:T(8,128)(2,1)} %tok_ref.3) | copy-start | bytes 786436
  45.5 20.5 %copy-start.1 = (bf16[1024,1024]{1,0:T(8,128)(2,1)S(1)}, bf16[1024,1024]{1,0:T(8,128)(2,1)}, u32[]{:S(2)}) copy-start(bf16[1024,1024]{1,0:T(8,128)(2,1)} %out_ref.3) | copy-start | bytes 6291460
  53.0 12.9 %copy-start = (bf16[1024,1024]{1,0:T(8,128)(2,1)S(1)}, bf16[1024,1024]{1,0:T(8,128)(2,1)}, u32[]{:S(2)}) copy-start(bf16[1024,1024]{1,0:T(8,128)(2,1)} %in_ref.3) | copy-start | bytes 6291460
  63.5 2.5 %collective-permute-start.2 = (bf16[128,1024]{1,0:T(8,128)(2,1)S(1)}, bf16[128,1024]{1,0:T(8,128)(2,1)S(1)}, u32[]{:S(2)}, u32[]{:S(2)}) collective-permute-start(bf16[128,1024]{1,0:T(8,128)(2,1)S(1)} %get-tuple-element.20.one_ref), channel_id=1, source_target_pairs={{0,32},{32,0},{1,33},{33,1},{2,34},{34,2},{3,35},{35,3},{4,36},{36... | collective-permute-start | bytes 786440 | tf_op jit(solution)/shard_map/ppermute | solution.py:328
  63.6 9.9 %collective-permute-start.3 = (bf16[128,1024]{1,0:T(8,128)(2,1)S(1)}, bf16[128,1024]{1,0:T(8,128)(2,1)S(1)}, u32[]{:S(2)}, u32[]{:S(2)}) collective-permute-start(bf16[128,1024]{1,0:T(8,128)(2,1)S(1)} %get-tuple-element.20.one_ref), channel_id=1, source_target_pairs={{0,65},{65,0},{1,64},{64,1},{2,67},{67,2},{3,66},{66,3},{4,69},{69... | collective-permute-start | bytes 786440 | tf_op jit(solution)/shard_map/ppermute | solution.py:327
  73.6 2.0 %collective-permute-start.4 = (bf16[2,128,1024]{2,1,0:T(8,128)(2,1)S(1)}, bf16[2,128,1024]{2,1,0:T(8,128)(2,1)S(1)}, u32[]{:S(2)}, u32[]{:S(2)}) collective-permute-start(bf16[2,128,1024]{2,1,0:T(8,128)(2,1)S(1)} %pack.1), channel_id=1, source_target_pairs={{0,32},{32,0},{1,33},{33,1},{2,34},{34,2},{3,35},{35,3},{4,36},{36... | collective-permute-start | bytes 1572872 | tf_op jit(solution)/shard_map/ppermute | solution.py:330
  76.8 1.6 %collective-permute-start.5 = (bf16[128,1024]{1,0:T(8,128)(2,1)S(1)}, bf16[128,1024]{1,0:T(8,128)(2,1)S(1)}, u32[]{:S(2)}, u32[]{:S(2)}) collective-permute-start(bf16[128,1024]{1,0:T(8,128)(2,1)S(1)} %get-tuple-element.24), channel_id=1, source_target_pairs={{0,32},{32,0},{1,33},{33,1},{2,34},{34,2},{3,35},{35,3},{4,36},{36... | collective-permute-start | bytes 786440 | tf_op jit(solution)/shard_map/ppermute | solution.py:332
  78.5 9.6 %collective-permute-start.6 = (bf16[128,1024]{1,0:T(8,128)(2,1)S(1)}, bf16[128,1024]{1,0:T(8,128)(2,1)S(1)}, u32[]{:S(2)}, u32[]{:S(2)}) collective-permute-start(bf16[128,1024]{1,0:T(8,128)(2,1)S(1)} %total.4), channel_id=1, source_target_pairs={{0,65},{65,0},{1,64},{64,1},{2,67},{67,2},{3,66},{66,3},{4,69},{69... | collective-permute-start | bytes 786440 | tf_op jit(solution)/shard_map/ppermute | solution.py:333

commit v3 on v2

--- a/solution.py
+++ b/solution.py
@@ -15,6 +15,10 @@
 ROWS = 128
 PAIRS = 8
 LANES = 128
+CHUNK = 512
+SHARE = 16
+SENT = 3 * ROWS + 2 * PREF_GRP * SHARE
+QUARTER = PAIRS * 2 * PREF_GRP * SHARE
 
 epsilon = 1e-06
 far_marks = (12, 16, 23, 32, 46, 64, 91)
@@ -42,55 +46,90 @@
 SMEM_SPEC = pl.BlockSpec(memory_space=pltpu.SMEM)
 
 
-def project_kernel(tok_ref, gain_ref, wq_ref, wk_ref, wv_ref, out_ref):
+def project_kernel(
+    tok_ref, gain_ref, cache_ref, wq_ref, wk_ref, wv_ref, out_ref, held, arrived
+):
+    columns = [slice(c * CHUNK, (c + 1) * CHUNK) for c in range(D // CHUNK)]
+    copies = [
+        [
+            pltpu.make_async_copy(w_ref.at[:, cut], held.at[kind, c], arrived.at[kind, c])
+            for c, cut in enumerate(columns)
+        ]
+        for kind, w_ref in enumerate((wq_ref, wk_ref, wv_ref))
+    ]
+    for row in copies:
+        for copy in row:
+            copy.start()
+    for part in range(PAIRS):
+        for kind in range(2):
+            for p in range(PREF_GRP):
+                at = 3 * ROWS + (kind * PREF_GRP + p) * SHARE
+                cut = slice(kind * D + part * LANES, kind * D + (part + 1) * LANES)
+                out_ref[part, at : at + SHARE] = cache_ref[p, :, cut]
     normed = norm_rows(tok_ref[...], gain_ref[...])
-    for kind, w_ref in enumerate((wq_ref, wk_ref, wv_ref)):
-        got = jnp.dot(normed, w_ref[...], preferred_element_type=jnp.float32)
-        got = got.astype(jnp.bfloat16)
-        for part in range(PAIRS):
-            out_ref[part, kind] = got[:, part * LANES : (part + 1) * LANES]
-
-
-def project(tokens, gain, w_query, w_key, w_value):
+    for kind, row in enumerate(copies):
+        for c, copy in enumerate(row):
+            copy.wait()
+            got = jnp.dot(normed, held[kind, c], preferred_element_type=jnp.float32)
+            got = got.astype(jnp.bfloat16)
+            for part in range(CHUNK // LANES):
+                to = c * (CHUNK // LANES) + part
+                out_ref[to, kind * ROWS : (kind + 1) * ROWS] = got[:, part * LANES : (part + 1) * LANES]
+
+
+def project(tokens, gain, w_query, w_key, w_value, prefix_cache):
+    anywhere = pl.BlockSpec(memory_space=pl.ANY)
     return pl.pallas_call(
         project_kernel,
-        in_specs=[VMEM_SPEC] * 5,
+        in_specs=[VMEM_SPEC] * 3 + [anywhere] * 3,
         out_specs=VMEM_SPEC,
-        out_shape=jax.ShapeDtypeStruct((PAIRS, 3, ROWS, LANES), jnp.bfloat16),
+        out_shape=pltpu.VMEM((PAIRS, SENT, LANES), jnp.bfloat16),
+        scratch_shapes=[
+            pltpu.VMEM((3, D // CHUNK, D, CHUNK), jnp.bfloat16),
+            pltpu.SemaphoreType.DMA((3, D // CHUNK)),
+        ],
         compiler_params=pltpu.CompilerParams(vmem_limit_bytes=VMEM_LIMIT),
         name="project",
-    )(*on_chip(tokens, gain.reshape(1, D), w_query, w_key, w_value))
-
-
-def after(value, other):
-    anywhere = pl.BlockSpec(memory_space=pl.ANY)
-    return pl.pallas_call(
-        lambda value_ref, other_ref, out_ref: None,
-        in_specs=[anywhere, anywhere],
-        out_specs=anywhere,
-        out_shape=jax.ShapeDtypeStruct(value.shape, value.dtype),
-        input_output_aliases={0: 0},
-        name="after",
-    )(value, other)
+    )(*on_chip(tokens, gain.reshape(1, D), prefix_cache), w_query, w_key, w_value)
+
+
+def spread_kernel(got_ref, up_ref, down_ref, far_ref):
+    for source in range(PAIRS):
+        rows = slice(source * 4 * SHARE, (source + 1) * 4 * SHARE)
+        held = got_ref[source, 3 * ROWS :]
+        up_ref[rows] = held
+        down_ref[rows] = held
+        far_ref[rows] = held
+    up_ref[QUARTER:] = got_ref[PAIRS - 1, ROWS : 3 * ROWS]
+    down_ref[QUARTER:] = got_ref[0, ROWS : 3 * ROWS]
+
+
+def spread(got):
+    shape = pltpu.VMEM((QUARTER + 2 * ROWS, LANES), jnp.bfloat16)
+    return pl.pallas_call(
+        spread_kernel,
+        in_specs=[VMEM_SPEC],
+        out_specs=(VMEM_SPEC,) * 3,
+        out_shape=(shape, shape, pltpu.VMEM((QUARTER, LANES), jnp.bfloat16)),
+        compiler_params=pltpu.CompilerParams(vmem_limit_bytes=VMEM_LIMIT),
+        name="spread",
+    )(*on_chip(got))
 
 
 def bias_line(rel_ref, head, first_bucket):
     lane = lax.broadcasted_iota(jnp.int32, (ROWS, LANES), 1)
-    line = jnp.full((ROWS, LANES), rel_ref[first_bucket, head], jnp.float32)
+    line = jnp.full((ROWS, LANES), rel_ref[head, first_bucket], jnp.float32)
     for bucket in range(1, 16):
         mark = bucket if bucket <= 8 else far_marks[bucket - 9]
-        line = jnp.where(lane >= mark, rel_ref[first_bucket + bucket, head], line)
+        line = jnp.where(lane >= mark, rel_ref[head, first_bucket + bucket], line)
     return line
 
 
-def prepare_kernel(pair_ref, rel_ref, pref_ref, keys_ref, values_ref, near_ref, line_ref):
+def tables_kernel(place_ref, rel_ref, len_ref, map_ref, near_ref, line_ref, meta_ref):
     row = lax.broadcasted_iota(jnp.int32, (ROWS, LANES), 0)
     lane = lax.broadcasted_iota(jnp.int32, (ROWS, LANES), 1)
-    for p in range(PREF_GRP):
-        keys_ref[p * LANES : (p + 1) * LANES, :] = jnp.transpose(pref_ref[:, 0, p].reshape(PLEN, LANES))
-        values_ref[:, p * LANES : (p + 1) * LANES] = pref_ref[:, 1, p].reshape(PLEN, LANES)
     for h in range(2):
-        head = pair_ref[0] * 2 + h
+        head = place_ref[1] * 2 + h
         before = bias_line(rel_ref, head, 0)
         after_it = bias_line(rel_ref, head, 16)
 
@@ -105,40 +144,77 @@
         near_ref[rows, 2 * LANES : 3 * LANES] = pick(after_it, lane + LANES - row)
         line_ref[rows, :] = before
 
-
-def prepare(pair, rel_bias, pref):
-    return pl.pallas_call(
-        prepare_kernel,
-        in_specs=[SMEM_SPEC, SMEM_SPEC, VMEM_SPEC],
-        out_specs=(VMEM_SPEC,) * 4,
+    requests = len_ref.shape[1]
+    down_it = lax.broadcasted_iota(jnp.int32, (requests, requests), 0)
+    along = lax.broadcasted_iota(jnp.int32, (requests, requests), 1)
+    length = jnp.broadcast_to(len_ref[...], (requests, requests)).astype(jnp.float32)
+    prefix = jnp.broadcast_to(map_ref[...], (requests, requests)).astype(jnp.float32)
+
+    def column(keep, values):
+        return jnp.sum(jnp.where(keep, values, 0.0), axis=1, keepdims=True)
+
+    starts = column(along < down_it, length)
+    ends = column(along <= down_it, length)
+    prefixes = column(along == down_it, prefix)
+    number = lax.broadcasted_iota(jnp.int32, (requests, LANES), 0).astype(jnp.float32) + 1.0
+    first = place_ref[0] * (PAIRS * ROWS) - ROWS
+    for b in range(PAIRS + 2):
+        ids = lax.broadcasted_iota(jnp.int32, (requests, LANES), 1) + (first + b * ROWS)
+        ids = ids.astype(jnp.float32)
+        member = (ids >= starts) & (ids < ends)
+        request = jnp.sum(jnp.where(member, number, 0.0), axis=0, keepdims=True) - 1.0
+        offset = ids[0:1] - jnp.sum(jnp.where(member, starts, 0.0), axis=0, keepdims=True)
+        chosen = jnp.sum(jnp.where(member, prefixes, 0.0), axis=0, keepdims=True)
+        meta_ref[b] = jnp.concatenate([request, offset, chosen] + [request] * 5, axis=0)
+
+
+def tables(place, rel_bias, lengths, prefix_map):
+    return pl.pallas_call(
+        tables_kernel,
+        in_specs=[SMEM_SPEC, SMEM_SPEC, VMEM_SPEC, VMEM_SPEC],
+        out_specs=(VMEM_SPEC,) * 3,
         out_shape=(
-            pltpu.VMEM((PREF_GRP * LANES, PLEN), jnp.bfloat16),
-            pltpu.VMEM((PLEN, PREF_GRP * LANES), jnp.bfloat16),
             pltpu.VMEM((2 * ROWS, 3 * LANES), jnp.float32),
             pltpu.VMEM((2 * ROWS, LANES), jnp.float32),
+            pltpu.VMEM((PAIRS + 2, 8, ROWS), jnp.float32),
         ),
         compiler_params=pltpu.CompilerParams(vmem_limit_bytes=VMEM_LIMIT),
-        name="prepare",
-    )(pair, rel_bias, *on_chip(pref))
+        name="tables",
+    )(place, rel_bias.T, *on_chip(lengths, prefix_map))
 
 
 def attend_kernel(
-    qkv_ref, prev_ref, next_ref, keys_ref, values_ref, near_ref, line_ref, meta_ref, out_ref, kwin, vwin
+    place_ref, got_ref, prev_ref, next_ref, far_ref, near_ref, line_ref, meta_ref, out_ref, keys, values, kwin, vwin
 ):
     lane = lax.broadcasted_iota(jnp.int32, (ROWS, LANES), 1)
     low = lane < DK
     for b in range(PAIRS + 2):
-        for dst, kind in ((kwin, 0), (vwin, 1)):
-            if b == 0:
-                block = prev_ref[kind]
-            elif b == PAIRS + 1:
-                block = next_ref[kind]
-            else:
-                block = qkv_ref[b - 1, kind + 1]
-            dst[b] = jnp.transpose(block) if kind == 0 else block
+        if b == 0:
+            key, value = prev_ref[QUARTER : QUARTER + ROWS], prev_ref[QUARTER + ROWS :]
+        elif b == PAIRS + 1:
+            key, value = next_ref[QUARTER : QUARTER + ROWS], next_ref[QUARTER + ROWS :]
+        else:
+            key, value = got_ref[b - 1, ROWS : 2 * ROWS], got_ref[b - 1, 2 * ROWS : 3 * ROWS]
+        kwin[b] = jnp.transpose(key)
+        vwin[b] = value
+    for turn, ref in ((0, None), (3, prev_ref), (1, next_ref), (2, far_ref)):
+        quarter = lax.rem(place_ref[0] + turn, 4)
+        for p in range(PREF_GRP):
+            pieces = [[], []]
+            for source in range(PAIRS):
+                for kind in range(2):
+                    at = (kind * PREF_GRP + p) * SHARE
+                    if ref is None:
+                        piece = got_ref[source, 3 * ROWS + at : 3 * ROWS + at + SHARE]
+                    else:
+                        at = at + source * 4 * SHARE
+                        piece = ref[at : at + SHARE]
+                    pieces[kind].append(piece)
+            keys[quarter, p * LANES : (p + 1) * LANES] = jnp.transpose(jnp.concatenate(pieces[0], axis=0))
+            values[quarter, :, p * LANES : (p + 1) * LANES] = jnp.concatenate(pieces[1], axis=0)
 
     def one(step, _):
-        query = qkv_ref[step, 0]
+        query = got_ref[step, 0:ROWS]
         own = jnp.transpose(meta_ref[step + 1])
         request, offset, chosen = own[:, 0:1], own[:, 1:2], own[:, 2:3]
         zero = jnp.zeros_like(query)
@@ -148,7 +224,8 @@
         split = jnp.concatenate(
             [jnp.where(second, zeros, stacked), jnp.where(second, stacked, zeros)], axis=1
         )
-        far_scores = jnp.dot(split, keys_ref[...], preferred_element_type=jnp.float32)
+        far_keys = jnp.concatenate([keys[b] for b in range(4)], axis=1)
+        far_scores = jnp.dot(split, far_keys, preferred_element_type=jnp.float32)
         near_keys = jnp.concatenate([kwin[step + b] for b in range(3)], axis=1)
         near_scores = jnp.dot(stacked, near_keys, preferred_element_type=jnp.float32)
         tail_at = jnp.minimum(LANES - lane + offset.astype(jnp.int32), LANES - 1)
@@ -167,7 +244,9 @@
         row_sum = jnp.sum(functools.reduce(jnp.add, terms), axis=1, keepdims=True)
         weights = [t.astype(jnp.bfloat16) for t in terms]
         far_out = jnp.dot(
-            jnp.concatenate(weights[:4], axis=1), values_ref[...], preferred_element_type=jnp.float32
+            jnp.concatenate(weights[:4], axis=1),
+            values[...].reshape(PLEN, PREF_GRP * LANES),
+            preferred_element_type=jnp.float32,
         )
         near_values = jnp.concatenate([vwin[step + b] for b in range(3)], axis=0)
         near_out = jnp.dot(
@@ -181,33 +260,21 @@
     lax.fori_loop(0, PAIRS, one, 0)
 
 
-def attend(qkv, prev, after_it, prepared, meta):
+def attend(place, got, prev, after_it, far, made):
     return pl.pallas_call(
         attend_kernel,
-        in_specs=[VMEM_SPEC] * 8,
+        in_specs=[SMEM_SPEC] + [VMEM_SPEC] * 7,
         out_specs=VMEM_SPEC,
         out_shape=pltpu.VMEM((PAIRS, ROWS, LANES), jnp.bfloat16),
         scratch_shapes=[
+            pltpu.VMEM((4, PREF_GRP * LANES, PLEN // 4), jnp.bfloat16),
+            pltpu.VMEM((4, PLEN // 4, PREF_GRP * LANES), jnp.bfloat16),
             pltpu.VMEM((PAIRS + 2, LANES, ROWS), jnp.bfloat16),
             pltpu.VMEM((PAIRS + 2, ROWS, LANES), jnp.bfloat16),
         ],
         compiler_params=pltpu.CompilerParams(vmem_limit_bytes=VMEM_LIMIT),
         name="attend",
-    )(*on_chip(qkv, prev, after_it, *prepared, meta))
-
-
-def token_table(lengths_row, prefix_row, first):
-    count = (PAIRS + 2) * ROWS
-    ends = jnp.cumsum(lengths_row)
-    starts = ends - lengths_row
-    ids = first + jnp.arange(count, dtype=jnp.int32)
-    member = ((ids[None, :] >= starts[:, None]) & (ids[None, :] < ends[:, None])).astype(jnp.int32)
-    numbers = jnp.arange(1, lengths_row.shape[0] + 1, dtype=jnp.int32)
-    request = jnp.sum(member * numbers[:, None], axis=0) - 1
-    offset = ids - jnp.sum(member * starts[:, None], axis=0)
-    chosen = jnp.sum(member * prefix_row[:, None], axis=0)
-    table = jnp.stack([request, offset, chosen] + [request] * 5, axis=0).astype(jnp.float32)
-    return table.reshape(8, PAIRS + 2, ROWS).transpose(1, 0, 2)
+    )(place, *on_chip(got, prev, after_it, far, *made))
 
 
 def join_kernel(att_ref, w_ref, tok_ref, gain_ref, hidden_ref, normed_ref):
@@ -303,23 +370,19 @@
     w_in,
     w_out,
 ):
-    plane_x = lax.axis_index("x")
     count_x = lax.axis_size("x")
-    pair = (lax.axis_index("z") * 2 + lax.axis_index("ylo")).astype(jnp.int32).reshape(1)
-
-    held = prefix_cache.reshape(PREF_GRP, -1, 2, PAIRS, LANES).transpose(3, 2, 0, 1, 4)
-    sent = jnp.broadcast_to(held[None], (count_x,) + held.shape).reshape((-1,) + held.shape[1:])
-    pref = lax.all_to_all(sent, REQ, 0, 0, tiled=True)
-
-    meta = token_table(lengths[0], prefix_map[0], plane_x * (PAIRS * ROWS) - ROWS)
-    blocks = after(project(tokens, attn_gain, w_query, w_key, w_value), pref[0, 0, 0])
-    qkv = lax.all_to_all(blocks, PLANE, 0, 0, tiled=True)
-    prepared = prepare(pair, rel_bias, pref)
-    up = [(i, (i + 1) % count_x) for i in range(count_x)]
-    down = [(j, i) for i, j in up]
-    before = lax.ppermute(qkv[PAIRS - 1, 1:], "x", up)
-    later = lax.ppermute(qkv[0, 1:], "x", down)
-    mixed = attend(qkv, before, later, prepared, meta)
+    plane = lax.axis_index("z") * 2 + lax.axis_index("ylo")
+    place = jnp.stack([lax.axis_index("x"), plane]).astype(jnp.int32)
+    made = tables(place, rel_bias, lengths, prefix_map)
+
+    blocks = project(tokens, attn_gain, w_query, w_key, w_value, prefix_cache)
+    got = lax.all_to_all(blocks, PLANE, 0, 0, tiled=True)
+    up, down, far = spread(got)
+    by = lambda d: [(i, (i + d) % count_x) for i in range(count_x)]
+    prev = lax.ppermute(up, "x", by(1))
+    later = lax.ppermute(down, "x", by(-1))
+    opposite = lax.ppermute(far, "x", by(2))
+    mixed = attend(place, got, prev, later, opposite, made)
     att = lax.all_to_all(mixed, PLANE, 0, 0, tiled=True)
     hidden, normed = join(att, w_attn_out, tokens, mlp_gain)
 

time: 89.9 us -> 87.5 us (0.973)
  blocking collectives: 9.83 us -> 31 us
  waiting for transfers between devices: 34.1 us -> 21.1 us
  starting transfers between devices: 21.2 us -> 10.2 us
  Pallas kernels: 14 us -> 17 us
  other arithmetic: 1.2 us -> 0.07 us
  local copies, waits for them, and re-layouts: 8.3 us -> 7.35 us
    all_to_all x0 -> x1, blocking collectives: none -> 20.8 us  [body(): got = lax.all_to_all(blocks, PLANE, 0, 0, tiled=True)]
    all_to_all x2 -> x0, waiting for transfers between devices: 17.1 us -> none  [the longest x1 10.6 us: body(): qkv = lax.all_to_all(blocks, PLANE, 0, 0, tiled=True)]
    all_to_all x2 -> x0, starting transfers between devices: 12.8 us -> none  [the longest x1 9.27 us: body(): pref = lax.all_to_all(sent, REQ, 0, 0, tiled=True)]
    ppermute x2 -> x3, waiting for transfers between devices: 0.3 us -> 4.35 us  [the longest x1 4.35 us: body(): opposite = lax.ppermute(far, 'x', by(2))]
    pallas_call x4, Pallas kernels: 9.93 us -> 12.9 us  [the longest x1 7.91 us: attend(): pl.pallas_call(attend_kernel, in_specs=[SMEM_SPEC] + [VMEM_SPEC] * 7, out...]
    unnamed x30 -> x28, local copies, waits for them, and re-layouts: 5.26 us -> 7.35 us
    ppermute x2 -> x3, starting transfers between devices: 3.24 us -> 5.06 us  [the longest x1 1.82 us: body(): opposite = lax.ppermute(far, 'x', by(2))]
    squeeze x2 -> x0, local copies, waits for them, and re-layouts: 1.25 us -> none  [the longest x1 0.66 us: body(): later = lax.ppermute(qkv[0, 1:], 'x', down)]
  transfers between devices with their start and end apart: 9 -> 8, of which waited for: 7 -> 5; matrix products, arithmetic and copies ran while one was open for 2% -> 0% of each run, Pallas kernels for 4% -> 3%
where the time goes in v3:
time: 87.5 us; the launch traced here: 86.9 us
  blocking collectives  31 us (35%)
  waiting for transfers between devices  21.1 us (24%)
  Pallas kernels  17 us (19%)
  starting transfers between devices  10.2 us (12%)
  local copies, waits for them, and re-layouts  7.35 us (8%)
    all_to_all x1, blocking collectives, body(): got = lax.all_to_all(blocks, PLANE, 0, 0, tiled=True)  20.8 us
    all_to_all x1, blocking collectives, body(): att = lax.all_to_all(mixed, PLANE, 0, 0, tiled=True)  10.3 us
    pallas_call x1, Pallas kernels, attend(): pl.pallas_call(attend_kernel, in_specs=[SMEM_SPEC] + [VMEM_SPEC] * 7, out...  7.91 us
    unnamed x28, local copies, waits for them, and re-layouts  7.35 us
    ppermute x1, waiting for transfers between devices, body(): back = lax.ppermute(far_sum, mirrored, MIRROR)  7.19 us
    ppermute x1, waiting for transfers between devices, body(): far = lax.ppermute(normed, mirrored, MIRROR)  6.26 us
    ppermute x1, waiting for transfers between devices, body(): opposite = lax.ppermute(far, 'x', by(2))  4.35 us
    pallas_call x1, Pallas kernels, project(): pl.pallas_call(project_kernel, in_specs=[VMEM_SPEC] * 3 + [anywhere] * 3,...  2.89 us
  transfers between devices with their start and end apart: 8, of which 5 were waited for; matrix products, arithmetic and copies ran while one was open for 0% of the time, Pallas kernels for 3%

profile of v3, /device:TPU:0, one launch (start us, length us, event | category | flops | bytes accessed | tf_op | source)
XLA Modules:
  0.0 86.9 jit_solution(7693353319398311231)
XLA Ops:
  0.0 1.6 %copy-done.2 = bf16[1024,1024]{1,0:T(8,128)(2,1)S(1)} copy-done((bf16[1024,1024]{1,0:T(8,128)(2,1)S(1)}, bf16[1024,1024]{1,0:T(8,128)(2,1)}, u32[]{:S(2)}) %copy-start.2) | copy-done | bytes 2097176
  1.6 1.6 %copy-done.3 = bf16[1024,1024]{1,0:T(8,128)(2,1)S(1)} copy-done((bf16[1024,1024]{1,0:T(8,128)(2,1)S(1)}, bf16[1024,1024]{1,0:T(8,128)(2,1)}, u32[]{:S(2)}) %copy-start.3) | copy-done | bytes 2097176
  3.2 1.6 %copy-done.4 = bf16[1024,1024]{1,0:T(8,128)(2,1)S(1)} copy-done((bf16[1024,1024]{1,0:T(8,128)(2,1)S(1)}, bf16[1024,1024]{1,0:T(8,128)(2,1)}, u32[]{:S(2)}) %copy-start.4) | copy-done | bytes 2097176
  4.8 0.9 %copy-done.6 = bf16[128,1024]{1,0:T(8,128)(2,1)S(1)} copy-done((bf16[128,1024]{1,0:T(8,128)(2,1)S(1)}, bf16[128,1024]{1,0:T(8,128)(2,1)}, u32[]{:S(2)}) %copy-start.6) | copy-done | bytes 262168
  5.7 0.9 %copy-done.8 = bf16[2,16,2048]{2,1,0:T(8,128)(2,1)S(1)} copy-done((bf16[2,16,2048]{2,1,0:T(8,128)(2,1)S(1)}, bf16[2,16,2048]{2,1,0:T(8,128)(2,1)}, u32[]{:S(2)}) %copy-start.8) | copy-done | bytes 131096
  6.6 0.7 copy-done.10
  7.3 2.9 %project.1 = bf16[8,448,128]{2,1,0:T(8,128)(2,1)S(1)} custom-call(bf16[128,1024]{1,0:T(8,128)(2,1)S(1)} %copy-done.6, f32[1,1024]{1,0:T(1,128)S(1)} %bitcast.6, bf16[2,16,2048]{2,1,0:T(8,128)(2,1)S(1)} %copy-done.8, bf16[1024,1024]{1,0:T(8,128)(2,1)S(1)} %copy-done.2, bf16[1024,1024]{1,0:T(8,128)(2,1)S(1)} %copy-done.3, bf16[1024,1024]{1,0:T(8,128)(2,1)S(1)} %copy-done.4), custom_call_target="tpu_custom_call" | custom-call | tf_op jit(solution)/shard_map/project/pallas_call | solution.py:82
  10.2 0.0 copy-start.9
  10.2 0.0 copy-start.12
  10.2 0.0 copy-start.13
  10.3 0.0 copy-start.7
  10.3 20.8 %all_to_all.10.got_ref = bf16[8,448,128]{2,1,0:T(8,128)(2,1)S(1)} all-to-all(bf16[8,448,128]{2,1,0:T(8,128)(2,1)S(1)} %project.1), channel_id=1, replica_groups=mesh['yhi'=2,'core'=2,'x'=4,'z'=4,'ylo'=2] {'z','ylo'}, dimensions={0} | all-to-all | bytes 1835008 | tf_op jit(solution)/shard_map/all_to_all | solution.py:379
  31.0 0.8 spread.1
  31.9 1.5 %collective-permute-start = (bf16[768,128]{1,0:T(8,128)(2,1)}, bf16[768,128]{1,0:T(8,128)(2,1)S(1)}, u32[]{:S(2)}, u32[]{:S(2)}) collective-permute-start(bf16[768,128]{1,0:T(8,128)(2,1)} %get-tuple-element.17), channel_id=1, source_target_pairs={{0,8},{8,16},{16,24},{24,0},{1,9},{9,17},{17,25},{25,1},{2,10},{10... | collective-permute-start | bytes 589832 | tf_op jit(solution)/shard_map/ppermute | solution.py:382
  33.3 1.8 %collective-permute-start.1 = (bf16[768,128]{1,0:T(8,128)(2,1)}, bf16[768,128]{1,0:T(8,128)(2,1)}, u32[]{:S(2)}, u32[]{:S(2)}) collective-permute-start(bf16[768,128]{1,0:T(8,128)(2,1)} %get-tuple-element.18), channel_id=1, source_target_pairs={{0,24},{8,0},{16,8},{24,16},{1,25},{9,1},{17,9},{25,17},{2,26},{10... | collective-permute-start | bytes 589832 | tf_op jit(solution)/shard_map/ppermute | solution.py:383
  35.1 1.8 %collective-permute-start.2 = (bf16[512,128]{1,0:T(8,128)(2,1)}, bf16[512,128]{1,0:T(8,128)(2,1)}, u32[]{:S(2)}, u32[]{:S(2)}) collective-permute-start(bf16[512,128]{1,0:T(8,128)(2,1)} %get-tuple-element.19), channel_id=1, source_target_pairs={{0,16},{8,24},{16,0},{24,8},{1,17},{9,25},{17,1},{25,9},{2,18},{10... | collective-permute-start | bytes 393224 | tf_op jit(solution)/shard_map/ppermute | solution.py:384
  36.9 0.1 pad_add_fusion.place_ref
  37.0 0.0 copy-done.9
  37.0 0.0 copy-done.12
  37.0 0.0 copy-done.13
  37.0 1.2 %tables.1 = (f32[256,384]{1,0:T(8,128)S(1)}, f32[256,128]{1,0:T(8,128)S(1)}, f32[10,8,128]{2,1,0:T(8,128)S(1)}) custom-call(s32[2]{0:T(128)S(1)} %pad_add_fusion.place_ref, f32[16,32]{1,0:T(8,128)S(1)} %bitcast.5, s32[1,64]{1,0:T(1,128)S(1)} %copy-done.12, s32[1,64]{1,0:T(1,128)S(1)} %copy-done.13), custom_call_target="tpu_custom_call" | custom-call | tf_op jit(solution)/shard_map/tables/pallas_call | solution.py:172
  38.2 4.3 %collective-permute-done.2.far_ref = bf16[512,128]{1,0:T(8,128)(2,1)} collective-permute-done((bf16[512,128]{1,0:T(8,128)(2,1)}, bf16[512,128]{1,0:T(8,128)(2,1)}, u32[]{:S(2)}, u32[]{:S(2)}) %collective-permute-start.2) | collective-permute-done | bytes 131104 | tf_op jit(solution)/shard_map/ppermute | solution.py:384
  42.6 0.0 collective-permute-done.prev_ref
  42.6 0.0 collective-permute-done.1.next_ref
  42.6 7.9 %attend.1 = bf16[8,128,128]{2,1,0:T(8,128)(2,1)S(1)} custom-call(s32[2]{0:T(128)S(1)} %pad_add_fusion.place_ref, bf16[8,448,128]{2,1,0:T(8,128)(2,1)S(1)} %all_to_all.10.got_ref, bf16[768,128]{1,0:T(8,128)(2,1)S(1)} %collective-permute-done.prev_ref, bf16[768,128]{1,0:T(8,128)(2,1)} %collective-permute-done.1.next_ref, ...), custom_call_target="tpu_custom_call" | custom-call | tf_op jit(solution)/shard_map/attend/pallas_call | solution.py:264
  50.5 0.0 copy-start
  50.5 10.3 %all_to_all.11.att_ref = bf16[8,128,128]{2,1,0:T(8,128)(2,1)S(1)} all-to-all(bf16[8,128,128]{2,1,0:T(8,128)(2,1)S(1)} %attend.1), channel_id=1, replica_groups=mesh['yhi'=2,'core'=2,'x'=4,'z'=4,'ylo'=2] {'z','ylo'}, dimensions={0} | all-to-all | bytes 524288 | tf_op jit(solution)/shard_map/all_to_all | solution.py:386
  60.8 0.0 copy-done.7
  60.8 0.0 copy-done.5
  60.8 0.0 copy-done.11
  60.8 0.6 join.1
  61.5 0.1 collective-permute-start.3
  61.6 2.4 %collective-permute-start.4 = (bf16[128,1024]{1,0:T(8,128)(2,1)S(1)}, bf16[128,1024]{1,0:T(8,128)(2,1)S(1)}, u32[]{:S(2)}, u32[]{:S(2)}) collective-permute-start(bf16[128,1024]{1,0:T(8,128)(2,1)S(1)} %get-tuple-element.24.one_ref), channel_id=1, source_target_pairs={{0,65},{65,0},{1,64},{64,1},{2,67},{67,2},{3,66},{66,3},{4,69},{69... | collective-permute-start | bytes 786440 | tf_op jit(solution)/shard_map/ppermute | solution.py:390
  63.9 0.0 collective-permute-done.3.two_ref
  63.9 0.0 copy-done.1
  63.9 0.0 copy-done
  63.9 1.3 %feed.2 = (bf16[128,1024]{1,0:T(8,128)(2,1)S(1)}, bf16[128,1024]{1,0:T(8,128)(2,1)S(1)}) custom-call(bf16[128,1024]{1,0:T(8,128)(2,1)S(1)} %get-tuple-element.24.one_ref, bf16[128,1024]{1,0:T(8,128)(2,1)S(1)} %collective-permute-done.3.two_ref, bf16[1024,1024]{1,0:T(8,128)(2,1)S(1)} %copy-done, bf16[1024,1024]{1,0:T(8,128)(2,1)S(1)} %copy-done.1), custom_call_target="tpu_custom_call" | custom-call | tf_op jit(solution)/shard_map/feed/pallas_call | solution.py:314
  65.2 6.3 %collective-permute-done.4.one_ref = bf16[128,1024]{1,0:T(8,128)(2,1)S(1)} collective-permute-done((bf16[128,1024]{1,0:T(8,128)(2,1)S(1)}, bf16[128,1024]{1,0:T(8,128)(2,1)S(1)}, u32[]{:S(2)}, u32[]{:S(2)}) %collective-permute-start.4) | collective-permute-done | bytes 262176 | tf_op jit(solution)/shard_map/ppermute | solution.py:390
  71.5 0.1 collective-permute-start.5
  71.6 1.9 %collective-permute-done.5.refs_2_.two_ref = bf16[2,128,1024]{2,1,0:T(8,128)(2,1)S(1)} collective-permute-done((bf16[2,128,1024]{2,1,0:T(8,128)(2,1)S(1)}, bf16[2,128,1024]{2,1,0:T(8,128)(2,1)S(1)}, u32[]{:S(2)}, u32[]{:S(2)}) %collective-permute-start.5) | collective-permute-done | bytes 524320 | tf_op jit(solution)/shard_map/ppermute | solution.py:393
  73.5 1.3 %feed.3 = (bf16[128,1024]{1,0:T(8,128)(2,1)S(1)}, bf16[128,1024]{1,0:T(8,128)(2,1)S(1)}) custom-call(bf16[128,1024]{1,0:T(8,128)(2,1)S(1)} %collective-permute-done.4.one_ref, bf16[2,128,1024]{2,1,0:T(8,128)(2,1)S(1)} %collective-permute-done.5.refs_2_.two_ref, bf16[1024,1024]{1,0:T(8,128)(2,1)S(1)} %copy-done, bf16[1024,1024]{1,0:T(8,128)(2,1)S(1)} %copy-done.1), custom_call_target="tpu_custom_call" | custom-call | tf_op jit(solution)/shard_map/feed/pallas_call | solution.py:314
  74.8 0.2 collective-permute-start.6
  75.0 1.4 %collective-permute-done.6.refs_1_ = bf16[128,1024]{1,0:T(8,128)(2,1)S(1)} collective-permute-done((bf16[128,1024]{1,0:T(8,128)(2,1)S(1)}, bf16[128,1024]{1,0:T(8,128)(2,1)S(1)}, u32[]{:S(2)}, u32[]{:S(2)}) %collective-permute-start.6) | collective-permute-done | bytes 262176 | tf_op jit(solution)/shard_map/ppermute | solution.py:395
  76.4 0.1 total.4
  76.5 2.4 %collective-permute-start.7 = (bf16[128,1024]{1,0:T(8,128)(2,1)S(1)}, bf16[128,1024]{1,0:T(8,128)(2,1)S(1)}, u32[]{:S(2)}, u32[]{:S(2)}) collective-permute-start(bf16[128,1024]{1,0:T(8,128)(2,1)S(1)} %total.4), channel_id=1, source_target_pairs={{0,65},{65,0},{1,64},{64,1},{2,67},{67,2},{3,66},{66,3},{4,69},{69... | collective-permute-start | bytes 786440 | tf_op jit(solution)/shard_map/ppermute | solution.py:396
  78.9 0.1 total.3.refs_0_
  78.9 7.2 %collective-permute-done.7.refs_1_ = bf16[128,1024]{1,0:T(8,128)(2,1)S(1)} collective-permute-done((bf16[128,1024]{1,0:T(8,128)(2,1)S(1)}, bf16[128,1024]{1,0:T(8,128)(2,1)S(1)}, u32[]{:S(2)}, u32[]{:S(2)}) %collective-permute-start.7) | collective-permute-done | bytes 262176 | tf_op jit(solution)/shard_map/ppermute | solution.py:396
  86.1 0.7 total.5
  (10 shorter events, 0.0 us)
Async XLA Ops:
  0.0 1.6 %copy-start.2 = (bf16[1024,1024]{1,0:T(8,128)(2,1)S(1)}, bf16[1024,1024]{1,0:T(8,128)(2,1)}, u32[]{:S(2)}) copy-start(bf16[1024,1024]{1,0:T(8,128)(2,1)} %wq_ref.1) | copy-start | bytes 6291460
  1.6 1.6 %copy-start.3 = (bf16[1024,1024]{1,0:T(8,128)(2,1)S(1)}, bf16[1024,1024]{1,0:T(8,128)(2,1)}, u32[]{:S(2)}) copy-start(bf16[1024,1024]{1,0:T(8,128)(2,1)} %wk_ref.1) | copy-start | bytes 6291460
  3.2 1.6 %copy-start.4 = (bf16[1024,1024]{1,0:T(8,128)(2,1)S(1)}, bf16[1024,1024]{1,0:T(8,128)(2,1)}, u32[]{:S(2)}) copy-start(bf16[1024,1024]{1,0:T(8,128)(2,1)} %wv_ref.1) | copy-start | bytes 6291460
  4.8 0.9 %copy-start.6 = (bf16[128,1024]{1,0:T(8,128)(2,1)S(1)}, bf16[128,1024]{1,0:T(8,128)(2,1)}, u32[]{:S(2)}) copy-start(bf16[128,1024]{1,0:T(8,128)(2,1)} %tok_ref.3) | copy-start | bytes 786436
  5.7 0.9 %copy-start.8 = (bf16[2,16,2048]{2,1,0:T(8,128)(2,1)S(1)}, bf16[2,16,2048]{2,1,0:T(8,128)(2,1)}, u32[]{:S(2)}) copy-start(bf16[2,16,2048]{2,1,0:T(8,128)(2,1)} %cache_ref.1) | copy-start | bytes 393220
  6.6 0.7 copy-start.10
  10.2 26.8 %copy-start.9 = (f32[32,16]{0,1:T(8,128)S(1)}, f32[32,16]{0,1:T(8,128)}, u32[]{:S(2)}) copy-start(f32[32,16]{0,1:T(8,128)} %param.19) | copy-start | bytes 6148
  10.2 26.8 %copy-start.12 = (s32[1,64]{1,0:T(1,128)S(1)}, s32[1,64]{1,0:T(1,128)}, u32[]{:S(2)}) copy-start(s32[1,64]{1,0:T(1,128)} %len_ref.1) | copy-start | bytes 772
  10.2 26.8 %copy-start.13 = (s32[1,64]{1,0:T(1,128)S(1)}, s32[1,64]{1,0:T(1,128)}, u32[]{:S(2)}) copy-start(s32[1,64]{1,0:T(1,128)} %map_ref.1) | copy-start | bytes 772
  10.3 50.6 %copy-start.7 = (bf16[128,1024]{1,0:T(8,128)(2,1)S(1)}, bf16[128,1024]{1,0:T(8,128)(2,1)}, u32[]{:S(2)}) copy-start(bf16[128,1024]{1,0:T(8,128)(2,1)} %tok_ref.3) | copy-start | bytes 786436
  31.0 29.8 %copy-start.5 = (bf16[1024,1024]{1,0:T(8,128)(2,1)S(1)}, bf16[1024,1024]{1,0:T(8,128)(2,1)}, u32[]{:S(2)}) copy-start(bf16[1024,1024]{1,0:T(8,128)(2,1)} %w_ref.1) | copy-start | bytes 6291460
  31.0 29.8 %copy-start.11 = (f32[1024]{0:T(1024)S(1)}, f32[1024]{0:T(1024)}, u32[]{:S(2)}) copy-start(f32[1024]{0:T(1024)} %param.23) | copy-start | bytes 12292
  31.9 10.7 %collective-permute-start = (bf16[768,128]{1,0:T(8,128)(2,1)}, bf16[768,128]{1,0:T(8,128)(2,1)S(1)}, u32[]{:S(2)}, u32[]{:S(2)}) collective-permute-start(bf16[768,128]{1,0:T(8,128)(2,1)} %get-tuple-element.17), channel_id=1, source_target_pairs={{0,8},{8,16},{16,24},{24,0},{1,9},{9,17},{17,25},{25,1},{2,10},{10... | collective-permute-start | bytes 589832 | tf_op jit(solution)/shard_map/ppermute | solution.py:382
  33.3 9.3 %collective-permute-start.1 = (bf16[768,128]{1,0:T(8,128)(2,1)}, bf16[768,128]{1,0:T(8,128)(2,1)}, u32[]{:S(2)}, u32[]{:S(2)}) collective-permute-start(bf16[768,128]{1,0:T(8,128)(2,1)} %get-tuple-element.18), channel_id=1, source_target_pairs={{0,24},{8,0},{16,8},{24,16},{1,25},{9,1},{17,9},{25,17},{2,26},{10... | collective-permute-start | bytes 589832 | tf_op jit(solution)/shard_map/ppermute | solution.py:383
  35.1 7.5 %collective-permute-start.2 = (bf16[512,128]{1,0:T(8,128)(2,1)}, bf16[512,128]{1,0:T(8,128)(2,1)}, u32[]{:S(2)}, u32[]{:S(2)}) collective-permute-start(bf16[512,128]{1,0:T(8,128)(2,1)} %get-tuple-element.19), channel_id=1, source_target_pairs={{0,16},{8,24},{16,0},{24,8},{1,17},{9,25},{17,1},{25,9},{2,18},{10... | collective-permute-start | bytes 393224 | tf_op jit(solution)/shard_map/ppermute | solution.py:384
  42.6 21.3 %copy-start.1 = (bf16[1024,1024]{1,0:T(8,128)(2,1)S(1)}, bf16[1024,1024]{1,0:T(8,128)(2,1)}, u32[]{:S(2)}) copy-start(bf16[1024,1024]{1,0:T(8,128)(2,1)} %out_ref.3) | copy-start | bytes 6291460
  50.5 13.4 %copy-start = (bf16[1024,1024]{1,0:T(8,128)(2,1)S(1)}, bf16[1024,1024]{1,0:T(8,128)(2,1)}, u32[]{:S(2)}) copy-start(bf16[1024,1024]{1,0:T(8,128)(2,1)} %in_ref.3) | copy-start | bytes 6291460
  61.5 2.5 %collective-permute-start.3 = (bf16[128,1024]{1,0:T(8,128)(2,1)S(1)}, bf16[128,1024]{1,0:T(8,128)(2,1)S(1)}, u32[]{:S(2)}, u32[]{:S(2)}) collective-permute-start(bf16[128,1024]{1,0:T(8,128)(2,1)S(1)} %get-tuple-element.24.one_ref), channel_id=1, source_target_pairs={{0,32},{32,0},{1,33},{33,1},{2,34},{34,2},{3,35},{35,3},{4,36},{36... | collective-permute-start | bytes 786440 | tf_op jit(solution)/shard_map/ppermute | solution.py:391
  61.6 9.9 %collective-permute-start.4 = (bf16[128,1024]{1,0:T(8,128)(2,1)S(1)}, bf16[128,1024]{1,0:T(8,128)(2,1)S(1)}, u32[]{:S(2)}, u32[]{:S(2)}) collective-permute-start(bf16[128,1024]{1,0:T(8,128)(2,1)S(1)} %get-tuple-element.24.one_ref), channel_id=1, source_target_pairs={{0,65},{65,0},{1,64},{64,1},{2,67},{67,2},{3,66},{66,3},{4,69},{69... | collective-permute-start | bytes 786440 | tf_op jit(solution)/shard_map/ppermute | solution.py:390
  71.5 2.0 %collective-permute-start.5 = (bf16[2,128,1024]{2,1,0:T(8,128)(2,1)S(1)}, bf16[2,128,1024]{2,1,0:T(8,128)(2,1)S(1)}, u32[]{:S(2)}, u32[]{:S(2)}) collective-permute-start(bf16[2,128,1024]{2,1,0:T(8,128)(2,1)S(1)} %pack.1), channel_id=1, source_target_pairs={{0,32},{32,0},{1,33},{33,1},{2,34},{34,2},{3,35},{35,3},{4,36},{36... | collective-permute-start | bytes 1572872 | tf_op jit(solution)/shard_map/ppermute | solution.py:393
  74.8 1.6 %collective-permute-start.6 = (bf16[128,1024]{1,0:T(8,128)(2,1)S(1)}, bf16[128,1024]{1,0:T(8,128)(2,1)S(1)}, u32[]{:S(2)}, u32[]{:S(2)}) collective-permute-start(bf16[128,1024]{1,0:T(8,128)(2,1)S(1)} %get-tuple-element.28), channel_id=1, source_target_pairs={{0,32},{32,0},{1,33},{33,1},{2,34},{34,2},{3,35},{35,3},{4,36},{36... | collective-permute-start | bytes 786440 | tf_op jit(solution)/shard_map/ppermute | solution.py:395
  76.5 9.6 %collective-permute-start.7 = (bf16[128,1024]{1,0:T(8,128)(2,1)S(1)}, bf16[128,1024]{1,0:T(8,128)(2,1)S(1)}, u32[]{:S(2)}, u32[]{:S(2)}) collective-permute-start(bf16[128,1024]{1,0:T(8,128)(2,1)S(1)} %total.4), channel_id=1, source_target_pairs={{0,65},{65,0},{1,64},{64,1},{2,67},{67,2},{3,66},{66,3},{4,69},{69... | collective-permute-start | bytes 786440 | tf_op jit(solution)/shard_map/ppermute | solution.py:396

commit v4 on v3

--- a/solution.py
+++ b/solution.py
@@ -47,26 +47,34 @@
 
 
 def project_kernel(
-    tok_ref, gain_ref, cache_ref, wq_ref, wk_ref, wv_ref, out_ref, held, arrived
+    tok_hbm, gain_hbm, cache_hbm, wq_hbm, wk_hbm, wv_hbm, out_ref, tok, gain, cache, held, arrived, landed
 ):
     columns = [slice(c * CHUNK, (c + 1) * CHUNK) for c in range(D // CHUNK)]
+    first = [
+        pltpu.make_async_copy(source, target, landed.at[i])
+        for i, (source, target) in enumerate(((tok_hbm, tok), (gain_hbm, gain), (cache_hbm, cache)))
+    ]
     copies = [
         [
-            pltpu.make_async_copy(w_ref.at[:, cut], held.at[kind, c], arrived.at[kind, c])
+            pltpu.make_async_copy(w_hbm.at[:, cut], held.at[kind, c], arrived.at[kind, c])
             for c, cut in enumerate(columns)
         ]
-        for kind, w_ref in enumerate((wq_ref, wk_ref, wv_ref))
+        for kind, w_hbm in enumerate((wq_hbm, wk_hbm, wv_hbm))
     ]
+    for copy in first:
+        copy.start()
     for row in copies:
         for copy in row:
             copy.start()
+    for copy in first:
+        copy.wait()
+    normed = norm_rows(tok[...], gain[...])
     for part in range(PAIRS):
         for kind in range(2):
             for p in range(PREF_GRP):
                 at = 3 * ROWS + (kind * PREF_GRP + p) * SHARE
                 cut = slice(kind * D + part * LANES, kind * D + (part + 1) * LANES)
-                out_ref[part, at : at + SHARE] = cache_ref[p, :, cut]
-    normed = norm_rows(tok_ref[...], gain_ref[...])
+                out_ref[part, at : at + SHARE] = cache[p, :, cut]
     for kind, row in enumerate(copies):
         for c, copy in enumerate(row):
             copy.wait()
@@ -78,22 +86,27 @@
 
 
 def project(tokens, gain, w_query, w_key, w_value, prefix_cache):
-    anywhere = pl.BlockSpec(memory_space=pl.ANY)
+    operands = (tokens, gain.reshape(1, D), prefix_cache, w_query, w_key, w_value)
     return pl.pallas_call(
         project_kernel,
-        in_specs=[VMEM_SPEC] * 3 + [anywhere] * 3,
+        in_specs=[pl.BlockSpec(memory_space=pltpu.HBM)] * 6,
         out_specs=VMEM_SPEC,
         out_shape=pltpu.VMEM((PAIRS, SENT, LANES), jnp.bfloat16),
         scratch_shapes=[
+            pltpu.VMEM((ROWS, D), jnp.bfloat16),
+            pltpu.VMEM((1, D), jnp.float32),
+            pltpu.VMEM(prefix_cache.shape, jnp.bfloat16),
             pltpu.VMEM((3, D // CHUNK, D, CHUNK), jnp.bfloat16),
             pltpu.SemaphoreType.DMA((3, D // CHUNK)),
+            pltpu.SemaphoreType.DMA((3,)),
         ],
         compiler_params=pltpu.CompilerParams(vmem_limit_bytes=VMEM_LIMIT),
         name="project",
-    )(*on_chip(tokens, gain.reshape(1, D), prefix_cache), w_query, w_key, w_value)
-
-
-def spread_kernel(got_ref, up_ref, down_ref, far_ref):
+    )(*(pltpu.with_memory_space_constraint(a, pltpu.HBM) for a in operands))
+
+
+def spread_kernel(got_ref, tok_ref, up_ref, down_ref, far_ref, same_ref):
+    same_ref[...] = tok_ref[...]
     for source in range(PAIRS):
         rows = slice(source * 4 * SHARE, (source + 1) * 4 * SHARE)
         held = got_ref[source, 3 * ROWS :]
@@ -104,16 +117,21 @@
     down_ref[QUARTER:] = got_ref[0, ROWS : 3 * ROWS]
 
 
-def spread(got):
+def spread(got, tokens):
     shape = pltpu.VMEM((QUARTER + 2 * ROWS, LANES), jnp.bfloat16)
     return pl.pallas_call(
         spread_kernel,
-        in_specs=[VMEM_SPEC],
-        out_specs=(VMEM_SPEC,) * 3,
-        out_shape=(shape, shape, pltpu.VMEM((QUARTER, LANES), jnp.bfloat16)),
+        in_specs=[VMEM_SPEC] * 2,
+        out_specs=(VMEM_SPEC,) * 4,
+        out_shape=(
+            shape,
+            shape,
+            pltpu.VMEM((QUARTER, LANES), jnp.bfloat16),
+            pltpu.VMEM((ROWS, D), jnp.bfloat16),
+        ),
         compiler_params=pltpu.CompilerParams(vmem_limit_bytes=VMEM_LIMIT),
         name="spread",
-    )(*on_chip(got))
+    )(*on_chip(got, tokens))
 
 
 def bias_line(rel_ref, head, first_bucket):
@@ -184,8 +202,34 @@
 
 
 def attend_kernel(
-    place_ref, got_ref, prev_ref, next_ref, far_ref, near_ref, line_ref, meta_ref, out_ref, keys, values, kwin, vwin
+    place_ref,
+    got_ref,
+    prev_ref,
+    next_ref,
+    far_ref,
+    near_ref,
+    line_ref,
+    meta_ref,
+    _,
+    w1_hbm,
+    w2_hbm,
+    w3_hbm,
+    out_ref,
+    w1_ref,
+    w2_ref,
+    w3_ref,
+    keys,
+    values,
+    kwin,
+    vwin,
+    landed,
 ):
+    copies = [
+        pltpu.make_async_copy(source, target, landed.at[i])
+        for i, (source, target) in enumerate(((w1_hbm, w1_ref), (w2_hbm, w2_ref), (w3_hbm, w3_ref)))
+    ]
+    for copy in copies:
+        copy.start()
     lane = lax.broadcasted_iota(jnp.int32, (ROWS, LANES), 1)
     low = lane < DK
     for b in range(PAIRS + 2):
@@ -254,93 +298,93 @@
         )
         total = jnp.where(second, far_out[:, LANES:], far_out[:, :LANES]) + near_out
         total = total / row_sum
-        out_ref[step] = jnp.where(low, total[:ROWS], total[ROWS:]).astype(jnp.bfloat16)
+        done = jnp.where(low, total[:ROWS], total[ROWS:]).astype(jnp.bfloat16)
+        side = place_ref[2]
+        out_ref[side * PAIRS + step] = done
+        out_ref[(1 - side) * PAIRS + jnp.bitwise_xor(step, 1)] = done
         return 0
 
     lax.fori_loop(0, PAIRS, one, 0)
-
-
-def attend(place, got, prev, after_it, far, made):
+    for copy in copies:
+        copy.wait()
+
+
+def attend(place, got, prev, after_it, far, made, ready, later_weights):
+    hbm = pl.BlockSpec(memory_space=pltpu.HBM)
     return pl.pallas_call(
         attend_kernel,
-        in_specs=[SMEM_SPEC] + [VMEM_SPEC] * 7,
-        out_specs=VMEM_SPEC,
-        out_shape=pltpu.VMEM((PAIRS, ROWS, LANES), jnp.bfloat16),
+        in_specs=[SMEM_SPEC] + [VMEM_SPEC] * 8 + [hbm] * 3,
+        out_specs=(VMEM_SPEC,) * 4,
+        out_shape=(pltpu.VMEM((2 * PAIRS, ROWS, LANES), jnp.bfloat16),)
+        + tuple(pltpu.VMEM(w.shape, w.dtype) for w in later_weights),
         scratch_shapes=[
             pltpu.VMEM((4, PREF_GRP * LANES, PLEN // 4), jnp.bfloat16),
             pltpu.VMEM((4, PLEN // 4, PREF_GRP * LANES), jnp.bfloat16),
             pltpu.VMEM((PAIRS + 2, LANES, ROWS), jnp.bfloat16),
             pltpu.VMEM((PAIRS + 2, ROWS, LANES), jnp.bfloat16),
+            pltpu.SemaphoreType.DMA((3,)),
         ],
         compiler_params=pltpu.CompilerParams(vmem_limit_bytes=VMEM_LIMIT),
         name="attend",
-    )(place, *on_chip(got, prev, after_it, far, *made))
-
-
-def join_kernel(att_ref, w_ref, tok_ref, gain_ref, hidden_ref, normed_ref):
-    attended = jnp.concatenate([att_ref[j] for j in range(PAIRS)], axis=1)
-    got = jnp.dot(attended, w_ref[...], preferred_element_type=jnp.float32)
-    hidden = (tok_ref[...].astype(jnp.float32) + got).astype(jnp.bfloat16)
-    hidden_ref[...] = hidden
-    normed_ref[...] = norm_rows(hidden, gain_ref[...])
-
-
-def join(att, w_attn_out, tokens, gain):
-    shape = pltpu.VMEM((ROWS, D), jnp.bfloat16)
+    )(
+        place,
+        *on_chip(got, prev, after_it, far, *made, ready),
+        *(pltpu.with_memory_space_constraint(w, pltpu.HBM) for w in later_weights),
+    )
+
+
+def join_kernel(place_ref, att_ref, w_ref, tok_ref, far_tok_ref, gain_ref, hidden_ref, normed_ref):
+    side = place_ref[2]
+    halves = [
+        jnp.concatenate([att_ref[at * PAIRS + j] for j in range(PAIRS)], axis=1) for at in (side, 1 - side)
+    ]
+    got = jnp.dot(jnp.concatenate(halves, axis=0), w_ref[...], preferred_element_type=jnp.float32)
+    for half, ref in enumerate((tok_ref, far_tok_ref)):
+        mine = got[half * ROWS : (half + 1) * ROWS]
+        hidden = (ref[...].astype(jnp.float32) + mine).astype(jnp.bfloat16)
+        if half == 0:
+            hidden_ref[...] = hidden
+        normed_ref[half] = norm_rows(hidden, gain_ref[...])
+
+
+def join(place, att, w_attn_out, tokens, far_tokens, gain):
     return pl.pallas_call(
         join_kernel,
-        in_specs=[VMEM_SPEC] * 4,
+        in_specs=[SMEM_SPEC] + [VMEM_SPEC] * 5,
         out_specs=(VMEM_SPEC,) * 2,
-        out_shape=(shape, shape),
+        out_shape=(pltpu.VMEM((ROWS, D), jnp.bfloat16), pltpu.VMEM((2, ROWS, D), jnp.bfloat16)),
         compiler_params=pltpu.CompilerParams(vmem_limit_bytes=VMEM_LIMIT),
         name="join",
-    )(*on_chip(att, w_attn_out, tokens, gain.reshape(1, D)))
-
-
-def feed_kernel(one_ref, two_ref, in_ref, out_ref, first_ref, second_ref):
-    two = two_ref[...] if len(two_ref.shape) == 2 else two_ref[0]
-    rows = jnp.concatenate([one_ref[...], two], axis=0)
+    )(place, *on_chip(att, w_attn_out, tokens, far_tokens, gain.reshape(1, D)))
+
+
+def feed_kernel(picked, rows_ref, in_ref, out_w_ref, *rest):
+    out_refs = rest[len(rest) - len(picked) :]
+    rows = jnp.concatenate([rows_ref[half] for half in picked], axis=0)
     units = lax.dot_general(
         rows, in_ref[...], (((1,), (1,)), ((), ())), preferred_element_type=jnp.float32
     )
     units = jnp.maximum(units, 0.0).astype(jnp.bfloat16)
-    got = jnp.dot(units, out_ref[...], preferred_element_type=jnp.float32).astype(jnp.bfloat16)
-    first_ref[...] = got[:ROWS]
-    second_ref[...] = got[ROWS:]
-
-
-def feed(one, two, w_in, w_out):
+    got = jnp.dot(units, out_w_ref[...], preferred_element_type=jnp.float32).astype(jnp.bfloat16)
+    for at, ref in enumerate(out_refs):
+        ref[...] = got[at * ROWS : (at + 1) * ROWS]
+
+
+def feed(picked, rows, w_in, w_out, *ready):
     shape = pltpu.VMEM((ROWS, D), jnp.bfloat16)
     return pl.pallas_call(
-        feed_kernel,
-        in_specs=[VMEM_SPEC] * 4,
-        out_specs=(VMEM_SPEC,) * 2,
-        out_shape=(shape, shape),
+        functools.partial(feed_kernel, picked),
+        in_specs=[VMEM_SPEC] * (3 + len(ready)),
+        out_specs=(VMEM_SPEC,) * len(picked),
+        out_shape=(shape,) * len(picked),
         compiler_params=pltpu.CompilerParams(vmem_limit_bytes=VMEM_LIMIT),
         name="feed",
-    )(*on_chip(one, two, w_in, w_out))
-
-
-def pack_kernel(one_ref, two_ref, out_ref):
-    out_ref[0] = one_ref[...]
-    out_ref[1] = two_ref[...]
-
-
-def pack(one, two):
-    return pl.pallas_call(
-        pack_kernel,
-        in_specs=[VMEM_SPEC] * 2,
-        out_specs=VMEM_SPEC,
-        out_shape=pltpu.VMEM((2,) + one.shape, one.dtype),
-        compiler_params=pltpu.CompilerParams(vmem_limit_bytes=VMEM_LIMIT),
-        name="pack",
-    )(*on_chip(one, two))
+    )(*on_chip(rows, w_in, w_out, *ready))
 
 
 def total_kernel(*refs):
     out_ref = refs[-1]
-    values = [ref[...] if len(ref.shape) == 2 else ref[1] for ref in refs[:-1]]
-    total = functools.reduce(jnp.add, [value.astype(jnp.float32) for value in values])
+    total = functools.reduce(jnp.add, [ref[...].astype(jnp.float32) for ref in refs[:-1]])
     out_ref[...] = total.astype(out_ref.dtype)
 
 
@@ -372,29 +416,31 @@
 ):
     count_x = lax.axis_size("x")
     plane = lax.axis_index("z") * 2 + lax.axis_index("ylo")
-    place = jnp.stack([lax.axis_index("x"), plane]).astype(jnp.int32)
+    place = jnp.stack([lax.axis_index("x"), plane, lax.axis_index("yhi")]).astype(jnp.int32)
     made = tables(place, rel_bias, lengths, prefix_map)
 
     blocks = project(tokens, attn_gain, w_query, w_key, w_value, prefix_cache)
     got = lax.all_to_all(blocks, PLANE, 0, 0, tiled=True)
-    up, down, far = spread(got)
+    up, down, far, same = spread(got, tokens)
     by = lambda d: [(i, (i + d) % count_x) for i in range(count_x)]
     prev = lax.ppermute(up, "x", by(1))
     later = lax.ppermute(down, "x", by(-1))
     opposite = lax.ppermute(far, "x", by(2))
-    mixed = attend(place, got, prev, later, opposite, made)
-    att = lax.all_to_all(mixed, PLANE, 0, 0, tiled=True)
-    hidden, normed = join(att, w_attn_out, tokens, mlp_gain)
-
     mirrored = ("yhi", "ylo")
-    far = lax.ppermute(normed, mirrored, MIRROR)
+    far_tokens = lax.ppermute(same, mirrored, MIRROR)
+    mixed, w_attn_out, w_in, w_out = attend(
+        place, got, prev, later, opposite, made, far_tokens, (w_attn_out, w_in, w_out)
+    )
+    att = lax.all_to_all(mixed, ("yhi",) + PLANE, 0, 0, tiled=True)
+    hidden, normed = join(place, att, w_attn_out, tokens, far_tokens, mlp_gain)
+
     other = lax.ppermute(normed, "core", SWAP)
-    mine, theirs = feed(normed, other, w_in, w_out)
-    pair_swap = lax.ppermute(pack(far, theirs), "core", SWAP)
-    far_mine, far_theirs = feed(far, pair_swap, w_in, w_out)
+    mine, far_mine = feed((0, 1), normed, w_in, w_out)
+    (far_theirs,) = feed((1,), other, w_in, w_out, mine)
     far_sum = total(jnp.bfloat16, far_mine, lax.ppermute(far_theirs, "core", SWAP))
     back = lax.ppermute(far_sum, mirrored, MIRROR)
-    local = total(jnp.float32, hidden, mine, pair_swap)
+    (theirs,) = feed((0,), other, w_in, w_out, far_theirs)
+    local = total(jnp.float32, hidden, mine, lax.ppermute(theirs, "core", SWAP))
     return total(jnp.bfloat16, local, back, last=True)
 
 

time: 87.5 us -> 75.6 us (0.86)
  waiting for transfers between devices: 21.1 us -> 12.2 us
  local copies, waits for them, and re-layouts: 7.35 us -> 0.03 us
  blocking collectives: 31 us -> 34.1 us
  Pallas kernels: 17 us -> 19.2 us
    ppermute x2, waiting for transfers between devices: 8.16 us -> 0.01 us  [the longest x1 0.01 us: body(): far_tokens = lax.ppermute(same, mirrored, MIRROR)]
    unnamed x28 -> x10, local copies, waits for them, and re-layouts: 7.35 us -> 0.03 us
    all_to_all x1, blocking collectives: 10.3 us -> 13.3 us  [body(): att = lax.all_to_all(mixed, ('yhi',) + PLANE, 0, 0, tiled=True)]
    pallas_call x7, Pallas kernels: 14.9 us -> 17.1 us  [the longest x1 7.34 us: attend(): pl.pallas_call(attend_kernel, in_specs=[SMEM_SPEC] + [VMEM_SPEC] * 8 + [h...]
    ppermute x1, waiting for transfers between devices: 1.4 us -> 0.01 us  [body(): lax.ppermute(far_theirs, 'core', SWAP)]
    ppermute x1, starting transfers between devices: 2.36 us -> 1.4 us  [body(): back = lax.ppermute(far_sum, mirrored, MIRROR)]
    ppermute x1, waiting for transfers between devices: 7.19 us -> 8.14 us  [body(): back = lax.ppermute(far_sum, mirrored, MIRROR)]
    ppermute x1, waiting for transfers between devices: 4.35 us -> 3.41 us  [body(): opposite = lax.ppermute(far, 'x', by(2))]
  transfers between devices with their start and end apart: 8 -> 8, of which waited for: 5 -> 3; matrix products, arithmetic and copies ran while one was open for 0% -> 0% of each run, Pallas kernels for 3% -> 5%
where the time goes in v4:
time: 75.6 us; the launch traced here: 75.2 us
  blocking collectives  34.1 us (45%)
  Pallas kernels  19.2 us (25%)
  waiting for transfers between devices  12.2 us (16%)
  starting transfers between devices  9.47 us (13%)
    all_to_all x1, blocking collectives, body(): got = lax.all_to_all(blocks, PLANE, 0, 0, tiled=True)  20.8 us
    all_to_all x1, blocking collectives, body(): att = lax.all_to_all(mixed, ('yhi',) + PLANE, 0, 0, tiled=True)  13.3 us
    ppermute x1, waiting for transfers between devices, body(): back = lax.ppermute(far_sum, mirrored, MIRROR)  8.14 us
    pallas_call x1, Pallas kernels, attend(): pl.pallas_call(attend_kernel, in_specs=[SMEM_SPEC] + [VMEM_SPEC] * 8 + [h...  7.34 us
    pallas_call x1, Pallas kernels, project(): pl.pallas_call(project_kernel, in_specs=[pl.BlockSpec(memory_space=pltpu....  4.73 us
    pallas_call x3, Pallas kernels, feed(): pl.pallas_call(functools.partial(feed_kernel, picked), in_specs=[VMEM_SPE...  3.51 us
    ppermute x1, waiting for transfers between devices, body(): opposite = lax.ppermute(far, 'x', by(2))  3.41 us
    ppermute x1, starting transfers between devices, body(): far_tokens = lax.ppermute(same, mirrored, MIRROR)  2.25 us
  transfers between devices with their start and end apart: 8, of which 3 were waited for; matrix products, arithmetic and copies ran while one was open for 0% of the time, Pallas kernels for 5%

profile of v4, /device:TPU:0, one launch (start us, length us, event | category | flops | bytes accessed | tf_op | source)
XLA Modules:
  0.0 75.2 jit_solution(3602677061190673746)
XLA Ops:
  0.0 0.0 copy-start
  0.0 4.7 %project.1 = bf16[8,448,128]{2,1,0:T(8,128)(2,1)S(1)} custom-call(bf16[128,1024]{1,0:T(8,128)(2,1)} %tok_ref.3, f32[1,1024]{1,0:T(1,128)} %bitcast.8, bf16[2,16,2048]{2,1,0:T(8,128)(2,1)} %cache_hbm.1, bf16[1024,1024]{1,0:T(8,128)(2,1)} %wq_hbm.1, bf16[1024,1024]{1,0:T(8,128)(2,1)} %wk_hbm.1, bf16[1024,1024]{1,0:T(8,128)(2,1)} %wv_hbm.1), custom_call_target="tpu_custom_call" | custom-call | tf_op jit(solution)/shard_map/project/pallas_call | solution.py:90
  4.7 0.0 copy-start.1
  4.8 0.0 copy-start.3
  4.8 0.0 copy-start.4
  4.8 20.8 %all_to_all.10.got_ref = bf16[8,448,128]{2,1,0:T(8,128)(2,1)S(1)} all-to-all(bf16[8,448,128]{2,1,0:T(8,128)(2,1)S(1)} %project.1), channel_id=1, replica_groups=mesh['yhi'=2,'core'=2,'x'=4,'z'=4,'ylo'=2] {'z','ylo'}, dimensions={0} | all-to-all | bytes 1835008 | tf_op jit(solution)/shard_map/all_to_all | solution.py:423
  25.5 0.0 copy-done
  25.5 0.1 spread.1
  25.6 2.2 %collective-permute-start.3 = (bf16[128,1024]{1,0:T(8,128)(2,1)S(1)}, bf16[128,1024]{1,0:T(8,128)(2,1)S(1)}, u32[]{:S(2)}, u32[]{:S(2)}) collective-permute-start(bf16[128,1024]{1,0:T(8,128)(2,1)S(1)} %get-tuple-element.26), channel_id=1, source_target_pairs={{0,65},{65,0},{1,64},{64,1},{2,67},{67,2},{3,66},{66,3},{4,69},{69... | collective-permute-start | bytes 786440 | tf_op jit(solution)/shard_map/ppermute | solution.py:430
  27.9 1.5 %collective-permute-start = (bf16[768,128]{1,0:T(8,128)(2,1)S(1)}, bf16[768,128]{1,0:T(8,128)(2,1)S(1)}, u32[]{:S(2)}, u32[]{:S(2)}) collective-permute-start(bf16[768,128]{1,0:T(8,128)(2,1)S(1)} %get-tuple-element.20), channel_id=1, source_target_pairs={{0,8},{8,16},{16,24},{24,0},{1,9},{9,17},{17,25},{25,1},{2,10},{10... | collective-permute-start | bytes 589832 | tf_op jit(solution)/shard_map/ppermute | solution.py:426
  29.4 1.8 %collective-permute-start.1 = (bf16[768,128]{1,0:T(8,128)(2,1)S(1)}, bf16[768,128]{1,0:T(8,128)(2,1)S(1)}, u32[]{:S(2)}, u32[]{:S(2)}) collective-permute-start(bf16[768,128]{1,0:T(8,128)(2,1)S(1)} %get-tuple-element.21), channel_id=1, source_target_pairs={{0,24},{8,0},{16,8},{24,16},{1,25},{9,1},{17,9},{25,17},{2,26},{10... | collective-permute-start | bytes 589832 | tf_op jit(solution)/shard_map/ppermute | solution.py:427
  31.1 1.8 %collective-permute-start.2 = (bf16[512,128]{1,0:T(8,128)(2,1)S(1)}, bf16[512,128]{1,0:T(8,128)(2,1)S(1)}, u32[]{:S(2)}, u32[]{:S(2)}) collective-permute-start(bf16[512,128]{1,0:T(8,128)(2,1)S(1)} %get-tuple-element.22), channel_id=1, source_target_pairs={{0,16},{8,24},{16,0},{24,8},{1,17},{9,25},{17,1},{25,9},{2,18},{10... | collective-permute-start | bytes 393224 | tf_op jit(solution)/shard_map/ppermute | solution.py:428
  32.9 0.1 pad_add_fusion.place_ref
  33.0 0.0 copy-done.1
  33.0 0.0 copy-done.3
  33.0 0.0 copy-done.4
  33.0 1.2 %tables.1 = (f32[256,384]{1,0:T(8,128)S(1)}, f32[256,128]{1,0:T(8,128)S(1)}, f32[10,8,128]{2,1,0:T(8,128)S(1)}) custom-call(s32[3]{0:T(128)S(1)} %pad_add_fusion.place_ref, f32[16,32]{1,0:T(8,128)S(1)} %bitcast.6, s32[1,64]{1,0:T(1,128)S(1)} %copy-done.3, s32[1,64]{1,0:T(1,128)S(1)} %copy-done.4), custom_call_target="tpu_custom_call" | custom-call | tf_op jit(solution)/shard_map/tables/pallas_call | solution.py:190
  34.3 3.4 %collective-permute-done.2.far_ref = bf16[512,128]{1,0:T(8,128)(2,1)S(1)} collective-permute-done((bf16[512,128]{1,0:T(8,128)(2,1)S(1)}, bf16[512,128]{1,0:T(8,128)(2,1)S(1)}, u32[]{:S(2)}, u32[]{:S(2)}) %collective-permute-start.2) | collective-permute-done | bytes 131104 | tf_op jit(solution)/shard_map/ppermute | solution.py:428
  37.7 0.0 collective-permute-done.prev_ref
  37.7 0.0 collective-permute-done.1.next_ref
  37.7 0.0 collective-permute-done.3._.far_tok_ref
  37.7 0.0 copy-start.2
  37.7 7.3 %attend.1 = (bf16[16,128,128]{2,1,0:T(8,128)(2,1)S(1)}, bf16[1024,1024]{1,0:T(8,128)(2,1)S(1)}, bf16[1024,1024]{1,0:T(8,128)(2,1)S(1)}, bf16[1024,1024]{1,0:T(8,128)(2,1)S(1)}) custom-call(s32[3]{0:T(128)S(1)} %pad_add_fusion.place_ref, bf16[8,448,128]{2,1,0:T(8,128)(2,1)S(1)} %all_to_all.10.got_ref, bf16[768,128]{1,0:T(8,128)(2,1)S(1)} %collective-permute-done.prev_ref, ...), custom_call_target="tpu_custom_call" | custom-call | tf_op jit(solution)/shard_map/attend/pallas_call | solution.py:314
  45.0 13.3 %all_to_all.11.att_ref = bf16[16,128,128]{2,1,0:T(8,128)(2,1)S(1)} all-to-all(bf16[16,128,128]{2,1,0:T(8,128)(2,1)S(1)} %get-tuple-element.27), channel_id=1, replica_groups=mesh['yhi'=2,'core'=2,'x'=4,'z'=4,'ylo'=2] {'yhi','z','ylo'}, dimensions={0} | all-to-all | bytes 1048576 | tf_op jit(solution)/shard_map/all_to_all | solution.py:434
  58.4 0.0 copy-done.2
  58.4 1.5 %join.1 = (bf16[128,1024]{1,0:T(8,128)(2,1)S(1)}, bf16[2,128,1024]{2,1,0:T(8,128)(2,1)S(1)}) custom-call(s32[3]{0:T(128)S(1)} %pad_add_fusion.place_ref, bf16[16,128,128]{2,1,0:T(8,128)(2,1)S(1)} %all_to_all.11.att_ref, bf16[1024,1024]{1,0:T(8,128)(2,1)S(1)} %get-tuple-element.28.w_ref, bf16[128,1024]{1,0:T(8,128)(2,1)S(1)} %copy-done, ...), custom_call_target="tpu_custom_call" | custom-call | tf_op jit(solution)/shard_map/join/pallas_call | solution.py:351
  59.9 0.1 collective-permute-start.4
  60.0 1.3 %feed.3 = (bf16[128,1024]{1,0:T(8,128)(2,1)S(1)}, bf16[128,1024]{1,0:T(8,128)(2,1)S(1)}) custom-call(bf16[2,128,1024]{2,1,0:T(8,128)(2,1)S(1)} %get-tuple-element.30.rows_ref, bf16[1024,1024]{1,0:T(8,128)(2,1)S(1)} %get-tuple-element.31.in_ref, bf16[1024,1024]{1,0:T(8,128)(2,1)S(1)} %get-tuple-element.32.out_w_ref), custom_call_target="tpu_custom_call" | custom-call | tf_op jit(solution)/shard_map/feed/pallas_call | solution.py:375
  61.2 0.6 collective-permute-done.4.rows_ref
  61.8 1.1 %feed.4.rest_0_ = bf16[128,1024]{1,0:T(8,128)(2,1)S(1)} custom-call(bf16[2,128,1024]{2,1,0:T(8,128)(2,1)S(1)} %collective-permute-done.4.rows_ref, bf16[1024,1024]{1,0:T(8,128)(2,1)S(1)} %get-tuple-element.31.in_ref, bf16[1024,1024]{1,0:T(8,128)(2,1)S(1)} %get-tuple-element.32.out_w_ref, bf16[128,1024]{1,0:T(8,128)(2,1)S(1)} %get-tuple-element.33.rest_0_.refs_1_), custom_call_target="tpu_custom_call" | custom-call | tf_op jit(solution)/shard_map/feed/pallas_call | solution.py:375
  63.0 0.2 collective-permute-start.6
  63.2 1.1 %feed.5 = bf16[128,1024]{1,0:T(8,128)(2,1)S(1)} custom-call(bf16[2,128,1024]{2,1,0:T(8,128)(2,1)S(1)} %collective-permute-done.4.rows_ref, bf16[1024,1024]{1,0:T(8,128)(2,1)S(1)} %get-tuple-element.31.in_ref, bf16[1024,1024]{1,0:T(8,128)(2,1)S(1)} %get-tuple-element.32.out_w_ref, bf16[128,1024]{1,0:T(8,128)(2,1)S(1)} %feed.4.rest_0_), custom_call_target="tpu_custom_call" | custom-call | tf_op jit(solution)/shard_map/feed/pallas_call | solution.py:375
  64.3 0.5 collective-permute-start.5
  64.8 0.0 collective-permute-done.6.refs_1_
  64.8 0.1 total.4
  64.8 1.4 %collective-permute-start.7 = (bf16[128,1024]{1,0:T(8,128)(2,1)S(1)}, bf16[128,1024]{1,0:T(8,128)(2,1)S(1)}, u32[]{:S(2)}, u32[]{:S(2)}) collective-permute-start(bf16[128,1024]{1,0:T(8,128)(2,1)S(1)} %total.4), channel_id=1, source_target_pairs={{0,65},{65,0},{1,64},{64,1},{2,67},{67,2},{3,66},{66,3},{4,69},{69... | collective-permute-start | bytes 786440 | tf_op jit(solution)/shard_map/ppermute | solution.py:441
  66.2 0.0 collective-permute-done.5.refs_2_
  66.2 0.1 total.3.refs_0_
  66.3 8.1 %collective-permute-done.7.refs_1_ = bf16[128,1024]{1,0:T(8,128)(2,1)S(1)} collective-permute-done((bf16[128,1024]{1,0:T(8,128)(2,1)S(1)}, bf16[128,1024]{1,0:T(8,128)(2,1)S(1)}, u32[]{:S(2)}, u32[]{:S(2)}) %collective-permute-start.7) | collective-permute-done | bytes 262176 | tf_op jit(solution)/shard_map/ppermute | solution.py:441
  74.5 0.7 total.5
Async XLA Ops:
  0.0 25.5 %copy-start = (bf16[128,1024]{1,0:T(8,128)(2,1)S(1)}, bf16[128,1024]{1,0:T(8,128)(2,1)}, u32[]{:S(2)}) copy-start(bf16[128,1024]{1,0:T(8,128)(2,1)} %tok_ref.3) | copy-start | bytes 786436
  4.7 28.3 %copy-start.1 = (f32[32,16]{0,1:T(8,128)S(1)}, f32[32,16]{0,1:T(8,128)}, u32[]{:S(2)}) copy-start(f32[32,16]{0,1:T(8,128)} %param.19) | copy-start | bytes 6148
  4.8 28.3 %copy-start.3 = (s32[1,64]{1,0:T(1,128)S(1)}, s32[1,64]{1,0:T(1,128)}, u32[]{:S(2)}) copy-start(s32[1,64]{1,0:T(1,128)} %len_ref.1) | copy-start | bytes 772
  4.8 28.2 %copy-start.4 = (s32[1,64]{1,0:T(1,128)S(1)}, s32[1,64]{1,0:T(1,128)}, u32[]{:S(2)}) copy-start(s32[1,64]{1,0:T(1,128)} %map_ref.1) | copy-start | bytes 772
  25.6 12.1 %collective-permute-start.3 = (bf16[128,1024]{1,0:T(8,128)(2,1)S(1)}, bf16[128,1024]{1,0:T(8,128)(2,1)S(1)}, u32[]{:S(2)}, u32[]{:S(2)}) collective-permute-start(bf16[128,1024]{1,0:T(8,128)(2,1)S(1)} %get-tuple-element.26), channel_id=1, source_target_pairs={{0,65},{65,0},{1,64},{64,1},{2,67},{67,2},{3,66},{66,3},{4,69},{69... | collective-permute-start | bytes 786440 | tf_op jit(solution)/shard_map/ppermute | solution.py:430
  27.9 9.8 %collective-permute-start = (bf16[768,128]{1,0:T(8,128)(2,1)S(1)}, bf16[768,128]{1,0:T(8,128)(2,1)S(1)}, u32[]{:S(2)}, u32[]{:S(2)}) collective-permute-start(bf16[768,128]{1,0:T(8,128)(2,1)S(1)} %get-tuple-element.20), channel_id=1, source_target_pairs={{0,8},{8,16},{16,24},{24,0},{1,9},{9,17},{17,25},{25,1},{2,10},{10... | collective-permute-start | bytes 589832 | tf_op jit(solution)/shard_map/ppermute | solution.py:426
  29.4 8.3 %collective-permute-start.1 = (bf16[768,128]{1,0:T(8,128)(2,1)S(1)}, bf16[768,128]{1,0:T(8,128)(2,1)S(1)}, u32[]{:S(2)}, u32[]{:S(2)}) collective-permute-start(bf16[768,128]{1,0:T(8,128)(2,1)S(1)} %get-tuple-element.21), channel_id=1, source_target_pairs={{0,24},{8,0},{16,8},{24,16},{1,25},{9,1},{17,9},{25,17},{2,26},{10... | collective-permute-start | bytes 589832 | tf_op jit(solution)/shard_map/ppermute | solution.py:427
  31.1 6.6 %collective-permute-start.2 = (bf16[512,128]{1,0:T(8,128)(2,1)S(1)}, bf16[512,128]{1,0:T(8,128)(2,1)S(1)}, u32[]{:S(2)}, u32[]{:S(2)}) collective-permute-start(bf16[512,128]{1,0:T(8,128)(2,1)S(1)} %get-tuple-element.22), channel_id=1, source_target_pairs={{0,16},{8,24},{16,0},{24,8},{1,17},{9,25},{17,1},{25,9},{2,18},{10... | collective-permute-start | bytes 393224 | tf_op jit(solution)/shard_map/ppermute | solution.py:428
  37.7 20.7 %copy-start.2 = (f32[1024]{0:T(1024)S(1)}, f32[1024]{0:T(1024)}, u32[]{:S(2)}) copy-start(f32[1024]{0:T(1024)} %param.23) | copy-start | bytes 12292
  59.9 2.0 %collective-permute-start.4 = (bf16[2,128,1024]{2,1,0:T(8,128)(2,1)S(1)}, bf16[2,128,1024]{2,1,0:T(8,128)(2,1)S(1)}, u32[]{:S(2)}, u32[]{:S(2)}) collective-permute-start(bf16[2,128,1024]{2,1,0:T(8,128)(2,1)S(1)} %get-tuple-element.30.rows_ref), channel_id=1, source_target_pairs={{0,32},{32,0},{1,33},{33,1},{2,34},{34,2},{3,35},{35,3},{4,36},{36... | collective-permute-start | bytes 1572872 | tf_op jit(solution)/shard_map/ppermute | solution.py:437
  63.0 1.8 %collective-permute-start.6 = (bf16[128,1024]{1,0:T(8,128)(2,1)S(1)}, bf16[128,1024]{1,0:T(8,128)(2,1)S(1)}, u32[]{:S(2)}, u32[]{:S(2)}) collective-permute-start(bf16[128,1024]{1,0:T(8,128)(2,1)S(1)} %feed.4.rest_0_), channel_id=1, source_target_pairs={{0,32},{32,0},{1,33},{33,1},{2,34},{34,2},{3,35},{35,3},{4,36},{36... | collective-permute-start | bytes 786440 | tf_op jit(solution)/shard_map/ppermute | solution.py:440
  64.3 1.9 %collective-permute-start.5 = (bf16[128,1024]{1,0:T(8,128)(2,1)S(1)}, bf16[128,1024]{1,0:T(8,128)(2,1)S(1)}, u32[]{:S(2)}, u32[]{:S(2)}) collective-permute-start(bf16[128,1024]{1,0:T(8,128)(2,1)S(1)} %feed.5), channel_id=1, source_target_pairs={{0,32},{32,0},{1,33},{33,1},{2,34},{34,2},{3,35},{35,3},{4,36},{36... | collective-permute-start | bytes 786440 | tf_op jit(solution)/shard_map/ppermute | solution.py:443
  64.8 9.6 %collective-permute-start.7 = (bf16[128,1024]{1,0:T(8,128)(2,1)S(1)}, bf16[128,1024]{1,0:T(8,128)(2,1)S(1)}, u32[]{:S(2)}, u32[]{:S(2)}) collective-permute-start(bf16[128,1024]{1,0:T(8,128)(2,1)S(1)} %total.4), channel_id=1, source_target_pairs={{0,65},{65,0},{1,64},{64,1},{2,67},{67,2},{3,66},{66,3},{4,69},{69... | collective-permute-start | bytes 786440 | tf_op jit(solution)/shard_map/ppermute | solution.py:441

commit v5 on v4

--- a/solution.py
+++ b/solution.py
@@ -24,6 +24,7 @@
 far_marks = (12, 16, 23, 32, 46, 64, 91)
 masked_score = -1e30
 VMEM_LIMIT = 16 * 1024 * 1024
+COST = pl.CostEstimate(flops=1000, transcendentals=0, bytes_accessed=1000)
 
 AXES = ("yhi", "core", "x", "z", "ylo")
 REQ = ("x", "z", "ylo")
@@ -42,7 +43,12 @@
     return tuple(pltpu.with_memory_space_constraint(a, pltpu.VMEM) for a in arrays)
 
 
+def off_chip(*arrays):
+    return tuple(pltpu.with_memory_space_constraint(a, pltpu.HBM) for a in arrays)
+
+
 VMEM_SPEC = pl.BlockSpec(memory_space=pltpu.VMEM)
+HBM_SPEC = pl.BlockSpec(memory_space=pltpu.HBM)
 SMEM_SPEC = pl.BlockSpec(memory_space=pltpu.SMEM)
 
 
@@ -89,9 +95,9 @@
     operands = (tokens, gain.reshape(1, D), prefix_cache, w_query, w_key, w_value)
     return pl.pallas_call(
         project_kernel,
-        in_specs=[pl.BlockSpec(memory_space=pltpu.HBM)] * 6,
+        in_specs=[HBM_SPEC] * 6,
         out_specs=VMEM_SPEC,
-        out_shape=pltpu.VMEM((PAIRS, SENT, LANES), jnp.bfloat16),
+        out_shape=pltpu.HBM((PAIRS, SENT, LANES), jnp.bfloat16),
         scratch_shapes=[
             pltpu.VMEM((ROWS, D), jnp.bfloat16),
             pltpu.VMEM((1, D), jnp.float32),
@@ -101,12 +107,13 @@
             pltpu.SemaphoreType.DMA((3,)),
         ],
         compiler_params=pltpu.CompilerParams(vmem_limit_bytes=VMEM_LIMIT),
+        cost_estimate=COST,
         name="project",
-    )(*(pltpu.with_memory_space_constraint(a, pltpu.HBM) for a in operands))
-
-
-def spread_kernel(got_ref, tok_ref, up_ref, down_ref, far_ref, same_ref):
-    same_ref[...] = tok_ref[...]
+    )(*off_chip(*operands))
+
+
+def spread_kernel(got_ref, *rest):
+    up_ref, down_ref, far_ref = rest[-3:]
     for source in range(PAIRS):
         rows = slice(source * 4 * SHARE, (source + 1) * 4 * SHARE)
         held = got_ref[source, 3 * ROWS :]
@@ -117,21 +124,17 @@
     down_ref[QUARTER:] = got_ref[0, ROWS : 3 * ROWS]
 
 
-def spread(got, tokens):
+def spread(got, *ready):
     shape = pltpu.VMEM((QUARTER + 2 * ROWS, LANES), jnp.bfloat16)
     return pl.pallas_call(
         spread_kernel,
-        in_specs=[VMEM_SPEC] * 2,
-        out_specs=(VMEM_SPEC,) * 4,
-        out_shape=(
-            shape,
-            shape,
-            pltpu.VMEM((QUARTER, LANES), jnp.bfloat16),
-            pltpu.VMEM((ROWS, D), jnp.bfloat16),
-        ),
-        compiler_params=pltpu.CompilerParams(vmem_limit_bytes=VMEM_LIMIT),
+        in_specs=[VMEM_SPEC] * (1 + len(ready)),
+        out_specs=(VMEM_SPEC,) * 3,
+        out_shape=(shape, shape, pltpu.VMEM((QUARTER, LANES), jnp.bfloat16)),
+        compiler_params=pltpu.CompilerParams(vmem_limit_bytes=VMEM_LIMIT),
+        cost_estimate=COST,
         name="spread",
-    )(*on_chip(got, tokens))
+    )(*on_chip(got, *ready))
 
 
 def bias_line(rel_ref, head, first_bucket):
@@ -197,89 +200,86 @@
             pltpu.VMEM((PAIRS + 2, 8, ROWS), jnp.float32),
         ),
         compiler_params=pltpu.CompilerParams(vmem_limit_bytes=VMEM_LIMIT),
+        cost_estimate=COST,
         name="tables",
     )(place, rel_bias.T, *on_chip(lengths, prefix_map))
 
 
-def attend_kernel(
-    place_ref,
-    got_ref,
-    prev_ref,
-    next_ref,
-    far_ref,
-    near_ref,
-    line_ref,
-    meta_ref,
-    _,
-    w1_hbm,
-    w2_hbm,
-    w3_hbm,
-    out_ref,
-    w1_ref,
-    w2_ref,
-    w3_ref,
-    keys,
-    values,
-    kwin,
-    vwin,
-    landed,
-):
-    copies = [
-        pltpu.make_async_copy(source, target, landed.at[i])
-        for i, (source, target) in enumerate(((w1_hbm, w1_ref), (w2_hbm, w2_ref), (w3_hbm, w3_ref)))
-    ]
+def masks_of(meta_ref, step):
+    own = jnp.transpose(meta_ref[step + 1])
+    second = jnp.concatenate([own[:, 2:3], own[:, 2:3]], axis=0) > 0.5
+    return own[:, 0:1], own[:, 1:2], second
+
+
+def queries(got_ref, step, second):
+    lane = lax.broadcasted_iota(jnp.int32, (ROWS, LANES), 1)
+    query = got_ref[step, 0:ROWS]
+    zero = jnp.zeros_like(query)
+    stacked = jnp.concatenate(
+        [jnp.where(lane < DK, query, zero), jnp.where(lane < DK, zero, query)], axis=0
+    )
+    zeros = jnp.zeros_like(stacked)
+    split = jnp.concatenate(
+        [jnp.where(second, zeros, stacked), jnp.where(second, stacked, zeros)], axis=1
+    )
+    return stacked, split
+
+
+def prefix_bias(line_ref, offset):
+    lane = lax.broadcasted_iota(jnp.int32, (ROWS, LANES), 1)
+    at = jnp.minimum(LANES - lane + offset.astype(jnp.int32), LANES - 1)
+    line = line_ref[...]
+    tail = jnp.take_along_axis(line, jnp.concatenate([at, at], axis=0), axis=1)
+    return tail, line[:, LANES - 1 :]
+
+
+def quarter_of(rows_at, keys_ref, values_ref):
+    for p in range(PREF_GRP):
+        pieces = [
+            jnp.concatenate(
+                [rows_at(source, (kind * PREF_GRP + p) * SHARE) for source in range(PAIRS)], axis=0
+            )
+            for kind in range(2)
+        ]
+        keys_ref[p * LANES : (p + 1) * LANES, :] = jnp.transpose(pieces[0])
+        values_ref[:, p * LANES : (p + 1) * LANES] = pieces[1]
+
+
+def dot(a, b):
+    return jnp.dot(a, b, preferred_element_type=jnp.float32)
+
+
+def start_copies(pairs, landed):
+    copies = [pltpu.make_async_copy(a, b, landed.at[i]) for i, (a, b) in enumerate(pairs)]
     for copy in copies:
         copy.start()
-    lane = lax.broadcasted_iota(jnp.int32, (ROWS, LANES), 1)
-    low = lane < DK
-    for b in range(PAIRS + 2):
-        if b == 0:
-            key, value = prev_ref[QUARTER : QUARTER + ROWS], prev_ref[QUARTER + ROWS :]
-        elif b == PAIRS + 1:
-            key, value = next_ref[QUARTER : QUARTER + ROWS], next_ref[QUARTER + ROWS :]
-        else:
-            key, value = got_ref[b - 1, ROWS : 2 * ROWS], got_ref[b - 1, 2 * ROWS : 3 * ROWS]
-        kwin[b] = jnp.transpose(key)
-        vwin[b] = value
-    for turn, ref in ((0, None), (3, prev_ref), (1, next_ref), (2, far_ref)):
-        quarter = lax.rem(place_ref[0] + turn, 4)
-        for p in range(PREF_GRP):
-            pieces = [[], []]
-            for source in range(PAIRS):
-                for kind in range(2):
-                    at = (kind * PREF_GRP + p) * SHARE
-                    if ref is None:
-                        piece = got_ref[source, 3 * ROWS + at : 3 * ROWS + at + SHARE]
-                    else:
-                        at = at + source * 4 * SHARE
-                        piece = ref[at : at + SHARE]
-                    pieces[kind].append(piece)
-            keys[quarter, p * LANES : (p + 1) * LANES] = jnp.transpose(jnp.concatenate(pieces[0], axis=0))
-            values[quarter, :, p * LANES : (p + 1) * LANES] = jnp.concatenate(pieces[1], axis=0)
+    return copies
+
+
+def own_kernel(
+    place_ref, got_ref, near_ref, line_ref, meta_ref, w1_hbm, w2_hbm,
+    stat_ref, acc_ref, w1_ref, w2_ref, keys, values, kwin, vwin, landed,
+):
+    copies = start_copies(((w1_hbm, w1_ref), (w2_hbm, w2_ref)), landed)
+    for b in (0, PAIRS + 1):
+        kwin[b] = jnp.zeros((LANES, ROWS), jnp.bfloat16)
+        vwin[b] = jnp.zeros((ROWS, LANES), jnp.bfloat16)
+    for b in range(PAIRS):
+        kwin[b + 1] = jnp.transpose(got_ref[b, ROWS : 2 * ROWS])
+        vwin[b + 1] = got_ref[b, 2 * ROWS : 3 * ROWS]
+    quarter_of(lambda s, at: got_ref[s, 3 * ROWS + at : 3 * ROWS + at + SHARE], keys, values)
+    is_last = place_ref[0] == 3
 
     def one(step, _):
-        query = got_ref[step, 0:ROWS]
-        own = jnp.transpose(meta_ref[step + 1])
-        request, offset, chosen = own[:, 0:1], own[:, 1:2], own[:, 2:3]
-        zero = jnp.zeros_like(query)
-        stacked = jnp.concatenate([jnp.where(low, query, zero), jnp.where(low, zero, query)], axis=0)
-        second = jnp.concatenate([chosen, chosen], axis=0) > 0.5
-        zeros = jnp.zeros_like(stacked)
-        split = jnp.concatenate(
-            [jnp.where(second, zeros, stacked), jnp.where(second, stacked, zeros)], axis=1
-        )
-        far_keys = jnp.concatenate([keys[b] for b in range(4)], axis=1)
-        far_scores = jnp.dot(split, far_keys, preferred_element_type=jnp.float32)
-        near_keys = jnp.concatenate([kwin[step + b] for b in range(3)], axis=1)
-        near_scores = jnp.dot(stacked, near_keys, preferred_element_type=jnp.float32)
-        tail_at = jnp.minimum(LANES - lane + offset.astype(jnp.int32), LANES - 1)
-        line = line_ref[...]
-        tail = jnp.take_along_axis(line, jnp.concatenate([tail_at, tail_at], axis=0), axis=1)
-        full = line[:, LANES - 1 :]
-        parts = [far_scores[:, b * LANES : (b + 1) * LANES] + full for b in range(3)]
-        parts.append(far_scores[:, 3 * LANES :] + tail)
+        request, offset, second = masks_of(meta_ref, step)
+        stacked, split = queries(got_ref, step, second)
+        tail, full = prefix_bias(line_ref, offset)
+        parts = [dot(split, keys[...]) + jnp.where(is_last, tail, full)]
+        near_scores = dot(stacked, jnp.concatenate([kwin[step + b] for b in range(3)], axis=1))
         for b in range(3):
-            mine = meta_ref[step + b, 0:1, :] == request
+            at_edge = (step + b == 0) | (step + b == PAIRS + 1)
+            names = jnp.where(at_edge, -2.0, meta_ref[step + b, 0:1, :])
+            mine = names == request
             mine = jnp.concatenate([mine, mine], axis=0)
             at = slice(b * LANES, (b + 1) * LANES)
             parts.append(jnp.where(mine, near_scores[:, at] + near_ref[:, at], masked_score))
@@ -287,50 +287,122 @@
         terms = [jnp.exp(part - row_max) for part in parts]
         row_sum = jnp.sum(functools.reduce(jnp.add, terms), axis=1, keepdims=True)
         weights = [t.astype(jnp.bfloat16) for t in terms]
-        far_out = jnp.dot(
-            jnp.concatenate(weights[:4], axis=1),
-            values[...].reshape(PLEN, PREF_GRP * LANES),
-            preferred_element_type=jnp.float32,
+        far_out = dot(weights[0], values[...])
+        near_values = jnp.concatenate([vwin[step + b] for b in range(3)], axis=0)
+        acc = jnp.where(second, far_out[:, LANES:], far_out[:, :LANES])
+        acc_ref[step] = acc + dot(jnp.concatenate(weights[1:], axis=1), near_values)
+        stat_ref[step, :, 0:1] = row_max
+        stat_ref[step, :, 1:2] = row_sum
+        return 0
+
+    lax.fori_loop(0, PAIRS, one, 0, unroll=2)
+    for copy in copies:
+        copy.wait()
+
+
+def attend_own(place, got, made, later_weights):
+    return pl.pallas_call(
+        own_kernel,
+        in_specs=[SMEM_SPEC] + [VMEM_SPEC] * 4 + [HBM_SPEC] * 2,
+        out_specs=(VMEM_SPEC,) * 4,
+        out_shape=(
+            pltpu.VMEM((PAIRS, 2 * ROWS, 2), jnp.float32),
+            pltpu.VMEM((PAIRS, 2 * ROWS, LANES), jnp.float32),
         )
-        near_values = jnp.concatenate([vwin[step + b] for b in range(3)], axis=0)
-        near_out = jnp.dot(
-            jnp.concatenate(weights[4:], axis=1), near_values, preferred_element_type=jnp.float32
+        + tuple(pltpu.VMEM(w.shape, w.dtype) for w in later_weights),
+        scratch_shapes=[
+            pltpu.VMEM((PREF_GRP * LANES, PLEN // 4), jnp.bfloat16),
+            pltpu.VMEM((PLEN // 4, PREF_GRP * LANES), jnp.bfloat16),
+            pltpu.VMEM((PAIRS + 2, LANES, ROWS), jnp.bfloat16),
+            pltpu.VMEM((PAIRS + 2, ROWS, LANES), jnp.bfloat16),
+            pltpu.SemaphoreType.DMA((2,)),
+        ],
+        compiler_params=pltpu.CompilerParams(vmem_limit_bytes=VMEM_LIMIT),
+        cost_estimate=COST,
+        name="attend_own",
+    )(place, *on_chip(got, *made), *off_chip(*later_weights))
+
+
+def rest_kernel(
+    place_ref, got_ref, prev_ref, next_ref, far_ref, near_ref, line_ref, meta_ref, stat_ref, acc_ref, w_hbm,
+    out_ref, w_ref, keys, values, kwin, vwin, landed,
+):
+    copies = start_copies(((w_hbm, w_ref),), landed)
+    turns = ((3, prev_ref), (1, next_ref), (2, far_ref))
+    for i, (_, ref) in enumerate(turns):
+        quarter_of(
+            lambda s, at, ref=ref: ref[s * 4 * SHARE + at : s * 4 * SHARE + at + SHARE], keys.at[i], values.at[i]
         )
-        total = jnp.where(second, far_out[:, LANES:], far_out[:, :LANES]) + near_out
-        total = total / row_sum
-        done = jnp.where(low, total[:ROWS], total[ROWS:]).astype(jnp.bfloat16)
-        side = place_ref[2]
+    for i, ref in enumerate((prev_ref, next_ref)):
+        kwin[i] = jnp.transpose(ref[QUARTER : QUARTER + ROWS])
+        vwin[i] = ref[QUARTER + ROWS :]
+    is_last = [lax.rem(place_ref[0] + turn, 4) == 3 for turn, _ in turns]
+    side = place_ref[2]
+    low = lax.broadcasted_iota(jnp.int32, (ROWS, LANES), 1) < DK
+
+    def one(step, edge=None):
+        request, offset, second = masks_of(meta_ref, step)
+        stacked, split = queries(got_ref, step, second)
+        tail, full = prefix_bias(line_ref, offset)
+        scores = dot(split, jnp.concatenate([keys[i] for i in range(3)], axis=1))
+        parts = [
+            scores[:, i * LANES : (i + 1) * LANES] + jnp.where(is_last[i], tail, full) for i in range(3)
+        ]
+        if edge is not None:
+            mine = meta_ref[edge * (PAIRS + 1), 0:1, :] == request
+            mine = jnp.concatenate([mine, mine], axis=0)
+            bias = near_ref[:, edge * 2 * LANES : (edge * 2 + 1) * LANES]
+            parts.append(jnp.where(mine, dot(stacked, kwin[edge]) + bias, masked_score))
+        before = stat_ref[step, :, 0:1]
+        row_max = jnp.max(functools.reduce(jnp.maximum, parts), axis=1, keepdims=True)
+        row_max = jnp.maximum(row_max, before)
+        shrink = jnp.exp(before - row_max)
+        terms = [jnp.exp(part - row_max) for part in parts]
+        row_sum = jnp.sum(functools.reduce(jnp.add, terms), axis=1, keepdims=True)
+        row_sum = row_sum + stat_ref[step, :, 1:2] * shrink
+        weights = [t.astype(jnp.bfloat16) for t in terms]
+        far_out = dot(
+            jnp.concatenate(weights[:3], axis=1), values[...].reshape(3 * PLEN // 4, PREF_GRP * LANES)
+        )
+        acc = acc_ref[step] * shrink + jnp.where(second, far_out[:, LANES:], far_out[:, :LANES])
+        if edge is not None:
+            acc = acc + dot(weights[3], vwin[edge])
+        acc = acc / row_sum
+        done = jnp.where(low, acc[:ROWS], acc[ROWS:]).astype(jnp.bfloat16)
         out_ref[side * PAIRS + step] = done
         out_ref[(1 - side) * PAIRS + jnp.bitwise_xor(step, 1)] = done
+
+    def middle(step, _):
+        one(step)
         return 0
 
-    lax.fori_loop(0, PAIRS, one, 0)
+    one(jnp.int32(0), 0)
+    lax.fori_loop(1, PAIRS - 1, middle, 0, unroll=2)
+    one(jnp.int32(PAIRS - 1), 1)
     for copy in copies:
         copy.wait()
 
 
-def attend(place, got, prev, after_it, far, made, ready, later_weights):
-    hbm = pl.BlockSpec(memory_space=pltpu.HBM)
-    return pl.pallas_call(
-        attend_kernel,
-        in_specs=[SMEM_SPEC] + [VMEM_SPEC] * 8 + [hbm] * 3,
-        out_specs=(VMEM_SPEC,) * 4,
-        out_shape=(pltpu.VMEM((2 * PAIRS, ROWS, LANES), jnp.bfloat16),)
-        + tuple(pltpu.VMEM(w.shape, w.dtype) for w in later_weights),
+def attend_rest(place, got, prev, after_it, far, made, part, weight):
+    return pl.pallas_call(
+        rest_kernel,
+        in_specs=[SMEM_SPEC] + [VMEM_SPEC] * 9 + [HBM_SPEC],
+        out_specs=(VMEM_SPEC,) * 2,
+        out_shape=(
+            pltpu.VMEM((2 * PAIRS, ROWS, LANES), jnp.bfloat16),
+            pltpu.VMEM(weight.shape, weight.dtype),
+        ),
         scratch_shapes=[
-            pltpu.VMEM((4, PREF_GRP * LANES, PLEN // 4), jnp.bfloat16),
-            pltpu.VMEM((4, PLEN // 4, PREF_GRP * LANES), jnp.bfloat16),
-            pltpu.VMEM((PAIRS + 2, LANES, ROWS), jnp.bfloat16),
-            pltpu.VMEM((PAIRS + 2, ROWS, LANES), jnp.bfloat16),
-            pltpu.SemaphoreType.DMA((3,)),
+            pltpu.VMEM((3, PREF_GRP * LANES, PLEN // 4), jnp.bfloat16),
+            pltpu.VMEM((3, PLEN // 4, PREF_GRP * LANES), jnp.bfloat16),
+            pltpu.VMEM((2, LANES, ROWS), jnp.bfloat16),
+            pltpu.VMEM((2, ROWS, LANES), jnp.bfloat16),
+            pltpu.SemaphoreType.DMA((1,)),
         ],
         compiler_params=pltpu.CompilerParams(vmem_limit_bytes=VMEM_LIMIT),
-        name="attend",
-    )(
-        place,
-        *on_chip(got, prev, after_it, far, *made, ready),
-        *(pltpu.with_memory_space_constraint(w, pltpu.HBM) for w in later_weights),
-    )
+        cost_estimate=COST,
+        name="attend_rest",
+    )(place, *on_chip(got, prev, after_it, far, *made, *part), *off_chip(weight))
 
 
 def join_kernel(place_ref, att_ref, w_ref, tok_ref, far_tok_ref, gain_ref, hidden_ref, normed_ref):
@@ -354,6 +426,7 @@
         out_specs=(VMEM_SPEC,) * 2,
         out_shape=(pltpu.VMEM((ROWS, D), jnp.bfloat16), pltpu.VMEM((2, ROWS, D), jnp.bfloat16)),
         compiler_params=pltpu.CompilerParams(vmem_limit_bytes=VMEM_LIMIT),
+        cost_estimate=COST,
         name="join",
     )(place, *on_chip(att, w_attn_out, tokens, far_tokens, gain.reshape(1, D)))
 
@@ -378,6 +451,7 @@
         out_specs=(VMEM_SPEC,) * len(picked),
         out_shape=(shape,) * len(picked),
         compiler_params=pltpu.CompilerParams(vmem_limit_bytes=VMEM_LIMIT),
+        cost_estimate=COST,
         name="feed",
     )(*on_chip(rows, w_in, w_out, *ready))
 
@@ -395,6 +469,7 @@
         out_specs=VMEM_SPEC,
         out_shape=(jax.ShapeDtypeStruct if last else pltpu.VMEM)(arrays[0].shape, dtype),
         compiler_params=pltpu.CompilerParams(vmem_limit_bytes=VMEM_LIMIT),
+        cost_estimate=COST,
         name="total",
     )(*on_chip(*arrays))
 
@@ -421,19 +496,18 @@
 
     blocks = project(tokens, attn_gain, w_query, w_key, w_value, prefix_cache)
     got = lax.all_to_all(blocks, PLANE, 0, 0, tiled=True)
-    up, down, far, same = spread(got, tokens)
+    mirrored = ("yhi", "ylo")
+    far_tokens = lax.ppermute(tokens, mirrored, MIRROR)
+    up, down, far = spread(got, far_tokens, *made)
     by = lambda d: [(i, (i + d) % count_x) for i in range(count_x)]
     prev = lax.ppermute(up, "x", by(1))
     later = lax.ppermute(down, "x", by(-1))
     opposite = lax.ppermute(far, "x", by(2))
-    mirrored = ("yhi", "ylo")
-    far_tokens = lax.ppermute(same, mirrored, MIRROR)
-    mixed, w_attn_out, w_in, w_out = attend(
-        place, got, prev, later, opposite, made, far_tokens, (w_attn_out, w_in, w_out)
-    )
+    stat, acc, w_attn_out, w_in = attend_own(place, got, made, (w_attn_out, w_in))
+    mixed, w_out = attend_rest(place, got, prev, later, opposite, made, (stat, acc), w_out)
     att = lax.all_to_all(mixed, ("yhi",) + PLANE, 0, 0, tiled=True)
+
     hidden, normed = join(place, att, w_attn_out, tokens, far_tokens, mlp_gain)
-
     other = lax.ppermute(normed, "core", SWAP)
     mine, far_mine = feed((0, 1), normed, w_in, w_out)
     (far_theirs,) = feed((1,), other, w_in, w_out, mine)

time: 75.6 us -> 77.5 us (1.025)
  blocking collectives: 34.1 us -> 15.7 us
  starting transfers between devices: 9.47 us -> 17.1 us
  Pallas kernels: 19.2 us -> 25.8 us
  waiting for transfers between devices: 12.2 us -> 18.3 us
    all_to_all x1 -> x0, blocking collectives: 20.8 us -> none  [body(): got = lax.all_to_all(blocks, PLANE, 0, 0, tiled=True)]
    pallas_call x3 -> x4, Pallas kernels: 12.1 us -> 18.7 us  [the longest x1 7 us: attend_rest(): pl.pallas_call(rest_kernel, in_specs=[SMEM_SPEC] + [VMEM_SPEC] * 9 + [HBM...]
    all_to_all x0 -> x1, starting transfers between devices: none -> 6.43 us  [body(): got = lax.all_to_all(blocks, PLANE, 0, 0, tiled=True)]
    all_to_all x0 -> x1, waiting for transfers between devices: none -> 5.09 us  [body(): got = lax.all_to_all(blocks, PLANE, 0, 0, tiled=True)]
    ppermute x1, waiting for transfers between devices: 0.01 us -> 4.41 us  [body(): far_tokens = lax.ppermute(tokens, mirrored, MIRROR)]
    ppermute x1, waiting for transfers between devices: 3.41 us -> 0.01 us  [body(): opposite = lax.ppermute(far, 'x', by(2))]
    all_to_all x1, blocking collectives: 13.3 us -> 15.7 us  [body(): att = lax.all_to_all(mixed, ('yhi',) + PLANE, 0, 0, tiled=True)]
    ppermute x1, starting transfers between devices: 2.25 us -> 3.46 us  [body(): far_tokens = lax.ppermute(tokens, mirrored, MIRROR)]
  transfers between devices with their start and end apart: 8 -> 9, of which waited for: 3 -> 4; matrix products, arithmetic and copies ran while one was open for 0% -> 0% of each run, Pallas kernels for 5% -> 12%
where the time goes in v5:
time: 77.5 us; the launch traced here: 77.1 us
  Pallas kernels  25.8 us (33%)
  waiting for transfers between devices  18.3 us (24%)
  starting transfers between devices  17.1 us (22%)
  blocking collectives  15.7 us (20%)
    all_to_all x1, blocking collectives, body(): att = lax.all_to_all(mixed, ('yhi',) + PLANE, 0, 0, tiled=True)  15.7 us
    ppermute x1, waiting for transfers between devices, body(): back = lax.ppermute(far_sum, mirrored, MIRROR)  8.15 us
    pallas_call x1, Pallas kernels, attend_rest(): pl.pallas_call(rest_kernel, in_specs=[SMEM_SPEC] + [VMEM_SPEC] * 9 + [HBM...  7 us
    all_to_all x1, starting transfers between devices, body(): got = lax.all_to_all(blocks, PLANE, 0, 0, tiled=True)  6.43 us
    pallas_call x1, Pallas kernels, attend_own(): pl.pallas_call(own_kernel, in_specs=[SMEM_SPEC] + [VMEM_SPEC] * 4 + [HBM_...  5.83 us
    pallas_call x1, Pallas kernels, project(): pl.pallas_call(project_kernel, in_specs=[HBM_SPEC] * 6, out_specs=VMEM_SP...  5.82 us
    all_to_all x1, waiting for transfers between devices, body(): got = lax.all_to_all(blocks, PLANE, 0, 0, tiled=True)  5.09 us
    ppermute x1, waiting for transfers between devices, body(): far_tokens = lax.ppermute(tokens, mirrored, MIRROR)  4.41 us
  transfers between devices with their start and end apart: 9, of which 4 were waited for; matrix products, arithmetic and copies ran while one was open for 0% of the time, Pallas kernels for 12%

profile of v5, /device:TPU:0, one launch (start us, length us, event | category | flops | bytes accessed | tf_op | source)
XLA Modules:
  0.0 77.1 jit_solution(7806586135316224300)
XLA Ops:
  0.0 0.0 copy-start
  0.0 0.0 copy-start.1
  0.0 0.0 copy-start.3
  0.0 0.0 copy-start.4
  0.0 5.8 %project.1 = bf16[8,448,128]{2,1,0:T(8,128)(2,1)} custom-call(bf16[128,1024]{1,0:T(8,128)(2,1)} %tok_ref.1, f32[1,1024]{1,0:T(1,128)} %bitcast.8, bf16[2,16,2048]{2,1,0:T(8,128)(2,1)} %cache_hbm.1, bf16[1024,1024]{1,0:T(8,128)(2,1)} %wq_hbm.1, bf16[1024,1024]{1,0:T(8,128)(2,1)} %wk_hbm.1, bf16[1024,1024]{1,0:T(8,128)(2,1)} %wv_hbm.1), custom_call_target="tpu_custom_call" | custom-call | flops 1000 | bytes 1000 | tf_op jit(solution)/shard_map/project/pallas_call | solution.py:96
  5.8 6.4 %all-to-all-start = ((bf16[8,448,128]{2,1,0:T(8,128)(2,1)}), bf16[8,448,128]{2,1,0:T(8,128)(2,1)S(1)}, u32[]{:S(2)}, u32[]{:S(2)}) async-start(bf16[8,448,128]{2,1,0:T(8,128)(2,1)} %project.1), calls=%async_computation | async-start | bytes 1835008 | tf_op jit(solution)/shard_map/all_to_all | solution.py:498
  12.3 0.0 copy-done
  12.3 3.5 %collective-permute-start = (bf16[128,1024]{1,0:T(8,128)(2,1)S(1)}, bf16[128,1024]{1,0:T(8,128)(2,1)S(1)}, u32[]{:S(2)}, u32[]{:S(2)}) collective-permute-start(bf16[128,1024]{1,0:T(8,128)(2,1)S(1)} %copy-done), channel_id=1, source_target_pairs={{0,65},{65,0},{1,64},{64,1},{2,67},{67,2},{3,66},{66,3},{4,69},{69... | collective-permute-start | bytes 786440 | tf_op jit(solution)/shard_map/ppermute | solution.py:500
  15.7 0.1 pad_add_fusion.place_ref
  15.8 0.0 copy-done.1
  15.8 0.0 copy-done.3
  15.8 0.0 copy-done.4
  15.8 1.2 %tables.1 = (f32[256,384]{1,0:T(8,128)S(1)}, f32[256,128]{1,0:T(8,128)S(1)}, f32[10,8,128]{2,1,0:T(8,128)S(1)}) custom-call(s32[3]{0:T(128)S(1)} %pad_add_fusion.place_ref, f32[16,32]{1,0:T(8,128)S(1)} %bitcast.6, s32[1,64]{1,0:T(1,128)S(1)} %copy-done.3, s32[1,64]{1,0:T(1,128)S(1)} %copy-done.4), custom_call_target="tpu_custom_call" | custom-call | flops 1000 | bytes 1000 | tf_op jit(solution)/shard_map/tables/pallas_call | solution.py:193
  17.1 4.4 %collective-permute-done.rest_0_.far_tok_ref = bf16[128,1024]{1,0:T(8,128)(2,1)S(1)} collective-permute-done((bf16[128,1024]{1,0:T(8,128)(2,1)S(1)}, bf16[128,1024]{1,0:T(8,128)(2,1)S(1)}, u32[]{:S(2)}, u32[]{:S(2)}) %collective-permute-start) | collective-permute-done | bytes 262176 | tf_op jit(solution)/shard_map/ppermute | solution.py:500
  21.5 5.1 %all-to-all-done.got_ref = bf16[8,448,128]{2,1,0:T(8,128)(2,1)S(1)} async-done(((bf16[8,448,128]{2,1,0:T(8,128)(2,1)}), bf16[8,448,128]{2,1,0:T(8,128)(2,1)S(1)}, u32[]{:S(2)}, u32[]{:S(2)}) %all-to-all-start) | async-done | bytes 917536 | tf_op jit(solution)/shard_map/all_to_all | solution.py:498
  26.6 0.1 spread.1
  26.6 1.6 %collective-permute-start.1 = (bf16[768,128]{1,0:T(8,128)(2,1)S(1)}, bf16[768,128]{1,0:T(8,128)(2,1)S(1)}, u32[]{:S(2)}, u32[]{:S(2)}) collective-permute-start(bf16[768,128]{1,0:T(8,128)(2,1)S(1)} %get-tuple-element.24), channel_id=1, source_target_pairs={{0,8},{8,16},{16,24},{24,0},{1,9},{9,17},{17,25},{25,1},{2,10},{10... | collective-permute-start | bytes 589832 | tf_op jit(solution)/shard_map/ppermute | solution.py:503
  28.2 1.7 %collective-permute-start.2 = (bf16[768,128]{1,0:T(8,128)(2,1)S(1)}, bf16[768,128]{1,0:T(8,128)(2,1)S(1)}, u32[]{:S(2)}, u32[]{:S(2)}) collective-permute-start(bf16[768,128]{1,0:T(8,128)(2,1)S(1)} %get-tuple-element.25), channel_id=1, source_target_pairs={{0,24},{8,0},{16,8},{24,16},{1,25},{9,1},{17,9},{25,17},{2,26},{10... | collective-permute-start | bytes 589832 | tf_op jit(solution)/shard_map/ppermute | solution.py:504
  29.9 1.8 %collective-permute-start.3 = (bf16[512,128]{1,0:T(8,128)(2,1)S(1)}, bf16[512,128]{1,0:T(8,128)(2,1)S(1)}, u32[]{:S(2)}, u32[]{:S(2)}) collective-permute-start(bf16[512,128]{1,0:T(8,128)(2,1)S(1)} %get-tuple-element.26), channel_id=1, source_target_pairs={{0,16},{8,24},{16,0},{24,8},{1,17},{9,25},{17,1},{25,9},{2,18},{10... | collective-permute-start | bytes 393224 | tf_op jit(solution)/shard_map/ppermute | solution.py:505
  31.7 5.8 %attend_own.1 = (f32[8,256,2]{2,1,0:T(8,128)S(1)}, f32[8,256,128]{2,1,0:T(8,128)S(1)}, bf16[1024,1024]{1,0:T(8,128)(2,1)S(1)}, bf16[1024,1024]{1,0:T(8,128)(2,1)S(1)}) custom-call(s32[3]{0:T(128)S(1)} %pad_add_fusion.place_ref, bf16[8,448,128]{2,1,0:T(8,128)(2,1)S(1)} %all-to-all-done.got_ref, f32[256,384]{1,0:T(8,128)S(1)} %get-tuple-element.21.rest_1_.near_ref, ...), custom_call_target="tpu_custom_call" | custom-call | flops 1000 | bytes 1000 | tf_op jit(solution)/shard_map/attend_own/pallas_call | solution.py:304
  37.6 0.0 collective-permute-done.3.far_ref
  37.6 0.0 collective-permute-done.1.prev_ref
  37.6 0.0 collective-permute-done.2.next_ref
  37.6 0.0 copy-start.2
  37.6 7.0 %attend_rest.1 = (bf16[16,128,128]{2,1,0:T(8,128)(2,1)S(1)}, bf16[1024,1024]{1,0:T(8,128)(2,1)S(1)}) custom-call(s32[3]{0:T(128)S(1)} %pad_add_fusion.place_ref, bf16[8,448,128]{2,1,0:T(8,128)(2,1)S(1)} %all-to-all-done.got_ref, bf16[768,128]{1,0:T(8,128)(2,1)S(1)} %collective-permute-done.1.prev_ref, bf16[768,128]{1,0:T(8,128)(2,1)S(1)} %collective-permute-done.2.next_ref, ...), custom_call_target="tpu_custom_call" | custom-call | flops 1000 | bytes 1000 | tf_op jit(solution)/shard_map/attend_rest/pallas_call | solution.py:387
  44.6 15.7 %all_to_all.10.att_ref = bf16[16,128,128]{2,1,0:T(8,128)(2,1)S(1)} all-to-all(bf16[16,128,128]{2,1,0:T(8,128)(2,1)S(1)} %get-tuple-element.29), channel_id=1, replica_groups=mesh['yhi'=2,'core'=2,'x'=4,'z'=4,'ylo'=2] {'yhi','z','ylo'}, dimensions={0} | all-to-all | bytes 1048576 | tf_op jit(solution)/shard_map/all_to_all | solution.py:508
  60.3 0.0 copy-done.2
  60.3 1.4 %join.1 = (bf16[128,1024]{1,0:T(8,128)(2,1)S(1)}, bf16[2,128,1024]{2,1,0:T(8,128)(2,1)S(1)}) custom-call(s32[3]{0:T(128)S(1)} %pad_add_fusion.place_ref, bf16[16,128,128]{2,1,0:T(8,128)(2,1)S(1)} %all_to_all.10.att_ref, bf16[1024,1024]{1,0:T(8,128)(2,1)S(1)} %get-tuple-element.30.w_ref, bf16[128,1024]{1,0:T(8,128)(2,1)S(1)} %copy-done, ...), custom_call_target="tpu_custom_call" | custom-call | flops 1000 | bytes 1000 | tf_op jit(solution)/shard_map/join/pallas_call | solution.py:423
  61.8 0.1 collective-permute-start.4
  61.8 1.3 %feed.3 = (bf16[128,1024]{1,0:T(8,128)(2,1)S(1)}, bf16[128,1024]{1,0:T(8,128)(2,1)S(1)}) custom-call(bf16[2,128,1024]{2,1,0:T(8,128)(2,1)S(1)} %get-tuple-element.32.rows_ref, bf16[1024,1024]{1,0:T(8,128)(2,1)S(1)} %get-tuple-element.33.in_ref, bf16[1024,1024]{1,0:T(8,128)(2,1)S(1)} %get-tuple-element.34.out_w_ref), custom_call_target="tpu_custom_call" | custom-call | flops 1000 | bytes 1000 | tf_op jit(solution)/shard_map/feed/pallas_call | solution.py:448
  63.1 0.6 collective-permute-done.4.rows_ref
  63.7 1.1 %feed.4.rest_0_ = bf16[128,1024]{1,0:T(8,128)(2,1)S(1)} custom-call(bf16[2,128,1024]{2,1,0:T(8,128)(2,1)S(1)} %collective-permute-done.4.rows_ref, bf16[1024,1024]{1,0:T(8,128)(2,1)S(1)} %get-tuple-element.33.in_ref, bf16[1024,1024]{1,0:T(8,128)(2,1)S(1)} %get-tuple-element.34.out_w_ref, bf16[128,1024]{1,0:T(8,128)(2,1)S(1)} %get-tuple-element.35.rest_0_.refs_1_), custom_call_target="tpu_custom_call" | custom-call | flops 1000 | bytes 1000 | tf_op jit(solution)/shard_map/feed/pallas_call | solution.py:448
  64.9 0.2 collective-permute-start.6
  65.1 1.1 %feed.5 = bf16[128,1024]{1,0:T(8,128)(2,1)S(1)} custom-call(bf16[2,128,1024]{2,1,0:T(8,128)(2,1)S(1)} %collective-permute-done.4.rows_ref, bf16[1024,1024]{1,0:T(8,128)(2,1)S(1)} %get-tuple-element.33.in_ref, bf16[1024,1024]{1,0:T(8,128)(2,1)S(1)} %get-tuple-element.34.out_w_ref, bf16[128,1024]{1,0:T(8,128)(2,1)S(1)} %feed.4.rest_0_), custom_call_target="tpu_custom_call" | custom-call | flops 1000 | bytes 1000 | tf_op jit(solution)/shard_map/feed/pallas_call | solution.py:448
  66.2 0.5 collective-permute-start.5
  66.6 0.0 collective-permute-done.6.refs_1_
  66.6 0.1 total.4
  66.7 1.4 %collective-permute-start.7 = (bf16[128,1024]{1,0:T(8,128)(2,1)S(1)}, bf16[128,1024]{1,0:T(8,128)(2,1)S(1)}, u32[]{:S(2)}, u32[]{:S(2)}) collective-permute-start(bf16[128,1024]{1,0:T(8,128)(2,1)S(1)} %total.4), channel_id=1, source_target_pairs={{0,65},{65,0},{1,64},{64,1},{2,67},{67,2},{3,66},{66,3},{4,69},{69... | collective-permute-start | bytes 786440 | tf_op jit(solution)/shard_map/ppermute | solution.py:515
  68.1 0.0 collective-permute-done.5.refs_2_
  68.1 0.1 total.3.refs_0_
  68.2 8.2 %collective-permute-done.7.refs_1_ = bf16[128,1024]{1,0:T(8,128)(2,1)S(1)} collective-permute-done((bf16[128,1024]{1,0:T(8,128)(2,1)S(1)}, bf16[128,1024]{1,0:T(8,128)(2,1)S(1)}, u32[]{:S(2)}, u32[]{:S(2)}) %collective-permute-start.7) | collective-permute-done | bytes 262176 | tf_op jit(solution)/shard_map/ppermute | solution.py:515
  76.3 0.7 total.5
Async XLA Ops:
  0.0 12.3 %copy-start = (bf16[128,1024]{1,0:T(8,128)(2,1)S(1)}, bf16[128,1024]{1,0:T(8,128)(2,1)}, u32[]{:S(2)}) copy-start(bf16[128,1024]{1,0:T(8,128)(2,1)} %tok_ref.1) | copy-start | bytes 786436
  0.0 15.8 %copy-start.1 = (f32[32,16]{0,1:T(8,128)S(1)}, f32[32,16]{0,1:T(8,128)}, u32[]{:S(2)}) copy-start(f32[32,16]{0,1:T(8,128)} %param.19) | copy-start | bytes 6148
  0.0 15.8 %copy-start.3 = (s32[1,64]{1,0:T(1,128)S(1)}, s32[1,64]{1,0:T(1,128)}, u32[]{:S(2)}) copy-start(s32[1,64]{1,0:T(1,128)} %len_ref.1) | copy-start | bytes 772
  0.0 15.8 %copy-start.4 = (s32[1,64]{1,0:T(1,128)S(1)}, s32[1,64]{1,0:T(1,128)}, u32[]{:S(2)}) copy-start(s32[1,64]{1,0:T(1,128)} %map_ref.1) | copy-start | bytes 772
  5.8 20.7 %all-to-all-start = ((bf16[8,448,128]{2,1,0:T(8,128)(2,1)}), bf16[8,448,128]{2,1,0:T(8,128)(2,1)S(1)}, u32[]{:S(2)}, u32[]{:S(2)}) async-start(bf16[8,448,128]{2,1,0:T(8,128)(2,1)} %project.1), calls=%async_computation | async-start | bytes 1835008 | tf_op jit(solution)/shard_map/all_to_all | solution.py:498
  12.3 9.2 %collective-permute-start = (bf16[128,1024]{1,0:T(8,128)(2,1)S(1)}, bf16[128,1024]{1,0:T(8,128)(2,1)S(1)}, u32[]{:S(2)}, u32[]{:S(2)}) collective-permute-start(bf16[128,1024]{1,0:T(8,128)(2,1)S(1)} %copy-done), channel_id=1, source_target_pairs={{0,65},{65,0},{1,64},{64,1},{2,67},{67,2},{3,66},{66,3},{4,69},{69... | collective-permute-start | bytes 786440 | tf_op jit(solution)/shard_map/ppermute | solution.py:500
  26.6 11.0 %collective-permute-start.1 = (bf16[768,128]{1,0:T(8,128)(2,1)S(1)}, bf16[768,128]{1,0:T(8,128)(2,1)S(1)}, u32[]{:S(2)}, u32[]{:S(2)}) collective-permute-start(bf16[768,128]{1,0:T(8,128)(2,1)S(1)} %get-tuple-element.24), channel_id=1, source_target_pairs={{0,8},{8,16},{16,24},{24,0},{1,9},{9,17},{17,25},{25,1},{2,10},{10... | collective-permute-start | bytes 589832 | tf_op jit(solution)/shard_map/ppermute | solution.py:503
  28.2 9.4 %collective-permute-start.2 = (bf16[768,128]{1,0:T(8,128)(2,1)S(1)}, bf16[768,128]{1,0:T(8,128)(2,1)S(1)}, u32[]{:S(2)}, u32[]{:S(2)}) collective-permute-start(bf16[768,128]{1,0:T(8,128)(2,1)S(1)} %get-tuple-element.25), channel_id=1, source_target_pairs={{0,24},{8,0},{16,8},{24,16},{1,25},{9,1},{17,9},{25,17},{2,26},{10... | collective-permute-start | bytes 589832 | tf_op jit(solution)/shard_map/ppermute | solution.py:504
  29.9 7.6 %collective-permute-start.3 = (bf16[512,128]{1,0:T(8,128)(2,1)S(1)}, bf16[512,128]{1,0:T(8,128)(2,1)S(1)}, u32[]{:S(2)}, u32[]{:S(2)}) collective-permute-start(bf16[512,128]{1,0:T(8,128)(2,1)S(1)} %get-tuple-element.26), channel_id=1, source_target_pairs={{0,16},{8,24},{16,0},{24,8},{1,17},{9,25},{17,1},{25,9},{2,18},{10... | collective-permute-start | bytes 393224 | tf_op jit(solution)/shard_map/ppermute | solution.py:505
  37.6 22.7 %copy-start.2 = (f32[1024]{0:T(1024)S(1)}, f32[1024]{0:T(1024)}, u32[]{:S(2)}) copy-start(f32[1024]{0:T(1024)} %param.23) | copy-start | bytes 12292
  61.8 2.0 %collective-permute-start.4 = (bf16[2,128,1024]{2,1,0:T(8,128)(2,1)S(1)}, bf16[2,128,1024]{2,1,0:T(8,128)(2,1)S(1)}, u32[]{:S(2)}, u32[]{:S(2)}) collective-permute-start(bf16[2,128,1024]{2,1,0:T(8,128)(2,1)S(1)} %get-tuple-element.32.rows_ref), channel_id=1, source_target_pairs={{0,32},{32,0},{1,33},{33,1},{2,34},{34,2},{3,35},{35,3},{4,36},{36... | collective-permute-start | bytes 1572872 | tf_op jit(solution)/shard_map/ppermute | solution.py:511
  64.9 1.8 %collective-permute-start.6 = (bf16[128,1024]{1,0:T(8,128)(2,1)S(1)}, bf16[128,1024]{1,0:T(8,128)(2,1)S(1)}, u32[]{:S(2)}, u32[]{:S(2)}) collective-permute-start(bf16[128,1024]{1,0:T(8,128)(2,1)S(1)} %feed.4.rest_0_), channel_id=1, source_target_pairs={{0,32},{32,0},{1,33},{33,1},{2,34},{34,2},{3,35},{35,3},{4,36},{36... | collective-permute-start | bytes 786440 | tf_op jit(solution)/shard_map/ppermute | solution.py:514
  66.2 1.9 %collective-permute-start.5 = (bf16[128,1024]{1,0:T(8,128)(2,1)S(1)}, bf16[128,1024]{1,0:T(8,128)(2,1)S(1)}, u32[]{:S(2)}, u32[]{:S(2)}) collective-permute-start(bf16[128,1024]{1,0:T(8,128)(2,1)S(1)} %feed.5), channel_id=1, source_target_pairs={{0,32},{32,0},{1,33},{33,1},{2,34},{34,2},{3,35},{35,3},{4,36},{36... | collective-permute-start | bytes 786440 | tf_op jit(solution)/shard_map/ppermute | solution.py:517
  66.7 9.6 %collective-permute-start.7 = (bf16[128,1024]{1,0:T(8,128)(2,1)S(1)}, bf16[128,1024]{1,0:T(8,128)(2,1)S(1)}, u32[]{:S(2)}, u32[]{:S(2)}) collective-permute-start(bf16[128,1024]{1,0:T(8,128)(2,1)S(1)} %total.4), channel_id=1, source_target_pairs={{0,65},{65,0},{1,64},{64,1},{2,67},{67,2},{3,66},{66,3},{4,69},{69... | collective-permute-start | bytes 786440 | tf_op jit(solution)/shard_map/ppermute | solution.py:515

commit v6 on v5

--- a/solution.py
+++ b/solution.py
@@ -53,7 +53,7 @@
 
 
 def project_kernel(
-    tok_hbm, gain_hbm, cache_hbm, wq_hbm, wk_hbm, wv_hbm, out_ref, tok, gain, cache, held, arrived, landed
+    tok_hbm, gain_hbm, cache_hbm, wq_hbm, wk_hbm, wv_hbm, out_hbm, tok, gain, cache, held, out_ref, arrived, landed, left
 ):
     columns = [slice(c * CHUNK, (c + 1) * CHUNK) for c in range(D // CHUNK)]
     first = [
@@ -81,6 +81,12 @@
                 at = 3 * ROWS + (kind * PREF_GRP + p) * SHARE
                 cut = slice(kind * D + part * LANES, kind * D + (part + 1) * LANES)
                 out_ref[part, at : at + SHARE] = cache[p, :, cut]
+    def send(at, i):
+        copy = pltpu.make_async_copy(out_ref.at[:, at], out_hbm.at[:, at], left.at[i])
+        copy.start()
+        return copy
+
+    sends = [send(slice(3 * ROWS, SENT), 3)]
     for kind, row in enumerate(copies):
         for c, copy in enumerate(row):
             copy.wait()
@@ -89,6 +95,9 @@
             for part in range(CHUNK // LANES):
                 to = c * (CHUNK // LANES) + part
                 out_ref[to, kind * ROWS : (kind + 1) * ROWS] = got[:, part * LANES : (part + 1) * LANES]
+        sends.append(send(slice(kind * ROWS, (kind + 1) * ROWS), kind))
+    for copy in sends:
+        copy.wait()
 
 
 def project(tokens, gain, w_query, w_key, w_value, prefix_cache):
@@ -96,15 +105,17 @@
     return pl.pallas_call(
         project_kernel,
         in_specs=[HBM_SPEC] * 6,
-        out_specs=VMEM_SPEC,
+        out_specs=HBM_SPEC,
         out_shape=pltpu.HBM((PAIRS, SENT, LANES), jnp.bfloat16),
         scratch_shapes=[
             pltpu.VMEM((ROWS, D), jnp.bfloat16),
             pltpu.VMEM((1, D), jnp.float32),
             pltpu.VMEM(prefix_cache.shape, jnp.bfloat16),
             pltpu.VMEM((3, D // CHUNK, D, CHUNK), jnp.bfloat16),
+            pltpu.VMEM((PAIRS, SENT, LANES), jnp.bfloat16),
             pltpu.SemaphoreType.DMA((3, D // CHUNK)),
             pltpu.SemaphoreType.DMA((3,)),
+            pltpu.SemaphoreType.DMA((4,)),
         ],
         compiler_params=pltpu.CompilerParams(vmem_limit_bytes=VMEM_LIMIT),
         cost_estimate=COST,
@@ -146,9 +157,12 @@
     return line
 
 
-def tables_kernel(place_ref, rel_ref, len_ref, map_ref, near_ref, line_ref, meta_ref):
+def tables_kernel(
+    place_ref, rel_ref, len_ref, map_ref, near_ref, name_ref, asked_ref, tail_ref, chosen_ref
+):
     row = lax.broadcasted_iota(jnp.int32, (ROWS, LANES), 0)
     lane = lax.broadcasted_iota(jnp.int32, (ROWS, LANES), 1)
+    lines = []
     for h in range(2):
         head = place_ref[1] * 2 + h
         before = bias_line(rel_ref, head, 0)
@@ -163,7 +177,7 @@
             lane > row, pick(after_it, lane - row), pick(before, row - lane)
         )
         near_ref[rows, 2 * LANES : 3 * LANES] = pick(after_it, lane + LANES - row)
-        line_ref[rows, :] = before
+        lines.append(before)
 
     requests = len_ref.shape[1]
     down_it = lax.broadcasted_iota(jnp.int32, (requests, requests), 0)
@@ -179,6 +193,7 @@
     prefixes = column(along == down_it, prefix)
     number = lax.broadcasted_iota(jnp.int32, (requests, LANES), 0).astype(jnp.float32) + 1.0
     first = place_ref[0] * (PAIRS * ROWS) - ROWS
+    facts = []
     for b in range(PAIRS + 2):
         ids = lax.broadcasted_iota(jnp.int32, (requests, LANES), 1) + (first + b * ROWS)
         ids = ids.astype(jnp.float32)
@@ -186,18 +201,30 @@
         request = jnp.sum(jnp.where(member, number, 0.0), axis=0, keepdims=True) - 1.0
         offset = ids[0:1] - jnp.sum(jnp.where(member, starts, 0.0), axis=0, keepdims=True)
         chosen = jnp.sum(jnp.where(member, prefixes, 0.0), axis=0, keepdims=True)
-        meta_ref[b] = jnp.concatenate([request, offset, chosen] + [request] * 5, axis=0)
+        name_ref[b] = jnp.broadcast_to(request, (8, LANES))
+        facts.append(jnp.concatenate([request, offset, chosen] + [request] * 5, axis=0))
+
+    for step in range(PAIRS):
+        own = jnp.transpose(facts[step + 1])
+        asked_ref[step] = jnp.broadcast_to(own[:, 0:1], (ROWS, LANES))
+        chosen_ref[step] = jnp.broadcast_to(own[:, 2:3], (ROWS, LANES)).astype(jnp.bfloat16)
+        offset = jnp.broadcast_to(own[:, 1:2], (ROWS, LANES)).astype(jnp.int32)
+        at = jnp.minimum(LANES - lane + offset, LANES - 1)
+        for h in range(2):
+            tail_ref[step, h * ROWS : (h + 1) * ROWS] = jnp.take_along_axis(lines[h], at, axis=1)
 
 
 def tables(place, rel_bias, lengths, prefix_map):
     return pl.pallas_call(
         tables_kernel,
         in_specs=[SMEM_SPEC, SMEM_SPEC, VMEM_SPEC, VMEM_SPEC],
-        out_specs=(VMEM_SPEC,) * 3,
+        out_specs=(VMEM_SPEC,) * 5,
         out_shape=(
             pltpu.VMEM((2 * ROWS, 3 * LANES), jnp.float32),
-            pltpu.VMEM((2 * ROWS, LANES), jnp.float32),
-            pltpu.VMEM((PAIRS + 2, 8, ROWS), jnp.float32),
+            pltpu.VMEM((PAIRS + 2, 8, LANES), jnp.float32),
+            pltpu.VMEM((PAIRS, ROWS, LANES), jnp.float32),
+            pltpu.VMEM((PAIRS, 2 * ROWS, LANES), jnp.float32),
+            pltpu.VMEM((PAIRS, ROWS, LANES), jnp.bfloat16),
         ),
         compiler_params=pltpu.CompilerParams(vmem_limit_bytes=VMEM_LIMIT),
         cost_estimate=COST,
@@ -205,32 +232,31 @@
     )(place, rel_bias.T, *on_chip(lengths, prefix_map))
 
 
-def masks_of(meta_ref, step):
-    own = jnp.transpose(meta_ref[step + 1])
-    second = jnp.concatenate([own[:, 2:3], own[:, 2:3]], axis=0) > 0.5
-    return own[:, 0:1], own[:, 1:2], second
-
-
-def queries(got_ref, step, second):
-    lane = lax.broadcasted_iota(jnp.int32, (ROWS, LANES), 1)
+def queries(got_ref, chosen_ref, step):
     query = got_ref[step, 0:ROWS]
-    zero = jnp.zeros_like(query)
-    stacked = jnp.concatenate(
-        [jnp.where(lane < DK, query, zero), jnp.where(lane < DK, zero, query)], axis=0
+    low = (lax.broadcasted_iota(jnp.int32, (ROWS, LANES), 1) < DK).astype(jnp.bfloat16)
+    stacked = jnp.concatenate([query * low, query * (1 - low)], axis=0)
+    chosen = chosen_ref[step]
+    chosen = jnp.concatenate([chosen, chosen], axis=0)
+    return stacked, jnp.concatenate([stacked * (1 - chosen), stacked * chosen], axis=1)
+
+
+def masked(scores, name_ref, block, asked_ref, step, bias):
+    mine = name_ref[block, 0:1] == asked_ref[step]
+    mine = jnp.concatenate([mine, mine], axis=0)
+    return jnp.where(mine, scores + bias, masked_score)
+
+
+def far_bias(place_ref, rel_ref):
+    return jnp.concatenate(
+        [jnp.full((ROWS, LANES), rel_ref[place_ref[1] * 2 + h, 15], jnp.float32) for h in range(2)], axis=0
     )
-    zeros = jnp.zeros_like(stacked)
-    split = jnp.concatenate(
-        [jnp.where(second, zeros, stacked), jnp.where(second, stacked, zeros)], axis=1
-    )
-    return stacked, split
-
-
-def prefix_bias(line_ref, offset):
-    lane = lax.broadcasted_iota(jnp.int32, (ROWS, LANES), 1)
-    at = jnp.minimum(LANES - lane + offset.astype(jnp.int32), LANES - 1)
-    line = line_ref[...]
-    tail = jnp.take_along_axis(line, jnp.concatenate([at, at], axis=0), axis=1)
-    return tail, line[:, LANES - 1 :]
+
+
+def select(chosen_ref, step, far_out):
+    second = chosen_ref[step].astype(jnp.float32) > 0.5
+    second = jnp.concatenate([second, second], axis=0)
+    return jnp.where(second, far_out[:, LANES:], far_out[:, :LANES])
 
 
 def quarter_of(rows_at, keys_ref, values_ref):
@@ -257,10 +283,10 @@
 
 
 def own_kernel(
-    place_ref, got_ref, near_ref, line_ref, meta_ref, w1_hbm, w2_hbm,
-    stat_ref, acc_ref, w1_ref, w2_ref, keys, values, kwin, vwin, landed,
+    place_ref, rel_ref, got_ref, near_ref, name_ref, asked_ref, tail_ref, chosen_ref, w1_hbm, w2_hbm, w3_hbm,
+    stat_ref, acc_ref, w1_ref, w2_ref, w3_ref, keys, values, kwin, vwin, landed,
 ):
-    copies = start_copies(((w1_hbm, w1_ref), (w2_hbm, w2_ref)), landed)
+    copies = start_copies(((w1_hbm, w1_ref), (w2_hbm, w2_ref), (w3_hbm, w3_ref)), landed)
     for b in (0, PAIRS + 1):
         kwin[b] = jnp.zeros((LANES, ROWS), jnp.bfloat16)
         vwin[b] = jnp.zeros((ROWS, LANES), jnp.bfloat16)
@@ -269,27 +295,24 @@
         vwin[b + 1] = got_ref[b, 2 * ROWS : 3 * ROWS]
     quarter_of(lambda s, at: got_ref[s, 3 * ROWS + at : 3 * ROWS + at + SHARE], keys, values)
     is_last = place_ref[0] == 3
+    full = far_bias(place_ref, rel_ref)
 
     def one(step, _):
-        request, offset, second = masks_of(meta_ref, step)
-        stacked, split = queries(got_ref, step, second)
-        tail, full = prefix_bias(line_ref, offset)
-        parts = [dot(split, keys[...]) + jnp.where(is_last, tail, full)]
+        stacked, split = queries(got_ref, chosen_ref, step)
+        parts = [dot(split, keys[...]) + jnp.where(is_last, tail_ref[step], full)]
         near_scores = dot(stacked, jnp.concatenate([kwin[step + b] for b in range(3)], axis=1))
         for b in range(3):
             at_edge = (step + b == 0) | (step + b == PAIRS + 1)
-            names = jnp.where(at_edge, -2.0, meta_ref[step + b, 0:1, :])
-            mine = names == request
-            mine = jnp.concatenate([mine, mine], axis=0)
-            at = slice(b * LANES, (b + 1) * LANES)
-            parts.append(jnp.where(mine, near_scores[:, at] + near_ref[:, at], masked_score))
+            cut = slice(b * LANES, (b + 1) * LANES)
+            bias = near_ref[:, cut] + jnp.where(at_edge, masked_score, 0.0)
+            parts.append(masked(near_scores[:, cut], name_ref, step + b, asked_ref, step, bias))
         row_max = jnp.max(functools.reduce(jnp.maximum, parts), axis=1, keepdims=True)
         terms = [jnp.exp(part - row_max) for part in parts]
         row_sum = jnp.sum(functools.reduce(jnp.add, terms), axis=1, keepdims=True)
         weights = [t.astype(jnp.bfloat16) for t in terms]
         far_out = dot(weights[0], values[...])
         near_values = jnp.concatenate([vwin[step + b] for b in range(3)], axis=0)
-        acc = jnp.where(second, far_out[:, LANES:], far_out[:, :LANES])
+        acc = select(chosen_ref, step, far_out)
         acc_ref[step] = acc + dot(jnp.concatenate(weights[1:], axis=1), near_values)
         stat_ref[step, :, 0:1] = row_max
         stat_ref[step, :, 1:2] = row_sum
@@ -300,11 +323,11 @@
         copy.wait()
 
 
-def attend_own(place, got, made, later_weights):
+def attend_own(place, rel_bias, got, made, later_weights):
     return pl.pallas_call(
         own_kernel,
-        in_specs=[SMEM_SPEC] + [VMEM_SPEC] * 4 + [HBM_SPEC] * 2,
-        out_specs=(VMEM_SPEC,) * 4,
+        in_specs=[SMEM_SPEC] * 2 + [VMEM_SPEC] * 6 + [HBM_SPEC] * 3,
+        out_specs=(VMEM_SPEC,) * 5,
         out_shape=(
             pltpu.VMEM((PAIRS, 2 * ROWS, 2), jnp.float32),
             pltpu.VMEM((PAIRS, 2 * ROWS, LANES), jnp.float32),
@@ -315,19 +338,19 @@
             pltpu.VMEM((PLEN // 4, PREF_GRP * LANES), jnp.bfloat16),
             pltpu.VMEM((PAIRS + 2, LANES, ROWS), jnp.bfloat16),
             pltpu.VMEM((PAIRS + 2, ROWS, LANES), jnp.bfloat16),
-            pltpu.SemaphoreType.DMA((2,)),
+            pltpu.SemaphoreType.DMA((3,)),
         ],
         compiler_params=pltpu.CompilerParams(vmem_limit_bytes=VMEM_LIMIT),
         cost_estimate=COST,
         name="attend_own",
-    )(place, *on_chip(got, *made), *off_chip(*later_weights))
+    )(place, rel_bias.T, *on_chip(got, *made), *off_chip(*later_weights))
 
 
 def rest_kernel(
-    place_ref, got_ref, prev_ref, next_ref, far_ref, near_ref, line_ref, meta_ref, stat_ref, acc_ref, w_hbm,
-    out_ref, w_ref, keys, values, kwin, vwin, landed,
+    place_ref, rel_ref, got_ref, prev_ref, next_ref, far_ref, near_ref, name_ref, asked_ref, tail_ref, chosen_ref,
+    stat_ref, acc_ref, w1_hbm, w2_hbm, out_ref, w1_ref, w2_ref, keys, values, kwin, vwin, landed,
 ):
-    copies = start_copies(((w_hbm, w_ref),), landed)
+    copies = start_copies(((w1_hbm, w1_ref), (w2_hbm, w2_ref)), landed)
     turns = ((3, prev_ref), (1, next_ref), (2, far_ref))
     for i, (_, ref) in enumerate(turns):
         quarter_of(
@@ -339,20 +362,20 @@
     is_last = [lax.rem(place_ref[0] + turn, 4) == 3 for turn, _ in turns]
     side = place_ref[2]
     low = lax.broadcasted_iota(jnp.int32, (ROWS, LANES), 1) < DK
+    full = far_bias(place_ref, rel_ref)
 
     def one(step, edge=None):
-        request, offset, second = masks_of(meta_ref, step)
-        stacked, split = queries(got_ref, step, second)
-        tail, full = prefix_bias(line_ref, offset)
+        stacked, split = queries(got_ref, chosen_ref, step)
+        tail = tail_ref[step]
         scores = dot(split, jnp.concatenate([keys[i] for i in range(3)], axis=1))
         parts = [
             scores[:, i * LANES : (i + 1) * LANES] + jnp.where(is_last[i], tail, full) for i in range(3)
         ]
         if edge is not None:
-            mine = meta_ref[edge * (PAIRS + 1), 0:1, :] == request
-            mine = jnp.concatenate([mine, mine], axis=0)
             bias = near_ref[:, edge * 2 * LANES : (edge * 2 + 1) * LANES]
-            parts.append(jnp.where(mine, dot(stacked, kwin[edge]) + bias, masked_score))
+            parts.append(
+                masked(dot(stacked, kwin[edge]), name_ref, edge * (PAIRS + 1), asked_ref, step, bias)
+            )
         before = stat_ref[step, :, 0:1]
         row_max = jnp.max(functools.reduce(jnp.maximum, parts), axis=1, keepdims=True)
         row_max = jnp.maximum(row_max, before)
@@ -364,7 +387,7 @@
         far_out = dot(
             jnp.concatenate(weights[:3], axis=1), values[...].reshape(3 * PLEN // 4, PREF_GRP * LANES)
         )
-        acc = acc_ref[step] * shrink + jnp.where(second, far_out[:, LANES:], far_out[:, :LANES])
+        acc = acc_ref[step] * shrink + select(chosen_ref, step, far_out)
         if edge is not None:
             acc = acc + dot(weights[3], vwin[edge])
         acc = acc / row_sum
@@ -383,77 +406,69 @@
         copy.wait()
 
 
-def attend_rest(place, got, prev, after_it, far, made, part, weight):
+def attend_rest(place, rel_bias, got, prev, after_it, far, made, part, later_weights):
     return pl.pallas_call(
         rest_kernel,
-        in_specs=[SMEM_SPEC] + [VMEM_SPEC] * 9 + [HBM_SPEC],
-        out_specs=(VMEM_SPEC,) * 2,
-        out_shape=(
-            pltpu.VMEM((2 * PAIRS, ROWS, LANES), jnp.bfloat16),
-            pltpu.VMEM(weight.shape, weight.dtype),
-        ),
+        in_specs=[SMEM_SPEC] * 2 + [VMEM_SPEC] * 11 + [HBM_SPEC] * 2,
+        out_specs=(VMEM_SPEC,) * 3,
+        out_shape=(pltpu.VMEM((2 * PAIRS, ROWS, LANES), jnp.bfloat16),)
+        + tuple(pltpu.VMEM(w.shape, w.dtype) for w in later_weights),
         scratch_shapes=[
             pltpu.VMEM((3, PREF_GRP * LANES, PLEN // 4), jnp.bfloat16),
             pltpu.VMEM((3, PLEN // 4, PREF_GRP * LANES), jnp.bfloat16),
             pltpu.VMEM((2, LANES, ROWS), jnp.bfloat16),
             pltpu.VMEM((2, ROWS, LANES), jnp.bfloat16),
-            pltpu.SemaphoreType.DMA((1,)),
+            pltpu.SemaphoreType.DMA((2,)),
         ],
         compiler_params=pltpu.CompilerParams(vmem_limit_bytes=VMEM_LIMIT),
         cost_estimate=COST,
         name="attend_rest",
-    )(place, *on_chip(got, prev, after_it, far, *made, *part), *off_chip(weight))
-
-
-def join_kernel(place_ref, att_ref, w_ref, tok_ref, far_tok_ref, gain_ref, hidden_ref, normed_ref):
-    side = place_ref[2]
-    halves = [
-        jnp.concatenate([att_ref[at * PAIRS + j] for j in range(PAIRS)], axis=1) for at in (side, 1 - side)
-    ]
-    got = jnp.dot(jnp.concatenate(halves, axis=0), w_ref[...], preferred_element_type=jnp.float32)
-    for half, ref in enumerate((tok_ref, far_tok_ref)):
-        mine = got[half * ROWS : (half + 1) * ROWS]
-        hidden = (ref[...].astype(jnp.float32) + mine).astype(jnp.bfloat16)
-        if half == 0:
-            hidden_ref[...] = hidden
-        normed_ref[half] = norm_rows(hidden, gain_ref[...])
-
-
-def join(place, att, w_attn_out, tokens, far_tokens, gain):
-    return pl.pallas_call(
-        join_kernel,
-        in_specs=[SMEM_SPEC] + [VMEM_SPEC] * 5,
-        out_specs=(VMEM_SPEC,) * 2,
-        out_shape=(pltpu.VMEM((ROWS, D), jnp.bfloat16), pltpu.VMEM((2, ROWS, D), jnp.bfloat16)),
+    )(place, rel_bias.T, *on_chip(got, prev, after_it, far, *made, *part), *off_chip(*later_weights))
+
+
+def join_kernel(away, place_ref, att_ref, w_ref, tok_ref, gain_ref, *rest):
+    at = (1 - place_ref[2] if away else place_ref[2]) * PAIRS
+    attended = jnp.concatenate([att_ref[at + j] for j in range(PAIRS)], axis=1)
+    hidden = (tok_ref[...].astype(jnp.float32) + dot(attended, w_ref[...])).astype(jnp.bfloat16)
+    rest[-1][...] = norm_rows(hidden, gain_ref[...])
+    if not away:
+        rest[-2][...] = hidden
+
+
+def join(away, place, att, w_attn_out, tokens, gain, *ready):
+    count = 1 if away else 2
+    return pl.pallas_call(
+        functools.partial(join_kernel, away),
+        in_specs=[SMEM_SPEC] + [VMEM_SPEC] * (4 + len(ready)),
+        out_specs=(VMEM_SPEC,) * count,
+        out_shape=(pltpu.VMEM((ROWS, D), jnp.bfloat16),) * count,
         compiler_params=pltpu.CompilerParams(vmem_limit_bytes=VMEM_LIMIT),
         cost_estimate=COST,
         name="join",
-    )(place, *on_chip(att, w_attn_out, tokens, far_tokens, gain.reshape(1, D)))
-
-
-def feed_kernel(picked, rows_ref, in_ref, out_w_ref, *rest):
-    out_refs = rest[len(rest) - len(picked) :]
-    rows = jnp.concatenate([rows_ref[half] for half in picked], axis=0)
-    units = lax.dot_general(
-        rows, in_ref[...], (((1,), (1,)), ((), ())), preferred_element_type=jnp.float32
-    )
-    units = jnp.maximum(units, 0.0).astype(jnp.bfloat16)
-    got = jnp.dot(units, out_w_ref[...], preferred_element_type=jnp.float32).astype(jnp.bfloat16)
-    for at, ref in enumerate(out_refs):
-        ref[...] = got[at * ROWS : (at + 1) * ROWS]
-
-
-def feed(picked, rows, w_in, w_out, *ready):
-    shape = pltpu.VMEM((ROWS, D), jnp.bfloat16)
-    return pl.pallas_call(
-        functools.partial(feed_kernel, picked),
-        in_specs=[VMEM_SPEC] * (3 + len(ready)),
-        out_specs=(VMEM_SPEC,) * len(picked),
-        out_shape=(shape,) * len(picked),
+    )(place, *on_chip(att, w_attn_out, tokens, gain.reshape(1, D), *ready))
+
+
+def feed_kernel(rows_ref, in_one, in_two, out_one, out_two, *rest):
+    got = None
+    for in_ref, out_w_ref in ((in_one, out_one), (in_two, out_two)):
+        units = lax.dot_general(
+            rows_ref[...], in_ref[...], (((1,), (1,)), ((), ())), preferred_element_type=jnp.float32
+        )
+        part = dot(jnp.maximum(units, 0.0).astype(jnp.bfloat16), out_w_ref[...])
+        got = part if got is None else got + part
+    rest[-1][...] = got.astype(rest[-1].dtype)
+
+
+def feed(dtype, rows, weights):
+    return pl.pallas_call(
+        feed_kernel,
+        in_specs=[VMEM_SPEC] * 5,
+        out_specs=VMEM_SPEC,
+        out_shape=pltpu.VMEM((ROWS, D), dtype),
         compiler_params=pltpu.CompilerParams(vmem_limit_bytes=VMEM_LIMIT),
         cost_estimate=COST,
         name="feed",
-    )(*on_chip(rows, w_in, w_out, *ready))
+    )(*on_chip(rows, *weights))
 
 
 def total_kernel(*refs):
@@ -498,24 +513,27 @@
     got = lax.all_to_all(blocks, PLANE, 0, 0, tiled=True)
     mirrored = ("yhi", "ylo")
     far_tokens = lax.ppermute(tokens, mirrored, MIRROR)
+    other_in = lax.ppermute(w_in, "core", SWAP)
+    other_out = lax.ppermute(w_out, "core", SWAP)
     up, down, far = spread(got, far_tokens, *made)
     by = lambda d: [(i, (i + d) % count_x) for i in range(count_x)]
     prev = lax.ppermute(up, "x", by(1))
     later = lax.ppermute(down, "x", by(-1))
     opposite = lax.ppermute(far, "x", by(2))
-    stat, acc, w_attn_out, w_in = attend_own(place, got, made, (w_attn_out, w_in))
-    mixed, w_out = attend_rest(place, got, prev, later, opposite, made, (stat, acc), w_out)
+    stat, acc, *own_weights = attend_own(place, rel_bias, got, made, (w_attn_out, w_in, w_out))
+    mixed, *other_weights = attend_rest(
+        place, rel_bias, got, prev, later, opposite, made, (stat, acc), (other_in, other_out)
+    )
+    w_attn_out = own_weights[0]
+    weights = (own_weights[1], other_weights[0], own_weights[2], other_weights[1])
     att = lax.all_to_all(mixed, ("yhi",) + PLANE, 0, 0, tiled=True)
 
-    hidden, normed = join(place, att, w_attn_out, tokens, far_tokens, mlp_gain)
-    other = lax.ppermute(normed, "core", SWAP)
-    mine, far_mine = feed((0, 1), normed, w_in, w_out)
-    (far_theirs,) = feed((1,), other, w_in, w_out, mine)
-    far_sum = total(jnp.bfloat16, far_mine, lax.ppermute(far_theirs, "core", SWAP))
+    (far_normed,) = join(True, place, att, w_attn_out, far_tokens, mlp_gain)
+    far_sum = feed(jnp.bfloat16, far_normed, weights)
     back = lax.ppermute(far_sum, mirrored, MIRROR)
-    (theirs,) = feed((0,), other, w_in, w_out, far_theirs)
-    local = total(jnp.float32, hidden, mine, lax.ppermute(theirs, "core", SWAP))
-    return total(jnp.bfloat16, local, back, last=True)
+    hidden, normed = join(False, place, att, w_attn_out, tokens, mlp_gain, far_sum)
+    mine = feed(jnp.float32, normed, weights)
+    return total(jnp.bfloat16, hidden, mine, back, last=True)
 
 
 def solution(mesh):

time: 77.5 us -> 72.4 us (0.934)
  waiting for transfers between devices: 18.3 us -> 11 us
  Pallas kernels: 25.8 us -> 27.6 us
    ppermute x1, waiting for transfers between devices: 8.15 us -> 3.03 us  [body(): back = lax.ppermute(far_sum, mirrored, MIRROR)]
    pallas_call x1, Pallas kernels: 1.24 us -> 3.22 us  [tables(): pl.pallas_call(tables_kernel, in_specs=[SMEM_SPEC, SMEM_SPEC, VMEM_SPEC,...]
    ppermute x1, waiting for transfers between devices: 4.41 us -> 2.71 us  [body(): far_tokens = lax.ppermute(tokens, mirrored, MIRROR)]
    pallas_call x7, Pallas kernels: 23.6 us -> 22.5 us  [the longest x1 5.57 us: project(): pl.pallas_call(project_kernel, in_specs=[HBM_SPEC] * 6, out_specs=HBM_SPE...]
    pallas_call x1, Pallas kernels: 0.06 us -> 1.01 us  [spread(): pl.pallas_call(spread_kernel, in_specs=[VMEM_SPEC] * (1 + len(ready)), ou...]
  transfers between devices with their start and end apart: 9 -> 8, of which waited for: 4 -> 4; matrix products, arithmetic and copies ran while one was open for 0% -> 0% of each run, Pallas kernels for 12% -> 25%
where the time goes in v6:
time: 72.4 us; the launch traced here: 72.2 us
  Pallas kernels  27.6 us (38%)
  starting transfers between devices  16.9 us (23%)
  blocking collectives  16.4 us (23%)
  waiting for transfers between devices  11 us (15%)
    all_to_all x1, blocking collectives, body(): att = lax.all_to_all(mixed, ('yhi',) + PLANE, 0, 0, tiled=True)  16.4 us
    all_to_all x1, starting transfers between devices, body(): got = lax.all_to_all(blocks, PLANE, 0, 0, tiled=True)  6.42 us
    pallas_call x1, Pallas kernels, project(): pl.pallas_call(project_kernel, in_specs=[HBM_SPEC] * 6, out_specs=HBM_SPE...  5.57 us
    pallas_call x1, Pallas kernels, attend_rest(): pl.pallas_call(rest_kernel, in_specs=[SMEM_SPEC] * 2 + [VMEM_SPEC] * 11 +...  5.17 us
    pallas_call x1, Pallas kernels, attend_own(): pl.pallas_call(own_kernel, in_specs=[SMEM_SPEC] * 2 + [VMEM_SPEC] * 6 + [...  4.99 us
    all_to_all x1, waiting for transfers between devices, body(): got = lax.all_to_all(blocks, PLANE, 0, 0, tiled=True)  4.99 us
    pallas_call x2, Pallas kernels, feed(): pl.pallas_call(feed_kernel, in_specs=[VMEM_SPEC] * 5, out_specs=VMEM_SPEC...  4.12 us
    ppermute x1, starting transfers between devices, body(): far_tokens = lax.ppermute(tokens, mirrored, MIRROR)  3.46 us
  transfers between devices with their start and end apart: 8, of which 4 were waited for; matrix products, arithmetic and copies ran while one was open for 0% of the time, Pallas kernels for 25%

profile of v6, /device:TPU:0, one launch (start us, length us, event | category | flops | bytes accessed | tf_op | source)
XLA Modules:
  0.0 72.2 jit_solution(6069975922417852785)
XLA Ops:
  0.0 0.0 collective-permute-start.4
  0.0 0.5 collective-permute-start.5
  0.5 0.0 copy-start
  0.5 0.0 copy-start.1
  0.5 0.0 copy-start.3
  0.5 0.0 copy-start.4
  0.5 5.6 %project.1 = bf16[8,448,128]{2,1,0:T(8,128)(2,1)} custom-call(bf16[128,1024]{1,0:T(8,128)(2,1)} %tok_ref.1, f32[1,1024]{1,0:T(1,128)} %bitcast.11, bf16[2,16,2048]{2,1,0:T(8,128)(2,1)} %cache_hbm.1, bf16[1024,1024]{1,0:T(8,128)(2,1)} %wq_hbm.1, bf16[1024,1024]{1,0:T(8,128)(2,1)} %wk_hbm.1, bf16[1024,1024]{1,0:T(8,128)(2,1)} %wv_hbm.1), custom_call_target="tpu_custom_call" | custom-call | flops 1000 | bytes 1000 | tf_op jit(solution)/shard_map/project/pallas_call | solution.py:105
  6.1 6.4 %all-to-all-start = ((bf16[8,448,128]{2,1,0:T(8,128)(2,1)}), bf16[8,448,128]{2,1,0:T(8,128)(2,1)S(1)}, u32[]{:S(2)}, u32[]{:S(2)}) async-start(bf16[8,448,128]{2,1,0:T(8,128)(2,1)} %project.1), calls=%async_computation | async-start | bytes 1835008 | tf_op jit(solution)/shard_map/all_to_all | solution.py:513
  12.5 0.0 copy-done
  12.5 3.5 %collective-permute-start = (bf16[128,1024]{1,0:T(8,128)(2,1)S(1)}, bf16[128,1024]{1,0:T(8,128)(2,1)}, u32[]{:S(2)}, u32[]{:S(2)}) collective-permute-start(bf16[128,1024]{1,0:T(8,128)(2,1)S(1)} %copy-done), channel_id=1, source_target_pairs={{0,65},{65,0},{1,64},{64,1},{2,67},{67,2},{3,66},{66,3},{4,69},{69... | collective-permute-start | bytes 786440 | tf_op jit(solution)/shard_map/ppermute | solution.py:515
  16.0 0.1 pad_add_fusion.place_ref
  16.1 0.0 copy-done.1
  16.1 0.0 copy-done.3
  16.1 0.0 copy-done.4
  16.1 3.2 %tables.1 = (f32[256,384]{1,0:T(8,128)S(1)}, f32[10,8,128]{2,1,0:T(8,128)S(1)}, f32[8,128,128]{2,1,0:T(8,128)S(1)}, f32[8,256,128]{2,1,0:T(8,128)S(1)}, bf16[8,128,128]{2,1,0:T(8,128)(2,1)S(1)}) custom-call(s32[3]{0:T(128)S(1)} %pad_add_fusion.place_ref, f32[16,32]{1,0:T(8,128)S(1)} %bitcast.6, s32[1,64]{1,0:T(1,128)S(1)} %copy-done.3, s32[1,64]{1,0:T(1,128)S(1)} %copy-done.4), custom_call_target="tpu_custom_call" | custom-call | flops 1000 | bytes 1000 | tf_op jit(solution)/shard_map/tables/pallas_call | solution.py:218
  19.3 2.7 %collective-permute-done.rest_0_.tok_ref = bf16[128,1024]{1,0:T(8,128)(2,1)} collective-permute-done((bf16[128,1024]{1,0:T(8,128)(2,1)S(1)}, bf16[128,1024]{1,0:T(8,128)(2,1)}, u32[]{:S(2)}, u32[]{:S(2)}) %collective-permute-start) | collective-permute-done | bytes 262176 | tf_op jit(solution)/shard_map/ppermute | solution.py:515
  22.0 5.0 %all-to-all-done.got_ref = bf16[8,448,128]{2,1,0:T(8,128)(2,1)S(1)} async-done(((bf16[8,448,128]{2,1,0:T(8,128)(2,1)}), bf16[8,448,128]{2,1,0:T(8,128)(2,1)S(1)}, u32[]{:S(2)}, u32[]{:S(2)}) %all-to-all-start) | async-done | bytes 917536 | tf_op jit(solution)/shard_map/all_to_all | solution.py:513
  27.0 1.0 %spread.1 = (bf16[768,128]{1,0:T(8,128)(2,1)S(1)}, bf16[768,128]{1,0:T(8,128)(2,1)S(1)}, bf16[512,128]{1,0:T(8,128)(2,1)S(1)}) custom-call(bf16[8,448,128]{2,1,0:T(8,128)(2,1)S(1)} %all-to-all-done.got_ref, bf16[128,1024]{1,0:T(8,128)(2,1)} %collective-permute-done.rest_0_.tok_ref, f32[256,384]{1,0:T(8,128)S(1)} %get-tuple-element.23.rest_1_.near_ref, ...), custom_call_target="tpu_custom_call" | custom-call | flops 1000 | bytes 1000 | tf_op jit(solution)/shard_map/spread/pallas_call | solution.py:140
  28.0 1.6 %collective-permute-start.1 = (bf16[768,128]{1,0:T(8,128)(2,1)S(1)}, bf16[768,128]{1,0:T(8,128)(2,1)S(1)}, u32[]{:S(2)}, u32[]{:S(2)}) collective-permute-start(bf16[768,128]{1,0:T(8,128)(2,1)S(1)} %get-tuple-element.28), channel_id=1, source_target_pairs={{0,8},{8,16},{16,24},{24,0},{1,9},{9,17},{17,25},{25,1},{2,10},{10... | collective-permute-start | bytes 589832 | tf_op jit(solution)/shard_map/ppermute | solution.py:520
  29.6 1.8 %collective-permute-start.2 = (bf16[768,128]{1,0:T(8,128)(2,1)S(1)}, bf16[768,128]{1,0:T(8,128)(2,1)S(1)}, u32[]{:S(2)}, u32[]{:S(2)}) collective-permute-start(bf16[768,128]{1,0:T(8,128)(2,1)S(1)} %get-tuple-element.29), channel_id=1, source_target_pairs={{0,24},{8,0},{16,8},{24,16},{1,25},{9,1},{17,9},{25,17},{2,26},{10... | collective-permute-start | bytes 589832 | tf_op jit(solution)/shard_map/ppermute | solution.py:521
  31.3 1.8 %collective-permute-start.3 = (bf16[512,128]{1,0:T(8,128)(2,1)S(1)}, bf16[512,128]{1,0:T(8,128)(2,1)S(1)}, u32[]{:S(2)}, u32[]{:S(2)}) collective-permute-start(bf16[512,128]{1,0:T(8,128)(2,1)S(1)} %get-tuple-element.30), channel_id=1, source_target_pairs={{0,16},{8,24},{16,0},{24,8},{1,17},{9,25},{17,1},{25,9},{2,18},{10... | collective-permute-start | bytes 393224 | tf_op jit(solution)/shard_map/ppermute | solution.py:522
  33.1 5.0 %attend_own.1 = (f32[8,256,2]{2,1,0:T(8,128)S(1)}, f32[8,256,128]{2,1,0:T(8,128)S(1)}, bf16[1024,1024]{1,0:T(8,128)(2,1)S(1)}, bf16[1024,1024]{1,0:T(8,128)(2,1)S(1)}, bf16[1024,1024]{1,0:T(8,128)(2,1)S(1)}) custom-call(s32[3]{0:T(128)S(1)} %pad_add_fusion.place_ref, f32[16,32]{1,0:T(8,128)S(1)} %bitcast.7, bf16[8,448,128]{2,1,0:T(8,128)(2,1)S(1)} %all-to-all-done.got_ref, ...), custom_call_target="tpu_custom_call" | custom-call | flops 1000 | bytes 1000 | tf_op jit(solution)/shard_map/attend_own/pallas_call | solution.py:327
  38.1 0.3 collective-permute-done.3.far_ref
  38.4 0.0 collective-permute-done.1.prev_ref
  38.4 0.0 collective-permute-done.2.next_ref
  38.4 0.0 collective-permute-done.4.w1_hbm
  38.4 0.0 collective-permute-done.5.w2_hbm
  38.5 0.0 copy-start.2
  38.5 5.2 %attend_rest.1 = (bf16[16,128,128]{2,1,0:T(8,128)(2,1)S(1)}, bf16[1024,1024]{1,0:T(8,128)(2,1)S(1)}, bf16[1024,1024]{1,0:T(8,128)(2,1)S(1)}) custom-call(s32[3]{0:T(128)S(1)} %pad_add_fusion.place_ref, f32[16,32]{1,0:T(8,128)S(1)} %bitcast.8, bf16[8,448,128]{2,1,0:T(8,128)(2,1)S(1)} %all-to-all-done.got_ref, ...), custom_call_target="tpu_custom_call" | custom-call | flops 1000 | bytes 1000 | tf_op jit(solution)/shard_map/attend_rest/pallas_call | solution.py:410
  43.6 16.4 %all_to_all.10.att_ref = bf16[16,128,128]{2,1,0:T(8,128)(2,1)S(1)} all-to-all(bf16[16,128,128]{2,1,0:T(8,128)(2,1)S(1)} %get-tuple-element.33), channel_id=1, replica_groups=mesh['yhi'=2,'core'=2,'x'=4,'z'=4,'ylo'=2] {'yhi','z','ylo'}, dimensions={0} | all-to-all | bytes 1048576 | tf_op jit(solution)/shard_map/all_to_all | solution.py:529
  60.1 0.0 copy-done.2
  60.1 1.5 %join.2.rows_ref = bf16[128,1024]{1,0:T(8,128)(2,1)S(1)} custom-call(s32[3]{0:T(128)S(1)} %pad_add_fusion.place_ref, bf16[16,128,128]{2,1,0:T(8,128)(2,1)S(1)} %all_to_all.10.att_ref, bf16[1024,1024]{1,0:T(8,128)(2,1)S(1)} %get-tuple-element.34.w_ref, bf16[128,1024]{1,0:T(8,128)(2,1)} %collective-permute-done.rest_0_.tok_ref, f32[1,1024]{1,0:T(1,128)S(1)} %bitcast.9), custom_call_target="tpu_custom_call" | custom-call | flops 1000 | bytes 1000 | tf_op jit(solution)/shard_map/join/pallas_call | solution.py:440
  61.6 2.1 %feed.2.rest_0_ = bf16[128,1024]{1,0:T(8,128)(2,1)S(1)} custom-call(bf16[128,1024]{1,0:T(8,128)(2,1)S(1)} %join.2.rows_ref, bf16[1024,1024]{1,0:T(8,128)(2,1)S(1)} %get-tuple-element.35.in_one, bf16[1024,1024]{1,0:T(8,128)(2,1)S(1)} %get-tuple-element.36.in_two, bf16[1024,1024]{1,0:T(8,128)(2,1)S(1)} %get-tuple-element.37.out_one, ...), custom_call_target="tpu_custom_call" | custom-call | flops 1000 | bytes 1000 | tf_op jit(solution)/shard_map/feed/pallas_call | solution.py:463
  63.7 1.4 %collective-permute-start.6 = (bf16[128,1024]{1,0:T(8,128)(2,1)S(1)}, bf16[128,1024]{1,0:T(8,128)(2,1)S(1)}, u32[]{:S(2)}, u32[]{:S(2)}) collective-permute-start(bf16[128,1024]{1,0:T(8,128)(2,1)S(1)} %feed.2.rest_0_), channel_id=1, source_target_pairs={{0,65},{65,0},{1,64},{64,1},{2,67},{67,2},{3,66},{66,3},{4,69},{69... | collective-permute-start | bytes 786440 | tf_op jit(solution)/shard_map/ppermute | solution.py:533
  65.1 1.1 %join.3 = (bf16[128,1024]{1,0:T(8,128)(2,1)S(1)}, bf16[128,1024]{1,0:T(8,128)(2,1)S(1)}) custom-call(s32[3]{0:T(128)S(1)} %pad_add_fusion.place_ref, bf16[16,128,128]{2,1,0:T(8,128)(2,1)S(1)} %all_to_all.10.att_ref, bf16[1024,1024]{1,0:T(8,128)(2,1)S(1)} %get-tuple-element.34.w_ref, bf16[128,1024]{1,0:T(8,128)(2,1)S(1)} %copy-done, f32[1,1024]{1,0:T(1,128)S(1)} %bitcast.10, ...), custom_call_target="tpu_custom_call" | custom-call | flops 1000 | bytes 1000 | tf_op jit(solution)/shard_map/join/pallas_call | solution.py:440
  66.3 2.1 %feed.3.refs_1_ = f32[128,1024]{1,0:T(8,128)S(1)} custom-call(bf16[128,1024]{1,0:T(8,128)(2,1)S(1)} %get-tuple-element.40.rows_ref, bf16[1024,1024]{1,0:T(8,128)(2,1)S(1)} %get-tuple-element.35.in_one, bf16[1024,1024]{1,0:T(8,128)(2,1)S(1)} %get-tuple-element.36.in_two, bf16[1024,1024]{1,0:T(8,128)(2,1)S(1)} %get-tuple-element.37.out_one, ...), custom_call_target="tpu_custom_call" | custom-call | flops 1000 | bytes 1000 | tf_op jit(solution)/shard_map/feed/pallas_call | solution.py:463
  68.3 3.0 %collective-permute-done.6.refs_2_ = bf16[128,1024]{1,0:T(8,128)(2,1)S(1)} collective-permute-done((bf16[128,1024]{1,0:T(8,128)(2,1)S(1)}, bf16[128,1024]{1,0:T(8,128)(2,1)S(1)}, u32[]{:S(2)}, u32[]{:S(2)}) %collective-permute-start.6) | collective-permute-done | bytes 262176 | tf_op jit(solution)/shard_map/ppermute | solution.py:533
  71.4 0.8 %total.1 = bf16[128,1024]{1,0:T(8,128)(2,1)} custom-call(bf16[128,1024]{1,0:T(8,128)(2,1)S(1)} %get-tuple-element.39.refs_0_, f32[128,1024]{1,0:T(8,128)S(1)} %feed.3.refs_1_, bf16[128,1024]{1,0:T(8,128)(2,1)S(1)} %collective-permute-done.6.refs_2_), custom_call_target="tpu_custom_call" | custom-call | flops 1000 | bytes 1000 | tf_op jit(solution)/shard_map/total/pallas_call | solution.py:481
Async XLA Ops:
  0.0 38.4 %collective-permute-start.4 = (bf16[1024,1024]{1,0:T(8,128)(2,1)}, bf16[1024,1024]{1,0:T(8,128)(2,1)}, u32[]{:S(2)}, u32[]{:S(2)}) collective-permute-start(bf16[1024,1024]{1,0:T(8,128)(2,1)} %w2_hbm.1), channel_id=1, source_target_pairs={{0,32},{32,0},{1,33},{33,1},{2,34},{34,2},{3,35},{35,3},{4,36},{36... | collective-permute-start | bytes 6291464 | tf_op jit(solution)/shard_map/ppermute | solution.py:516
  0.0 38.4 %collective-permute-start.5 = (bf16[1024,1024]{1,0:T(8,128)(2,1)}, bf16[1024,1024]{1,0:T(8,128)(2,1)}, u32[]{:S(2)}, u32[]{:S(2)}) collective-permute-start(bf16[1024,1024]{1,0:T(8,128)(2,1)} %w3_hbm.1), channel_id=1, source_target_pairs={{0,32},{32,0},{1,33},{33,1},{2,34},{34,2},{3,35},{35,3},{4,36},{36... | collective-permute-start | bytes 6291464 | tf_op jit(solution)/shard_map/ppermute | solution.py:517
  0.5 12.0 %copy-start = (bf16[128,1024]{1,0:T(8,128)(2,1)S(1)}, bf16[128,1024]{1,0:T(8,128)(2,1)}, u32[]{:S(2)}) copy-start(bf16[128,1024]{1,0:T(8,128)(2,1)} %tok_ref.1) | copy-start | bytes 786436
  0.5 15.6 %copy-start.1 = (f32[32,16]{0,1:T(8,128)S(1)}, f32[32,16]{0,1:T(8,128)}, u32[]{:S(2)}) copy-start(f32[32,16]{0,1:T(8,128)} %param.19) | copy-start | bytes 6148
  0.5 15.6 %copy-start.3 = (s32[1,64]{1,0:T(1,128)S(1)}, s32[1,64]{1,0:T(1,128)}, u32[]{:S(2)}) copy-start(s32[1,64]{1,0:T(1,128)} %len_ref.1) | copy-start | bytes 772
  0.5 15.6 %copy-start.4 = (s32[1,64]{1,0:T(1,128)S(1)}, s32[1,64]{1,0:T(1,128)}, u32[]{:S(2)}) copy-start(s32[1,64]{1,0:T(1,128)} %map_ref.1) | copy-start | bytes 772
  6.1 20.9 %all-to-all-start = ((bf16[8,448,128]{2,1,0:T(8,128)(2,1)}), bf16[8,448,128]{2,1,0:T(8,128)(2,1)S(1)}, u32[]{:S(2)}, u32[]{:S(2)}) async-start(bf16[8,448,128]{2,1,0:T(8,128)(2,1)} %project.1), calls=%async_computation | async-start | bytes 1835008 | tf_op jit(solution)/shard_map/all_to_all | solution.py:513
  12.5 9.5 %collective-permute-start = (bf16[128,1024]{1,0:T(8,128)(2,1)S(1)}, bf16[128,1024]{1,0:T(8,128)(2,1)}, u32[]{:S(2)}, u32[]{:S(2)}) collective-permute-start(bf16[128,1024]{1,0:T(8,128)(2,1)S(1)} %copy-done), channel_id=1, source_target_pairs={{0,65},{65,0},{1,64},{64,1},{2,67},{67,2},{3,66},{66,3},{4,69},{69... | collective-permute-start | bytes 786440 | tf_op jit(solution)/shard_map/ppermute | solution.py:515
  28.0 10.4 %collective-permute-start.1 = (bf16[768,128]{1,0:T(8,128)(2,1)S(1)}, bf16[768,128]{1,0:T(8,128)(2,1)S(1)}, u32[]{:S(2)}, u32[]{:S(2)}) collective-permute-start(bf16[768,128]{1,0:T(8,128)(2,1)S(1)} %get-tuple-element.28), channel_id=1, source_target_pairs={{0,8},{8,16},{16,24},{24,0},{1,9},{9,17},{17,25},{25,1},{2,10},{10... | collective-permute-start | bytes 589832 | tf_op jit(solution)/shard_map/ppermute | solution.py:520
  29.6 8.9 %collective-permute-start.2 = (bf16[768,128]{1,0:T(8,128)(2,1)S(1)}, bf16[768,128]{1,0:T(8,128)(2,1)S(1)}, u32[]{:S(2)}, u32[]{:S(2)}) collective-permute-start(bf16[768,128]{1,0:T(8,128)(2,1)S(1)} %get-tuple-element.29), channel_id=1, source_target_pairs={{0,24},{8,0},{16,8},{24,16},{1,25},{9,1},{17,9},{25,17},{2,26},{10... | collective-permute-start | bytes 589832 | tf_op jit(solution)/shard_map/ppermute | solution.py:521
  31.3 7.1 %collective-permute-start.3 = (bf16[512,128]{1,0:T(8,128)(2,1)S(1)}, bf16[512,128]{1,0:T(8,128)(2,1)S(1)}, u32[]{:S(2)}, u32[]{:S(2)}) collective-permute-start(bf16[512,128]{1,0:T(8,128)(2,1)S(1)} %get-tuple-element.30), channel_id=1, source_target_pairs={{0,16},{8,24},{16,0},{24,8},{1,17},{9,25},{17,1},{25,9},{2,18},{10... | collective-permute-start | bytes 393224 | tf_op jit(solution)/shard_map/ppermute | solution.py:522
  38.5 21.6 %copy-start.2 = (f32[1024]{0:T(1024)S(1)}, f32[1024]{0:T(1024)}, u32[]{:S(2)}) copy-start(f32[1024]{0:T(1024)} %param.23) | copy-start | bytes 12292
  63.7 7.7 %collective-permute-start.6 = (bf16[128,1024]{1,0:T(8,128)(2,1)S(1)}, bf16[128,1024]{1,0:T(8,128)(2,1)S(1)}, u32[]{:S(2)}, u32[]{:S(2)}) collective-permute-start(bf16[128,1024]{1,0:T(8,128)(2,1)S(1)} %feed.2.rest_0_), channel_id=1, source_target_pairs={{0,65},{65,0},{1,64},{64,1},{2,67},{67,2},{3,66},{66,3},{4,69},{69... | collective-permute-start | bytes 786440 | tf_op jit(solution)/shard_map/ppermute | solution.py:533

commit v7 on v6

v7 whole, which is shorter than its diff:
```python
import functools

import jax
import jax.numpy as jnp
from jax import lax
from jax.experimental import pallas as pl
from jax.experimental.pallas import tpu as pltpu
from jax.sharding import Mesh, PartitionSpec as P

D = 1024
H = 16
DK = 64
PLEN = 512
PREF_GRP = 2
ROWS = 128
PAIRS = 8
LANES = 128
CHUNK = 1024
SHARE = 16
SENT = 3 * ROWS + 2 * PREF_GRP * SHARE
QUARTER = PAIRS * 2 * PREF_GRP * SHARE

epsilon = 1e-06
far_marks = (12, 16, 23, 32, 46, 64, 91)
masked_score = -1e30
VMEM_LIMIT = 16 * 1024 * 1024
COST = pl.CostEstimate(flops=1000, transcendentals=0, bytes_accessed=1000)

AXES = ("yhi", "core", "x", "z", "ylo")
REQ = ("x", "z", "ylo")
PLANE = ("z", "ylo")
MIRROR = [(0, 3), (3, 0), (1, 2), (2, 1)]
SWAP = [(0, 1), (1, 0)]


def norm_rows(values_in, gain):
    widened = values_in.astype(jnp.float32)
    scale = lax.rsqrt(jnp.mean(widened * widened, axis=-1, keepdims=True) + epsilon)
    return (widened * scale * gain).astype(jnp.bfloat16)


def dot(a, b):
    return jnp.dot(a, b, preferred_element_type=jnp.float32)


def on_chip(*arrays):
    return tuple(pltpu.with_memory_space_constraint(a, pltpu.VMEM) for a in arrays)


def off_chip(*arrays):
    return tuple(pltpu.with_memory_space_constraint(a, pltpu.HBM) for a in arrays)


VMEM_SPEC = pl.BlockSpec(memory_space=pltpu.VMEM)
HBM_SPEC = pl.BlockSpec(memory_space=pltpu.HBM)
SMEM_SPEC = pl.BlockSpec(memory_space=pltpu.SMEM)


def project_kernel(
    tok_hbm, gain_hbm, cache_hbm, wq_hbm, wk_hbm, wv_hbm, out_hbm, tok, gain, cache, held, out_ref, arrived, landed, left
):
    chunks = [slice(c * CHUNK, (c + 1) * CHUNK) for c in range(D // CHUNK)]
    first = [
        pltpu.make_async_copy(source, target, landed.at[i])
        for i, (source, target) in enumerate(((tok_hbm, tok), (gain_hbm, gain), (cache_hbm, cache)))
    ]
    copies = [
        [
            pltpu.make_async_copy(w_hbm.at[cut], held.at[kind, cut], arrived.at[kind, c])
            for c, cut in enumerate(chunks)
        ]
        for kind, w_hbm in enumerate((wq_hbm, wk_hbm, wv_hbm))
    ]
    for copy in first:
        copy.start()
    for row in copies:
        for copy in row:
            copy.start()
    for copy in first:
        copy.wait()
    normed = norm_rows(tok[...], gain[...])
    for part in range(PAIRS):
        for kind in range(2):
            for p in range(PREF_GRP):
                at = 3 * ROWS + (kind * PREF_GRP + p) * SHARE
                cut = slice(kind * D + part * LANES, kind * D + (part + 1) * LANES)
                out_ref[part, at : at + SHARE] = cache[p, :, cut]
    def send(at, i):
        copy = pltpu.make_async_copy(out_ref.at[:, at], out_hbm.at[:, at], left.at[i])
        copy.start()
        return copy

    sends = [send(slice(3 * ROWS, SENT), 3)]
    for kind, row in enumerate(copies):
        got = None
        for cut, copy in zip(chunks, row):
            copy.wait()
            part = dot(normed[:, cut], held[kind, cut])
            got = part if got is None else got + part
        got = got.astype(jnp.bfloat16)
        for to in range(PAIRS):
            out_ref[to, kind * ROWS : (kind + 1) * ROWS] = got[:, to * LANES : (to + 1) * LANES]
        sends.append(send(slice(kind * ROWS, (kind + 1) * ROWS), kind))
    for copy in sends:
        copy.wait()


def project(tokens, gain, w_query, w_key, w_value, prefix_cache):
    operands = (tokens, gain.reshape(1, D), prefix_cache, w_query, w_key, w_value)
    return pl.pallas_call(
        project_kernel,
        in_specs=[HBM_SPEC] * 6,
        out_specs=HBM_SPEC,
        out_shape=pltpu.HBM((PAIRS, SENT, LANES), jnp.bfloat16),
        scratch_shapes=[
            pltpu.VMEM((ROWS, D), jnp.bfloat16),
            pltpu.VMEM((1, D), jnp.float32),
            pltpu.VMEM(prefix_cache.shape, jnp.bfloat16),
            pltpu.VMEM((3, D, D), jnp.bfloat16),
            pltpu.VMEM((PAIRS, SENT, LANES), jnp.bfloat16),
            pltpu.SemaphoreType.DMA((3, D // CHUNK)),
            pltpu.SemaphoreType.DMA((3,)),
            pltpu.SemaphoreType.DMA((4,)),
        ],
        compiler_params=pltpu.CompilerParams(vmem_limit_bytes=VMEM_LIMIT),
        cost_estimate=COST,
        name="project",
    )(*off_chip(*operands))


def spread_kernel(got_ref, *rest):
    up_ref, down_ref, far_ref = rest[-3:]
    for source in range(PAIRS):
        rows = slice(source * 4 * SHARE, (source + 1) * 4 * SHARE)
        held = got_ref[source, 3 * ROWS :]
        up_ref[rows] = held
        down_ref[rows] = held
        far_ref[rows] = held
    up_ref[QUARTER:] = got_ref[PAIRS - 1, ROWS : 3 * ROWS]
    down_ref[QUARTER:] = got_ref[0, ROWS : 3 * ROWS]


def spread(got, arrived, *ready):
    shape = pltpu.VMEM((QUARTER + 2 * ROWS, LANES), jnp.bfloat16)
    return pl.pallas_call(
        spread_kernel,
        in_specs=[VMEM_SPEC] * (1 + len(ready)) + [HBM_SPEC],
        out_specs=(VMEM_SPEC,) * 3,
        out_shape=(shape, shape, pltpu.VMEM((QUARTER, LANES), jnp.bfloat16)),
        compiler_params=pltpu.CompilerParams(vmem_limit_bytes=VMEM_LIMIT),
        cost_estimate=COST,
        name="spread",
    )(*on_chip(got, *ready), *off_chip(arrived))


def bias_line(rel_ref, head, first_bucket):
    lane = lax.broadcasted_iota(jnp.int32, (ROWS, LANES), 1)
    line = jnp.full((ROWS, LANES), rel_ref[head, first_bucket], jnp.float32)
    for bucket in range(1, 16):
        mark = bucket if bucket <= 8 else far_marks[bucket - 9]
        line = jnp.where(lane >= mark, rel_ref[head, first_bucket + bucket], line)
    return line


def tables_kernel(
    place_ref, rel_ref, len_ref, map_ref, near_ref, name_ref, asked_ref, tail_ref, chosen_ref
):
    row = lax.broadcasted_iota(jnp.int32, (ROWS, LANES), 0)
    lane = lax.broadcasted_iota(jnp.int32, (ROWS, LANES), 1)
    lines = []
    for h in range(2):
        head = place_ref[1] * 2 + h
        before = bias_line(rel_ref, head, 0)
        after_it = bias_line(rel_ref, head, 16)

        def pick(line, distance):
            return jnp.take_along_axis(line, jnp.clip(distance, 0, LANES - 1), axis=1)

        cut = slice(h * ROWS, (h + 1) * ROWS)
        near_ref[0:ROWS, cut] = pick(before, lane + ROWS - row)
        near_ref[ROWS : 2 * ROWS, cut] = jnp.where(
            row > lane, pick(after_it, row - lane), pick(before, lane - row)
        )
        near_ref[2 * ROWS : 3 * ROWS, cut] = pick(after_it, row + ROWS - lane)
        lines.append(before)

    requests = len_ref.shape[1]
    down_it = lax.broadcasted_iota(jnp.int32, (requests, requests), 0)
    along = lax.broadcasted_iota(jnp.int32, (requests, requests), 1)
    length = jnp.broadcast_to(len_ref[...], (requests, requests)).astype(jnp.float32)
    prefix = jnp.broadcast_to(map_ref[...], (requests, requests)).astype(jnp.float32)

    def column(keep, values):
        return jnp.sum(jnp.where(keep, values, 0.0), axis=1, keepdims=True)

    starts = column(along < down_it, length)
    ends = column(along <= down_it, length)
    prefixes = column(along == down_it, prefix)
    number = lax.broadcasted_iota(jnp.int32, (requests, LANES), 0).astype(jnp.float32) + 1.0
    first = place_ref[0] * (PAIRS * ROWS) - ROWS
    for b in range(PAIRS + 2):
        ids = lax.broadcasted_iota(jnp.int32, (requests, LANES), 1) + (first + b * ROWS)
        ids = ids.astype(jnp.float32)
        member = (ids >= starts) & (ids < ends)
        request = jnp.sum(jnp.where(member, number, 0.0), axis=0, keepdims=True) - 1.0
        offset = ids[0:1] - jnp.sum(jnp.where(member, starts, 0.0), axis=0, keepdims=True)
        chosen = jnp.sum(jnp.where(member, prefixes, 0.0), axis=0, keepdims=True)
        facts = jnp.concatenate([request, offset, chosen] + [request] * 5, axis=0)
        name_ref[b] = jnp.broadcast_to(jnp.transpose(facts)[:, 0:1], (ROWS, LANES)).astype(jnp.bfloat16)
        if 0 < b < PAIRS + 1:
            step = b - 1
            asked_ref[step] = facts
            chosen_ref[step] = jnp.broadcast_to(chosen, (ROWS, LANES)).astype(jnp.bfloat16)
            at = jnp.minimum(ROWS - row + jnp.broadcast_to(offset, (ROWS, LANES)).astype(jnp.int32), LANES - 1)
            for h in range(2):
                tail_ref[step, :, h * ROWS : (h + 1) * ROWS] = jnp.take_along_axis(lines[h], at, axis=1)


def tables(place, rel_bias, lengths, prefix_map):
    return pl.pallas_call(
        tables_kernel,
        in_specs=[SMEM_SPEC, SMEM_SPEC, VMEM_SPEC, VMEM_SPEC],
        out_specs=(VMEM_SPEC,) * 5,
        out_shape=(
            pltpu.VMEM((3 * ROWS, 2 * ROWS), jnp.float32),
            pltpu.VMEM((PAIRS + 2, ROWS, LANES), jnp.bfloat16),
            pltpu.VMEM((PAIRS, 8, ROWS), jnp.float32),
            pltpu.VMEM((PAIRS, ROWS, 2 * ROWS), jnp.float32),
            pltpu.VMEM((PAIRS, ROWS, ROWS), jnp.bfloat16),
        ),
        compiler_params=pltpu.CompilerParams(vmem_limit_bytes=VMEM_LIMIT),
        cost_estimate=COST,
        name="tables",
    )(place, rel_bias.T, *on_chip(lengths, prefix_map))


def queries(got_ref, chosen_ref, step):
    query = jnp.transpose(got_ref[step, 0:ROWS])
    zero = jnp.zeros((DK, ROWS), jnp.bfloat16)
    stacked = jnp.concatenate(
        [jnp.concatenate([query[:DK], zero], axis=0), jnp.concatenate([zero, query[DK:]], axis=0)], axis=1
    )
    chosen = jnp.concatenate([chosen_ref[step], chosen_ref[step]], axis=1)
    return stacked, jnp.concatenate([stacked * (1 - chosen), stacked * chosen], axis=0)


def masked(scores, name_ref, block, asked_ref, step, bias):
    mine = name_ref[block].astype(jnp.float32) == asked_ref[step, 0:1]
    mine = jnp.concatenate([mine, mine], axis=1)
    return jnp.where(mine, scores + bias, masked_score)


def far_bias(place_ref, rel_ref):
    lane = lax.broadcasted_iota(jnp.int32, (1, 2 * ROWS), 1)
    head = place_ref[1] * 2
    return jnp.where(lane < ROWS, rel_ref[head, 15], rel_ref[head + 1, 15])


def own_head(values):
    return jnp.concatenate([values[:DK, :ROWS], values[DK:, ROWS:]], axis=0)


def by_feature(line):
    return jnp.concatenate(
        [jnp.broadcast_to(line[:, :ROWS], (DK, ROWS)), jnp.broadcast_to(line[:, ROWS:], (DK, ROWS))], axis=0
    )


def select(asked_ref, step, far_out):
    second = jnp.broadcast_to(asked_ref[step, 2:3], (LANES, ROWS)) > 0.5
    return jnp.where(second, own_head(far_out[LANES:]), own_head(far_out[:LANES]))


def quarter_of(rows_at, keys_ref, values_ref):
    for p in range(PREF_GRP):
        pieces = [
            jnp.concatenate(
                [rows_at(source, (kind * PREF_GRP + p) * SHARE) for source in range(PAIRS)], axis=0
            )
            for kind in range(2)
        ]
        keys_ref[:, p * LANES : (p + 1) * LANES] = pieces[0]
        values_ref[p * LANES : (p + 1) * LANES, :] = jnp.transpose(pieces[1])


def start_copies(pairs, landed):
    copies = [pltpu.make_async_copy(a, b, landed.at[i]) for i, (a, b) in enumerate(pairs)]
    for copy in copies:
        copy.start()
    return copies


def own_kernel(
    place_ref, rel_ref, got_ref, near_ref, name_ref, asked_ref, tail_ref, chosen_ref, w1_hbm, w2_hbm, w3_hbm,
    stat_ref, acc_ref, w1_ref, w2_ref, w3_ref, keys, values, kwin, vwin, landed,
):
    copies = start_copies(((w1_hbm, w1_ref), (w2_hbm, w2_ref), (w3_hbm, w3_ref)), landed)
    for b in (0, PAIRS + 1):
        kwin[b] = jnp.zeros((ROWS, LANES), jnp.bfloat16)
        vwin[b] = jnp.zeros((LANES, ROWS), jnp.bfloat16)
    for b in range(PAIRS):
        kwin[b + 1] = got_ref[b, ROWS : 2 * ROWS]
        vwin[b + 1] = jnp.transpose(got_ref[b, 2 * ROWS : 3 * ROWS])
    quarter_of(lambda s, at: got_ref[s, 3 * ROWS + at : 3 * ROWS + at + SHARE], keys, values)
    is_last = place_ref[0] == 3
    full = far_bias(place_ref, rel_ref)

    def one(step, _):
        stacked, split = queries(got_ref, chosen_ref, step)
        parts = [dot(keys[...], split) + jnp.where(is_last, tail_ref[step], full)]
        near_scores = dot(kwin[pl.ds(step, 3)].reshape(3 * ROWS, LANES), stacked)
        for b in range(3):
            at_edge = (step + b == 0) | (step + b == PAIRS + 1)
            cut = slice(b * ROWS, (b + 1) * ROWS)
            bias = near_ref[cut] + jnp.where(at_edge, masked_score, 0.0)
            parts.append(masked(near_scores[cut], name_ref, step + b, asked_ref, step, bias))
        top = jnp.max(functools.reduce(jnp.maximum, parts), axis=0, keepdims=True)
        terms = [jnp.exp(part - top) for part in parts]
        row_sum = jnp.sum(functools.reduce(jnp.add, terms), axis=0, keepdims=True)
        weights = [t.astype(jnp.bfloat16) for t in terms]
        near_values = jnp.concatenate([vwin[step + b] for b in range(3)], axis=1)
        near_out = dot(near_values, jnp.concatenate(weights[1:], axis=0))
        acc_ref[step] = select(asked_ref, step, dot(values[...], weights[0])) + own_head(near_out)
        stat_ref[step, 0:1] = top
        stat_ref[step, 1:2] = row_sum
        return 0

    lax.fori_loop(0, PAIRS, one, 0, unroll=4)
    for copy in copies:
        copy.wait()


def attend_own(place, rel_bias, got, made, later_weights):
    return pl.pallas_call(
        own_kernel,
        in_specs=[SMEM_SPEC] * 2 + [VMEM_SPEC] * 6 + [HBM_SPEC] * 3,
        out_specs=(VMEM_SPEC,) * 5,
        out_shape=(
            pltpu.VMEM((PAIRS, 8, 2 * ROWS), jnp.float32),
            pltpu.VMEM((PAIRS, LANES, ROWS), jnp.float32),
        )
        + tuple(pltpu.VMEM(w.shape, w.dtype) for w in later_weights),
        scratch_shapes=[
            pltpu.VMEM((PLEN // 4, PREF_GRP * LANES), jnp.bfloat16),
            pltpu.VMEM((PREF_GRP * LANES, PLEN // 4), jnp.bfloat16),
            pltpu.VMEM((PAIRS + 2, ROWS, LANES), jnp.bfloat16),
            pltpu.VMEM((PAIRS + 2, LANES, ROWS), jnp.bfloat16),
            pltpu.SemaphoreType.DMA((3,)),
        ],
        compiler_params=pltpu.CompilerParams(vmem_limit_bytes=VMEM_LIMIT),
        cost_estimate=COST,
        name="attend_own",
    )(place, rel_bias.T, *on_chip(got, *made), *off_chip(*later_weights))


def rest_kernel(
    place_ref, rel_ref, got_ref, prev_ref, next_ref, far_ref, near_ref, name_ref, asked_ref, tail_ref, chosen_ref,
    stat_ref, acc_ref, w1_hbm, w2_hbm, w3_hbm, out_ref, w1_ref, w2_ref, w3_ref, keys, values, kwin, vwin, landed,
):
    copies = start_copies(((w1_hbm, w1_ref), (w2_hbm, w2_ref), (w3_hbm, w3_ref)), landed)
    turns = ((3, prev_ref), (1, next_ref), (2, far_ref))
    for i, (_, ref) in enumerate(turns):
        quarter_of(
            lambda s, at, ref=ref: ref[s * 4 * SHARE + at : s * 4 * SHARE + at + SHARE], keys.at[i], values.at[i]
        )
    for i, ref in enumerate((prev_ref, next_ref)):
        kwin[i] = ref[QUARTER : QUARTER + ROWS]
        vwin[i] = jnp.transpose(ref[QUARTER + ROWS :])
    is_last = [lax.rem(place_ref[0] + turn, 4) == 3 for turn, _ in turns]
    side = place_ref[2]
    full = far_bias(place_ref, rel_ref)

    def one(step, edge=None):
        stacked, split = queries(got_ref, chosen_ref, step)
        tail = tail_ref[step]
        scores = dot(keys[...].reshape(3 * PLEN // 4, PREF_GRP * LANES), split)
        parts = [
            scores[i * ROWS : (i + 1) * ROWS] + jnp.where(is_last[i], tail, full) for i in range(3)
        ]
        if edge is not None:
            bias = near_ref[edge * 2 * ROWS : (edge * 2 + 1) * ROWS]
            parts.append(
                masked(dot(kwin[edge], stacked), name_ref, edge * (PAIRS + 1), asked_ref, step, bias)
            )
        before = stat_ref[step, 0:1]
        top = jnp.max(functools.reduce(jnp.maximum, parts), axis=0, keepdims=True)
        top = jnp.maximum(top, before)
        shrink = jnp.exp(before - top)
        terms = [jnp.exp(part - top) for part in parts]
        row_sum = jnp.sum(functools.reduce(jnp.add, terms), axis=0, keepdims=True)
        row_sum = row_sum + stat_ref[step, 1:2] * shrink
        weights = [t.astype(jnp.bfloat16) for t in terms]
        far_values = jnp.concatenate([values[i] for i in range(3)], axis=1)
        far_out = dot(far_values, jnp.concatenate(weights[:3], axis=0))
        acc = acc_ref[step] * by_feature(shrink) + select(asked_ref, step, far_out)
        if edge is not None:
            acc = acc + own_head(dot(vwin[edge], weights[3]))
        done = jnp.transpose(acc * by_feature(1.0 / row_sum)).astype(jnp.bfloat16)
        out_ref[side * PAIRS + step] = done
        out_ref[(1 - side) * PAIRS + jnp.bitwise_xor(step, 1)] = done

    def middle(step, _):
        one(step)
        return 0

    one(jnp.int32(0), 0)
    lax.fori_loop(1, PAIRS - 1, middle, 0, unroll=3)
    one(jnp.int32(PAIRS - 1), 1)
    for copy in copies:
        copy.wait()


def attend_rest(place, rel_bias, got, prev, after_it, far, made, part, later_weights):
    return pl.pallas_call(
        rest_kernel,
        in_specs=[SMEM_SPEC] * 2 + [VMEM_SPEC] * 11 + [HBM_SPEC] * 3,
        out_specs=(VMEM_SPEC,) * 4,
        out_shape=(pltpu.VMEM((2 * PAIRS, ROWS, LANES), jnp.bfloat16),)
        + tuple(pltpu.VMEM(w.shape, w.dtype) for w in later_weights),
        scratch_shapes=[
            pltpu.VMEM((3, PLEN // 4, PREF_GRP * LANES), jnp.bfloat16),
            pltpu.VMEM((3, PREF_GRP * LANES, PLEN // 4), jnp.bfloat16),
            pltpu.VMEM((2, ROWS, LANES), jnp.bfloat16),
            pltpu.VMEM((2, LANES, ROWS), jnp.bfloat16),
            pltpu.SemaphoreType.DMA((3,)),
        ],
        compiler_params=pltpu.CompilerParams(vmem_limit_bytes=VMEM_LIMIT),
        cost_estimate=COST,
        name="attend_rest",
    )(place, rel_bias.T, *on_chip(got, prev, after_it, far, *made, *part), *off_chip(*later_weights))


def finish_kernel(away, place_ref, att_ref, w_ref, tok_ref, gain_ref, in_one, in_two, out_one, out_two, *rest):
    at = (1 - place_ref[2] if away else place_ref[2]) * PAIRS
    attended = jnp.concatenate([att_ref[at + j] for j in range(PAIRS)], axis=1)
    hidden = (tok_ref[...].astype(jnp.float32) + dot(attended, w_ref[...])).astype(jnp.bfloat16)
    normed = norm_rows(hidden, gain_ref[...])
    got = None if away else hidden.astype(jnp.float32)
    for in_ref, out_w_ref in ((in_one, out_one), (in_two, out_two)):
        units = lax.dot_general(
            normed, in_ref[...], (((1,), (1,)), ((), ())), preferred_element_type=jnp.float32
        )
        part = dot(jnp.maximum(units, 0.0).astype(jnp.bfloat16), out_w_ref[...])
        got = part if got is None else got + part
    rest[-1][...] = got.astype(rest[-1].dtype)


def finish(away, place, att, w_attn_out, tokens, gain, weights, *ready):
    return pl.pallas_call(
        functools.partial(finish_kernel, away),
        in_specs=[SMEM_SPEC] + [VMEM_SPEC] * (8 + len(ready)),
        out_specs=VMEM_SPEC,
        out_shape=pltpu.VMEM((ROWS, D), jnp.bfloat16 if away else jnp.float32),
        compiler_params=pltpu.CompilerParams(vmem_limit_bytes=VMEM_LIMIT),
        cost_estimate=COST,
        name="finish",
    )(place, *on_chip(att, w_attn_out, tokens, gain.reshape(1, D), *weights, *ready))


def total_kernel(*refs):
    out_ref = refs[-1]
    total = functools.reduce(jnp.add, [ref[...].astype(jnp.float32) for ref in refs[:-1]])
    out_ref[...] = total.astype(out_ref.dtype)


def total(dtype, *arrays, last=False):
    return pl.pallas_call(
        total_kernel,
        in_specs=[VMEM_SPEC] * len(arrays),
        out_specs=VMEM_SPEC,
        out_shape=(jax.ShapeDtypeStruct if last else pltpu.VMEM)(arrays[0].shape, dtype),
        compiler_params=pltpu.CompilerParams(vmem_limit_bytes=VMEM_LIMIT),
        cost_estimate=COST,
        name="total",
    )(*on_chip(*arrays))


def body(
    tokens,
    attn_gain,
    w_query,
    w_key,
    w_value,
    w_attn_out,
    rel_bias,
    prefix_cache,
    lengths,
    prefix_map,
    mlp_gain,
    w_in,
    w_out,
):
    count_x = lax.axis_size("x")
    plane = lax.axis_index("z") * 2 + lax.axis_index("ylo")
    place = jnp.stack([lax.axis_index("x"), plane, lax.axis_index("yhi")]).astype(jnp.int32)
    made = tables(place, rel_bias, lengths, prefix_map)

    blocks = project(tokens, attn_gain, w_query, w_key, w_value, prefix_cache)
    got = lax.all_to_all(blocks, PLANE, 0, 0, tiled=True)
    mirrored = ("yhi", "ylo")
    far_tokens = lax.ppermute(tokens, mirrored, MIRROR)
    other_in = lax.ppermute(w_in, "core", SWAP)
    other_out = lax.ppermute(w_out, "core", SWAP)
    up, down, far = spread(got, far_tokens, *made)
    by = lambda d: [(i, (i + d) % count_x) for i in range(count_x)]
    prev = lax.ppermute(up, "x", by(1))
    later = lax.ppermute(down, "x", by(-1))
    opposite = lax.ppermute(far, "x", by(2))
    stat, acc, *own_weights = attend_own(place, rel_bias, got, made, (w_attn_out, w_in, w_out))
    mixed, *other_weights = attend_rest(
        place, rel_bias, got, prev, later, opposite, made, (stat, acc), (other_in, other_out, far_tokens)
    )
    w_attn_out = own_weights[0]
    weights = (own_weights[1], other_weights[0], own_weights[2], other_weights[1])
    att = lax.all_to_all(mixed, ("yhi",) + PLANE, 0, 0, tiled=True)

    far_sum = finish(True, place, att, w_attn_out, other_weights[2], mlp_gain, weights)
    back = lax.ppermute(far_sum, mirrored, MIRROR)
    local = finish(False, place, att, w_attn_out, tokens, mlp_gain, weights, far_sum)
    return total(jnp.bfloat16, local, back, last=True)


def solution(mesh):
    split = Mesh(mesh.devices.reshape(2, 2, 4, 4, 2), AXES)
    grp, req = ("yhi", "core"), REQ
    return jax.shard_map(
        body,
        mesh=split,
        in_specs=(
            P(grp + req, None),
            P(),
            P(),
            P(),
            P(),
            P(),
            P(),
            P(grp, req, None),
            P(grp, None),
            P(grp, None),
            P(),
            P(grp, None),
            P(grp, None),
        ),
        out_specs=P(grp + req, None),
        check_vma=False,
    )
```

time: 72.4 us -> 69.4 us (0.959)
  Pallas kernels: 27.6 us -> 22.2 us
  waiting for transfers between devices: 11 us -> 13.5 us
    pallas_call x5 -> x3, Pallas kernels: 7.82 us -> 6.26 us  [the longest x2 6.2 us: finish(): pl.pallas_call(functools.partial(finish_kernel, away), in_specs=[SMEM_SPE...]
    ppermute x1, waiting for transfers between devices: 0.3 us -> 1.55 us  [body(): opposite = lax.ppermute(far, 'x', by(2))]
    pallas_call x1, Pallas kernels: 4.99 us -> 3.75 us  [attend_own(): pl.pallas_call(own_kernel, in_specs=[SMEM_SPEC] * 2 + [VMEM_SPEC] * 6 + [...]
    pallas_call x1, Pallas kernels: 3.22 us -> 2.13 us  [tables(): pl.pallas_call(tables_kernel, in_specs=[SMEM_SPEC, SMEM_SPEC, VMEM_SPEC,...]
    ppermute x1, waiting for transfers between devices: 2.71 us -> 3.7 us  [body(): far_tokens = lax.ppermute(tokens, mirrored, MIRROR)]
    pallas_call x1, Pallas kernels: 5.57 us -> 4.62 us  [project(): pl.pallas_call(project_kernel, in_specs=[HBM_SPEC] * 6, out_specs=HBM_SPE...]
  transfers between devices with their start and end apart: 8 -> 8, of which waited for: 4 -> 4; matrix products, arithmetic and copies ran while one was open for 0% -> 0% of each run, Pallas kernels for 25% -> 20%
where the time goes in v7:
time: 69.4 us; the launch traced here: 69.2 us
  Pallas kernels  22.2 us (32%)
  starting transfers between devices  16.9 us (24%)
  blocking collectives  16.4 us (24%)
  waiting for transfers between devices  13.5 us (19%)
    all_to_all x1, blocking collectives, body(): att = lax.all_to_all(mixed, ('yhi',) + PLANE, 0, 0, tiled=True)  16.4 us
    all_to_all x1, starting transfers between devices, body(): got = lax.all_to_all(blocks, PLANE, 0, 0, tiled=True)  6.42 us
    pallas_call x2, Pallas kernels, finish(): pl.pallas_call(functools.partial(finish_kernel, away), in_specs=[SMEM_SPE...  6.2 us
    all_to_all x1, waiting for transfers between devices, body(): got = lax.all_to_all(blocks, PLANE, 0, 0, tiled=True)  5.09 us
    pallas_call x1, Pallas kernels, attend_rest(): pl.pallas_call(rest_kernel, in_specs=[SMEM_SPEC] * 2 + [VMEM_SPEC] * 11 +...  4.66 us
    pallas_call x1, Pallas kernels, project(): pl.pallas_call(project_kernel, in_specs=[HBM_SPEC] * 6, out_specs=HBM_SPE...  4.62 us
    pallas_call x1, Pallas kernels, attend_own(): pl.pallas_call(own_kernel, in_specs=[SMEM_SPEC] * 2 + [VMEM_SPEC] * 6 + [...  3.75 us
    ppermute x1, waiting for transfers between devices, body(): far_tokens = lax.ppermute(tokens, mirrored, MIRROR)  3.7 us
  transfers between devices with their start and end apart: 8, of which 4 were waited for; matrix products, arithmetic and copies ran while one was open for 0% of the time, Pallas kernels for 20%

profile of v7, /device:TPU:0, one launch (start us, length us, event | category | flops | bytes accessed | tf_op | source)
XLA Modules:
  0.0 69.2 jit_solution(7611702100614884957)
XLA Ops:
  0.0 0.0 collective-permute-start.4
  0.0 0.5 collective-permute-start.5
  0.5 0.0 copy-start
  0.5 0.0 copy-start.1
  0.5 0.0 copy-start.3
  0.5 0.0 copy-start.4
  0.5 4.6 %project.1 = bf16[8,448,128]{2,1,0:T(8,128)(2,1)} custom-call(bf16[128,1024]{1,0:T(8,128)(2,1)} %tok_ref.1, f32[1,1024]{1,0:T(1,128)} %bitcast.11, bf16[2,16,2048]{2,1,0:T(8,128)(2,1)} %cache_hbm.1, bf16[1024,1024]{1,0:T(8,128)(2,1)} %wq_hbm.1, bf16[1024,1024]{1,0:T(8,128)(2,1)} %wk_hbm.1, bf16[1024,1024]{1,0:T(8,128)(2,1)} %wv_hbm.1), custom_call_target="tpu_custom_call" | custom-call | flops 1000 | bytes 1000 | tf_op jit(solution)/shard_map/project/pallas_call | solution.py:110
  5.2 6.4 %all-to-all-start = ((bf16[8,448,128]{2,1,0:T(8,128)(2,1)}), bf16[8,448,128]{2,1,0:T(8,128)(2,1)S(1)}, u32[]{:S(2)}, u32[]{:S(2)}) async-start(bf16[8,448,128]{2,1,0:T(8,128)(2,1)} %project.1), calls=%async_computation | async-start | bytes 1835008 | tf_op jit(solution)/shard_map/all_to_all | solution.py:499
  11.6 0.0 copy-done
  11.6 3.5 %collective-permute-start = (bf16[128,1024]{1,0:T(8,128)(2,1)S(1)}, bf16[128,1024]{1,0:T(8,128)(2,1)S(1)}, u32[]{:S(2)}, u32[]{:S(2)}) collective-permute-start(bf16[128,1024]{1,0:T(8,128)(2,1)S(1)} %copy-done), channel_id=1, source_target_pairs={{0,65},{65,0},{1,64},{64,1},{2,67},{67,2},{3,66},{66,3},{4,69},{69... | collective-permute-start | bytes 786440 | tf_op jit(solution)/shard_map/ppermute | solution.py:501
  15.0 0.1 pad_add_fusion.place_ref
  15.1 0.0 copy-done.1
  15.1 0.0 copy-done.3
  15.1 0.0 copy-done.4
  15.1 2.1 %tables.1 = (f32[384,256]{1,0:T(8,128)S(1)}, bf16[10,128,128]{2,1,0:T(8,128)(2,1)S(1)}, f32[8,8,128]{2,1,0:T(8,128)S(1)}, f32[8,128,256]{2,1,0:T(8,128)S(1)}, bf16[8,128,128]{2,1,0:T(8,128)(2,1)S(1)}) custom-call(s32[3]{0:T(128)S(1)} %pad_add_fusion.place_ref, f32[16,32]{1,0:T(8,128)S(1)} %bitcast.6, s32[1,64]{1,0:T(1,128)S(1)} %copy-done.3, ...), custom_call_target="tpu_custom_call" | custom-call | flops 1000 | bytes 1000 | tf_op jit(solution)/shard_map/tables/pallas_call | solution.py:220
  17.3 3.7 %collective-permute-done.rest_5_.w3_hbm = bf16[128,1024]{1,0:T(8,128)(2,1)S(1)} collective-permute-done((bf16[128,1024]{1,0:T(8,128)(2,1)S(1)}, bf16[128,1024]{1,0:T(8,128)(2,1)S(1)}, u32[]{:S(2)}, u32[]{:S(2)}) %collective-permute-start) | collective-permute-done | bytes 262176 | tf_op jit(solution)/shard_map/ppermute | solution.py:501
  21.0 0.0 copy-start.5
  21.0 5.1 %all-to-all-done.got_ref = bf16[8,448,128]{2,1,0:T(8,128)(2,1)S(1)} async-done(((bf16[8,448,128]{2,1,0:T(8,128)(2,1)}), bf16[8,448,128]{2,1,0:T(8,128)(2,1)S(1)}, u32[]{:S(2)}, u32[]{:S(2)}) %all-to-all-start) | async-done | bytes 917536 | tf_op jit(solution)/shard_map/all_to_all | solution.py:499
  26.1 0.0 copy-done.5
  26.1 0.1 spread.1
  26.1 1.6 %collective-permute-start.1 = (bf16[768,128]{1,0:T(8,128)(2,1)S(1)}, bf16[768,128]{1,0:T(8,128)(2,1)S(1)}, u32[]{:S(2)}, u32[]{:S(2)}) collective-permute-start(bf16[768,128]{1,0:T(8,128)(2,1)S(1)} %get-tuple-element.27), channel_id=1, source_target_pairs={{0,8},{8,16},{16,24},{24,0},{1,9},{9,17},{17,25},{25,1},{2,10},{10... | collective-permute-start | bytes 589832 | tf_op jit(solution)/shard_map/ppermute | solution.py:506
  27.7 1.7 %collective-permute-start.2 = (bf16[768,128]{1,0:T(8,128)(2,1)S(1)}, bf16[768,128]{1,0:T(8,128)(2,1)S(1)}, u32[]{:S(2)}, u32[]{:S(2)}) collective-permute-start(bf16[768,128]{1,0:T(8,128)(2,1)S(1)} %get-tuple-element.28), channel_id=1, source_target_pairs={{0,24},{8,0},{16,8},{24,16},{1,25},{9,1},{17,9},{25,17},{2,26},{10... | collective-permute-start | bytes 589832 | tf_op jit(solution)/shard_map/ppermute | solution.py:507
  29.4 1.8 %collective-permute-start.3 = (bf16[512,128]{1,0:T(8,128)(2,1)S(1)}, bf16[512,128]{1,0:T(8,128)(2,1)S(1)}, u32[]{:S(2)}, u32[]{:S(2)}) collective-permute-start(bf16[512,128]{1,0:T(8,128)(2,1)S(1)} %get-tuple-element.29), channel_id=1, source_target_pairs={{0,16},{8,24},{16,0},{24,8},{1,17},{9,25},{17,1},{25,9},{2,18},{10... | collective-permute-start | bytes 393224 | tf_op jit(solution)/shard_map/ppermute | solution.py:508
  31.2 3.8 %attend_own.1 = (f32[8,8,256]{2,1,0:T(8,128)S(1)}, f32[8,128,128]{2,1,0:T(8,128)S(1)}, bf16[1024,1024]{1,0:T(8,128)(2,1)S(1)}, bf16[1024,1024]{1,0:T(8,128)(2,1)S(1)}, bf16[1024,1024]{1,0:T(8,128)(2,1)S(1)}) custom-call(s32[3]{0:T(128)S(1)} %pad_add_fusion.place_ref, f32[16,32]{1,0:T(8,128)S(1)} %bitcast.7, bf16[8,448,128]{2,1,0:T(8,128)(2,1)S(1)} %all-to-all-done.got_ref, ...), custom_call_target="tpu_custom_call" | custom-call | flops 1000 | bytes 1000 | tf_op jit(solution)/shard_map/attend_own/pallas_call | solution.py:334
  35.0 1.6 %collective-permute-done.3.far_ref = bf16[512,128]{1,0:T(8,128)(2,1)S(1)} collective-permute-done((bf16[512,128]{1,0:T(8,128)(2,1)S(1)}, bf16[512,128]{1,0:T(8,128)(2,1)S(1)}, u32[]{:S(2)}, u32[]{:S(2)}) %collective-permute-start.3) | collective-permute-done | bytes 131104 | tf_op jit(solution)/shard_map/ppermute | solution.py:508
  36.5 0.0 collective-permute-done.1.prev_ref
  36.5 0.0 collective-permute-done.2.next_ref
  36.5 0.0 collective-permute-done.4.w1_hbm
  36.6 0.0 collective-permute-done.5.w2_hbm
  36.6 0.0 copy-start.2
  36.6 4.7 %attend_rest.1 = (bf16[16,128,128]{2,1,0:T(8,128)(2,1)S(1)}, bf16[1024,1024]{1,0:T(8,128)(2,1)S(1)}, bf16[1024,1024]{1,0:T(8,128)(2,1)S(1)}, bf16[128,1024]{1,0:T(8,128)(2,1)S(1)}) custom-call(s32[3]{0:T(128)S(1)} %pad_add_fusion.place_ref, f32[16,32]{1,0:T(8,128)S(1)} %bitcast.8, bf16[8,448,128]{2,1,0:T(8,128)(2,1)S(1)} %all-to-all-done.got_ref, ...), custom_call_target="tpu_custom_call" | custom-call | flops 1000 | bytes 1000 | tf_op jit(solution)/shard_map/attend_rest/pallas_call | solution.py:414
  41.2 16.4 %all_to_all.10.att_ref = bf16[16,128,128]{2,1,0:T(8,128)(2,1)S(1)} all-to-all(bf16[16,128,128]{2,1,0:T(8,128)(2,1)S(1)} %get-tuple-element.32), channel_id=1, replica_groups=mesh['yhi'=2,'core'=2,'x'=4,'z'=4,'ylo'=2] {'yhi','z','ylo'}, dimensions={0} | all-to-all | bytes 1048576 | tf_op jit(solution)/shard_map/all_to_all | solution.py:515
  57.7 0.0 copy-done.2
  57.7 3.1 %finish.2.rest_0_ = bf16[128,1024]{1,0:T(8,128)(2,1)S(1)} custom-call(s32[3]{0:T(128)S(1)} %pad_add_fusion.place_ref, bf16[16,128,128]{2,1,0:T(8,128)(2,1)S(1)} %all_to_all.10.att_ref, bf16[1024,1024]{1,0:T(8,128)(2,1)S(1)} %get-tuple-element.33.w_ref, bf16[128,1024]{1,0:T(8,128)(2,1)S(1)} %get-tuple-element.38.tok_ref, f32[1,1024]{1,0:T(1,128)S(1)} %bitcast.9, ...), custom_call_target="tpu_custom_call" | custom-call | flops 1000 | bytes 1000 | tf_op jit(solution)/shard_map/finish/pallas_call | solution.py:449
  60.8 1.4 %collective-permute-start.6 = (bf16[128,1024]{1,0:T(8,128)(2,1)S(1)}, bf16[128,1024]{1,0:T(8,128)(2,1)S(1)}, u32[]{:S(2)}, u32[]{:S(2)}) collective-permute-start(bf16[128,1024]{1,0:T(8,128)(2,1)S(1)} %finish.2.rest_0_), channel_id=1, source_target_pairs={{0,65},{65,0},{1,64},{64,1},{2,67},{67,2},{3,66},{66,3},{4,69},{69... | collective-permute-start | bytes 786440 | tf_op jit(solution)/shard_map/ppermute | solution.py:518
  62.2 3.1 %finish.3.refs_0_ = f32[128,1024]{1,0:T(8,128)S(1)} custom-call(s32[3]{0:T(128)S(1)} %pad_add_fusion.place_ref, bf16[16,128,128]{2,1,0:T(8,128)(2,1)S(1)} %all_to_all.10.att_ref, bf16[1024,1024]{1,0:T(8,128)(2,1)S(1)} %get-tuple-element.33.w_ref, bf16[128,1024]{1,0:T(8,128)(2,1)S(1)} %copy-done, f32[1,1024]{1,0:T(1,128)S(1)} %bitcast.10, ...), custom_call_target="tpu_custom_call" | custom-call | flops 1000 | bytes 1000 | tf_op jit(solution)/shard_map/finish/pallas_call | solution.py:449
  65.3 3.1 %collective-permute-done.6.refs_1_ = bf16[128,1024]{1,0:T(8,128)(2,1)S(1)} collective-permute-done((bf16[128,1024]{1,0:T(8,128)(2,1)S(1)}, bf16[128,1024]{1,0:T(8,128)(2,1)S(1)}, u32[]{:S(2)}, u32[]{:S(2)}) %collective-permute-start.6) | collective-permute-done | bytes 262176 | tf_op jit(solution)/shard_map/ppermute | solution.py:518
  68.4 0.7 %total.1 = bf16[128,1024]{1,0:T(8,128)(2,1)} custom-call(f32[128,1024]{1,0:T(8,128)S(1)} %finish.3.refs_0_, bf16[128,1024]{1,0:T(8,128)(2,1)S(1)} %collective-permute-done.6.refs_1_), custom_call_target="tpu_custom_call" | custom-call | flops 1000 | bytes 1000 | tf_op jit(solution)/shard_map/total/pallas_call | solution.py:467
Async XLA Ops:
  0.0 36.6 %collective-permute-start.4 = (bf16[1024,1024]{1,0:T(8,128)(2,1)}, bf16[1024,1024]{1,0:T(8,128)(2,1)}, u32[]{:S(2)}, u32[]{:S(2)}) collective-permute-start(bf16[1024,1024]{1,0:T(8,128)(2,1)} %w2_hbm.1), channel_id=1, source_target_pairs={{0,32},{32,0},{1,33},{33,1},{2,34},{34,2},{3,35},{35,3},{4,36},{36... | collective-permute-start | bytes 6291464 | tf_op jit(solution)/shard_map/ppermute | solution.py:502
  0.0 36.6 %collective-permute-start.5 = (bf16[1024,1024]{1,0:T(8,128)(2,1)}, bf16[1024,1024]{1,0:T(8,128)(2,1)}, u32[]{:S(2)}, u32[]{:S(2)}) collective-permute-start(bf16[1024,1024]{1,0:T(8,128)(2,1)} %w3_hbm.1), channel_id=1, source_target_pairs={{0,32},{32,0},{1,33},{33,1},{2,34},{34,2},{3,35},{35,3},{4,36},{36... | collective-permute-start | bytes 6291464 | tf_op jit(solution)/shard_map/ppermute | solution.py:503
  0.5 11.1 %copy-start = (bf16[128,1024]{1,0:T(8,128)(2,1)S(1)}, bf16[128,1024]{1,0:T(8,128)(2,1)}, u32[]{:S(2)}) copy-start(bf16[128,1024]{1,0:T(8,128)(2,1)} %tok_ref.1) | copy-start | bytes 786436
  0.5 14.6 %copy-start.1 = (f32[32,16]{0,1:T(8,128)S(1)}, f32[32,16]{0,1:T(8,128)}, u32[]{:S(2)}) copy-start(f32[32,16]{0,1:T(8,128)} %param.19) | copy-start | bytes 6148
  0.5 14.6 %copy-start.3 = (s32[1,64]{1,0:T(1,128)S(1)}, s32[1,64]{1,0:T(1,128)}, u32[]{:S(2)}) copy-start(s32[1,64]{1,0:T(1,128)} %len_ref.1) | copy-start | bytes 772
  0.5 14.6 %copy-start.4 = (s32[1,64]{1,0:T(1,128)S(1)}, s32[1,64]{1,0:T(1,128)}, u32[]{:S(2)}) copy-start(s32[1,64]{1,0:T(1,128)} %map_ref.1) | copy-start | bytes 772
  5.2 20.9 %all-to-all-start = ((bf16[8,448,128]{2,1,0:T(8,128)(2,1)}), bf16[8,448,128]{2,1,0:T(8,128)(2,1)S(1)}, u32[]{:S(2)}, u32[]{:S(2)}) async-start(bf16[8,448,128]{2,1,0:T(8,128)(2,1)} %project.1), calls=%async_computation | async-start | bytes 1835008 | tf_op jit(solution)/shard_map/all_to_all | solution.py:499
  11.6 9.4 %collective-permute-start = (bf16[128,1024]{1,0:T(8,128)(2,1)S(1)}, bf16[128,1024]{1,0:T(8,128)(2,1)S(1)}, u32[]{:S(2)}, u32[]{:S(2)}) collective-permute-start(bf16[128,1024]{1,0:T(8,128)(2,1)S(1)} %copy-done), channel_id=1, source_target_pairs={{0,65},{65,0},{1,64},{64,1},{2,67},{67,2},{3,66},{66,3},{4,69},{69... | collective-permute-start | bytes 786440 | tf_op jit(solution)/shard_map/ppermute | solution.py:501
  21.0 5.1 %copy-start.5 = (bf16[128,1024]{1,0:T(8,128)(2,1)}, bf16[128,1024]{1,0:T(8,128)(2,1)S(1)}, u32[]{:S(2)}) copy-start(bf16[128,1024]{1,0:T(8,128)(2,1)S(1)} %collective-permute-done.rest_5_.w3_hbm) | copy-start | bytes 786436
  26.1 10.4 %collective-permute-start.1 = (bf16[768,128]{1,0:T(8,128)(2,1)S(1)}, bf16[768,128]{1,0:T(8,128)(2,1)S(1)}, u32[]{:S(2)}, u32[]{:S(2)}) collective-permute-start(bf16[768,128]{1,0:T(8,128)(2,1)S(1)} %get-tuple-element.27), channel_id=1, source_target_pairs={{0,8},{8,16},{16,24},{24,0},{1,9},{9,17},{17,25},{25,1},{2,10},{10... | collective-permute-start | bytes 589832 | tf_op jit(solution)/shard_map/ppermute | solution.py:506
  27.7 8.9 %collective-permute-start.2 = (bf16[768,128]{1,0:T(8,128)(2,1)S(1)}, bf16[768,128]{1,0:T(8,128)(2,1)S(1)}, u32[]{:S(2)}, u32[]{:S(2)}) collective-permute-start(bf16[768,128]{1,0:T(8,128)(2,1)S(1)} %get-tuple-element.28), channel_id=1, source_target_pairs={{0,24},{8,0},{16,8},{24,16},{1,25},{9,1},{17,9},{25,17},{2,26},{10... | collective-permute-start | bytes 589832 | tf_op jit(solution)/shard_map/ppermute | solution.py:507
  29.4 7.1 %collective-permute-start.3 = (bf16[512,128]{1,0:T(8,128)(2,1)S(1)}, bf16[512,128]{1,0:T(8,128)(2,1)S(1)}, u32[]{:S(2)}, u32[]{:S(2)}) collective-permute-start(bf16[512,128]{1,0:T(8,128)(2,1)S(1)} %get-tuple-element.29), channel_id=1, source_target_pairs={{0,16},{8,24},{16,0},{24,8},{1,17},{9,25},{17,1},{25,9},{2,18},{10... | collective-permute-start | bytes 393224 | tf_op jit(solution)/shard_map/ppermute | solution.py:508
  36.6 21.1 %copy-start.2 = (f32[1024]{0:T(1024)S(1)}, f32[1024]{0:T(1024)}, u32[]{:S(2)}) copy-start(f32[1024]{0:T(1024)} %param.23) | copy-start | bytes 12292
  60.8 7.7 %collective-permute-start.6 = (bf16[128,1024]{1,0:T(8,128)(2,1)S(1)}, bf16[128,1024]{1,0:T(8,128)(2,1)S(1)}, u32[]{:S(2)}, u32[]{:S(2)}) collective-permute-start(bf16[128,1024]{1,0:T(8,128)(2,1)S(1)} %finish.2.rest_0_), channel_id=1, source_target_pairs={{0,65},{65,0},{1,64},{64,1},{2,67},{67,2},{3,66},{66,3},{4,69},{69... | collective-permute-start | bytes 786440 | tf_op jit(solution)/shard_map/ppermute | solution.py:518

commit v8 on v7

--- a/solution.py
+++ b/solution.py
@@ -15,7 +15,6 @@
 ROWS = 128
 PAIRS = 8
 LANES = 128
-CHUNK = 1024
 SHARE = 16
 SENT = 3 * ROWS + 2 * PREF_GRP * SHARE
 QUARTER = PAIRS * 2 * PREF_GRP * SHARE
@@ -56,113 +55,20 @@
 SMEM_SPEC = pl.BlockSpec(memory_space=pltpu.SMEM)
 
 
-def project_kernel(
-    tok_hbm, gain_hbm, cache_hbm, wq_hbm, wk_hbm, wv_hbm, out_hbm, tok, gain, cache, held, out_ref, arrived, landed, left
-):
-    chunks = [slice(c * CHUNK, (c + 1) * CHUNK) for c in range(D // CHUNK)]
-    first = [
-        pltpu.make_async_copy(source, target, landed.at[i])
-        for i, (source, target) in enumerate(((tok_hbm, tok), (gain_hbm, gain), (cache_hbm, cache)))
-    ]
-    copies = [
-        [
-            pltpu.make_async_copy(w_hbm.at[cut], held.at[kind, cut], arrived.at[kind, c])
-            for c, cut in enumerate(chunks)
-        ]
-        for kind, w_hbm in enumerate((wq_hbm, wk_hbm, wv_hbm))
-    ]
-    for copy in first:
-        copy.start()
-    for row in copies:
-        for copy in row:
-            copy.start()
-    for copy in first:
-        copy.wait()
-    normed = norm_rows(tok[...], gain[...])
-    for part in range(PAIRS):
-        for kind in range(2):
-            for p in range(PREF_GRP):
-                at = 3 * ROWS + (kind * PREF_GRP + p) * SHARE
-                cut = slice(kind * D + part * LANES, kind * D + (part + 1) * LANES)
-                out_ref[part, at : at + SHARE] = cache[p, :, cut]
-    def send(at, i):
-        copy = pltpu.make_async_copy(out_ref.at[:, at], out_hbm.at[:, at], left.at[i])
-        copy.start()
-        return copy
-
-    sends = [send(slice(3 * ROWS, SENT), 3)]
-    for kind, row in enumerate(copies):
-        got = None
-        for cut, copy in zip(chunks, row):
-            copy.wait()
-            part = dot(normed[:, cut], held[kind, cut])
-            got = part if got is None else got + part
-        got = got.astype(jnp.bfloat16)
-        for to in range(PAIRS):
-            out_ref[to, kind * ROWS : (kind + 1) * ROWS] = got[:, to * LANES : (to + 1) * LANES]
-        sends.append(send(slice(kind * ROWS, (kind + 1) * ROWS), kind))
-    for copy in sends:
-        copy.wait()
-
-
-def project(tokens, gain, w_query, w_key, w_value, prefix_cache):
-    operands = (tokens, gain.reshape(1, D), prefix_cache, w_query, w_key, w_value)
-    return pl.pallas_call(
-        project_kernel,
-        in_specs=[HBM_SPEC] * 6,
-        out_specs=HBM_SPEC,
-        out_shape=pltpu.HBM((PAIRS, SENT, LANES), jnp.bfloat16),
-        scratch_shapes=[
-            pltpu.VMEM((ROWS, D), jnp.bfloat16),
-            pltpu.VMEM((1, D), jnp.float32),
-            pltpu.VMEM(prefix_cache.shape, jnp.bfloat16),
-            pltpu.VMEM((3, D, D), jnp.bfloat16),
-            pltpu.VMEM((PAIRS, SENT, LANES), jnp.bfloat16),
-            pltpu.SemaphoreType.DMA((3, D // CHUNK)),
-            pltpu.SemaphoreType.DMA((3,)),
-            pltpu.SemaphoreType.DMA((4,)),
-        ],
-        compiler_params=pltpu.CompilerParams(vmem_limit_bytes=VMEM_LIMIT),
-        cost_estimate=COST,
-        name="project",
-    )(*off_chip(*operands))
-
-
-def spread_kernel(got_ref, *rest):
-    up_ref, down_ref, far_ref = rest[-3:]
-    for source in range(PAIRS):
-        rows = slice(source * 4 * SHARE, (source + 1) * 4 * SHARE)
-        held = got_ref[source, 3 * ROWS :]
-        up_ref[rows] = held
-        down_ref[rows] = held
-        far_ref[rows] = held
-    up_ref[QUARTER:] = got_ref[PAIRS - 1, ROWS : 3 * ROWS]
-    down_ref[QUARTER:] = got_ref[0, ROWS : 3 * ROWS]
-
-
-def spread(got, arrived, *ready):
-    shape = pltpu.VMEM((QUARTER + 2 * ROWS, LANES), jnp.bfloat16)
-    return pl.pallas_call(
-        spread_kernel,
-        in_specs=[VMEM_SPEC] * (1 + len(ready)) + [HBM_SPEC],
-        out_specs=(VMEM_SPEC,) * 3,
-        out_shape=(shape, shape, pltpu.VMEM((QUARTER, LANES), jnp.bfloat16)),
-        compiler_params=pltpu.CompilerParams(vmem_limit_bytes=VMEM_LIMIT),
-        cost_estimate=COST,
-        name="spread",
-    )(*on_chip(got, *ready), *off_chip(arrived))
-
-
 def bias_line(rel_ref, head, first_bucket):
-    lane = lax.broadcasted_iota(jnp.int32, (ROWS, LANES), 1)
-    line = jnp.full((ROWS, LANES), rel_ref[head, first_bucket], jnp.float32)
+    lane = lax.broadcasted_iota(jnp.int32, (8, LANES), 1)
+
+    def of(bucket):
+        return rel_ref[pl.ds(head, 1), first_bucket + bucket : first_bucket + bucket + 1]
+
+    line = jnp.broadcast_to(of(0), (8, LANES))
     for bucket in range(1, 16):
         mark = bucket if bucket <= 8 else far_marks[bucket - 9]
-        line = jnp.where(lane >= mark, rel_ref[head, first_bucket + bucket], line)
-    return line
-
-
-def tables_kernel(
+        line = jnp.where(lane >= mark, of(bucket), line)
+    return jnp.broadcast_to(line[0:1], (ROWS, LANES))
+
+
+def write_tables(
     place_ref, rel_ref, len_ref, map_ref, near_ref, name_ref, asked_ref, tail_ref, chosen_ref
 ):
     row = lax.broadcasted_iota(jnp.int32, (ROWS, LANES), 0)
@@ -216,22 +122,103 @@
                 tail_ref[step, :, h * ROWS : (h + 1) * ROWS] = jnp.take_along_axis(lines[h], at, axis=1)
 
 
-def tables(place, rel_bias, lengths, prefix_map):
+def project_kernel(
+    x_ref, pair_ref, side_ref, tok_hbm, gain_hbm, cache_hbm, rel_hbm, len_hbm, map_hbm, wq_hbm, wk_hbm, wv_hbm,
+    out_ref, near_ref, name_ref, asked_ref, tail_ref, chosen_ref,
+    tok, gain, cache, rel, lengths, prefix_map, held, arrived, landed,
+):
+    place_ref = (x_ref[0], pair_ref[0], side_ref[0])
+    first = [
+        pltpu.make_async_copy(source, target, landed.at[i])
+        for i, (source, target) in enumerate(
+            (
+                (tok_hbm, tok), (gain_hbm, gain), (cache_hbm, cache),
+                (rel_hbm, rel), (len_hbm, lengths), (map_hbm, prefix_map),
+            )
+        )
+    ]
+    copies = [
+        pltpu.make_async_copy(w_hbm, held.at[kind], arrived.at[kind])
+        for kind, w_hbm in enumerate((wq_hbm, wk_hbm, wv_hbm))
+    ]
+    for copy in first + copies:
+        copy.start()
+    for copy in first:
+        copy.wait()
+    normed = norm_rows(tok[...], gain[...])
+    for part in range(PAIRS):
+        for kind in range(2):
+            for p in range(PREF_GRP):
+                at = 3 * ROWS + (kind * PREF_GRP + p) * SHARE
+                cut = slice(kind * D + part * LANES, kind * D + (part + 1) * LANES)
+                out_ref[part, at : at + SHARE] = cache[p, :, cut]
+    write_tables(
+        place_ref, rel, lengths, prefix_map, near_ref, name_ref, asked_ref, tail_ref, chosen_ref
+    )
+    for kind, copy in enumerate(copies):
+        copy.wait()
+        got = dot(normed, held[kind]).astype(jnp.bfloat16)
+        for to in range(PAIRS):
+            out_ref[to, kind * ROWS : (kind + 1) * ROWS] = got[:, to * LANES : (to + 1) * LANES]
+
+
+def project(place, tokens, gain, prefix_cache, rel_bias, lengths, prefix_map, w_query, w_key, w_value):
+    small = (tokens, gain.reshape(1, D), prefix_cache, rel_bias.T, lengths, prefix_map)
+    out_shape = (
+        pltpu.VMEM((PAIRS, SENT, LANES), jnp.bfloat16),
+        pltpu.VMEM((3 * ROWS, 2 * ROWS), jnp.float32),
+        pltpu.VMEM((PAIRS + 2, ROWS, LANES), jnp.bfloat16),
+        pltpu.VMEM((PAIRS, 8, ROWS), jnp.float32),
+        pltpu.VMEM((PAIRS, ROWS, 2 * ROWS), jnp.float32),
+        pltpu.VMEM((PAIRS, ROWS, ROWS), jnp.bfloat16),
+    )
+    blocks, *made = pl.pallas_call(
+        project_kernel,
+        in_specs=[SMEM_SPEC] * 3 + [HBM_SPEC] * 9,
+        out_specs=(VMEM_SPEC,) * 6,
+        out_shape=out_shape,
+        scratch_shapes=[pltpu.VMEM(value.shape, value.dtype) for value in small]
+        + [
+            pltpu.VMEM((3, D, D), jnp.bfloat16),
+            pltpu.SemaphoreType.DMA((3,)),
+            pltpu.SemaphoreType.DMA((6,)),
+        ],
+        compiler_params=pltpu.CompilerParams(vmem_limit_bytes=VMEM_LIMIT),
+        cost_estimate=COST,
+        name="project",
+    )(*place, *off_chip(*small, w_query, w_key, w_value))
+    return blocks, made
+
+
+def spread_kernel(got_ref, tok_ref, *rest):
+    up_ref, down_ref, far_ref, same_ref = rest[-4:]
+    for source in range(PAIRS):
+        rows = slice(source * 4 * SHARE, (source + 1) * 4 * SHARE)
+        held = got_ref[source, 3 * ROWS :]
+        up_ref[rows] = held
+        down_ref[rows] = held
+        far_ref[rows] = held
+    up_ref[QUARTER:] = got_ref[PAIRS - 1, ROWS : 3 * ROWS]
+    down_ref[QUARTER:] = got_ref[0, ROWS : 3 * ROWS]
+    same_ref[...] = tok_ref[...]
+
+
+def spread(got, tokens, on, off):
+    shape = pltpu.VMEM((QUARTER + 2 * ROWS, LANES), jnp.bfloat16)
     return pl.pallas_call(
-        tables_kernel,
-        in_specs=[SMEM_SPEC, SMEM_SPEC, VMEM_SPEC, VMEM_SPEC],
-        out_specs=(VMEM_SPEC,) * 5,
+        spread_kernel,
+        in_specs=[VMEM_SPEC] * 3 + [HBM_SPEC],
+        out_specs=(VMEM_SPEC,) * 4,
         out_shape=(
-            pltpu.VMEM((3 * ROWS, 2 * ROWS), jnp.float32),
-            pltpu.VMEM((PAIRS + 2, ROWS, LANES), jnp.bfloat16),
-            pltpu.VMEM((PAIRS, 8, ROWS), jnp.float32),
-            pltpu.VMEM((PAIRS, ROWS, 2 * ROWS), jnp.float32),
-            pltpu.VMEM((PAIRS, ROWS, ROWS), jnp.bfloat16),
+            shape,
+            shape,
+            pltpu.VMEM((QUARTER, LANES), jnp.bfloat16),
+            pltpu.VMEM((ROWS, D), jnp.bfloat16),
         ),
         compiler_params=pltpu.CompilerParams(vmem_limit_bytes=VMEM_LIMIT),
         cost_estimate=COST,
-        name="tables",
-    )(place, rel_bias.T, *on_chip(lengths, prefix_map))
+        name="spread",
+    )(*on_chip(got, tokens, on), *off_chip(off))
 
 
 def queries(got_ref, chosen_ref, step):
@@ -291,10 +278,11 @@
 
 
 def own_kernel(
-    place_ref, rel_ref, got_ref, near_ref, name_ref, asked_ref, tail_ref, chosen_ref, w1_hbm, w2_hbm, w3_hbm,
-    stat_ref, acc_ref, w1_ref, w2_ref, w3_ref, keys, values, kwin, vwin, landed,
+    x_ref, pair_ref, side_ref, rel_ref, got_ref, near_ref, name_ref, asked_ref, tail_ref, chosen_ref, w1_hbm,
+    stat_ref, acc_ref, w1_ref, keys, values, kwin, vwin, landed,
 ):
-    copies = start_copies(((w1_hbm, w1_ref), (w2_hbm, w2_ref), (w3_hbm, w3_ref)), landed)
+    place_ref = (x_ref[0], pair_ref[0], side_ref[0])
+    copies = start_copies(((w1_hbm, w1_ref),), landed)
     for b in (0, PAIRS + 1):
         kwin[b] = jnp.zeros((ROWS, LANES), jnp.bfloat16)
         vwin[b] = jnp.zeros((LANES, ROWS), jnp.bfloat16)
@@ -333,8 +321,8 @@
 def attend_own(place, rel_bias, got, made, later_weights):
     return pl.pallas_call(
         own_kernel,
-        in_specs=[SMEM_SPEC] * 2 + [VMEM_SPEC] * 6 + [HBM_SPEC] * 3,
-        out_specs=(VMEM_SPEC,) * 5,
+        in_specs=[SMEM_SPEC] * 4 + [VMEM_SPEC] * 6 + [HBM_SPEC],
+        out_specs=(VMEM_SPEC,) * 3,
         out_shape=(
             pltpu.VMEM((PAIRS, 8, 2 * ROWS), jnp.float32),
             pltpu.VMEM((PAIRS, LANES, ROWS), jnp.float32),
@@ -345,19 +333,19 @@
             pltpu.VMEM((PREF_GRP * LANES, PLEN // 4), jnp.bfloat16),
             pltpu.VMEM((PAIRS + 2, ROWS, LANES), jnp.bfloat16),
             pltpu.VMEM((PAIRS + 2, LANES, ROWS), jnp.bfloat16),
-            pltpu.SemaphoreType.DMA((3,)),
+            pltpu.SemaphoreType.DMA((1,)),
         ],
         compiler_params=pltpu.CompilerParams(vmem_limit_bytes=VMEM_LIMIT),
         cost_estimate=COST,
         name="attend_own",
-    )(place, rel_bias.T, *on_chip(got, *made), *off_chip(*later_weights))
+    )(*place, rel_bias.T, *on_chip(got, *made), *off_chip(*later_weights))
 
 
 def rest_kernel(
-    place_ref, rel_ref, got_ref, prev_ref, next_ref, far_ref, near_ref, name_ref, asked_ref, tail_ref, chosen_ref,
-    stat_ref, acc_ref, w1_hbm, w2_hbm, w3_hbm, out_ref, w1_ref, w2_ref, w3_ref, keys, values, kwin, vwin, landed,
+    x_ref, pair_ref, side_ref, rel_ref, got_ref, prev_ref, next_ref, far_ref, near_ref, name_ref, asked_ref, tail_ref, chosen_ref,
+    stat_ref, acc_ref, _, out_ref, keys, values, kwin, vwin,
 ):
-    copies = start_copies(((w1_hbm, w1_ref), (w2_hbm, w2_ref), (w3_hbm, w3_ref)), landed)
+    place_ref = (x_ref[0], pair_ref[0], side_ref[0])
     turns = ((3, prev_ref), (1, next_ref), (2, far_ref))
     for i, (_, ref) in enumerate(turns):
         quarter_of(
@@ -406,32 +394,28 @@
     one(jnp.int32(0), 0)
     lax.fori_loop(1, PAIRS - 1, middle, 0, unroll=3)
     one(jnp.int32(PAIRS - 1), 1)
-    for copy in copies:
-        copy.wait()
-
-
-def attend_rest(place, rel_bias, got, prev, after_it, far, made, part, later_weights):
+
+
+def attend_rest(place, rel_bias, got, prev, after_it, far, made, part, ready):
     return pl.pallas_call(
         rest_kernel,
-        in_specs=[SMEM_SPEC] * 2 + [VMEM_SPEC] * 11 + [HBM_SPEC] * 3,
-        out_specs=(VMEM_SPEC,) * 4,
-        out_shape=(pltpu.VMEM((2 * PAIRS, ROWS, LANES), jnp.bfloat16),)
-        + tuple(pltpu.VMEM(w.shape, w.dtype) for w in later_weights),
+        in_specs=[SMEM_SPEC] * 4 + [VMEM_SPEC] * 12,
+        out_specs=VMEM_SPEC,
+        out_shape=pltpu.VMEM((2 * PAIRS, ROWS, LANES), jnp.bfloat16),
         scratch_shapes=[
             pltpu.VMEM((3, PLEN // 4, PREF_GRP * LANES), jnp.bfloat16),
             pltpu.VMEM((3, PREF_GRP * LANES, PLEN // 4), jnp.bfloat16),
             pltpu.VMEM((2, ROWS, LANES), jnp.bfloat16),
             pltpu.VMEM((2, LANES, ROWS), jnp.bfloat16),
-            pltpu.SemaphoreType.DMA((3,)),
         ],
         compiler_params=pltpu.CompilerParams(vmem_limit_bytes=VMEM_LIMIT),
         cost_estimate=COST,
         name="attend_rest",
-    )(place, rel_bias.T, *on_chip(got, prev, after_it, far, *made, *part), *off_chip(*later_weights))
-
-
-def finish_kernel(away, place_ref, att_ref, w_ref, tok_ref, gain_ref, in_one, in_two, out_one, out_two, *rest):
-    at = (1 - place_ref[2] if away else place_ref[2]) * PAIRS
+    )(*place, rel_bias.T, *on_chip(got, prev, after_it, far, *made, *part, ready))
+
+
+def finish_kernel(away, side_ref, att_ref, w_ref, tok_ref, gain_ref, in_one, in_two, out_one, out_two, *rest):
+    at = (1 - side_ref[0] if away else side_ref[0]) * PAIRS
     attended = jnp.concatenate([att_ref[at + j] for j in range(PAIRS)], axis=1)
     hidden = (tok_ref[...].astype(jnp.float32) + dot(attended, w_ref[...])).astype(jnp.bfloat16)
     normed = norm_rows(hidden, gain_ref[...])
@@ -445,7 +429,7 @@
     rest[-1][...] = got.astype(rest[-1].dtype)
 
 
-def finish(away, place, att, w_attn_out, tokens, gain, weights, *ready):
+def finish(away, side, att, w_attn_out, tokens, gain, weights, *ready):
     return pl.pallas_call(
         functools.partial(finish_kernel, away),
         in_specs=[SMEM_SPEC] + [VMEM_SPEC] * (8 + len(ready)),
@@ -454,7 +438,7 @@
         compiler_params=pltpu.CompilerParams(vmem_limit_bytes=VMEM_LIMIT),
         cost_estimate=COST,
         name="finish",
-    )(place, *on_chip(att, w_attn_out, tokens, gain.reshape(1, D), *weights, *ready))
+    )(side, *on_chip(att, w_attn_out, tokens, gain.reshape(1, D), *weights, *ready))
 
 
 def total_kernel(*refs):
@@ -492,31 +476,30 @@
 ):
     count_x = lax.axis_size("x")
     plane = lax.axis_index("z") * 2 + lax.axis_index("ylo")
-    place = jnp.stack([lax.axis_index("x"), plane, lax.axis_index("yhi")]).astype(jnp.int32)
-    made = tables(place, rel_bias, lengths, prefix_map)
-
-    blocks = project(tokens, attn_gain, w_query, w_key, w_value, prefix_cache)
+    place = tuple(
+        at.astype(jnp.int32).reshape(1) for at in (lax.axis_index("x"), plane, lax.axis_index("yhi"))
+    )
+    other_in = lax.ppermute(w_in, "core", SWAP)
+    other_out = lax.ppermute(w_out, "core", SWAP)
+    blocks, made = project(
+        place, tokens, attn_gain, prefix_cache, rel_bias, lengths, prefix_map, w_query, w_key, w_value
+    )
     got = lax.all_to_all(blocks, PLANE, 0, 0, tiled=True)
     mirrored = ("yhi", "ylo")
-    far_tokens = lax.ppermute(tokens, mirrored, MIRROR)
-    other_in = lax.ppermute(w_in, "core", SWAP)
-    other_out = lax.ppermute(w_out, "core", SWAP)
-    up, down, far = spread(got, far_tokens, *made)
+    up, down, far, same = spread(got, tokens, other_in, other_out)
     by = lambda d: [(i, (i + d) % count_x) for i in range(count_x)]
+    opposite = lax.ppermute(far, "x", by(2))
     prev = lax.ppermute(up, "x", by(1))
     later = lax.ppermute(down, "x", by(-1))
-    opposite = lax.ppermute(far, "x", by(2))
-    stat, acc, *own_weights = attend_own(place, rel_bias, got, made, (w_attn_out, w_in, w_out))
-    mixed, *other_weights = attend_rest(
-        place, rel_bias, got, prev, later, opposite, made, (stat, acc), (other_in, other_out, far_tokens)
-    )
-    w_attn_out = own_weights[0]
-    weights = (own_weights[1], other_weights[0], own_weights[2], other_weights[1])
+    far_tokens = lax.ppermute(same, mirrored, MIRROR)
+    stat, acc, other_out = attend_own(place, rel_bias, got, made, (other_out,))
+    mixed = attend_rest(place, rel_bias, got, prev, later, opposite, made, (stat, acc), far_tokens)
+    weights = (w_in, other_in, w_out, other_out)
     att = lax.all_to_all(mixed, ("yhi",) + PLANE, 0, 0, tiled=True)
 
-    far_sum = finish(True, place, att, w_attn_out, other_weights[2], mlp_gain, weights)
+    far_sum = finish(True, place[2], att, w_attn_out, far_tokens, mlp_gain, weights)
     back = lax.ppermute(far_sum, mirrored, MIRROR)
-    local = finish(False, place, att, w_attn_out, tokens, mlp_gain, weights, far_sum)
+    local = finish(False, place[2], att, w_attn_out, tokens, mlp_gain, weights, far_sum)
     return total(jnp.bfloat16, local, back, last=True)
 
 

time: 69.4 us -> 68.4 us (0.986)
  blocking collectives: 16.4 us -> 33.5 us
  waiting for transfers between devices: 13.5 us -> 5.66 us
  starting transfers between devices: 16.9 us -> 9.18 us
  Pallas kernels: 22.2 us -> 19.7 us
    all_to_all x0 -> x1, blocking collectives: none -> 20.8 us  [body(): got = lax.all_to_all(blocks, PLANE, 0, 0, tiled=True)]
    all_to_all x1 -> x0, starting transfers between devices: 6.42 us -> none  [body(): got = lax.all_to_all(blocks, PLANE, 0, 0, tiled=True)]
    all_to_all x1 -> x0, waiting for transfers between devices: 5.09 us -> none  [body(): got = lax.all_to_all(blocks, PLANE, 0, 0, tiled=True)]
    ppermute x1, waiting for transfers between devices: 3.7 us -> 0.01 us  [body(): far_tokens = lax.ppermute(same, mirrored, MIRROR)]
    all_to_all x1, blocking collectives: 16.4 us -> 12.8 us  [body(): att = lax.all_to_all(mixed, ('yhi',) + PLANE, 0, 0, tiled=True)]
    pallas_call x5 -> x4, Pallas kernels: 15.2 us -> 13.8 us  [the longest x1 5.41 us: project(): pl.pallas_call(project_kernel, in_specs=[SMEM_SPEC] * 3 + [HBM_SPEC] * 9,...]
    ppermute x1, starting transfers between devices: 3.46 us -> 2.27 us  [body(): far_tokens = lax.ppermute(same, mirrored, MIRROR)]
    pallas_call x2, Pallas kernels: 6.2 us -> 5.14 us  [finish(): pl.pallas_call(functools.partial(finish_kernel, away), in_specs=[SMEM_SPE...]
  transfers between devices with their start and end apart: 8 -> 7, of which waited for: 4 -> 2; matrix products, arithmetic and copies ran while one was open for 0% -> 0% of each run, Pallas kernels for 20% -> 17%
where the time goes in v8:
time: 68.4 us; the launch traced here: 68.2 us
  blocking collectives  33.5 us (49%)
  Pallas kernels  19.7 us (29%)
  starting transfers between devices  9.18 us (13%)
  waiting for transfers between devices  5.66 us (8%)
    all_to_all x1, blocking collectives, body(): got = lax.all_to_all(blocks, PLANE, 0, 0, tiled=True)  20.8 us
    all_to_all x1, blocking collectives, body(): att = lax.all_to_all(mixed, ('yhi',) + PLANE, 0, 0, tiled=True)  12.8 us
    pallas_call x1, Pallas kernels, project(): pl.pallas_call(project_kernel, in_specs=[SMEM_SPEC] * 3 + [HBM_SPEC] * 9,...  5.41 us
    pallas_call x2, Pallas kernels, finish(): pl.pallas_call(functools.partial(finish_kernel, away), in_specs=[SMEM_SPE...  5.14 us
    pallas_call x1, Pallas kernels, attend_rest(): pl.pallas_call(rest_kernel, in_specs=[SMEM_SPEC] * 4 + [VMEM_SPEC] * 12,...  4.61 us
    pallas_call x1, Pallas kernels, attend_own(): pl.pallas_call(own_kernel, in_specs=[SMEM_SPEC] * 4 + [VMEM_SPEC] * 6 + [...  3.72 us
    ppermute x1, waiting for transfers between devices, body(): back = lax.ppermute(far_sum, mirrored, MIRROR)  3.7 us
    ppermute x1, starting transfers between devices, body(): far_tokens = lax.ppermute(same, mirrored, MIRROR)  2.27 us
  transfers between devices with their start and end apart: 7, of which 2 were waited for; matrix products, arithmetic and copies ran while one was open for 0% of the time, Pallas kernels for 17%

profile of v8, /device:TPU:0, one launch (start us, length us, event | category | flops | bytes accessed | tf_op | source)
XLA Modules:
  0.0 68.2 jit_solution(12481734495952957321)
XLA Ops:
  0.0 0.0 collective-permute-start
  0.0 0.5 collective-permute-start.1
  0.5 0.0 copy-start.3
  0.5 5.4 %project.1 = (bf16[8,448,128]{2,1,0:T(8,128)(2,1)S(1)}, f32[384,256]{1,0:T(8,128)S(1)}, bf16[10,128,128]{2,1,0:T(8,128)(2,1)S(1)}, f32[8,8,128]{2,1,0:T(8,128)S(...) custom-call(s32[1]{0:T(128)} %bitcast.1.x_ref, s32[1]{0:T(128)} %bitcast.2.pair_ref, s32[1]{0:T(128)} %bitcast.side_ref, ...), custom_call_target="tpu_custom_call" | custom-call | flops 1000 | bytes 1000 | tf_op jit(solution)/shard_map/project/pallas_call | solution.py:175
  5.9 20.8 %all_to_all.10.got_ref = bf16[8,448,128]{2,1,0:T(8,128)(2,1)S(1)} all-to-all(bf16[8,448,128]{2,1,0:T(8,128)(2,1)S(1)} %get-tuple-element.18), channel_id=1, replica_groups=mesh['yhi'=2,'core'=2,'x'=4,'z'=4,'ylo'=2] {'z','ylo'}, dimensions={0} | all-to-all | bytes 1835008 | tf_op jit(solution)/shard_map/all_to_all | solution.py:487
  26.7 0.0 copy-start.4
  26.7 0.0 collective-permute-done.rest_0_.in_two
  26.7 0.0 collective-permute-done.1.rest_1_.w1_hbm
  26.7 0.0 copy-done.3
  26.7 0.1 spread.1
  26.8 2.3 %collective-permute-start.5 = (bf16[128,1024]{1,0:T(8,128)(2,1)S(1)}, bf16[128,1024]{1,0:T(8,128)(2,1)S(1)}, u32[]{:S(2)}, u32[]{:S(2)}) collective-permute-start(bf16[128,1024]{1,0:T(8,128)(2,1)S(1)} %get-tuple-element.29), channel_id=1, source_target_pairs={{0,65},{65,0},{1,64},{64,1},{2,67},{67,2},{3,66},{66,3},{4,69},{69... | collective-permute-start | bytes 786440 | tf_op jit(solution)/shard_map/ppermute | solution.py:494
  29.1 1.5 %collective-permute-start.2 = (bf16[768,128]{1,0:T(8,128)(2,1)S(1)}, bf16[768,128]{1,0:T(8,128)(2,1)S(1)}, u32[]{:S(2)}, u32[]{:S(2)}) collective-permute-start(bf16[768,128]{1,0:T(8,128)(2,1)S(1)} %get-tuple-element.19), channel_id=1, source_target_pairs={{0,8},{8,16},{16,24},{24,0},{1,9},{9,17},{17,25},{25,1},{2,10},{10... | collective-permute-start | bytes 589832 | tf_op jit(solution)/shard_map/ppermute | solution.py:492
  30.6 1.8 %collective-permute-start.3 = (bf16[768,128]{1,0:T(8,128)(2,1)S(1)}, bf16[768,128]{1,0:T(8,128)(2,1)S(1)}, u32[]{:S(2)}, u32[]{:S(2)}) collective-permute-start(bf16[768,128]{1,0:T(8,128)(2,1)S(1)} %get-tuple-element.20), channel_id=1, source_target_pairs={{0,24},{8,0},{16,8},{24,16},{1,25},{9,1},{17,9},{25,17},{2,26},{10... | collective-permute-start | bytes 589832 | tf_op jit(solution)/shard_map/ppermute | solution.py:493
  32.3 1.8 %collective-permute-start.4 = (bf16[512,128]{1,0:T(8,128)(2,1)S(1)}, bf16[512,128]{1,0:T(8,128)(2,1)S(1)}, u32[]{:S(2)}, u32[]{:S(2)}) collective-permute-start(bf16[512,128]{1,0:T(8,128)(2,1)S(1)} %get-tuple-element.21), channel_id=1, source_target_pairs={{0,16},{8,24},{16,0},{24,8},{1,17},{9,25},{17,1},{25,9},{2,18},{10... | collective-permute-start | bytes 393224 | tf_op jit(solution)/shard_map/ppermute | solution.py:491
  34.1 0.0 copy-done.4
  34.1 0.0 copy-start.2
  34.1 3.7 %attend_own.1 = (f32[8,8,256]{2,1,0:T(8,128)S(1)}, f32[8,128,128]{2,1,0:T(8,128)S(1)}, bf16[1024,1024]{1,0:T(8,128)(2,1)S(1)}) custom-call(s32[1]{0:T(128)} %bitcast.1.x_ref, s32[1]{0:T(128)} %bitcast.2.pair_ref, s32[1]{0:T(128)} %bitcast.side_ref, f32[16,32]{1,0:T(8,128)S(1)} %bitcast.7, bf16[8,448,128]{2,1,0:T(8,128)(2,1)S(1)} %all_to_all.10.got_ref, ...), custom_call_target="tpu_custom_call" | custom-call | flops 1000 | bytes 1000 | tf_op jit(solution)/shard_map/attend_own/pallas_call | solution.py:322
  37.9 1.9 %collective-permute-done.4.far_ref = bf16[512,128]{1,0:T(8,128)(2,1)S(1)} collective-permute-done((bf16[512,128]{1,0:T(8,128)(2,1)S(1)}, bf16[512,128]{1,0:T(8,128)(2,1)S(1)}, u32[]{:S(2)}, u32[]{:S(2)}) %collective-permute-start.4) | collective-permute-done | bytes 131104 | tf_op jit(solution)/shard_map/ppermute | solution.py:491
  39.8 0.0 collective-permute-done.2.prev_ref
  39.8 0.0 collective-permute-done.3.next_ref
  39.8 0.0 collective-permute-done.5._.tok_ref
  39.8 0.0 copy-start
  39.8 0.0 copy-start.1
  39.9 0.0 copy-start.5
  39.9 4.6 %attend_rest.1 = bf16[16,128,128]{2,1,0:T(8,128)(2,1)S(1)} custom-call(s32[1]{0:T(128)} %bitcast.1.x_ref, s32[1]{0:T(128)} %bitcast.2.pair_ref, s32[1]{0:T(128)} %bitcast.side_ref, f32[16,32]{1,0:T(8,128)S(1)} %bitcast.8, bf16[8,448,128]{2,1,0:T(8,128)(2,1)S(1)} %all_to_all.10.got_ref, bf16[768,128]{1,0:T(8,128)(2,1)S(1)} %collective-permute-done.2.prev_ref, ...), custom_call_target="tpu_custom_call" | custom-call | flops 1000 | bytes 1000 | tf_op jit(solution)/shard_map/attend_rest/pallas_call | solution.py:400
  44.5 12.8 %all_to_all.11.att_ref = bf16[16,128,128]{2,1,0:T(8,128)(2,1)S(1)} all-to-all(bf16[16,128,128]{2,1,0:T(8,128)(2,1)S(1)} %attend_rest.1), channel_id=1, replica_groups=mesh['yhi'=2,'core'=2,'x'=4,'z'=4,'ylo'=2] {'yhi','z','ylo'}, dimensions={0} | all-to-all | bytes 1048576 | tf_op jit(solution)/shard_map/all_to_all | solution.py:498
  57.3 0.0 copy-done.2
  57.3 0.0 copy-done
  57.3 0.0 copy-done.1
  57.3 0.0 copy-done.5
  57.3 2.6 %finish.2.rest_0_ = bf16[128,1024]{1,0:T(8,128)(2,1)S(1)} custom-call(s32[1]{0:T(128)} %bitcast.side_ref, bf16[16,128,128]{2,1,0:T(8,128)(2,1)S(1)} %all_to_all.11.att_ref, bf16[1024,1024]{1,0:T(8,128)(2,1)S(1)} %copy-done.2, bf16[128,1024]{1,0:T(8,128)(2,1)S(1)} %collective-permute-done.5._.tok_ref, f32[1,1024]{1,0:T(1,128)S(1)} %bitcast.9, ...), custom_call_target="tpu_custom_call" | custom-call | flops 1000 | bytes 1000 | tf_op jit(solution)/shard_map/finish/pallas_call | solution.py:433
  59.8 1.4 %collective-permute-start.6 = (bf16[128,1024]{1,0:T(8,128)(2,1)S(1)}, bf16[128,1024]{1,0:T(8,128)(2,1)S(1)}, u32[]{:S(2)}, u32[]{:S(2)}) collective-permute-start(bf16[128,1024]{1,0:T(8,128)(2,1)S(1)} %finish.2.rest_0_), channel_id=1, source_target_pairs={{0,65},{65,0},{1,64},{64,1},{2,67},{67,2},{3,66},{66,3},{4,69},{69... | collective-permute-start | bytes 786440 | tf_op jit(solution)/shard_map/ppermute | solution.py:501
  61.2 2.6 %finish.3.refs_0_ = f32[128,1024]{1,0:T(8,128)S(1)} custom-call(s32[1]{0:T(128)} %bitcast.side_ref, bf16[16,128,128]{2,1,0:T(8,128)(2,1)S(1)} %all_to_all.11.att_ref, bf16[1024,1024]{1,0:T(8,128)(2,1)S(1)} %copy-done.2, bf16[128,1024]{1,0:T(8,128)(2,1)S(1)} %copy-done.3, f32[1,1024]{1,0:T(1,128)S(1)} %bitcast.10, bf16[1024,1024]{1,0:T(8,128)(2,1)S(1)} %copy-done, ...), custom_call_target="tpu_custom_call" | custom-call | flops 1000 | bytes 1000 | tf_op jit(solution)/shard_map/finish/pallas_call | solution.py:433
  63.8 3.7 %collective-permute-done.6.refs_1_ = bf16[128,1024]{1,0:T(8,128)(2,1)S(1)} collective-permute-done((bf16[128,1024]{1,0:T(8,128)(2,1)S(1)}, bf16[128,1024]{1,0:T(8,128)(2,1)S(1)}, u32[]{:S(2)}, u32[]{:S(2)}) %collective-permute-start.6) | collective-permute-done | bytes 262176 | tf_op jit(solution)/shard_map/ppermute | solution.py:501
  67.5 0.7 %total.1 = bf16[128,1024]{1,0:T(8,128)(2,1)} custom-call(f32[128,1024]{1,0:T(8,128)S(1)} %finish.3.refs_0_, bf16[128,1024]{1,0:T(8,128)(2,1)S(1)} %collective-permute-done.6.refs_1_), custom_call_target="tpu_custom_call" | custom-call | flops 1000 | bytes 1000 | tf_op jit(solution)/shard_map/total/pallas_call | solution.py:451
Async XLA Ops:
  0.0 26.7 %collective-permute-start = (bf16[1024,1024]{1,0:T(8,128)(2,1)}, bf16[1024,1024]{1,0:T(8,128)(2,1)S(1)}, u32[]{:S(2)}, u32[]{:S(2)}) collective-permute-start(bf16[1024,1024]{1,0:T(8,128)(2,1)} %in_one.3), channel_id=1, source_target_pairs={{0,32},{32,0},{1,33},{33,1},{2,34},{34,2},{3,35},{35,3},{4,36},{36... | collective-permute-start | bytes 6291464 | tf_op jit(solution)/shard_map/ppermute | solution.py:482
  0.0 26.7 %collective-permute-start.1 = (bf16[1024,1024]{1,0:T(8,128)(2,1)}, bf16[1024,1024]{1,0:T(8,128)(2,1)}, u32[]{:S(2)}, u32[]{:S(2)}) collective-permute-start(bf16[1024,1024]{1,0:T(8,128)(2,1)} %out_one.3), channel_id=1, source_target_pairs={{0,32},{32,0},{1,33},{33,1},{2,34},{34,2},{3,35},{35,3},{4,36},{36... | collective-permute-start | bytes 6291464 | tf_op jit(solution)/shard_map/ppermute | solution.py:483
  0.5 26.2 %copy-start.3 = (bf16[128,1024]{1,0:T(8,128)(2,1)S(1)}, bf16[128,1024]{1,0:T(8,128)(2,1)}, u32[]{:S(2)}) copy-start(bf16[128,1024]{1,0:T(8,128)(2,1)} %tok_ref.3) | copy-start | bytes 786436
  26.7 7.4 %copy-start.4 = (f32[32,16]{0,1:T(8,128)S(1)}, f32[32,16]{0,1:T(8,128)}, u32[]{:S(2)}) copy-start(f32[32,16]{0,1:T(8,128)} %param.19) | copy-start | bytes 6148
  26.8 13.0 %collective-permute-start.5 = (bf16[128,1024]{1,0:T(8,128)(2,1)S(1)}, bf16[128,1024]{1,0:T(8,128)(2,1)S(1)}, u32[]{:S(2)}, u32[]{:S(2)}) collective-permute-start(bf16[128,1024]{1,0:T(8,128)(2,1)S(1)} %get-tuple-element.29), channel_id=1, source_target_pairs={{0,65},{65,0},{1,64},{64,1},{2,67},{67,2},{3,66},{66,3},{4,69},{69... | collective-permute-start | bytes 786440 | tf_op jit(solution)/shard_map/ppermute | solution.py:494
  29.1 10.7 %collective-permute-start.2 = (bf16[768,128]{1,0:T(8,128)(2,1)S(1)}, bf16[768,128]{1,0:T(8,128)(2,1)S(1)}, u32[]{:S(2)}, u32[]{:S(2)}) collective-permute-start(bf16[768,128]{1,0:T(8,128)(2,1)S(1)} %get-tuple-element.19), channel_id=1, source_target_pairs={{0,8},{8,16},{16,24},{24,0},{1,9},{9,17},{17,25},{25,1},{2,10},{10... | collective-permute-start | bytes 589832 | tf_op jit(solution)/shard_map/ppermute | solution.py:492
  30.6 9.2 %collective-permute-start.3 = (bf16[768,128]{1,0:T(8,128)(2,1)S(1)}, bf16[768,128]{1,0:T(8,128)(2,1)S(1)}, u32[]{:S(2)}, u32[]{:S(2)}) collective-permute-start(bf16[768,128]{1,0:T(8,128)(2,1)S(1)} %get-tuple-element.20), channel_id=1, source_target_pairs={{0,24},{8,0},{16,8},{24,16},{1,25},{9,1},{17,9},{25,17},{2,26},{10... | collective-permute-start | bytes 589832 | tf_op jit(solution)/shard_map/ppermute | solution.py:493
  32.3 7.5 %collective-permute-start.4 = (bf16[512,128]{1,0:T(8,128)(2,1)S(1)}, bf16[512,128]{1,0:T(8,128)(2,1)S(1)}, u32[]{:S(2)}, u32[]{:S(2)}) collective-permute-start(bf16[512,128]{1,0:T(8,128)(2,1)S(1)} %get-tuple-element.21), channel_id=1, source_target_pairs={{0,16},{8,24},{16,0},{24,8},{1,17},{9,25},{17,1},{25,9},{2,18},{10... | collective-permute-start | bytes 393224 | tf_op jit(solution)/shard_map/ppermute | solution.py:491
  34.1 23.1 %copy-start.2 = (bf16[1024,1024]{1,0:T(8,128)(2,1)S(1)}, bf16[1024,1024]{1,0:T(8,128)(2,1)}, u32[]{:S(2)}) copy-start(bf16[1024,1024]{1,0:T(8,128)(2,1)} %w_ref.3) | copy-start | bytes 6291460
  39.8 17.4 %copy-start = (bf16[1024,1024]{1,0:T(8,128)(2,1)S(1)}, bf16[1024,1024]{1,0:T(8,128)(2,1)}, u32[]{:S(2)}) copy-start(bf16[1024,1024]{1,0:T(8,128)(2,1)} %in_one.3) | copy-start | bytes 6291460
  39.8 17.4 %copy-start.1 = (bf16[1024,1024]{1,0:T(8,128)(2,1)S(1)}, bf16[1024,1024]{1,0:T(8,128)(2,1)}, u32[]{:S(2)}) copy-start(bf16[1024,1024]{1,0:T(8,128)(2,1)} %out_one.3) | copy-start | bytes 6291460
  39.9 17.4 %copy-start.5 = (f32[1024]{0:T(1024)S(1)}, f32[1024]{0:T(1024)}, u32[]{:S(2)}) copy-start(f32[1024]{0:T(1024)} %param.23) | copy-start | bytes 12292
  59.8 7.7 %collective-permute-start.6 = (bf16[128,1024]{1,0:T(8,128)(2,1)S(1)}, bf16[128,1024]{1,0:T(8,128)(2,1)S(1)}, u32[]{:S(2)}, u32[]{:S(2)}) collective-permute-start(bf16[128,1024]{1,0:T(8,128)(2,1)S(1)} %finish.2.rest_0_), channel_id=1, source_target_pairs={{0,65},{65,0},{1,64},{64,1},{2,67},{67,2},{3,66},{66,3},{4,69},{69... | collective-permute-start | bytes 786440 | tf_op jit(solution)/shard_map/ppermute | solution.py:501

commit v9 on v8

--- a/solution.py
+++ b/solution.py
@@ -141,7 +141,7 @@
         pltpu.make_async_copy(w_hbm, held.at[kind], arrived.at[kind])
         for kind, w_hbm in enumerate((wq_hbm, wk_hbm, wv_hbm))
     ]
-    for copy in first + copies:
+    for copy in first + copies[:2]:
         copy.start()
     for copy in first:
         copy.wait()
@@ -157,6 +157,8 @@
     )
     for kind, copy in enumerate(copies):
         copy.wait()
+        if kind == 0:
+            copies[2].start()
         got = dot(normed, held[kind]).astype(jnp.bfloat16)
         for to in range(PAIRS):
             out_ref[to, kind * ROWS : (kind + 1) * ROWS] = got[:, to * LANES : (to + 1) * LANES]
@@ -190,8 +192,21 @@
     return blocks, made
 
 
-def spread_kernel(got_ref, tok_ref, *rest):
-    up_ref, down_ref, far_ref, same_ref = rest[-4:]
+def hold(value, arrived):
+    return pl.pallas_call(
+        lambda value_ref, arrived_ref, out_ref: None,
+        in_specs=[VMEM_SPEC] * 2,
+        out_specs=VMEM_SPEC,
+        out_shape=pltpu.VMEM(value.shape, value.dtype),
+        input_output_aliases={0: 0},
+        compiler_params=pltpu.CompilerParams(vmem_limit_bytes=VMEM_LIMIT),
+        cost_estimate=COST,
+        name="hold",
+    )(*on_chip(value, arrived))
+
+
+def spread_kernel(got_ref, *rest):
+    up_ref, down_ref, far_ref = rest[-3:]
     for source in range(PAIRS):
         rows = slice(source * 4 * SHARE, (source + 1) * 4 * SHARE)
         held = got_ref[source, 3 * ROWS :]
@@ -200,25 +215,19 @@
         far_ref[rows] = held
     up_ref[QUARTER:] = got_ref[PAIRS - 1, ROWS : 3 * ROWS]
     down_ref[QUARTER:] = got_ref[0, ROWS : 3 * ROWS]
-    same_ref[...] = tok_ref[...]
-
-
-def spread(got, tokens, on, off):
+
+
+def spread(got, on, off):
     shape = pltpu.VMEM((QUARTER + 2 * ROWS, LANES), jnp.bfloat16)
     return pl.pallas_call(
         spread_kernel,
-        in_specs=[VMEM_SPEC] * 3 + [HBM_SPEC],
-        out_specs=(VMEM_SPEC,) * 4,
-        out_shape=(
-            shape,
-            shape,
-            pltpu.VMEM((QUARTER, LANES), jnp.bfloat16),
-            pltpu.VMEM((ROWS, D), jnp.bfloat16),
-        ),
+        in_specs=[VMEM_SPEC] * 2 + [HBM_SPEC],
+        out_specs=(VMEM_SPEC,) * 3,
+        out_shape=(shape, shape, pltpu.VMEM((QUARTER, LANES), jnp.bfloat16)),
         compiler_params=pltpu.CompilerParams(vmem_limit_bytes=VMEM_LIMIT),
         cost_estimate=COST,
         name="spread",
-    )(*on_chip(got, tokens, on), *off_chip(off))
+    )(*on_chip(got, on), *off_chip(off))
 
 
 def queries(got_ref, chosen_ref, step):
@@ -279,7 +288,7 @@
 
 def own_kernel(
     x_ref, pair_ref, side_ref, rel_ref, got_ref, near_ref, name_ref, asked_ref, tail_ref, chosen_ref, w1_hbm,
-    stat_ref, acc_ref, w1_ref, keys, values, kwin, vwin, landed,
+    stat_ref, acc_ref, split_ref, w1_ref, keys, values, kwin, vwin, landed,
 ):
     place_ref = (x_ref[0], pair_ref[0], side_ref[0])
     copies = start_copies(((w1_hbm, w1_ref),), landed)
@@ -295,6 +304,7 @@
 
     def one(step, _):
         stacked, split = queries(got_ref, chosen_ref, step)
+        split_ref[step] = split
         parts = [dot(keys[...], split) + jnp.where(is_last, tail_ref[step], full)]
         near_scores = dot(kwin[pl.ds(step, 3)].reshape(3 * ROWS, LANES), stacked)
         for b in range(3):
@@ -322,10 +332,11 @@
     return pl.pallas_call(
         own_kernel,
         in_specs=[SMEM_SPEC] * 4 + [VMEM_SPEC] * 6 + [HBM_SPEC],
-        out_specs=(VMEM_SPEC,) * 3,
+        out_specs=(VMEM_SPEC,) * 4,
         out_shape=(
             pltpu.VMEM((PAIRS, 8, 2 * ROWS), jnp.float32),
             pltpu.VMEM((PAIRS, LANES, ROWS), jnp.float32),
+            pltpu.VMEM((PAIRS, PREF_GRP * LANES, 2 * ROWS), jnp.bfloat16),
         )
         + tuple(pltpu.VMEM(w.shape, w.dtype) for w in later_weights),
         scratch_shapes=[
@@ -342,8 +353,8 @@
 
 
 def rest_kernel(
-    x_ref, pair_ref, side_ref, rel_ref, got_ref, prev_ref, next_ref, far_ref, near_ref, name_ref, asked_ref, tail_ref, chosen_ref,
-    stat_ref, acc_ref, _, out_ref, keys, values, kwin, vwin,
+    x_ref, pair_ref, side_ref, rel_ref, prev_ref, next_ref, far_ref, near_ref, name_ref, asked_ref, tail_ref,
+    stat_ref, acc_ref, split_ref, out_ref, keys, values, kwin, vwin,
 ):
     place_ref = (x_ref[0], pair_ref[0], side_ref[0])
     turns = ((3, prev_ref), (1, next_ref), (2, far_ref))
@@ -359,7 +370,7 @@
     full = far_bias(place_ref, rel_ref)
 
     def one(step, edge=None):
-        stacked, split = queries(got_ref, chosen_ref, step)
+        split = split_ref[step]
         tail = tail_ref[step]
         scores = dot(keys[...].reshape(3 * PLEN // 4, PREF_GRP * LANES), split)
         parts = [
@@ -368,7 +379,7 @@
         if edge is not None:
             bias = near_ref[edge * 2 * ROWS : (edge * 2 + 1) * ROWS]
             parts.append(
-                masked(dot(kwin[edge], stacked), name_ref, edge * (PAIRS + 1), asked_ref, step, bias)
+                masked(dot(kwin[edge], split[:LANES] + split[LANES:]), name_ref, edge * (PAIRS + 1), asked_ref, step, bias)
             )
         before = stat_ref[step, 0:1]
         top = jnp.max(functools.reduce(jnp.maximum, parts), axis=0, keepdims=True)
@@ -396,10 +407,10 @@
     one(jnp.int32(PAIRS - 1), 1)
 
 
-def attend_rest(place, rel_bias, got, prev, after_it, far, made, part, ready):
+def attend_rest(place, rel_bias, prev, after_it, far, made, part):
     return pl.pallas_call(
         rest_kernel,
-        in_specs=[SMEM_SPEC] * 4 + [VMEM_SPEC] * 12,
+        in_specs=[SMEM_SPEC] * 4 + [VMEM_SPEC] * 10,
         out_specs=VMEM_SPEC,
         out_shape=pltpu.VMEM((2 * PAIRS, ROWS, LANES), jnp.bfloat16),
         scratch_shapes=[
@@ -411,7 +422,7 @@
         compiler_params=pltpu.CompilerParams(vmem_limit_bytes=VMEM_LIMIT),
         cost_estimate=COST,
         name="attend_rest",
-    )(*place, rel_bias.T, *on_chip(got, prev, after_it, far, *made, *part, ready))
+    )(*place, rel_bias.T, *on_chip(prev, after_it, far, *made[:-1], *part))
 
 
 def finish_kernel(away, side_ref, att_ref, w_ref, tok_ref, gain_ref, in_one, in_two, out_one, out_two, *rest):
@@ -479,21 +490,22 @@
     place = tuple(
         at.astype(jnp.int32).reshape(1) for at in (lax.axis_index("x"), plane, lax.axis_index("yhi"))
     )
+    mirrored = ("yhi", "ylo")
+    far_tokens = lax.ppermute(tokens, mirrored, MIRROR)
     other_in = lax.ppermute(w_in, "core", SWAP)
     other_out = lax.ppermute(w_out, "core", SWAP)
     blocks, made = project(
         place, tokens, attn_gain, prefix_cache, rel_bias, lengths, prefix_map, w_query, w_key, w_value
     )
+    blocks = hold(blocks, far_tokens)
     got = lax.all_to_all(blocks, PLANE, 0, 0, tiled=True)
-    mirrored = ("yhi", "ylo")
-    up, down, far, same = spread(got, tokens, other_in, other_out)
+    up, down, far = spread(got, other_in, other_out)
     by = lambda d: [(i, (i + d) % count_x) for i in range(count_x)]
     opposite = lax.ppermute(far, "x", by(2))
     prev = lax.ppermute(up, "x", by(1))
     later = lax.ppermute(down, "x", by(-1))
-    far_tokens = lax.ppermute(same, mirrored, MIRROR)
-    stat, acc, other_out = attend_own(place, rel_bias, got, made, (other_out,))
-    mixed = attend_rest(place, rel_bias, got, prev, later, opposite, made, (stat, acc), far_tokens)
+    *part, other_out = attend_own(place, rel_bias, got, made, (other_out,))
+    mixed = attend_rest(place, rel_bias, prev, later, opposite, made, part)
     weights = (w_in, other_in, w_out, other_out)
     att = lax.all_to_all(mixed, ("yhi",) + PLANE, 0, 0, tiled=True)
 

time: 68.4 us -> 70.5 us (1.031)
  blocking collectives: 33.5 us -> 34.5 us
  starting transfers between devices: 9.18 us -> 10.1 us
    all_to_all x1, blocking collectives: 12.8 us -> 15.7 us  [body(): att = lax.all_to_all(mixed, ('yhi',) + PLANE, 0, 0, tiled=True)]
    all_to_all x1, blocking collectives: 20.8 us -> 18.9 us  [body(): got = lax.all_to_all(blocks, PLANE, 0, 0, tiled=True)]
    ppermute x1, waiting for transfers between devices: 0.01 us -> 1.24 us  [body(): far_tokens = lax.ppermute(tokens, mirrored, MIRROR)]
    ppermute x1, waiting for transfers between devices: 1.95 us -> 0.91 us  [body(): opposite = lax.ppermute(far, 'x', by(2))]
    ppermute x1, starting transfers between devices: 2.27 us -> 3.1 us  [body(): far_tokens = lax.ppermute(tokens, mirrored, MIRROR)]
    pallas_call x2 -> x3, Pallas kernels: 4.69 us -> 4.52 us  [the longest x1 4.46 us: attend_rest(): pl.pallas_call(rest_kernel, in_specs=[SMEM_SPEC] * 4 + [VMEM_SPEC] * 10,...]
  transfers between devices with their start and end apart: 7 -> 7, of which waited for: 2 -> 3; matrix products, arithmetic and copies ran while one was open for 0% -> 0% of each run, Pallas kernels for 17% -> 17%
where the time goes in v9:
time: 70.5 us; the launch traced here: 70.3 us
  blocking collectives  34.5 us (49%)
  Pallas kernels  19.7 us (28%)
  starting transfers between devices  10.1 us (14%)
  waiting for transfers between devices  5.78 us (8%)
    all_to_all x1, blocking collectives, body(): got = lax.all_to_all(blocks, PLANE, 0, 0, tiled=True)  18.9 us
    all_to_all x1, blocking collectives, body(): att = lax.all_to_all(mixed, ('yhi',) + PLANE, 0, 0, tiled=True)  15.7 us
    pallas_call x1, Pallas kernels, project(): pl.pallas_call(project_kernel, in_specs=[SMEM_SPEC] * 3 + [HBM_SPEC] * 9,...  5.44 us
    pallas_call x2, Pallas kernels, finish(): pl.pallas_call(functools.partial(finish_kernel, away), in_specs=[SMEM_SPE...  5.18 us
    pallas_call x1, Pallas kernels, attend_rest(): pl.pallas_call(rest_kernel, in_specs=[SMEM_SPEC] * 4 + [VMEM_SPEC] * 10,...  4.46 us
    pallas_call x1, Pallas kernels, attend_own(): pl.pallas_call(own_kernel, in_specs=[SMEM_SPEC] * 4 + [VMEM_SPEC] * 6 + [...  3.79 us
    ppermute x1, waiting for transfers between devices, body(): back = lax.ppermute(far_sum, mirrored, MIRROR)  3.62 us
    ppermute x1, starting transfers between devices, body(): far_tokens = lax.ppermute(tokens, mirrored, MIRROR)  3.1 us
  transfers between devices with their start and end apart: 7, of which 3 were waited for; matrix products, arithmetic and copies ran while one was open for 0% of the time, Pallas kernels for 17%

profile of v9, /device:TPU:0, one launch (start us, length us, event | category | flops | bytes accessed | tf_op | source)
XLA Modules:
  0.0 70.3 jit_solution(10859389961982886655)
XLA Ops:
  0.0 0.0 collective-permute-start.2
  0.0 0.5 collective-permute-start.1
  0.5 3.1 %collective-permute-start = (bf16[128,1024]{1,0:T(8,128)(2,1)}, bf16[128,1024]{1,0:T(8,128)(2,1)S(1)}, u32[]{:S(2)}, u32[]{:S(2)}) collective-permute-start(bf16[128,1024]{1,0:T(8,128)(2,1)} %tok_ref.1), channel_id=1, source_target_pairs={{0,65},{65,0},{1,64},{64,1},{2,67},{67,2},{3,66},{66,3},{4,69},{69... | collective-permute-start | bytes 786440 | tf_op jit(solution)/shard_map/ppermute | solution.py:494
  3.6 5.4 %project.1 = (bf16[8,448,128]{2,1,0:T(8,128)(2,1)S(1)}, f32[384,256]{1,0:T(8,128)S(1)}, bf16[10,128,128]{2,1,0:T(8,128)(2,1)S(1)}, f32[8,8,128]{2,1,0:T(8,128)S(...) custom-call(s32[1]{0:T(128)} %bitcast.1.x_ref, s32[1]{0:T(128)} %bitcast.2.pair_ref, s32[1]{0:T(128)} %bitcast.side_ref, ...), custom_call_target="tpu_custom_call" | custom-call | flops 1000 | bytes 1000 | tf_op jit(solution)/shard_map/project/pallas_call | solution.py:177
  9.1 1.2 %collective-permute-done.arrived_ref.tok_ref = bf16[128,1024]{1,0:T(8,128)(2,1)S(1)} collective-permute-done((bf16[128,1024]{1,0:T(8,128)(2,1)}, bf16[128,1024]{1,0:T(8,128)(2,1)S(1)}, u32[]{:S(2)}, u32[]{:S(2)}) %collective-permute-start) | collective-permute-done | bytes 262176 | tf_op jit(solution)/shard_map/ppermute | solution.py:494
  10.3 18.9 %all_to_all.10.got_ref = bf16[8,448,128]{2,1,0:T(8,128)(2,1)S(1)} all-to-all(bf16[8,448,128]{2,1,0:T(8,128)(2,1)S(1)} %hold.1), channel_id=1, replica_groups=mesh['yhi'=2,'core'=2,'x'=4,'z'=4,'ylo'=2] {'z','ylo'}, dimensions={0} | all-to-all | bytes 1835008 | tf_op jit(solution)/shard_map/all_to_all | solution.py:501
  29.2 0.0 copy-start.4
  29.2 0.0 collective-permute-done.2.rest_1_.w1_hbm
  29.2 0.0 collective-permute-done.1.rest_0_.in_two
  29.2 0.1 spread.1
  29.3 1.6 %collective-permute-start.3 = (bf16[768,128]{1,0:T(8,128)(2,1)S(1)}, bf16[768,128]{1,0:T(8,128)(2,1)S(1)}, u32[]{:S(2)}, u32[]{:S(2)}) collective-permute-start(bf16[768,128]{1,0:T(8,128)(2,1)S(1)} %get-tuple-element.19), channel_id=1, source_target_pairs={{0,8},{8,16},{16,24},{24,0},{1,9},{9,17},{17,25},{25,1},{2,10},{10... | collective-permute-start | bytes 589832 | tf_op jit(solution)/shard_map/ppermute | solution.py:505
  30.8 1.7 %collective-permute-start.4 = (bf16[768,128]{1,0:T(8,128)(2,1)S(1)}, bf16[768,128]{1,0:T(8,128)(2,1)S(1)}, u32[]{:S(2)}, u32[]{:S(2)}) collective-permute-start(bf16[768,128]{1,0:T(8,128)(2,1)S(1)} %get-tuple-element.20), channel_id=1, source_target_pairs={{0,24},{8,0},{16,8},{24,16},{1,25},{9,1},{17,9},{25,17},{2,26},{10... | collective-permute-start | bytes 589832 | tf_op jit(solution)/shard_map/ppermute | solution.py:506
  32.6 1.8 %collective-permute-start.5 = (bf16[512,128]{1,0:T(8,128)(2,1)S(1)}, bf16[512,128]{1,0:T(8,128)(2,1)S(1)}, u32[]{:S(2)}, u32[]{:S(2)}) collective-permute-start(bf16[512,128]{1,0:T(8,128)(2,1)S(1)} %get-tuple-element.21), channel_id=1, source_target_pairs={{0,16},{8,24},{16,0},{24,8},{1,17},{9,25},{17,1},{25,9},{2,18},{10... | collective-permute-start | bytes 393224 | tf_op jit(solution)/shard_map/ppermute | solution.py:504
  34.4 0.0 copy-done.4
  34.4 0.0 copy-start.2
  34.4 3.8 %attend_own.1 = (f32[8,8,256]{2,1,0:T(8,128)S(1)}, f32[8,128,128]{2,1,0:T(8,128)S(1)}, bf16[8,256,256]{2,1,0:T(8,128)(2,1)S(1)}, bf16[1024,1024]{1,0:T(8,128)(2,1)S(1)}) custom-call(s32[1]{0:T(128)} %bitcast.1.x_ref, s32[1]{0:T(128)} %bitcast.2.pair_ref, s32[1]{0:T(128)} %bitcast.side_ref, f32[16,32]{1,0:T(8,128)S(1)} %bitcast.7, ...), custom_call_target="tpu_custom_call" | custom-call | flops 1000 | bytes 1000 | tf_op jit(solution)/shard_map/attend_own/pallas_call | solution.py:332
  38.2 0.9 %collective-permute-done.5.far_ref = bf16[512,128]{1,0:T(8,128)(2,1)S(1)} collective-permute-done((bf16[512,128]{1,0:T(8,128)(2,1)S(1)}, bf16[512,128]{1,0:T(8,128)(2,1)S(1)}, u32[]{:S(2)}, u32[]{:S(2)}) %collective-permute-start.5) | collective-permute-done | bytes 131104 | tf_op jit(solution)/shard_map/ppermute | solution.py:504
  39.1 0.0 collective-permute-done.3.prev_ref
  39.1 0.0 collective-permute-done.4.next_ref
  39.1 0.0 copy-start
  39.1 0.0 copy-start.1
  39.1 0.0 copy-start.5
  39.1 4.5 %attend_rest.1 = bf16[16,128,128]{2,1,0:T(8,128)(2,1)S(1)} custom-call(s32[1]{0:T(128)} %bitcast.1.x_ref, s32[1]{0:T(128)} %bitcast.2.pair_ref, s32[1]{0:T(128)} %bitcast.side_ref, f32[16,32]{1,0:T(8,128)S(1)} %bitcast.8, bf16[768,128]{1,0:T(8,128)(2,1)S(1)} %collective-permute-done.3.prev_ref, bf16[768,128]{1,0:T(8,128)(2,1)S(1)} %collective-permute-done.4.next_ref, ...), custom_call_target="tpu_custom_call" | custom-call | flops 1000 | bytes 1000 | tf_op jit(solution)/shard_map/attend_rest/pallas_call | solution.py:411
  43.6 15.7 %all_to_all.11.att_ref = bf16[16,128,128]{2,1,0:T(8,128)(2,1)S(1)} all-to-all(bf16[16,128,128]{2,1,0:T(8,128)(2,1)S(1)} %attend_rest.1), channel_id=1, replica_groups=mesh['yhi'=2,'core'=2,'x'=4,'z'=4,'ylo'=2] {'yhi','z','ylo'}, dimensions={0} | all-to-all | bytes 1048576 | tf_op jit(solution)/shard_map/all_to_all | solution.py:510
  59.2 0.0 copy-done.2
  59.3 0.0 copy-done
  59.3 0.0 copy-done.1
  59.3 0.0 copy-done.5
  59.3 0.0 copy-start.3
  59.3 2.6 %finish.2.rest_0_ = bf16[128,1024]{1,0:T(8,128)(2,1)S(1)} custom-call(s32[1]{0:T(128)} %bitcast.side_ref, bf16[16,128,128]{2,1,0:T(8,128)(2,1)S(1)} %all_to_all.11.att_ref, bf16[1024,1024]{1,0:T(8,128)(2,1)S(1)} %copy-done.2, bf16[128,1024]{1,0:T(8,128)(2,1)S(1)} %collective-permute-done.arrived_ref.tok_ref, f32[1,1024]{1,0:T(1,128)S(1)} %bitcast.9, ...), custom_call_target="tpu_custom_call" | custom-call | flops 1000 | bytes 1000 | tf_op jit(solution)/shard_map/finish/pallas_call | solution.py:444
  61.9 1.4 %collective-permute-start.6 = (bf16[128,1024]{1,0:T(8,128)(2,1)S(1)}, bf16[128,1024]{1,0:T(8,128)(2,1)S(1)}, u32[]{:S(2)}, u32[]{:S(2)}) collective-permute-start(bf16[128,1024]{1,0:T(8,128)(2,1)S(1)} %finish.2.rest_0_), channel_id=1, source_target_pairs={{0,65},{65,0},{1,64},{64,1},{2,67},{67,2},{3,66},{66,3},{4,69},{69... | collective-permute-start | bytes 786440 | tf_op jit(solution)/shard_map/ppermute | solution.py:513
  63.3 0.0 copy-done.3
  63.3 2.6 %finish.3.refs_0_ = f32[128,1024]{1,0:T(8,128)S(1)} custom-call(s32[1]{0:T(128)} %bitcast.side_ref, bf16[16,128,128]{2,1,0:T(8,128)(2,1)S(1)} %all_to_all.11.att_ref, bf16[1024,1024]{1,0:T(8,128)(2,1)S(1)} %copy-done.2, bf16[128,1024]{1,0:T(8,128)(2,1)S(1)} %copy-done.3, f32[1,1024]{1,0:T(1,128)S(1)} %bitcast.10, bf16[1024,1024]{1,0:T(8,128)(2,1)S(1)} %copy-done, ...), custom_call_target="tpu_custom_call" | custom-call | flops 1000 | bytes 1000 | tf_op jit(solution)/shard_map/finish/pallas_call | solution.py:444
  65.9 3.6 %collective-permute-done.6.refs_1_ = bf16[128,1024]{1,0:T(8,128)(2,1)S(1)} collective-permute-done((bf16[128,1024]{1,0:T(8,128)(2,1)S(1)}, bf16[128,1024]{1,0:T(8,128)(2,1)S(1)}, u32[]{:S(2)}, u32[]{:S(2)}) %collective-permute-start.6) | collective-permute-done | bytes 262176 | tf_op jit(solution)/shard_map/ppermute | solution.py:513
  69.5 0.8 %total.1 = bf16[128,1024]{1,0:T(8,128)(2,1)} custom-call(f32[128,1024]{1,0:T(8,128)S(1)} %finish.3.refs_0_, bf16[128,1024]{1,0:T(8,128)(2,1)S(1)} %collective-permute-done.6.refs_1_), custom_call_target="tpu_custom_call" | custom-call | flops 1000 | bytes 1000 | tf_op jit(solution)/shard_map/total/pallas_call | solution.py:462
  (1 shorter events, 0.0 us)
Async XLA Ops:
  0.0 29.2 %collective-permute-start.2 = (bf16[1024,1024]{1,0:T(8,128)(2,1)}, bf16[1024,1024]{1,0:T(8,128)(2,1)}, u32[]{:S(2)}, u32[]{:S(2)}) collective-permute-start(bf16[1024,1024]{1,0:T(8,128)(2,1)} %out_one.3), channel_id=1, source_target_pairs={{0,32},{32,0},{1,33},{33,1},{2,34},{34,2},{3,35},{35,3},{4,36},{36... | collective-permute-start | bytes 6291464 | tf_op jit(solution)/shard_map/ppermute | solution.py:496
  0.0 29.2 %collective-permute-start.1 = (bf16[1024,1024]{1,0:T(8,128)(2,1)}, bf16[1024,1024]{1,0:T(8,128)(2,1)S(1)}, u32[]{:S(2)}, u32[]{:S(2)}) collective-permute-start(bf16[1024,1024]{1,0:T(8,128)(2,1)} %in_one.3), channel_id=1, source_target_pairs={{0,32},{32,0},{1,33},{33,1},{2,34},{34,2},{3,35},{35,3},{4,36},{36... | collective-permute-start | bytes 6291464 | tf_op jit(solution)/shard_map/ppermute | solution.py:495
  0.5 9.8 %collective-permute-start = (bf16[128,1024]{1,0:T(8,128)(2,1)}, bf16[128,1024]{1,0:T(8,128)(2,1)S(1)}, u32[]{:S(2)}, u32[]{:S(2)}) collective-permute-start(bf16[128,1024]{1,0:T(8,128)(2,1)} %tok_ref.1), channel_id=1, source_target_pairs={{0,65},{65,0},{1,64},{64,1},{2,67},{67,2},{3,66},{66,3},{4,69},{69... | collective-permute-start | bytes 786440 | tf_op jit(solution)/shard_map/ppermute | solution.py:494
  29.2 5.2 %copy-start.4 = (f32[32,16]{0,1:T(8,128)S(1)}, f32[32,16]{0,1:T(8,128)}, u32[]{:S(2)}) copy-start(f32[32,16]{0,1:T(8,128)} %param.19) | copy-start | bytes 6148
  29.3 9.8 %collective-permute-start.3 = (bf16[768,128]{1,0:T(8,128)(2,1)S(1)}, bf16[768,128]{1,0:T(8,128)(2,1)S(1)}, u32[]{:S(2)}, u32[]{:S(2)}) collective-permute-start(bf16[768,128]{1,0:T(8,128)(2,1)S(1)} %get-tuple-element.19), channel_id=1, source_target_pairs={{0,8},{8,16},{16,24},{24,0},{1,9},{9,17},{17,25},{25,1},{2,10},{10... | collective-permute-start | bytes 589832 | tf_op jit(solution)/shard_map/ppermute | solution.py:505
  30.8 8.3 %collective-permute-start.4 = (bf16[768,128]{1,0:T(8,128)(2,1)S(1)}, bf16[768,128]{1,0:T(8,128)(2,1)S(1)}, u32[]{:S(2)}, u32[]{:S(2)}) collective-permute-start(bf16[768,128]{1,0:T(8,128)(2,1)S(1)} %get-tuple-element.20), channel_id=1, source_target_pairs={{0,24},{8,0},{16,8},{24,16},{1,25},{9,1},{17,9},{25,17},{2,26},{10... | collective-permute-start | bytes 589832 | tf_op jit(solution)/shard_map/ppermute | solution.py:506
  32.6 6.5 %collective-permute-start.5 = (bf16[512,128]{1,0:T(8,128)(2,1)S(1)}, bf16[512,128]{1,0:T(8,128)(2,1)S(1)}, u32[]{:S(2)}, u32[]{:S(2)}) collective-permute-start(bf16[512,128]{1,0:T(8,128)(2,1)S(1)} %get-tuple-element.21), channel_id=1, source_target_pairs={{0,16},{8,24},{16,0},{24,8},{1,17},{9,25},{17,1},{25,9},{2,18},{10... | collective-permute-start | bytes 393224 | tf_op jit(solution)/shard_map/ppermute | solution.py:504
  34.4 24.9 %copy-start.2 = (bf16[1024,1024]{1,0:T(8,128)(2,1)S(1)}, bf16[1024,1024]{1,0:T(8,128)(2,1)}, u32[]{:S(2)}) copy-start(bf16[1024,1024]{1,0:T(8,128)(2,1)} %w_ref.3) | copy-start | bytes 6291460
  39.1 20.1 %copy-start = (bf16[1024,1024]{1,0:T(8,128)(2,1)S(1)}, bf16[1024,1024]{1,0:T(8,128)(2,1)}, u32[]{:S(2)}) copy-start(bf16[1024,1024]{1,0:T(8,128)(2,1)} %in_one.3) | copy-start | bytes 6291460
  39.1 20.1 %copy-start.1 = (bf16[1024,1024]{1,0:T(8,128)(2,1)S(1)}, bf16[1024,1024]{1,0:T(8,128)(2,1)}, u32[]{:S(2)}) copy-start(bf16[1024,1024]{1,0:T(8,128)(2,1)} %out_one.3) | copy-start | bytes 6291460
  39.1 20.1 %copy-start.5 = (f32[1024]{0:T(1024)S(1)}, f32[1024]{0:T(1024)}, u32[]{:S(2)}) copy-start(f32[1024]{0:T(1024)} %param.23) | copy-start | bytes 12292
  59.3 4.0 %copy-start.3 = (bf16[128,1024]{1,0:T(8,128)(2,1)S(1)}, bf16[128,1024]{1,0:T(8,128)(2,1)}, u32[]{:S(2)}) copy-start(bf16[128,1024]{1,0:T(8,128)(2,1)} %tok_ref.1) | copy-start | bytes 786436
  61.9 7.7 %collective-permute-start.6 = (bf16[128,1024]{1,0:T(8,128)(2,1)S(1)}, bf16[128,1024]{1,0:T(8,128)(2,1)S(1)}, u32[]{:S(2)}, u32[]{:S(2)}) collective-permute-start(bf16[128,1024]{1,0:T(8,128)(2,1)S(1)} %finish.2.rest_0_), channel_id=1, source_target_pairs={{0,65},{65,0},{1,64},{64,1},{2,67},{67,2},{3,66},{66,3},{4,69},{69... | collective-permute-start | bytes 786440 | tf_op jit(solution)/shard_map/ppermute | solution.py:513

commit v10 on v8

--- a/solution.py
+++ b/solution.py
@@ -69,11 +69,10 @@
 
 
 def write_tables(
-    place_ref, rel_ref, len_ref, map_ref, near_ref, name_ref, asked_ref, tail_ref, chosen_ref
+    place_ref, rel_ref, len_ref, map_ref, near_ref, name_ref, asked_ref, line_ref, chosen_ref
 ):
     row = lax.broadcasted_iota(jnp.int32, (ROWS, LANES), 0)
     lane = lax.broadcasted_iota(jnp.int32, (ROWS, LANES), 1)
-    lines = []
     for h in range(2):
         head = place_ref[1] * 2 + h
         before = bias_line(rel_ref, head, 0)
@@ -88,7 +87,7 @@
             row > lane, pick(after_it, row - lane), pick(before, lane - row)
         )
         near_ref[2 * ROWS : 3 * ROWS, cut] = pick(after_it, row + ROWS - lane)
-        lines.append(before)
+        line_ref[h] = before[:8]
 
     requests = len_ref.shape[1]
     down_it = lax.broadcasted_iota(jnp.int32, (requests, requests), 0)
@@ -117,14 +116,11 @@
             step = b - 1
             asked_ref[step] = facts
             chosen_ref[step] = jnp.broadcast_to(chosen, (ROWS, LANES)).astype(jnp.bfloat16)
-            at = jnp.minimum(ROWS - row + jnp.broadcast_to(offset, (ROWS, LANES)).astype(jnp.int32), LANES - 1)
-            for h in range(2):
-                tail_ref[step, :, h * ROWS : (h + 1) * ROWS] = jnp.take_along_axis(lines[h], at, axis=1)
 
 
 def project_kernel(
     x_ref, pair_ref, side_ref, tok_hbm, gain_hbm, cache_hbm, rel_hbm, len_hbm, map_hbm, wq_hbm, wk_hbm, wv_hbm,
-    out_ref, near_ref, name_ref, asked_ref, tail_ref, chosen_ref,
+    out_ref, near_ref, name_ref, asked_ref, line_ref, chosen_ref,
     tok, gain, cache, rel, lengths, prefix_map, held, arrived, landed,
 ):
     place_ref = (x_ref[0], pair_ref[0], side_ref[0])
@@ -153,7 +149,7 @@
                 cut = slice(kind * D + part * LANES, kind * D + (part + 1) * LANES)
                 out_ref[part, at : at + SHARE] = cache[p, :, cut]
     write_tables(
-        place_ref, rel, lengths, prefix_map, near_ref, name_ref, asked_ref, tail_ref, chosen_ref
+        place_ref, rel, lengths, prefix_map, near_ref, name_ref, asked_ref, line_ref, chosen_ref
     )
     for kind, copy in enumerate(copies):
         copy.wait()
@@ -169,7 +165,7 @@
         pltpu.VMEM((3 * ROWS, 2 * ROWS), jnp.float32),
         pltpu.VMEM((PAIRS + 2, ROWS, LANES), jnp.bfloat16),
         pltpu.VMEM((PAIRS, 8, ROWS), jnp.float32),
-        pltpu.VMEM((PAIRS, ROWS, 2 * ROWS), jnp.float32),
+        pltpu.VMEM((2, 8, LANES), jnp.float32),
         pltpu.VMEM((PAIRS, ROWS, ROWS), jnp.bfloat16),
     )
     blocks, *made = pl.pallas_call(
@@ -278,8 +274,8 @@
 
 
 def own_kernel(
-    x_ref, pair_ref, side_ref, rel_ref, got_ref, near_ref, name_ref, asked_ref, tail_ref, chosen_ref, w1_hbm,
-    stat_ref, acc_ref, w1_ref, keys, values, kwin, vwin, landed,
+    x_ref, pair_ref, side_ref, rel_ref, got_ref, near_ref, name_ref, asked_ref, line_ref, chosen_ref, w1_hbm,
+    stat_ref, acc_ref, tail_ref, w1_ref, keys, values, kwin, vwin, landed,
 ):
     place_ref = (x_ref[0], pair_ref[0], side_ref[0])
     copies = start_copies(((w1_hbm, w1_ref),), landed)
@@ -293,9 +289,16 @@
     is_last = place_ref[0] == 3
     full = far_bias(place_ref, rel_ref)
 
+    row = lax.broadcasted_iota(jnp.int32, (ROWS, LANES), 0)
+    lines = [jnp.broadcast_to(line_ref[h, 0:1], (ROWS, LANES)) for h in range(2)]
+
     def one(step, _):
+        offset = jnp.broadcast_to(asked_ref[step, 1:2], (ROWS, LANES)).astype(jnp.int32)
+        at = jnp.minimum(ROWS - row + offset, LANES - 1)
+        tail = jnp.concatenate([jnp.take_along_axis(line, at, axis=1) for line in lines], axis=1)
+        tail_ref[step] = tail
         stacked, split = queries(got_ref, chosen_ref, step)
-        parts = [dot(keys[...], split) + jnp.where(is_last, tail_ref[step], full)]
+        parts = [dot(keys[...], split) + jnp.where(is_last, tail, full)]
         near_scores = dot(kwin[pl.ds(step, 3)].reshape(3 * ROWS, LANES), stacked)
         for b in range(3):
             at_edge = (step + b == 0) | (step + b == PAIRS + 1)
@@ -322,10 +325,11 @@
     return pl.pallas_call(
         own_kernel,
         in_specs=[SMEM_SPEC] * 4 + [VMEM_SPEC] * 6 + [HBM_SPEC],
-        out_specs=(VMEM_SPEC,) * 3,
+        out_specs=(VMEM_SPEC,) * 4,
         out_shape=(
             pltpu.VMEM((PAIRS, 8, 2 * ROWS), jnp.float32),
             pltpu.VMEM((PAIRS, LANES, ROWS), jnp.float32),
+            pltpu.VMEM((PAIRS, ROWS, 2 * ROWS), jnp.float32),
         )
         + tuple(pltpu.VMEM(w.shape, w.dtype) for w in later_weights),
         scratch_shapes=[
@@ -342,8 +346,8 @@
 
 
 def rest_kernel(
-    x_ref, pair_ref, side_ref, rel_ref, got_ref, prev_ref, next_ref, far_ref, near_ref, name_ref, asked_ref, tail_ref, chosen_ref,
-    stat_ref, acc_ref, _, out_ref, keys, values, kwin, vwin,
+    x_ref, pair_ref, side_ref, rel_ref, got_ref, prev_ref, next_ref, far_ref, near_ref, name_ref, asked_ref, chosen_ref,
+    stat_ref, acc_ref, tail_ref, _, out_ref, keys, values, kwin, vwin,
 ):
     place_ref = (x_ref[0], pair_ref[0], side_ref[0])
     turns = ((3, prev_ref), (1, next_ref), (2, far_ref))
@@ -411,7 +415,7 @@
         compiler_params=pltpu.CompilerParams(vmem_limit_bytes=VMEM_LIMIT),
         cost_estimate=COST,
         name="attend_rest",
-    )(*place, rel_bias.T, *on_chip(got, prev, after_it, far, *made, *part, ready))
+    )(*place, rel_bias.T, *on_chip(got, prev, after_it, far, *made[:3], made[4], *part, ready))
 
 
 def finish_kernel(away, side_ref, att_ref, w_ref, tok_ref, gain_ref, in_one, in_two, out_one, out_two, *rest):
@@ -492,8 +496,8 @@
     prev = lax.ppermute(up, "x", by(1))
     later = lax.ppermute(down, "x", by(-1))
     far_tokens = lax.ppermute(same, mirrored, MIRROR)
-    stat, acc, other_out = attend_own(place, rel_bias, got, made, (other_out,))
-    mixed = attend_rest(place, rel_bias, got, prev, later, opposite, made, (stat, acc), far_tokens)
+    *part, other_out = attend_own(place, rel_bias, got, made, (other_out,))
+    mixed = attend_rest(place, rel_bias, got, prev, later, opposite, made, part, far_tokens)
     weights = (w_in, other_in, w_out, other_out)
     att = lax.all_to_all(mixed, ("yhi",) + PLANE, 0, 0, tiled=True)
 

time: 68.4 us -> 67.8 us (level)
  no operation moved by 1% of the time
where the time goes in v10:
time: 67.8 us; the launch traced here: 67.6 us
  blocking collectives  33.5 us (49%)
  Pallas kernels  19.2 us (28%)
  starting transfers between devices  9.16 us (14%)
  waiting for transfers between devices  5.6 us (8%)
    all_to_all x1, blocking collectives, body(): got = lax.all_to_all(blocks, PLANE, 0, 0, tiled=True)  20.8 us
    all_to_all x1, blocking collectives, body(): att = lax.all_to_all(mixed, ('yhi',) + PLANE, 0, 0, tiled=True)  12.8 us
    pallas_call x2, Pallas kernels, finish(): pl.pallas_call(functools.partial(finish_kernel, away), in_specs=[SMEM_SPE...  5.18 us
    pallas_call x1, Pallas kernels, project(): pl.pallas_call(project_kernel, in_specs=[SMEM_SPEC] * 3 + [HBM_SPEC] * 9,...  4.77 us
    pallas_call x1, Pallas kernels, attend_rest(): pl.pallas_call(rest_kernel, in_specs=[SMEM_SPEC] * 4 + [VMEM_SPEC] * 12,...  4.61 us
    pallas_call x1, Pallas kernels, attend_own(): pl.pallas_call(own_kernel, in_specs=[SMEM_SPEC] * 4 + [VMEM_SPEC] * 6 + [...  3.8 us
    ppermute x1, waiting for transfers between devices, body(): back = lax.ppermute(far_sum, mirrored, MIRROR)  3.72 us
    ppermute x1, starting transfers between devices, body(): far_tokens = lax.ppermute(same, mirrored, MIRROR)  2.27 us
  transfers between devices with their start and end apart: 7, of which 2 were waited for; matrix products, arithmetic and copies ran while one was open for 0% of the time, Pallas kernels for 17%

profile of v10, /device:TPU:0, one launch (start us, length us, event | category | flops | bytes accessed | tf_op | source)
XLA Modules:
  0.0 67.6 jit_solution(6098697188203059118)
XLA Ops:
  0.0 0.0 collective-permute-start.1
  0.0 0.5 collective-permute-start
  0.5 0.0 copy-start.3
  0.5 4.8 %project.1 = (bf16[8,448,128]{2,1,0:T(8,128)(2,1)S(1)}, f32[384,256]{1,0:T(8,128)S(1)}, bf16[10,128,128]{2,1,0:T(8,128)(2,1)S(1)}, f32[8,8,128]{2,1,0:T(8,128)S(...) custom-call(s32[1]{0:T(128)} %bitcast.1.x_ref, s32[1]{0:T(128)} %bitcast.2.pair_ref, s32[1]{0:T(128)} %bitcast.side_ref, ...), custom_call_target="tpu_custom_call" | custom-call | flops 1000 | bytes 1000 | tf_op jit(solution)/shard_map/project/pallas_call | solution.py:171
  5.3 20.8 %all_to_all.10.got_ref = bf16[8,448,128]{2,1,0:T(8,128)(2,1)S(1)} all-to-all(bf16[8,448,128]{2,1,0:T(8,128)(2,1)S(1)} %get-tuple-element.19), channel_id=1, replica_groups=mesh['yhi'=2,'core'=2,'x'=4,'z'=4,'ylo'=2] {'z','ylo'}, dimensions={0} | all-to-all | bytes 1835008 | tf_op jit(solution)/shard_map/all_to_all | solution.py:491
  26.1 0.0 copy-start.4
  26.1 0.0 collective-permute-done.1.rest_1_.w1_hbm
  26.1 0.0 collective-permute-done.rest_0_.in_two
  26.1 0.0 copy-done.3
  26.1 0.1 spread.1
  26.2 2.3 %collective-permute-start.5 = (bf16[128,1024]{1,0:T(8,128)(2,1)S(1)}, bf16[128,1024]{1,0:T(8,128)(2,1)S(1)}, u32[]{:S(2)}, u32[]{:S(2)}) collective-permute-start(bf16[128,1024]{1,0:T(8,128)(2,1)S(1)} %get-tuple-element.31), channel_id=1, source_target_pairs={{0,65},{65,0},{1,64},{64,1},{2,67},{67,2},{3,66},{66,3},{4,69},{69... | collective-permute-start | bytes 786440 | tf_op jit(solution)/shard_map/ppermute | solution.py:498
  28.5 1.5 %collective-permute-start.2 = (bf16[768,128]{1,0:T(8,128)(2,1)S(1)}, bf16[768,128]{1,0:T(8,128)(2,1)S(1)}, u32[]{:S(2)}, u32[]{:S(2)}) collective-permute-start(bf16[768,128]{1,0:T(8,128)(2,1)S(1)} %get-tuple-element.20), channel_id=1, source_target_pairs={{0,8},{8,16},{16,24},{24,0},{1,9},{9,17},{17,25},{25,1},{2,10},{10... | collective-permute-start | bytes 589832 | tf_op jit(solution)/shard_map/ppermute | solution.py:496
  29.9 1.8 %collective-permute-start.3 = (bf16[768,128]{1,0:T(8,128)(2,1)S(1)}, bf16[768,128]{1,0:T(8,128)(2,1)S(1)}, u32[]{:S(2)}, u32[]{:S(2)}) collective-permute-start(bf16[768,128]{1,0:T(8,128)(2,1)S(1)} %get-tuple-element.21), channel_id=1, source_target_pairs={{0,24},{8,0},{16,8},{24,16},{1,25},{9,1},{17,9},{25,17},{2,26},{10... | collective-permute-start | bytes 589832 | tf_op jit(solution)/shard_map/ppermute | solution.py:497
  31.7 1.8 %collective-permute-start.4 = (bf16[512,128]{1,0:T(8,128)(2,1)S(1)}, bf16[512,128]{1,0:T(8,128)(2,1)S(1)}, u32[]{:S(2)}, u32[]{:S(2)}) collective-permute-start(bf16[512,128]{1,0:T(8,128)(2,1)S(1)} %get-tuple-element.22), channel_id=1, source_target_pairs={{0,16},{8,24},{16,0},{24,8},{1,17},{9,25},{17,1},{25,9},{2,18},{10... | collective-permute-start | bytes 393224 | tf_op jit(solution)/shard_map/ppermute | solution.py:495
  33.5 0.0 copy-done.4
  33.5 0.0 copy-start.2
  33.5 3.8 %attend_own.1 = (f32[8,8,256]{2,1,0:T(8,128)S(1)}, f32[8,128,128]{2,1,0:T(8,128)S(1)}, f32[8,128,256]{2,1,0:T(8,128)S(1)}, bf16[1024,1024]{1,0:T(8,128)(2,1)S(1)}) custom-call(s32[1]{0:T(128)} %bitcast.1.x_ref, s32[1]{0:T(128)} %bitcast.2.pair_ref, s32[1]{0:T(128)} %bitcast.side_ref, f32[16,32]{1,0:T(8,128)S(1)} %bitcast.7, ...), custom_call_target="tpu_custom_call" | custom-call | flops 1000 | bytes 1000 | tf_op jit(solution)/shard_map/attend_own/pallas_call | solution.py:325
  37.3 1.9 %collective-permute-done.4.far_ref = bf16[512,128]{1,0:T(8,128)(2,1)S(1)} collective-permute-done((bf16[512,128]{1,0:T(8,128)(2,1)S(1)}, bf16[512,128]{1,0:T(8,128)(2,1)S(1)}, u32[]{:S(2)}, u32[]{:S(2)}) %collective-permute-start.4) | collective-permute-done | bytes 131104 | tf_op jit(solution)/shard_map/ppermute | solution.py:495
  39.2 0.0 collective-permute-done.2.prev_ref
  39.2 0.0 collective-permute-done.3.next_ref
  39.2 0.0 collective-permute-done.5._.tok_ref
  39.2 0.0 copy-start
  39.2 0.0 copy-start.1
  39.2 0.0 copy-start.5
  39.2 4.6 %attend_rest.1 = bf16[16,128,128]{2,1,0:T(8,128)(2,1)S(1)} custom-call(s32[1]{0:T(128)} %bitcast.1.x_ref, s32[1]{0:T(128)} %bitcast.2.pair_ref, s32[1]{0:T(128)} %bitcast.side_ref, f32[16,32]{1,0:T(8,128)S(1)} %bitcast.8, bf16[8,448,128]{2,1,0:T(8,128)(2,1)S(1)} %all_to_all.10.got_ref, bf16[768,128]{1,0:T(8,128)(2,1)S(1)} %collective-permute-done.2.prev_ref, ...), custom_call_target="tpu_custom_call" | custom-call | flops 1000 | bytes 1000 | tf_op jit(solution)/shard_map/attend_rest/pallas_call | solution.py:404
  43.8 12.8 %all_to_all.11.att_ref = bf16[16,128,128]{2,1,0:T(8,128)(2,1)S(1)} all-to-all(bf16[16,128,128]{2,1,0:T(8,128)(2,1)S(1)} %attend_rest.1), channel_id=1, replica_groups=mesh['yhi'=2,'core'=2,'x'=4,'z'=4,'ylo'=2] {'yhi','z','ylo'}, dimensions={0} | all-to-all | bytes 1048576 | tf_op jit(solution)/shard_map/all_to_all | solution.py:502
  56.6 0.0 copy-done.2
  56.6 0.0 copy-done
  56.6 0.0 copy-done.1
  56.6 0.0 copy-done.5
  56.6 2.6 %finish.2.rest_0_ = bf16[128,1024]{1,0:T(8,128)(2,1)S(1)} custom-call(s32[1]{0:T(128)} %bitcast.side_ref, bf16[16,128,128]{2,1,0:T(8,128)(2,1)S(1)} %all_to_all.11.att_ref, bf16[1024,1024]{1,0:T(8,128)(2,1)S(1)} %copy-done.2, bf16[128,1024]{1,0:T(8,128)(2,1)S(1)} %collective-permute-done.5._.tok_ref, f32[1,1024]{1,0:T(1,128)S(1)} %bitcast.9, ...), custom_call_target="tpu_custom_call" | custom-call | flops 1000 | bytes 1000 | tf_op jit(solution)/shard_map/finish/pallas_call | solution.py:437
  59.2 1.3 %collective-permute-start.6 = (bf16[128,1024]{1,0:T(8,128)(2,1)S(1)}, bf16[128,1024]{1,0:T(8,128)(2,1)S(1)}, u32[]{:S(2)}, u32[]{:S(2)}) collective-permute-start(bf16[128,1024]{1,0:T(8,128)(2,1)S(1)} %finish.2.rest_0_), channel_id=1, source_target_pairs={{0,65},{65,0},{1,64},{64,1},{2,67},{67,2},{3,66},{66,3},{4,69},{69... | collective-permute-start | bytes 786440 | tf_op jit(solution)/shard_map/ppermute | solution.py:505
  60.6 2.6 %finish.3.refs_0_ = f32[128,1024]{1,0:T(8,128)S(1)} custom-call(s32[1]{0:T(128)} %bitcast.side_ref, bf16[16,128,128]{2,1,0:T(8,128)(2,1)S(1)} %all_to_all.11.att_ref, bf16[1024,1024]{1,0:T(8,128)(2,1)S(1)} %copy-done.2, bf16[128,1024]{1,0:T(8,128)(2,1)S(1)} %copy-done.3, f32[1,1024]{1,0:T(1,128)S(1)} %bitcast.10, bf16[1024,1024]{1,0:T(8,128)(2,1)S(1)} %copy-done, ...), custom_call_target="tpu_custom_call" | custom-call | flops 1000 | bytes 1000 | tf_op jit(solution)/shard_map/finish/pallas_call | solution.py:437
  63.2 3.7 %collective-permute-done.6.refs_1_ = bf16[128,1024]{1,0:T(8,128)(2,1)S(1)} collective-permute-done((bf16[128,1024]{1,0:T(8,128)(2,1)S(1)}, bf16[128,1024]{1,0:T(8,128)(2,1)S(1)}, u32[]{:S(2)}, u32[]{:S(2)}) %collective-permute-start.6) | collective-permute-done | bytes 262176 | tf_op jit(solution)/shard_map/ppermute | solution.py:505
  66.9 0.7 %total.1 = bf16[128,1024]{1,0:T(8,128)(2,1)} custom-call(f32[128,1024]{1,0:T(8,128)S(1)} %finish.3.refs_0_, bf16[128,1024]{1,0:T(8,128)(2,1)S(1)} %collective-permute-done.6.refs_1_), custom_call_target="tpu_custom_call" | custom-call | flops 1000 | bytes 1000 | tf_op jit(solution)/shard_map/total/pallas_call | solution.py:455
Async XLA Ops:
  0.0 26.1 %collective-permute-start.1 = (bf16[1024,1024]{1,0:T(8,128)(2,1)}, bf16[1024,1024]{1,0:T(8,128)(2,1)}, u32[]{:S(2)}, u32[]{:S(2)}) collective-permute-start(bf16[1024,1024]{1,0:T(8,128)(2,1)} %out_one.3), channel_id=1, source_target_pairs={{0,32},{32,0},{1,33},{33,1},{2,34},{34,2},{3,35},{35,3},{4,36},{36... | collective-permute-start | bytes 6291464 | tf_op jit(solution)/shard_map/ppermute | solution.py:487
  0.0 26.1 %collective-permute-start = (bf16[1024,1024]{1,0:T(8,128)(2,1)}, bf16[1024,1024]{1,0:T(8,128)(2,1)S(1)}, u32[]{:S(2)}, u32[]{:S(2)}) collective-permute-start(bf16[1024,1024]{1,0:T(8,128)(2,1)} %in_one.3), channel_id=1, source_target_pairs={{0,32},{32,0},{1,33},{33,1},{2,34},{34,2},{3,35},{35,3},{4,36},{36... | collective-permute-start | bytes 6291464 | tf_op jit(solution)/shard_map/ppermute | solution.py:486
  0.5 25.6 %copy-start.3 = (bf16[128,1024]{1,0:T(8,128)(2,1)S(1)}, bf16[128,1024]{1,0:T(8,128)(2,1)}, u32[]{:S(2)}) copy-start(bf16[128,1024]{1,0:T(8,128)(2,1)} %tok_ref.3) | copy-start | bytes 786436
  26.1 7.4 %copy-start.4 = (f32[32,16]{0,1:T(8,128)S(1)}, f32[32,16]{0,1:T(8,128)}, u32[]{:S(2)}) copy-start(f32[32,16]{0,1:T(8,128)} %param.19) | copy-start | bytes 6148
  26.2 13.0 %collective-permute-start.5 = (bf16[128,1024]{1,0:T(8,128)(2,1)S(1)}, bf16[128,1024]{1,0:T(8,128)(2,1)S(1)}, u32[]{:S(2)}, u32[]{:S(2)}) collective-permute-start(bf16[128,1024]{1,0:T(8,128)(2,1)S(1)} %get-tuple-element.31), channel_id=1, source_target_pairs={{0,65},{65,0},{1,64},{64,1},{2,67},{67,2},{3,66},{66,3},{4,69},{69... | collective-permute-start | bytes 786440 | tf_op jit(solution)/shard_map/ppermute | solution.py:498
  28.5 10.7 %collective-permute-start.2 = (bf16[768,128]{1,0:T(8,128)(2,1)S(1)}, bf16[768,128]{1,0:T(8,128)(2,1)S(1)}, u32[]{:S(2)}, u32[]{:S(2)}) collective-permute-start(bf16[768,128]{1,0:T(8,128)(2,1)S(1)} %get-tuple-element.20), channel_id=1, source_target_pairs={{0,8},{8,16},{16,24},{24,0},{1,9},{9,17},{17,25},{25,1},{2,10},{10... | collective-permute-start | bytes 589832 | tf_op jit(solution)/shard_map/ppermute | solution.py:496
  29.9 9.2 %collective-permute-start.3 = (bf16[768,128]{1,0:T(8,128)(2,1)S(1)}, bf16[768,128]{1,0:T(8,128)(2,1)S(1)}, u32[]{:S(2)}, u32[]{:S(2)}) collective-permute-start(bf16[768,128]{1,0:T(8,128)(2,1)S(1)} %get-tuple-element.21), channel_id=1, source_target_pairs={{0,24},{8,0},{16,8},{24,16},{1,25},{9,1},{17,9},{25,17},{2,26},{10... | collective-permute-start | bytes 589832 | tf_op jit(solution)/shard_map/ppermute | solution.py:497
  31.7 7.5 %collective-permute-start.4 = (bf16[512,128]{1,0:T(8,128)(2,1)S(1)}, bf16[512,128]{1,0:T(8,128)(2,1)S(1)}, u32[]{:S(2)}, u32[]{:S(2)}) collective-permute-start(bf16[512,128]{1,0:T(8,128)(2,1)S(1)} %get-tuple-element.22), channel_id=1, source_target_pairs={{0,16},{8,24},{16,0},{24,8},{1,17},{9,25},{17,1},{25,9},{2,18},{10... | collective-permute-start | bytes 393224 | tf_op jit(solution)/shard_map/ppermute | solution.py:495
  33.5 23.1 %copy-start.2 = (bf16[1024,1024]{1,0:T(8,128)(2,1)S(1)}, bf16[1024,1024]{1,0:T(8,128)(2,1)}, u32[]{:S(2)}) copy-start(bf16[1024,1024]{1,0:T(8,128)(2,1)} %w_ref.3) | copy-start | bytes 6291460
  39.2 17.4 %copy-start = (bf16[1024,1024]{1,0:T(8,128)(2,1)S(1)}, bf16[1024,1024]{1,0:T(8,128)(2,1)}, u32[]{:S(2)}) copy-start(bf16[1024,1024]{1,0:T(8,128)(2,1)} %in_one.3) | copy-start | bytes 6291460
  39.2 17.4 %copy-start.1 = (bf16[1024,1024]{1,0:T(8,128)(2,1)S(1)}, bf16[1024,1024]{1,0:T(8,128)(2,1)}, u32[]{:S(2)}) copy-start(bf16[1024,1024]{1,0:T(8,128)(2,1)} %out_one.3) | copy-start | bytes 6291460
  39.2 17.4 %copy-start.5 = (f32[1024]{0:T(1024)S(1)}, f32[1024]{0:T(1024)}, u32[]{:S(2)}) copy-start(f32[1024]{0:T(1024)} %param.23) | copy-start | bytes 12292
  59.2 7.7 %collective-permute-start.6 = (bf16[128,1024]{1,0:T(8,128)(2,1)S(1)}, bf16[128,1024]{1,0:T(8,128)(2,1)S(1)}, u32[]{:S(2)}, u32[]{:S(2)}) collective-permute-start(bf16[128,1024]{1,0:T(8,128)(2,1)S(1)} %finish.2.rest_0_), channel_id=1, source_target_pairs={{0,65},{65,0},{1,64},{64,1},{2,67},{67,2},{3,66},{66,3},{4,69},{69... | collective-permute-start | bytes 786440 | tf_op jit(solution)/shard_map/ppermute | solution.py:505

commit v11 on v10

--- a/solution.py
+++ b/solution.py
@@ -15,6 +15,7 @@
 ROWS = 128
 PAIRS = 8
 LANES = 128
+FIRST = 640
 SHARE = 16
 SENT = 3 * ROWS + 2 * PREF_GRP * SHARE
 QUARTER = PAIRS * 2 * PREF_GRP * SHARE
@@ -275,7 +276,7 @@
 
 def own_kernel(
     x_ref, pair_ref, side_ref, rel_ref, got_ref, near_ref, name_ref, asked_ref, line_ref, chosen_ref, w1_hbm,
-    stat_ref, acc_ref, tail_ref, w1_ref, keys, values, kwin, vwin, landed,
+    stat_ref, acc_ref, tail_ref, split_ref, w1_ref, keys, values, kwin, vwin, landed,
 ):
     place_ref = (x_ref[0], pair_ref[0], side_ref[0])
     copies = start_copies(((w1_hbm, w1_ref),), landed)
@@ -298,6 +299,7 @@
         tail = jnp.concatenate([jnp.take_along_axis(line, at, axis=1) for line in lines], axis=1)
         tail_ref[step] = tail
         stacked, split = queries(got_ref, chosen_ref, step)
+        split_ref[step] = split
         parts = [dot(keys[...], split) + jnp.where(is_last, tail, full)]
         near_scores = dot(kwin[pl.ds(step, 3)].reshape(3 * ROWS, LANES), stacked)
         for b in range(3):
@@ -325,11 +327,12 @@
     return pl.pallas_call(
         own_kernel,
         in_specs=[SMEM_SPEC] * 4 + [VMEM_SPEC] * 6 + [HBM_SPEC],
-        out_specs=(VMEM_SPEC,) * 4,
+        out_specs=(VMEM_SPEC,) * 5,
         out_shape=(
             pltpu.VMEM((PAIRS, 8, 2 * ROWS), jnp.float32),
             pltpu.VMEM((PAIRS, LANES, ROWS), jnp.float32),
             pltpu.VMEM((PAIRS, ROWS, 2 * ROWS), jnp.float32),
+            pltpu.VMEM((PAIRS, PREF_GRP * LANES, 2 * ROWS), jnp.bfloat16),
         )
         + tuple(pltpu.VMEM(w.shape, w.dtype) for w in later_weights),
         scratch_shapes=[
@@ -346,8 +349,8 @@
 
 
 def rest_kernel(
-    x_ref, pair_ref, side_ref, rel_ref, got_ref, prev_ref, next_ref, far_ref, near_ref, name_ref, asked_ref, chosen_ref,
-    stat_ref, acc_ref, tail_ref, _, out_ref, keys, values, kwin, vwin,
+    x_ref, pair_ref, side_ref, rel_ref, prev_ref, next_ref, far_ref, near_ref, name_ref, asked_ref,
+    stat_ref, acc_ref, tail_ref, split_ref, _, out_ref, keys, values, kwin, vwin,
 ):
     place_ref = (x_ref[0], pair_ref[0], side_ref[0])
     turns = ((3, prev_ref), (1, next_ref), (2, far_ref))
@@ -363,7 +366,7 @@
     full = far_bias(place_ref, rel_ref)
 
     def one(step, edge=None):
-        stacked, split = queries(got_ref, chosen_ref, step)
+        split = split_ref[step]
         tail = tail_ref[step]
         scores = dot(keys[...].reshape(3 * PLEN // 4, PREF_GRP * LANES), split)
         parts = [
@@ -372,7 +375,7 @@
         if edge is not None:
             bias = near_ref[edge * 2 * ROWS : (edge * 2 + 1) * ROWS]
             parts.append(
-                masked(dot(kwin[edge], stacked), name_ref, edge * (PAIRS + 1), asked_ref, step, bias)
+                masked(dot(kwin[edge], split[:LANES] + split[LANES:]), name_ref, edge * (PAIRS + 1), asked_ref, step, bias)
             )
         before = stat_ref[step, 0:1]
         top = jnp.max(functools.reduce(jnp.maximum, parts), axis=0, keepdims=True)
@@ -400,10 +403,10 @@
     one(jnp.int32(PAIRS - 1), 1)
 
 
-def attend_rest(place, rel_bias, got, prev, after_it, far, made, part, ready):
+def attend_rest(place, rel_bias, prev, after_it, far, made, part, ready):
     return pl.pallas_call(
         rest_kernel,
-        in_specs=[SMEM_SPEC] * 4 + [VMEM_SPEC] * 12,
+        in_specs=[SMEM_SPEC] * 4 + [VMEM_SPEC] * 11,
         out_specs=VMEM_SPEC,
         out_shape=pltpu.VMEM((2 * PAIRS, ROWS, LANES), jnp.bfloat16),
         scratch_shapes=[
@@ -415,52 +418,97 @@
         compiler_params=pltpu.CompilerParams(vmem_limit_bytes=VMEM_LIMIT),
         cost_estimate=COST,
         name="attend_rest",
-    )(*place, rel_bias.T, *on_chip(got, prev, after_it, far, *made[:3], made[4], *part, ready))
-
-
-def finish_kernel(away, side_ref, att_ref, w_ref, tok_ref, gain_ref, in_one, in_two, out_one, out_two, *rest):
-    at = (1 - side_ref[0] if away else side_ref[0]) * PAIRS
-    attended = jnp.concatenate([att_ref[at + j] for j in range(PAIRS)], axis=1)
-    hidden = (tok_ref[...].astype(jnp.float32) + dot(attended, w_ref[...])).astype(jnp.bfloat16)
+    )(*place, rel_bias.T, *on_chip(prev, after_it, far, *made[:3], *part, ready))
+
+
+def join(side, att_ref, w_ref, tok_ref):
+    attended = jnp.concatenate([att_ref[side * PAIRS + j] for j in range(PAIRS)], axis=1)
+    return (tok_ref[...].astype(jnp.float32) + dot(attended, w_ref[...])).astype(jnp.bfloat16)
+
+
+def units_of(normed, in_ref):
+    units = lax.dot_general(
+        normed, in_ref[...], (((1,), (1,)), ((), ())), preferred_element_type=jnp.float32
+    )
+    return jnp.maximum(units, 0.0).astype(jnp.bfloat16)
+
+
+def finish_kernel(side_ref, att_ref, w_ref, tok_ref, gain_ref, in_one, in_two, out_one, out_two, *rest):
+    hidden = join(side_ref[0], att_ref, w_ref, tok_ref)
     normed = norm_rows(hidden, gain_ref[...])
-    got = None if away else hidden.astype(jnp.float32)
+    got = hidden.astype(jnp.float32)
     for in_ref, out_w_ref in ((in_one, out_one), (in_two, out_two)):
-        units = lax.dot_general(
-            normed, in_ref[...], (((1,), (1,)), ((), ())), preferred_element_type=jnp.float32
-        )
-        part = dot(jnp.maximum(units, 0.0).astype(jnp.bfloat16), out_w_ref[...])
-        got = part if got is None else got + part
-    rest[-1][...] = got.astype(rest[-1].dtype)
-
-
-def finish(away, side, att, w_attn_out, tokens, gain, weights, *ready):
-    return pl.pallas_call(
-        functools.partial(finish_kernel, away),
+        got = got + dot(units_of(normed, in_ref), out_w_ref[...])
+    rest[-1][...] = got
+
+
+def finish(side, att, w_attn_out, tokens, gain, weights, *ready):
+    return pl.pallas_call(
+        finish_kernel,
         in_specs=[SMEM_SPEC] + [VMEM_SPEC] * (8 + len(ready)),
         out_specs=VMEM_SPEC,
-        out_shape=pltpu.VMEM((ROWS, D), jnp.bfloat16 if away else jnp.float32),
+        out_shape=pltpu.VMEM((ROWS, D), jnp.float32),
         compiler_params=pltpu.CompilerParams(vmem_limit_bytes=VMEM_LIMIT),
         cost_estimate=COST,
         name="finish",
     )(side, *on_chip(att, w_attn_out, tokens, gain.reshape(1, D), *weights, *ready))
 
 
-def total_kernel(*refs):
-    out_ref = refs[-1]
-    total = functools.reduce(jnp.add, [ref[...].astype(jnp.float32) for ref in refs[:-1]])
-    out_ref[...] = total.astype(out_ref.dtype)
-
-
-def total(dtype, *arrays, last=False):
+def away_kernel(
+    side_ref, att_ref, w_ref, tok_ref, gain_ref, in_one, in_two, out_one, out_two, half_ref, units_ref
+):
+    hidden = join(1 - side_ref[0], att_ref, w_ref, tok_ref)
+    normed = norm_rows(hidden, gain_ref[...])
+    units_ref[0] = units_of(normed, in_one)
+    units_ref[1] = units_of(normed, in_two)
+    got = dot(units_ref[0], out_one[:, :FIRST]) + dot(units_ref[1], out_two[:, :FIRST])
+    half_ref[...] = got.astype(half_ref.dtype)
+
+
+def away(side, att, w_attn_out, tokens, gain, weights):
+    return pl.pallas_call(
+        away_kernel,
+        in_specs=[SMEM_SPEC] + [VMEM_SPEC] * 8,
+        out_specs=(VMEM_SPEC,) * 2,
+        out_shape=(pltpu.VMEM((ROWS, FIRST), jnp.bfloat16), pltpu.VMEM((2, ROWS, D), jnp.bfloat16)),
+        compiler_params=pltpu.CompilerParams(vmem_limit_bytes=VMEM_LIMIT),
+        cost_estimate=COST,
+        name="away",
+    )(side, *on_chip(att, w_attn_out, tokens, gain.reshape(1, D), *weights))
+
+
+def remainder_kernel(units_ref, out_one, out_two, half_ref):
+    got = dot(units_ref[0], out_one[:, FIRST:]) + dot(units_ref[1], out_two[:, FIRST:])
+    half_ref[...] = got.astype(half_ref.dtype)
+
+
+def remainder(units, out_one, out_two):
+    return pl.pallas_call(
+        remainder_kernel,
+        in_specs=[VMEM_SPEC] * 3,
+        out_specs=VMEM_SPEC,
+        out_shape=pltpu.VMEM((ROWS, D - FIRST), jnp.bfloat16),
+        compiler_params=pltpu.CompilerParams(vmem_limit_bytes=VMEM_LIMIT),
+        cost_estimate=COST,
+        name="remainder",
+    )(*on_chip(units, out_one, out_two))
+
+
+def total_kernel(home_ref, first_ref, second_ref, out_ref):
+    for cut, ref in ((slice(0, FIRST), first_ref), (slice(FIRST, D), second_ref)):
+        out_ref[:, cut] = (home_ref[:, cut] + ref[...].astype(jnp.float32)).astype(jnp.bfloat16)
+
+
+def total(home, first, second):
     return pl.pallas_call(
         total_kernel,
-        in_specs=[VMEM_SPEC] * len(arrays),
+        in_specs=[VMEM_SPEC] * 3,
         out_specs=VMEM_SPEC,
-        out_shape=(jax.ShapeDtypeStruct if last else pltpu.VMEM)(arrays[0].shape, dtype),
+        out_shape=jax.ShapeDtypeStruct((ROWS, D), jnp.bfloat16),
         compiler_params=pltpu.CompilerParams(vmem_limit_bytes=VMEM_LIMIT),
         cost_estimate=COST,
         name="total",
-    )(*on_chip(*arrays))
+    )(*on_chip(home, first, second))
 
 
 def body(
@@ -497,14 +545,16 @@
     later = lax.ppermute(down, "x", by(-1))
     far_tokens = lax.ppermute(same, mirrored, MIRROR)
     *part, other_out = attend_own(place, rel_bias, got, made, (other_out,))
-    mixed = attend_rest(place, rel_bias, got, prev, later, opposite, made, part, far_tokens)
+    mixed = attend_rest(place, rel_bias, prev, later, opposite, made, part, far_tokens)
     weights = (w_in, other_in, w_out, other_out)
     att = lax.all_to_all(mixed, ("yhi",) + PLANE, 0, 0, tiled=True)
 
-    far_sum = finish(True, place[2], att, w_attn_out, far_tokens, mlp_gain, weights)
-    back = lax.ppermute(far_sum, mirrored, MIRROR)
-    local = finish(False, place[2], att, w_attn_out, tokens, mlp_gain, weights, far_sum)
-    return total(jnp.bfloat16, local, back, last=True)
+    first, units = away(place[2], att, w_attn_out, far_tokens, mlp_gain, weights)
+    first_back = lax.ppermute(first, mirrored, MIRROR)
+    second = remainder(units, *weights[2:])
+    second_back = lax.ppermute(second, mirrored, MIRROR)
+    local = finish(place[2], att, w_attn_out, tokens, mlp_gain, weights, second)
+    return total(local, first_back, second_back)
 
 
 def solution(mesh):

time: 67.8 us -> 67.6 us (level)
  waiting for transfers between devices: 5.6 us -> 3.08 us
  starting transfers between devices: 9.16 us -> 11.2 us
    ppermute x1 -> x2, waiting for transfers between devices: 3.72 us -> 1.26 us  [the longest x1 1.25 us: body(): second_back = lax.ppermute(second, mirrored, MIRROR)]
    ppermute x1 -> x2, starting transfers between devices: 1.34 us -> 3.4 us  [the longest x1 2.05 us: body(): second_back = lax.ppermute(second, mirrored, MIRROR)]
    pallas_call x4 -> x5, Pallas kernels: 10.5 us -> 10.7 us  [the longest x1 4.45 us: attend_rest(): pl.pallas_call(rest_kernel, in_specs=[SMEM_SPEC] * 4 + [VMEM_SPEC] * 11,...]
  transfers between devices with their start and end apart: 7 -> 8, of which waited for: 2 -> 2; matrix products, arithmetic and copies ran while one was open for 0% -> 0% of each run, Pallas kernels for 17% -> 17%
where the time goes in v11:
time: 67.6 us; the launch traced here: 67.4 us
  blocking collectives  33.5 us (50%)
  Pallas kernels  19.4 us (29%)
  starting transfers between devices  11.2 us (17%)
  waiting for transfers between devices  3.08 us (5%)
    all_to_all x1, blocking collectives, body(): got = lax.all_to_all(blocks, PLANE, 0, 0, tiled=True)  20.8 us
    all_to_all x1, blocking collectives, body(): att = lax.all_to_all(mixed, ('yhi',) + PLANE, 0, 0, tiled=True)  12.8 us
    pallas_call x1, Pallas kernels, project(): pl.pallas_call(project_kernel, in_specs=[SMEM_SPEC] * 3 + [HBM_SPEC] * 9,...  4.77 us
    pallas_call x1, Pallas kernels, attend_rest(): pl.pallas_call(rest_kernel, in_specs=[SMEM_SPEC] * 4 + [VMEM_SPEC] * 11,...  4.45 us
    pallas_call x1, Pallas kernels, attend_own(): pl.pallas_call(own_kernel, in_specs=[SMEM_SPEC] * 4 + [VMEM_SPEC] * 6 + [...  3.87 us
    pallas_call x1, Pallas kernels, finish(): pl.pallas_call(finish_kernel, in_specs=[SMEM_SPEC] + [VMEM_SPEC] * (8 + l...  2.59 us
    pallas_call x1, Pallas kernels, away(): pl.pallas_call(away_kernel, in_specs=[SMEM_SPEC] + [VMEM_SPEC] * 8, out_s...  2.47 us
    ppermute x1, starting transfers between devices, body(): far_tokens = lax.ppermute(same, mirrored, MIRROR)  2.27 us
  transfers between devices with their start and end apart: 8, of which 2 were waited for; matrix products, arithmetic and copies ran while one was open for 0% of the time, Pallas kernels for 17%

profile of v11, /device:TPU:0, one launch (start us, length us, event | category | flops | bytes accessed | tf_op | source)
XLA Modules:
  0.0 67.4 jit_solution(10387005742617596433)
XLA Ops:
  0.0 0.0 collective-permute-start.1
  0.0 0.5 collective-permute-start
  0.5 0.0 copy-start.3
  0.5 4.8 %project.1 = (bf16[8,448,128]{2,1,0:T(8,128)(2,1)S(1)}, f32[384,256]{1,0:T(8,128)S(1)}, bf16[10,128,128]{2,1,0:T(8,128)(2,1)S(1)}, f32[8,8,128]{2,1,0:T(8,128)S(...) custom-call(s32[1]{0:T(128)} %bitcast.1.x_ref, s32[1]{0:T(128)} %bitcast.2.pair_ref, s32[1]{0:T(128)} %bitcast.side_ref, ...), custom_call_target="tpu_custom_call" | custom-call | flops 1000 | bytes 1000 | tf_op jit(solution)/shard_map/project/pallas_call | solution.py:172
  5.3 20.8 %all_to_all.10.got_ref = bf16[8,448,128]{2,1,0:T(8,128)(2,1)S(1)} all-to-all(bf16[8,448,128]{2,1,0:T(8,128)(2,1)S(1)} %get-tuple-element.22), channel_id=1, replica_groups=mesh['yhi'=2,'core'=2,'x'=4,'z'=4,'ylo'=2] {'z','ylo'}, dimensions={0} | all-to-all | bytes 1835008 | tf_op jit(solution)/shard_map/all_to_all | solution.py:539
  26.1 0.0 copy-start.4
  26.1 0.0 collective-permute-done.1.rest_1_.w1_hbm
  26.1 0.0 collective-permute-done.rest_0_.in_two
  26.1 0.0 copy-done.3
  26.1 0.1 spread.1
  26.2 2.3 %collective-permute-start.5 = (bf16[128,1024]{1,0:T(8,128)(2,1)S(1)}, bf16[128,1024]{1,0:T(8,128)(2,1)S(1)}, u32[]{:S(2)}, u32[]{:S(2)}) collective-permute-start(bf16[128,1024]{1,0:T(8,128)(2,1)S(1)} %get-tuple-element.35), channel_id=1, source_target_pairs={{0,65},{65,0},{1,64},{64,1},{2,67},{67,2},{3,66},{66,3},{4,69},{69... | collective-permute-start | bytes 786440 | tf_op jit(solution)/shard_map/ppermute | solution.py:546
  28.5 1.5 %collective-permute-start.2 = (bf16[768,128]{1,0:T(8,128)(2,1)S(1)}, bf16[768,128]{1,0:T(8,128)(2,1)S(1)}, u32[]{:S(2)}, u32[]{:S(2)}) collective-permute-start(bf16[768,128]{1,0:T(8,128)(2,1)S(1)} %get-tuple-element.23), channel_id=1, source_target_pairs={{0,8},{8,16},{16,24},{24,0},{1,9},{9,17},{17,25},{25,1},{2,10},{10... | collective-permute-start | bytes 589832 | tf_op jit(solution)/shard_map/ppermute | solution.py:544
  29.9 1.8 %collective-permute-start.3 = (bf16[768,128]{1,0:T(8,128)(2,1)S(1)}, bf16[768,128]{1,0:T(8,128)(2,1)S(1)}, u32[]{:S(2)}, u32[]{:S(2)}) collective-permute-start(bf16[768,128]{1,0:T(8,128)(2,1)S(1)} %get-tuple-element.24), channel_id=1, source_target_pairs={{0,24},{8,0},{16,8},{24,16},{1,25},{9,1},{17,9},{25,17},{2,26},{10... | collective-permute-start | bytes 589832 | tf_op jit(solution)/shard_map/ppermute | solution.py:545
  31.7 1.8 %collective-permute-start.4 = (bf16[512,128]{1,0:T(8,128)(2,1)S(1)}, bf16[512,128]{1,0:T(8,128)(2,1)S(1)}, u32[]{:S(2)}, u32[]{:S(2)}) collective-permute-start(bf16[512,128]{1,0:T(8,128)(2,1)S(1)} %get-tuple-element.25), channel_id=1, source_target_pairs={{0,16},{8,24},{16,0},{24,8},{1,17},{9,25},{17,1},{25,9},{2,18},{10... | collective-permute-start | bytes 393224 | tf_op jit(solution)/shard_map/ppermute | solution.py:543
  33.5 0.0 copy-done.4
  33.5 0.0 copy-start.2
  33.5 3.9 %attend_own.1 = (f32[8,8,256]{2,1,0:T(8,128)S(1)}, f32[8,128,128]{2,1,0:T(8,128)S(1)}, f32[8,128,256]{2,1,0:T(8,128)S(1)}, bf16[8,256,256]{2,1,0:T(8,128)(2,1)S(1)}, bf16[1024,1024]{1,0:T(8,128)(2,1)S(1)}) custom-call(s32[1]{0:T(128)} %bitcast.1.x_ref, s32[1]{0:T(128)} %bitcast.2.pair_ref, s32[1]{0:T(128)} %bitcast.side_ref, f32[16,32]{1,0:T(8,128)S(1)} %bitcast.7, ...), custom_call_target="tpu_custom_call" | custom-call | flops 1000 | bytes 1000 | tf_op jit(solution)/shard_map/attend_own/pallas_call | solution.py:327
  37.4 1.8 %collective-permute-done.4.far_ref = bf16[512,128]{1,0:T(8,128)(2,1)S(1)} collective-permute-done((bf16[512,128]{1,0:T(8,128)(2,1)S(1)}, bf16[512,128]{1,0:T(8,128)(2,1)S(1)}, u32[]{:S(2)}, u32[]{:S(2)}) %collective-permute-start.4) | collective-permute-done | bytes 131104 | tf_op jit(solution)/shard_map/ppermute | solution.py:543
  39.2 0.0 collective-permute-done.2.prev_ref
  39.2 0.0 collective-permute-done.3.next_ref
  39.2 0.0 collective-permute-done.5._.tok_ref
  39.2 0.0 copy-start
  39.2 0.0 copy-start.1
  39.2 0.0 copy-start.5
  39.2 4.5 %attend_rest.1 = bf16[16,128,128]{2,1,0:T(8,128)(2,1)S(1)} custom-call(s32[1]{0:T(128)} %bitcast.1.x_ref, s32[1]{0:T(128)} %bitcast.2.pair_ref, s32[1]{0:T(128)} %bitcast.side_ref, f32[16,32]{1,0:T(8,128)S(1)} %bitcast.8, bf16[768,128]{1,0:T(8,128)(2,1)S(1)} %collective-permute-done.2.prev_ref, bf16[768,128]{1,0:T(8,128)(2,1)S(1)} %collective-permute-done.3.next_ref, ...), custom_call_target="tpu_custom_call" | custom-call | flops 1000 | bytes 1000 | tf_op jit(solution)/shard_map/attend_rest/pallas_call | solution.py:407
  43.7 12.8 %all_to_all.11.att_ref = bf16[16,128,128]{2,1,0:T(8,128)(2,1)S(1)} all-to-all(bf16[16,128,128]{2,1,0:T(8,128)(2,1)S(1)} %attend_rest.1), channel_id=1, replica_groups=mesh['yhi'=2,'core'=2,'x'=4,'z'=4,'ylo'=2] {'yhi','z','ylo'}, dimensions={0} | all-to-all | bytes 1048576 | tf_op jit(solution)/shard_map/all_to_all | solution.py:550
  56.4 0.0 copy-done.2
  56.4 0.0 copy-done
  56.4 0.0 copy-done.1
  56.5 0.0 copy-done.5
  56.5 2.5 %away.1 = (bf16[128,640]{1,0:T(8,128)(2,1)S(1)}, bf16[2,128,1024]{2,1,0:T(8,128)(2,1)S(1)}) custom-call(s32[1]{0:T(128)} %bitcast.side_ref, bf16[16,128,128]{2,1,0:T(8,128)(2,1)S(1)} %all_to_all.11.att_ref, bf16[1024,1024]{1,0:T(8,128)(2,1)S(1)} %copy-done.2, bf16[128,1024]{1,0:T(8,128)(2,1)S(1)} %collective-permute-done.5._.tok_ref, f32[1,1024]{1,0:T(1,128)S(1)} %bitcast.9, ...), custom_call_target="tpu_custom_call" | custom-call | flops 1000 | bytes 1000 | tf_op jit(solution)/shard_map/away/pallas_call | solution.py:469
  58.9 1.3 %collective-permute-start.6 = (bf16[128,640]{1,0:T(8,128)(2,1)S(1)}, bf16[128,640]{1,0:T(8,128)(2,1)S(1)}, u32[]{:S(2)}, u32[]{:S(2)}) collective-permute-start(bf16[128,640]{1,0:T(8,128)(2,1)S(1)} %get-tuple-element.38), channel_id=1, source_target_pairs={{0,65},{65,0},{1,64},{64,1},{2,67},{67,2},{3,66},{66,3},{4,69},{69... | collective-permute-start | bytes 491528 | tf_op jit(solution)/shard_map/ppermute | solution.py:553
  60.3 0.4 remainder.1.rest_0_
  60.7 2.1 %collective-permute-start.7 = (bf16[128,384]{1,0:T(8,128)(2,1)S(1)}, bf16[128,384]{1,0:T(8,128)(2,1)S(1)}, u32[]{:S(2)}, u32[]{:S(2)}) collective-permute-start(bf16[128,384]{1,0:T(8,128)(2,1)S(1)} %remainder.1.rest_0_), channel_id=1, source_target_pairs={{0,65},{65,0},{1,64},{64,1},{2,67},{67,2},{3,66},{66,3},{4,69},{69... | collective-permute-start | bytes 294920 | tf_op jit(solution)/shard_map/ppermute | solution.py:555
  62.8 2.6 %finish.1.home_ref = f32[128,1024]{1,0:T(8,128)S(1)} custom-call(s32[1]{0:T(128)} %bitcast.side_ref, bf16[16,128,128]{2,1,0:T(8,128)(2,1)S(1)} %all_to_all.11.att_ref, bf16[1024,1024]{1,0:T(8,128)(2,1)S(1)} %copy-done.2, bf16[128,1024]{1,0:T(8,128)(2,1)S(1)} %copy-done.3, f32[1,1024]{1,0:T(1,128)S(1)} %bitcast.10, bf16[1024,1024]{1,0:T(8,128)(2,1)S(1)} %copy-done.1, ...), custom_call_target="tpu_custom_call" | custom-call | flops 1000 | bytes 1000 | tf_op jit(solution)/shard_map/finish/pallas_call | solution.py:446
  65.4 1.3 %collective-permute-done.7.second_ref = bf16[128,384]{1,0:T(8,128)(2,1)S(1)} collective-permute-done((bf16[128,384]{1,0:T(8,128)(2,1)S(1)}, bf16[128,384]{1,0:T(8,128)(2,1)S(1)}, u32[]{:S(2)}, u32[]{:S(2)}) %collective-permute-start.7) | collective-permute-done | bytes 98336 | tf_op jit(solution)/shard_map/ppermute | solution.py:555
  66.6 0.0 collective-permute-done.6.first_ref
  66.6 0.8 %total.1 = bf16[128,1024]{1,0:T(8,128)(2,1)} custom-call(f32[128,1024]{1,0:T(8,128)S(1)} %finish.1.home_ref, bf16[128,640]{1,0:T(8,128)(2,1)S(1)} %collective-permute-done.6.first_ref, bf16[128,384]{1,0:T(8,128)(2,1)S(1)} %collective-permute-done.7.second_ref), custom_call_target="tpu_custom_call" | custom-call | flops 1000 | bytes 1000 | tf_op jit(solution)/shard_map/total/pallas_call | solution.py:503
Async XLA Ops:
  0.0 26.1 %collective-permute-start.1 = (bf16[1024,1024]{1,0:T(8,128)(2,1)}, bf16[1024,1024]{1,0:T(8,128)(2,1)}, u32[]{:S(2)}, u32[]{:S(2)}) collective-permute-start(bf16[1024,1024]{1,0:T(8,128)(2,1)} %out_one.5), channel_id=1, source_target_pairs={{0,32},{32,0},{1,33},{33,1},{2,34},{34,2},{3,35},{35,3},{4,36},{36... | collective-permute-start | bytes 6291464 | tf_op jit(solution)/shard_map/ppermute | solution.py:535
  0.0 26.1 %collective-permute-start = (bf16[1024,1024]{1,0:T(8,128)(2,1)}, bf16[1024,1024]{1,0:T(8,128)(2,1)S(1)}, u32[]{:S(2)}, u32[]{:S(2)}) collective-permute-start(bf16[1024,1024]{1,0:T(8,128)(2,1)} %in_one.3), channel_id=1, source_target_pairs={{0,32},{32,0},{1,33},{33,1},{2,34},{34,2},{3,35},{35,3},{4,36},{36... | collective-permute-start | bytes 6291464 | tf_op jit(solution)/shard_map/ppermute | solution.py:534
  0.5 25.6 %copy-start.3 = (bf16[128,1024]{1,0:T(8,128)(2,1)S(1)}, bf16[128,1024]{1,0:T(8,128)(2,1)}, u32[]{:S(2)}) copy-start(bf16[128,1024]{1,0:T(8,128)(2,1)} %tok_ref.3) | copy-start | bytes 786436
  26.1 7.4 %copy-start.4 = (f32[32,16]{0,1:T(8,128)S(1)}, f32[32,16]{0,1:T(8,128)}, u32[]{:S(2)}) copy-start(f32[32,16]{0,1:T(8,128)} %param.19) | copy-start | bytes 6148
  26.2 13.0 %collective-permute-start.5 = (bf16[128,1024]{1,0:T(8,128)(2,1)S(1)}, bf16[128,1024]{1,0:T(8,128)(2,1)S(1)}, u32[]{:S(2)}, u32[]{:S(2)}) collective-permute-start(bf16[128,1024]{1,0:T(8,128)(2,1)S(1)} %get-tuple-element.35), channel_id=1, source_target_pairs={{0,65},{65,0},{1,64},{64,1},{2,67},{67,2},{3,66},{66,3},{4,69},{69... | collective-permute-start | bytes 786440 | tf_op jit(solution)/shard_map/ppermute | solution.py:546
  28.5 10.7 %collective-permute-start.2 = (bf16[768,128]{1,0:T(8,128)(2,1)S(1)}, bf16[768,128]{1,0:T(8,128)(2,1)S(1)}, u32[]{:S(2)}, u32[]{:S(2)}) collective-permute-start(bf16[768,128]{1,0:T(8,128)(2,1)S(1)} %get-tuple-element.23), channel_id=1, source_target_pairs={{0,8},{8,16},{16,24},{24,0},{1,9},{9,17},{17,25},{25,1},{2,10},{10... | collective-permute-start | bytes 589832 | tf_op jit(solution)/shard_map/ppermute | solution.py:544
  29.9 9.2 %collective-permute-start.3 = (bf16[768,128]{1,0:T(8,128)(2,1)S(1)}, bf16[768,128]{1,0:T(8,128)(2,1)S(1)}, u32[]{:S(2)}, u32[]{:S(2)}) collective-permute-start(bf16[768,128]{1,0:T(8,128)(2,1)S(1)} %get-tuple-element.24), channel_id=1, source_target_pairs={{0,24},{8,0},{16,8},{24,16},{1,25},{9,1},{17,9},{25,17},{2,26},{10... | collective-permute-start | bytes 589832 | tf_op jit(solution)/shard_map/ppermute | solution.py:545
  31.7 7.5 %collective-permute-start.4 = (bf16[512,128]{1,0:T(8,128)(2,1)S(1)}, bf16[512,128]{1,0:T(8,128)(2,1)S(1)}, u32[]{:S(2)}, u32[]{:S(2)}) collective-permute-start(bf16[512,128]{1,0:T(8,128)(2,1)S(1)} %get-tuple-element.25), channel_id=1, source_target_pairs={{0,16},{8,24},{16,0},{24,8},{1,17},{9,25},{17,1},{25,9},{2,18},{10... | collective-permute-start | bytes 393224 | tf_op jit(solution)/shard_map/ppermute | solution.py:543
  33.5 22.9 %copy-start.2 = (bf16[1024,1024]{1,0:T(8,128)(2,1)S(1)}, bf16[1024,1024]{1,0:T(8,128)(2,1)}, u32[]{:S(2)}) copy-start(bf16[1024,1024]{1,0:T(8,128)(2,1)} %w_ref.3) | copy-start | bytes 6291460
  39.2 17.3 %copy-start = (bf16[1024,1024]{1,0:T(8,128)(2,1)S(1)}, bf16[1024,1024]{1,0:T(8,128)(2,1)}, u32[]{:S(2)}) copy-start(bf16[1024,1024]{1,0:T(8,128)(2,1)} %out_one.5) | copy-start | bytes 6291460
  39.2 17.2 %copy-start.1 = (bf16[1024,1024]{1,0:T(8,128)(2,1)S(1)}, bf16[1024,1024]{1,0:T(8,128)(2,1)}, u32[]{:S(2)}) copy-start(bf16[1024,1024]{1,0:T(8,128)(2,1)} %in_one.3) | copy-start | bytes 6291460
  39.2 17.2 %copy-start.5 = (f32[1024]{0:T(1024)S(1)}, f32[1024]{0:T(1024)}, u32[]{:S(2)}) copy-start(f32[1024]{0:T(1024)} %param.23) | copy-start | bytes 12292
  58.9 7.7 %collective-permute-start.6 = (bf16[128,640]{1,0:T(8,128)(2,1)S(1)}, bf16[128,640]{1,0:T(8,128)(2,1)S(1)}, u32[]{:S(2)}, u32[]{:S(2)}) collective-permute-start(bf16[128,640]{1,0:T(8,128)(2,1)S(1)} %get-tuple-element.38), channel_id=1, source_target_pairs={{0,65},{65,0},{1,64},{64,1},{2,67},{67,2},{3,66},{66,3},{4,69},{69... | collective-permute-start | bytes 491528 | tf_op jit(solution)/shard_map/ppermute | solution.py:553
  60.7 5.9 %collective-permute-start.7 = (bf16[128,384]{1,0:T(8,128)(2,1)S(1)}, bf16[128,384]{1,0:T(8,128)(2,1)S(1)}, u32[]{:S(2)}, u32[]{:S(2)}) collective-permute-start(bf16[128,384]{1,0:T(8,128)(2,1)S(1)} %remainder.1.rest_0_), channel_id=1, source_target_pairs={{0,65},{65,0},{1,64},{64,1},{2,67},{67,2},{3,66},{66,3},{4,69},{69... | collective-permute-start | bytes 294920 | tf_op jit(solution)/shard_map/ppermute | solution.py:555

commit v12 on v11

--- a/solution.py
+++ b/solution.py
@@ -275,11 +275,12 @@
 
 
 def own_kernel(
-    x_ref, pair_ref, side_ref, rel_ref, got_ref, near_ref, name_ref, asked_ref, line_ref, chosen_ref, w1_hbm,
-    stat_ref, acc_ref, tail_ref, split_ref, w1_ref, keys, values, kwin, vwin, landed,
+    x_ref, pair_ref, side_ref, rel_ref, got_ref, near_ref, name_ref, asked_ref, line_ref, chosen_ref, in_two, out_hbm, in_hbm,
+    stat_ref, acc_ref, tail_ref, split_ref, out_two, turned_one, turned_two,
+    keys, values, kwin, vwin, in_one, landed,
 ):
     place_ref = (x_ref[0], pair_ref[0], side_ref[0])
-    copies = start_copies(((w1_hbm, w1_ref),), landed)
+    copies = start_copies(((out_hbm, out_two), (in_hbm, in_one)), landed)
     for b in (0, PAIRS + 1):
         kwin[b] = jnp.zeros((ROWS, LANES), jnp.bfloat16)
         vwin[b] = jnp.zeros((LANES, ROWS), jnp.bfloat16)
@@ -321,31 +322,35 @@
     lax.fori_loop(0, PAIRS, one, 0, unroll=4)
     for copy in copies:
         copy.wait()
-
-
-def attend_own(place, rel_bias, got, made, later_weights):
+    for source, target in ((in_two, turned_two), (in_one, turned_one)):
+        for at in range(0, D, LANES):
+            target[:, at : at + LANES] = jnp.transpose(source[at : at + LANES])
+
+
+def attend_own(place, rel_bias, got, made, in_one, in_two, out_two):
     return pl.pallas_call(
         own_kernel,
-        in_specs=[SMEM_SPEC] * 4 + [VMEM_SPEC] * 6 + [HBM_SPEC],
-        out_specs=(VMEM_SPEC,) * 5,
+        in_specs=[SMEM_SPEC] * 4 + [VMEM_SPEC] * 7 + [HBM_SPEC] * 2,
+        out_specs=(VMEM_SPEC,) * 7,
         out_shape=(
             pltpu.VMEM((PAIRS, 8, 2 * ROWS), jnp.float32),
             pltpu.VMEM((PAIRS, LANES, ROWS), jnp.float32),
             pltpu.VMEM((PAIRS, ROWS, 2 * ROWS), jnp.float32),
             pltpu.VMEM((PAIRS, PREF_GRP * LANES, 2 * ROWS), jnp.bfloat16),
         )
-        + tuple(pltpu.VMEM(w.shape, w.dtype) for w in later_weights),
+        + (pltpu.VMEM((D, D), jnp.bfloat16),) * 3,
         scratch_shapes=[
             pltpu.VMEM((PLEN // 4, PREF_GRP * LANES), jnp.bfloat16),
             pltpu.VMEM((PREF_GRP * LANES, PLEN // 4), jnp.bfloat16),
             pltpu.VMEM((PAIRS + 2, ROWS, LANES), jnp.bfloat16),
             pltpu.VMEM((PAIRS + 2, LANES, ROWS), jnp.bfloat16),
-            pltpu.SemaphoreType.DMA((1,)),
+            pltpu.VMEM((D, D), jnp.bfloat16),
+            pltpu.SemaphoreType.DMA((2,)),
         ],
         compiler_params=pltpu.CompilerParams(vmem_limit_bytes=VMEM_LIMIT),
         cost_estimate=COST,
         name="attend_own",
-    )(*place, rel_bias.T, *on_chip(got, *made), *off_chip(*later_weights))
+    )(*place, rel_bias.T, *on_chip(got, *made, in_two), *off_chip(out_two, in_one))
 
 
 def rest_kernel(
@@ -427,10 +432,7 @@
 
 
 def units_of(normed, in_ref):
-    units = lax.dot_general(
-        normed, in_ref[...], (((1,), (1,)), ((), ())), preferred_element_type=jnp.float32
-    )
-    return jnp.maximum(units, 0.0).astype(jnp.bfloat16)
+    return jnp.maximum(dot(normed, in_ref[...]), 0.0).astype(jnp.bfloat16)
 
 
 def finish_kernel(side_ref, att_ref, w_ref, tok_ref, gain_ref, in_one, in_two, out_one, out_two, *rest):
@@ -544,9 +546,11 @@
     prev = lax.ppermute(up, "x", by(1))
     later = lax.ppermute(down, "x", by(-1))
     far_tokens = lax.ppermute(same, mirrored, MIRROR)
-    *part, other_out = attend_own(place, rel_bias, got, made, (other_out,))
+    *part, other_out, turned, other_turned = attend_own(
+        place, rel_bias, got, made, w_in, other_in, other_out
+    )
     mixed = attend_rest(place, rel_bias, prev, later, opposite, made, part, far_tokens)
-    weights = (w_in, other_in, w_out, other_out)
+    weights = (turned, other_turned, w_out, other_out)
     att = lax.all_to_all(mixed, ("yhi",) + PLANE, 0, 0, tiled=True)
 
     first, units = away(place[2], att, w_attn_out, far_tokens, mlp_gain, weights)

time: 67.6 us -> 66.8 us (0.988)
    pallas_call x1, Pallas kernels: 3.87 us -> 5.18 us  [attend_own(): pl.pallas_call(own_kernel, in_specs=[SMEM_SPEC] * 4 + [VMEM_SPEC] * 7 + [...]
    ppermute x1, waiting for transfers between devices: 1.81 us -> 0.49 us  [body(): opposite = lax.ppermute(far, 'x', by(2))]
    ppermute x1, waiting for transfers between devices: 1.25 us -> 2.01 us  [body(): second_back = lax.ppermute(second, mirrored, MIRROR)]
    pallas_call x1, Pallas kernels: 2.47 us -> 1.72 us  [away(): pl.pallas_call(away_kernel, in_specs=[SMEM_SPEC] + [VMEM_SPEC] * 8, out_s...]
    pallas_call x1, Pallas kernels: 2.59 us -> 1.86 us  [finish(): pl.pallas_call(finish_kernel, in_specs=[SMEM_SPEC] + [VMEM_SPEC] * (8 + l...]
  transfers between devices with their start and end apart: 8 -> 8, of which waited for: 2 -> 2; matrix products, arithmetic and copies ran while one was open for 0% -> 0% of each run, Pallas kernels for 17% -> 18%
where the time goes in v12:
time: 66.8 us; the launch traced here: 66.7 us
  blocking collectives  33.5 us (50%)
  Pallas kernels  19.2 us (29%)
  starting transfers between devices  11.2 us (17%)
  waiting for transfers between devices  2.52 us (4%)
    all_to_all x1, blocking collectives, body(): got = lax.all_to_all(blocks, PLANE, 0, 0, tiled=True)  20.8 us
    all_to_all x1, blocking collectives, body(): att = lax.all_to_all(mixed, ('yhi',) + PLANE, 0, 0, tiled=True)  12.8 us
    pallas_call x1, Pallas kernels, attend_own(): pl.pallas_call(own_kernel, in_specs=[SMEM_SPEC] * 4 + [VMEM_SPEC] * 7 + [...  5.18 us
    pallas_call x1, Pallas kernels, project(): pl.pallas_call(project_kernel, in_specs=[SMEM_SPEC] * 3 + [HBM_SPEC] * 9,...  4.77 us
    pallas_call x1, Pallas kernels, attend_rest(): pl.pallas_call(rest_kernel, in_specs=[SMEM_SPEC] * 4 + [VMEM_SPEC] * 11,...  4.44 us
    ppermute x1, starting transfers between devices, body(): far_tokens = lax.ppermute(same, mirrored, MIRROR)  2.27 us
    ppermute x1, starting transfers between devices, body(): second_back = lax.ppermute(second, mirrored, MIRROR)  2.03 us
    ppermute x1, waiting for transfers between devices, body(): second_back = lax.ppermute(second, mirrored, MIRROR)  2.01 us
  transfers between devices with their start and end apart: 8, of which 2 were waited for; matrix products, arithmetic and copies ran while one was open for 0% of the time, Pallas kernels for 18%

profile of v12, /device:TPU:0, one launch (start us, length us, event | category | flops | bytes accessed | tf_op | source)
XLA Modules:
  0.0 66.7 jit_solution(2202757202486390227)
XLA Ops:
  0.0 0.0 collective-permute-start
  0.0 0.5 collective-permute-start.1
  0.5 0.0 copy-start.2
  0.5 4.8 %project.1 = (bf16[8,448,128]{2,1,0:T(8,128)(2,1)S(1)}, f32[384,256]{1,0:T(8,128)S(1)}, bf16[10,128,128]{2,1,0:T(8,128)(2,1)S(1)}, f32[8,8,128]{2,1,0:T(8,128)S(...) custom-call(s32[1]{0:T(128)} %bitcast.1.x_ref, s32[1]{0:T(128)} %bitcast.2.pair_ref, s32[1]{0:T(128)} %bitcast.side_ref, ...), custom_call_target="tpu_custom_call" | custom-call | flops 1000 | bytes 1000 | tf_op jit(solution)/shard_map/project/pallas_call | solution.py:172
  5.3 20.8 %all_to_all.10.got_ref = bf16[8,448,128]{2,1,0:T(8,128)(2,1)S(1)} all-to-all(bf16[8,448,128]{2,1,0:T(8,128)(2,1)S(1)} %get-tuple-element.24), channel_id=1, replica_groups=mesh['yhi'=2,'core'=2,'x'=4,'z'=4,'ylo'=2] {'z','ylo'}, dimensions={0} | all-to-all | bytes 1835008 | tf_op jit(solution)/shard_map/all_to_all | solution.py:541
  26.1 0.0 copy-start.3
  26.1 0.0 collective-permute-done.rest_0_.in_two
  26.1 0.0 collective-permute-done.1.rest_1_.out_hbm
  26.1 0.0 copy-done.2
  26.1 0.1 spread.1
  26.2 2.3 %collective-permute-start.5 = (bf16[128,1024]{1,0:T(8,128)(2,1)S(1)}, bf16[128,1024]{1,0:T(8,128)(2,1)S(1)}, u32[]{:S(2)}, u32[]{:S(2)}) collective-permute-start(bf16[128,1024]{1,0:T(8,128)(2,1)S(1)} %get-tuple-element.37), channel_id=1, source_target_pairs={{0,65},{65,0},{1,64},{64,1},{2,67},{67,2},{3,66},{66,3},{4,69},{69... | collective-permute-start | bytes 786440 | tf_op jit(solution)/shard_map/ppermute | solution.py:548
  28.5 1.5 %collective-permute-start.2 = (bf16[768,128]{1,0:T(8,128)(2,1)S(1)}, bf16[768,128]{1,0:T(8,128)(2,1)S(1)}, u32[]{:S(2)}, u32[]{:S(2)}) collective-permute-start(bf16[768,128]{1,0:T(8,128)(2,1)S(1)} %get-tuple-element.25), channel_id=1, source_target_pairs={{0,8},{8,16},{16,24},{24,0},{1,9},{9,17},{17,25},{25,1},{2,10},{10... | collective-permute-start | bytes 589832 | tf_op jit(solution)/shard_map/ppermute | solution.py:546
  29.9 1.8 %collective-permute-start.3 = (bf16[768,128]{1,0:T(8,128)(2,1)S(1)}, bf16[768,128]{1,0:T(8,128)(2,1)S(1)}, u32[]{:S(2)}, u32[]{:S(2)}) collective-permute-start(bf16[768,128]{1,0:T(8,128)(2,1)S(1)} %get-tuple-element.26), channel_id=1, source_target_pairs={{0,24},{8,0},{16,8},{24,16},{1,25},{9,1},{17,9},{25,17},{2,26},{10... | collective-permute-start | bytes 589832 | tf_op jit(solution)/shard_map/ppermute | solution.py:547
  31.7 1.8 %collective-permute-start.4 = (bf16[512,128]{1,0:T(8,128)(2,1)S(1)}, bf16[512,128]{1,0:T(8,128)(2,1)S(1)}, u32[]{:S(2)}, u32[]{:S(2)}) collective-permute-start(bf16[512,128]{1,0:T(8,128)(2,1)S(1)} %get-tuple-element.27), channel_id=1, source_target_pairs={{0,16},{8,24},{16,0},{24,8},{1,17},{9,25},{17,1},{25,9},{2,18},{10... | collective-permute-start | bytes 393224 | tf_op jit(solution)/shard_map/ppermute | solution.py:545
  33.5 0.0 copy-done.3
  33.5 5.2 %attend_own.1 = (f32[8,8,256]{2,1,0:T(8,128)S(1)}, f32[8,128,128]{2,1,0:T(8,128)S(1)}, f32[8,128,256]{2,1,0:T(8,128)S(1)}, bf16[8,256,256]{2,1,0:T(8,128)(2,1)S(...) custom-call(s32[1]{0:T(128)} %bitcast.1.x_ref, ...), custom_call_target="tpu_custom_call" | custom-call | flops 1000 | bytes 1000 | tf_op jit(solution)/shard_map/attend_own/pallas_call | solution.py:331
  38.7 0.5 collective-permute-done.4.far_ref
  39.2 0.0 collective-permute-done.2.prev_ref
  39.2 0.0 collective-permute-done.3.next_ref
  39.2 0.0 collective-permute-done.5._.tok_ref
  39.2 0.0 copy-start
  39.2 0.0 copy-start.1
  39.2 0.0 copy-start.4
  39.2 4.4 %attend_rest.1 = bf16[16,128,128]{2,1,0:T(8,128)(2,1)S(1)} custom-call(s32[1]{0:T(128)} %bitcast.1.x_ref, s32[1]{0:T(128)} %bitcast.2.pair_ref, s32[1]{0:T(128)} %bitcast.side_ref, f32[16,32]{1,0:T(8,128)S(1)} %bitcast.8, bf16[768,128]{1,0:T(8,128)(2,1)S(1)} %collective-permute-done.2.prev_ref, bf16[768,128]{1,0:T(8,128)(2,1)S(1)} %collective-permute-done.3.next_ref, ...), custom_call_target="tpu_custom_call" | custom-call | flops 1000 | bytes 1000 | tf_op jit(solution)/shard_map/attend_rest/pallas_call | solution.py:412
  43.7 12.8 %all_to_all.11.att_ref = bf16[16,128,128]{2,1,0:T(8,128)(2,1)S(1)} all-to-all(bf16[16,128,128]{2,1,0:T(8,128)(2,1)S(1)} %attend_rest.1), channel_id=1, replica_groups=mesh['yhi'=2,'core'=2,'x'=4,'z'=4,'ylo'=2] {'yhi','z','ylo'}, dimensions={0} | all-to-all | bytes 1048576 | tf_op jit(solution)/shard_map/all_to_all | solution.py:554
  56.4 0.0 copy-done
  56.4 0.0 copy-done.1
  56.4 0.0 copy-done.4
  56.4 1.7 %away.1 = (bf16[128,640]{1,0:T(8,128)(2,1)S(1)}, bf16[2,128,1024]{2,1,0:T(8,128)(2,1)S(1)}) custom-call(s32[1]{0:T(128)} %bitcast.side_ref, bf16[16,128,128]{2,1,0:T(8,128)(2,1)S(1)} %all_to_all.11.att_ref, bf16[1024,1024]{1,0:T(8,128)(2,1)S(1)} %copy-done.1, bf16[128,1024]{1,0:T(8,128)(2,1)S(1)} %collective-permute-done.5._.tok_ref, f32[1,1024]{1,0:T(1,128)S(1)} %bitcast.9, ...), custom_call_target="tpu_custom_call" | custom-call | flops 1000 | bytes 1000 | tf_op jit(solution)/shard_map/away/pallas_call | solution.py:471
  58.2 1.4 %collective-permute-start.6 = (bf16[128,640]{1,0:T(8,128)(2,1)S(1)}, bf16[128,640]{1,0:T(8,128)(2,1)S(1)}, u32[]{:S(2)}, u32[]{:S(2)}) collective-permute-start(bf16[128,640]{1,0:T(8,128)(2,1)S(1)} %get-tuple-element.42), channel_id=1, source_target_pairs={{0,65},{65,0},{1,64},{64,1},{2,67},{67,2},{3,66},{66,3},{4,69},{69... | collective-permute-start | bytes 491528 | tf_op jit(solution)/shard_map/ppermute | solution.py:557
  59.5 0.4 remainder.1.rest_0_
  60.0 2.0 %collective-permute-start.7 = (bf16[128,384]{1,0:T(8,128)(2,1)S(1)}, bf16[128,384]{1,0:T(8,128)(2,1)S(1)}, u32[]{:S(2)}, u32[]{:S(2)}) collective-permute-start(bf16[128,384]{1,0:T(8,128)(2,1)S(1)} %remainder.1.rest_0_), channel_id=1, source_target_pairs={{0,65},{65,0},{1,64},{64,1},{2,67},{67,2},{3,66},{66,3},{4,69},{69... | collective-permute-start | bytes 294920 | tf_op jit(solution)/shard_map/ppermute | solution.py:559
  62.0 1.9 %finish.1.home_ref = f32[128,1024]{1,0:T(8,128)S(1)} custom-call(s32[1]{0:T(128)} %bitcast.side_ref, bf16[16,128,128]{2,1,0:T(8,128)(2,1)S(1)} %all_to_all.11.att_ref, bf16[1024,1024]{1,0:T(8,128)(2,1)S(1)} %copy-done.1, bf16[128,1024]{1,0:T(8,128)(2,1)S(1)} %copy-done.2, f32[1,1024]{1,0:T(1,128)S(1)} %bitcast.10, ...), custom_call_target="tpu_custom_call" | custom-call | flops 1000 | bytes 1000 | tf_op jit(solution)/shard_map/finish/pallas_call | solution.py:448
  63.9 2.0 %collective-permute-done.7.second_ref = bf16[128,384]{1,0:T(8,128)(2,1)S(1)} collective-permute-done((bf16[128,384]{1,0:T(8,128)(2,1)S(1)}, bf16[128,384]{1,0:T(8,128)(2,1)S(1)}, u32[]{:S(2)}, u32[]{:S(2)}) %collective-permute-start.7) | collective-permute-done | bytes 98336 | tf_op jit(solution)/shard_map/ppermute | solution.py:559
  65.9 0.0 collective-permute-done.6.first_ref
  65.9 0.8 %total.1 = bf16[128,1024]{1,0:T(8,128)(2,1)} custom-call(f32[128,1024]{1,0:T(8,128)S(1)} %finish.1.home_ref, bf16[128,640]{1,0:T(8,128)(2,1)S(1)} %collective-permute-done.6.first_ref, bf16[128,384]{1,0:T(8,128)(2,1)S(1)} %collective-permute-done.7.second_ref), custom_call_target="tpu_custom_call" | custom-call | flops 1000 | bytes 1000 | tf_op jit(solution)/shard_map/total/pallas_call | solution.py:505
Async XLA Ops:
  0.0 26.1 %collective-permute-start = (bf16[1024,1024]{1,0:T(8,128)(2,1)}, bf16[1024,1024]{1,0:T(8,128)(2,1)S(1)}, u32[]{:S(2)}, u32[]{:S(2)}) collective-permute-start(bf16[1024,1024]{1,0:T(8,128)(2,1)} %in_hbm.1), channel_id=1, source_target_pairs={{0,32},{32,0},{1,33},{33,1},{2,34},{34,2},{3,35},{35,3},{4,36},{36... | collective-permute-start | bytes 6291464 | tf_op jit(solution)/shard_map/ppermute | solution.py:536
  0.0 26.1 %collective-permute-start.1 = (bf16[1024,1024]{1,0:T(8,128)(2,1)}, bf16[1024,1024]{1,0:T(8,128)(2,1)}, u32[]{:S(2)}, u32[]{:S(2)}) collective-permute-start(bf16[1024,1024]{1,0:T(8,128)(2,1)} %out_one.5), channel_id=1, source_target_pairs={{0,32},{32,0},{1,33},{33,1},{2,34},{34,2},{3,35},{35,3},{4,36},{36... | collective-permute-start | bytes 6291464 | tf_op jit(solution)/shard_map/ppermute | solution.py:537
  0.5 25.6 %copy-start.2 = (bf16[128,1024]{1,0:T(8,128)(2,1)S(1)}, bf16[128,1024]{1,0:T(8,128)(2,1)}, u32[]{:S(2)}) copy-start(bf16[128,1024]{1,0:T(8,128)(2,1)} %tok_ref.3) | copy-start | bytes 786436
  26.1 7.4 %copy-start.3 = (f32[32,16]{0,1:T(8,128)S(1)}, f32[32,16]{0,1:T(8,128)}, u32[]{:S(2)}) copy-start(f32[32,16]{0,1:T(8,128)} %param.19) | copy-start | bytes 6148
  26.2 13.0 %collective-permute-start.5 = (bf16[128,1024]{1,0:T(8,128)(2,1)S(1)}, bf16[128,1024]{1,0:T(8,128)(2,1)S(1)}, u32[]{:S(2)}, u32[]{:S(2)}) collective-permute-start(bf16[128,1024]{1,0:T(8,128)(2,1)S(1)} %get-tuple-element.37), channel_id=1, source_target_pairs={{0,65},{65,0},{1,64},{64,1},{2,67},{67,2},{3,66},{66,3},{4,69},{69... | collective-permute-start | bytes 786440 | tf_op jit(solution)/shard_map/ppermute | solution.py:548
  28.5 10.7 %collective-permute-start.2 = (bf16[768,128]{1,0:T(8,128)(2,1)S(1)}, bf16[768,128]{1,0:T(8,128)(2,1)S(1)}, u32[]{:S(2)}, u32[]{:S(2)}) collective-permute-start(bf16[768,128]{1,0:T(8,128)(2,1)S(1)} %get-tuple-element.25), channel_id=1, source_target_pairs={{0,8},{8,16},{16,24},{24,0},{1,9},{9,17},{17,25},{25,1},{2,10},{10... | collective-permute-start | bytes 589832 | tf_op jit(solution)/shard_map/ppermute | solution.py:546
  29.9 9.2 %collective-permute-start.3 = (bf16[768,128]{1,0:T(8,128)(2,1)S(1)}, bf16[768,128]{1,0:T(8,128)(2,1)S(1)}, u32[]{:S(2)}, u32[]{:S(2)}) collective-permute-start(bf16[768,128]{1,0:T(8,128)(2,1)S(1)} %get-tuple-element.26), channel_id=1, source_target_pairs={{0,24},{8,0},{16,8},{24,16},{1,25},{9,1},{17,9},{25,17},{2,26},{10... | collective-permute-start | bytes 589832 | tf_op jit(solution)/shard_map/ppermute | solution.py:547
  31.7 7.5 %collective-permute-start.4 = (bf16[512,128]{1,0:T(8,128)(2,1)S(1)}, bf16[512,128]{1,0:T(8,128)(2,1)S(1)}, u32[]{:S(2)}, u32[]{:S(2)}) collective-permute-start(bf16[512,128]{1,0:T(8,128)(2,1)S(1)} %get-tuple-element.27), channel_id=1, source_target_pairs={{0,16},{8,24},{16,0},{24,8},{1,17},{9,25},{17,1},{25,9},{2,18},{10... | collective-permute-start | bytes 393224 | tf_op jit(solution)/shard_map/ppermute | solution.py:545
  39.2 17.2 %copy-start = (bf16[1024,1024]{1,0:T(8,128)(2,1)S(1)}, bf16[1024,1024]{1,0:T(8,128)(2,1)}, u32[]{:S(2)}) copy-start(bf16[1024,1024]{1,0:T(8,128)(2,1)} %out_one.5) | copy-start | bytes 6291460
  39.2 17.2 %copy-start.1 = (bf16[1024,1024]{1,0:T(8,128)(2,1)S(1)}, bf16[1024,1024]{1,0:T(8,128)(2,1)}, u32[]{:S(2)}) copy-start(bf16[1024,1024]{1,0:T(8,128)(2,1)} %w_ref.3) | copy-start | bytes 6291460
  39.2 17.2 %copy-start.4 = (f32[1024]{0:T(1024)S(1)}, f32[1024]{0:T(1024)}, u32[]{:S(2)}) copy-start(f32[1024]{0:T(1024)} %param.23) | copy-start | bytes 12292
  58.2 7.7 %collective-permute-start.6 = (bf16[128,640]{1,0:T(8,128)(2,1)S(1)}, bf16[128,640]{1,0:T(8,128)(2,1)S(1)}, u32[]{:S(2)}, u32[]{:S(2)}) collective-permute-start(bf16[128,640]{1,0:T(8,128)(2,1)S(1)} %get-tuple-element.42), channel_id=1, source_target_pairs={{0,65},{65,0},{1,64},{64,1},{2,67},{67,2},{3,66},{66,3},{4,69},{69... | collective-permute-start | bytes 491528 | tf_op jit(solution)/shard_map/ppermute | solution.py:557
  60.0 5.9 %collective-permute-start.7 = (bf16[128,384]{1,0:T(8,128)(2,1)S(1)}, bf16[128,384]{1,0:T(8,128)(2,1)S(1)}, u32[]{:S(2)}, u32[]{:S(2)}) collective-permute-start(bf16[128,384]{1,0:T(8,128)(2,1)S(1)} %remainder.1.rest_0_), channel_id=1, source_target_pairs={{0,65},{65,0},{1,64},{64,1},{2,67},{67,2},{3,66},{66,3},{4,69},{69... | collective-permute-start | bytes 294920 | tf_op jit(solution)/shard_map/ppermute | solution.py:559

commit v13 on v12

--- a/solution.py
+++ b/solution.py
@@ -319,7 +319,7 @@
         stat_ref[step, 1:2] = row_sum
         return 0
 
-    lax.fori_loop(0, PAIRS, one, 0, unroll=4)
+    lax.fori_loop(0, PAIRS, one, 0, unroll=PAIRS)
     for copy in copies:
         copy.wait()
     for source, target in ((in_two, turned_two), (in_one, turned_one)):
@@ -404,7 +404,7 @@
         return 0
 
     one(jnp.int32(0), 0)
-    lax.fori_loop(1, PAIRS - 1, middle, 0, unroll=3)
+    lax.fori_loop(1, PAIRS - 1, middle, 0, unroll=PAIRS - 2)
     one(jnp.int32(PAIRS - 1), 1)
 
 

time: 66.8 us -> 66.6 us (level)
    pallas_call x1, Pallas kernels: 4.44 us -> 3.19 us  [attend_rest(): pl.pallas_call(rest_kernel, in_specs=[SMEM_SPEC] * 4 + [VMEM_SPEC] * 11,...]
    pallas_call x1, Pallas kernels: 5.18 us -> 6.37 us  [attend_own(): pl.pallas_call(own_kernel, in_specs=[SMEM_SPEC] * 4 + [VMEM_SPEC] * 7 + [...]
  transfers between devices with their start and end apart: 8 -> 8, of which waited for: 2 -> 1; matrix products, arithmetic and copies ran while one was open for 0% -> 0% of each run, Pallas kernels for 18% -> 20%
where the time goes in v13:
time: 66.6 us; the launch traced here: 66.5 us
  blocking collectives  33.9 us (51%)
  Pallas kernels  19.2 us (29%)
  starting transfers between devices  11.2 us (17%)
  waiting for transfers between devices  2.06 us (3%)
    all_to_all x1, blocking collectives, body(): got = lax.all_to_all(blocks, PLANE, 0, 0, tiled=True)  20.8 us
    all_to_all x1, blocking collectives, body(): att = lax.all_to_all(mixed, ('yhi',) + PLANE, 0, 0, tiled=True)  13.1 us
    pallas_call x1, Pallas kernels, attend_own(): pl.pallas_call(own_kernel, in_specs=[SMEM_SPEC] * 4 + [VMEM_SPEC] * 7 + [...  6.37 us
    pallas_call x1, Pallas kernels, project(): pl.pallas_call(project_kernel, in_specs=[SMEM_SPEC] * 3 + [HBM_SPEC] * 9,...  4.77 us
    pallas_call x1, Pallas kernels, attend_rest(): pl.pallas_call(rest_kernel, in_specs=[SMEM_SPEC] * 4 + [VMEM_SPEC] * 11,...  3.19 us
    ppermute x1, starting transfers between devices, body(): far_tokens = lax.ppermute(same, mirrored, MIRROR)  2.27 us
    ppermute x1, waiting for transfers between devices, body(): second_back = lax.ppermute(second, mirrored, MIRROR)  2.04 us
    ppermute x1, starting transfers between devices, body(): second_back = lax.ppermute(second, mirrored, MIRROR)  2 us
  transfers between devices with their start and end apart: 8, of which 1 were waited for; matrix products, arithmetic and copies ran while one was open for 0% of the time, Pallas kernels for 20%

profile of v13, /device:TPU:0, one launch (start us, length us, event | category | flops | bytes accessed | tf_op | source)
XLA Modules:
  0.0 66.5 jit_solution(2404606872433080642)
XLA Ops:
  0.0 0.0 collective-permute-start
  0.0 0.5 collective-permute-start.1
  0.5 0.0 copy-start.2
  0.5 4.8 %project.1 = (bf16[8,448,128]{2,1,0:T(8,128)(2,1)S(1)}, f32[384,256]{1,0:T(8,128)S(1)}, bf16[10,128,128]{2,1,0:T(8,128)(2,1)S(1)}, f32[8,8,128]{2,1,0:T(8,128)S(...) custom-call(s32[1]{0:T(128)} %bitcast.1.x_ref, s32[1]{0:T(128)} %bitcast.2.pair_ref, s32[1]{0:T(128)} %bitcast.side_ref, ...), custom_call_target="tpu_custom_call" | custom-call | flops 1000 | bytes 1000 | tf_op jit(solution)/shard_map/project/pallas_call | solution.py:172
  5.3 20.8 %all_to_all.10.got_ref = bf16[8,448,128]{2,1,0:T(8,128)(2,1)S(1)} all-to-all(bf16[8,448,128]{2,1,0:T(8,128)(2,1)S(1)} %get-tuple-element.24), channel_id=1, replica_groups=mesh['yhi'=2,'core'=2,'x'=4,'z'=4,'ylo'=2] {'z','ylo'}, dimensions={0} | all-to-all | bytes 1835008 | tf_op jit(solution)/shard_map/all_to_all | solution.py:541
  26.1 0.0 copy-start.3
  26.1 0.0 collective-permute-done.rest_0_.in_two
  26.1 0.0 collective-permute-done.1.rest_1_.out_hbm
  26.1 0.0 copy-done.2
  26.1 0.1 spread.1
  26.2 2.3 %collective-permute-start.5 = (bf16[128,1024]{1,0:T(8,128)(2,1)S(1)}, bf16[128,1024]{1,0:T(8,128)(2,1)S(1)}, u32[]{:S(2)}, u32[]{:S(2)}) collective-permute-start(bf16[128,1024]{1,0:T(8,128)(2,1)S(1)} %get-tuple-element.37), channel_id=1, source_target_pairs={{0,65},{65,0},{1,64},{64,1},{2,67},{67,2},{3,66},{66,3},{4,69},{69... | collective-permute-start | bytes 786440 | tf_op jit(solution)/shard_map/ppermute | solution.py:548
  28.5 1.5 %collective-permute-start.2 = (bf16[768,128]{1,0:T(8,128)(2,1)S(1)}, bf16[768,128]{1,0:T(8,128)(2,1)S(1)}, u32[]{:S(2)}, u32[]{:S(2)}) collective-permute-start(bf16[768,128]{1,0:T(8,128)(2,1)S(1)} %get-tuple-element.25), channel_id=1, source_target_pairs={{0,8},{8,16},{16,24},{24,0},{1,9},{9,17},{17,25},{25,1},{2,10},{10... | collective-permute-start | bytes 589832 | tf_op jit(solution)/shard_map/ppermute | solution.py:546
  29.9 1.8 %collective-permute-start.3 = (bf16[768,128]{1,0:T(8,128)(2,1)S(1)}, bf16[768,128]{1,0:T(8,128)(2,1)S(1)}, u32[]{:S(2)}, u32[]{:S(2)}) collective-permute-start(bf16[768,128]{1,0:T(8,128)(2,1)S(1)} %get-tuple-element.26), channel_id=1, source_target_pairs={{0,24},{8,0},{16,8},{24,16},{1,25},{9,1},{17,9},{25,17},{2,26},{10... | collective-permute-start | bytes 589832 | tf_op jit(solution)/shard_map/ppermute | solution.py:547
  31.7 1.8 %collective-permute-start.4 = (bf16[512,128]{1,0:T(8,128)(2,1)S(1)}, bf16[512,128]{1,0:T(8,128)(2,1)S(1)}, u32[]{:S(2)}, u32[]{:S(2)}) collective-permute-start(bf16[512,128]{1,0:T(8,128)(2,1)S(1)} %get-tuple-element.27), channel_id=1, source_target_pairs={{0,16},{8,24},{16,0},{24,8},{1,17},{9,25},{17,1},{25,9},{2,18},{10... | collective-permute-start | bytes 393224 | tf_op jit(solution)/shard_map/ppermute | solution.py:545
  33.5 0.0 copy-done.3
  33.5 6.4 %attend_own.1 = (f32[8,8,256]{2,1,0:T(8,128)S(1)}, f32[8,128,128]{2,1,0:T(8,128)S(1)}, f32[8,128,256]{2,1,0:T(8,128)S(1)}, bf16[8,256,256]{2,1,0:T(8,128)(2,1)S(...) custom-call(s32[1]{0:T(128)} %bitcast.1.x_ref, ...), custom_call_target="tpu_custom_call" | custom-call | flops 1000 | bytes 1000 | tf_op jit(solution)/shard_map/attend_own/pallas_call | solution.py:331
  39.9 0.0 collective-permute-done.4.far_ref
  39.9 0.0 collective-permute-done.2.prev_ref
  39.9 0.0 collective-permute-done.3.next_ref
  39.9 0.0 collective-permute-done.5._.tok_ref
  39.9 0.0 copy-start
  39.9 0.0 copy-start.1
  39.9 0.0 copy-start.4
  39.9 3.2 %attend_rest.1 = bf16[16,128,128]{2,1,0:T(8,128)(2,1)S(1)} custom-call(s32[1]{0:T(128)} %bitcast.1.x_ref, s32[1]{0:T(128)} %bitcast.2.pair_ref, s32[1]{0:T(128)} %bitcast.side_ref, f32[16,32]{1,0:T(8,128)S(1)} %bitcast.8, bf16[768,128]{1,0:T(8,128)(2,1)S(1)} %collective-permute-done.2.prev_ref, bf16[768,128]{1,0:T(8,128)(2,1)S(1)} %collective-permute-done.3.next_ref, ...), custom_call_target="tpu_custom_call" | custom-call | flops 1000 | bytes 1000 | tf_op jit(solution)/shard_map/attend_rest/pallas_call | solution.py:412
  43.1 13.1 %all_to_all.11.att_ref = bf16[16,128,128]{2,1,0:T(8,128)(2,1)S(1)} all-to-all(bf16[16,128,128]{2,1,0:T(8,128)(2,1)S(1)} %attend_rest.1), channel_id=1, replica_groups=mesh['yhi'=2,'core'=2,'x'=4,'z'=4,'ylo'=2] {'yhi','z','ylo'}, dimensions={0} | all-to-all | bytes 1048576 | tf_op jit(solution)/shard_map/all_to_all | solution.py:554
  56.2 0.0 copy-done
  56.2 0.0 copy-done.1
  56.2 0.0 copy-done.4
  56.2 1.7 %away.1 = (bf16[128,640]{1,0:T(8,128)(2,1)S(1)}, bf16[2,128,1024]{2,1,0:T(8,128)(2,1)S(1)}) custom-call(s32[1]{0:T(128)} %bitcast.side_ref, bf16[16,128,128]{2,1,0:T(8,128)(2,1)S(1)} %all_to_all.11.att_ref, bf16[1024,1024]{1,0:T(8,128)(2,1)S(1)} %copy-done.1, bf16[128,1024]{1,0:T(8,128)(2,1)S(1)} %collective-permute-done.5._.tok_ref, f32[1,1024]{1,0:T(1,128)S(1)} %bitcast.9, ...), custom_call_target="tpu_custom_call" | custom-call | flops 1000 | bytes 1000 | tf_op jit(solution)/shard_map/away/pallas_call | solution.py:471
  58.0 1.4 %collective-permute-start.6 = (bf16[128,640]{1,0:T(8,128)(2,1)S(1)}, bf16[128,640]{1,0:T(8,128)(2,1)S(1)}, u32[]{:S(2)}, u32[]{:S(2)}) collective-permute-start(bf16[128,640]{1,0:T(8,128)(2,1)S(1)} %get-tuple-element.42), channel_id=1, source_target_pairs={{0,65},{65,0},{1,64},{64,1},{2,67},{67,2},{3,66},{66,3},{4,69},{69... | collective-permute-start | bytes 491528 | tf_op jit(solution)/shard_map/ppermute | solution.py:557
  59.3 0.4 remainder.1.rest_0_
  59.8 2.0 %collective-permute-start.7 = (bf16[128,384]{1,0:T(8,128)(2,1)S(1)}, bf16[128,384]{1,0:T(8,128)(2,1)S(1)}, u32[]{:S(2)}, u32[]{:S(2)}) collective-permute-start(bf16[128,384]{1,0:T(8,128)(2,1)S(1)} %remainder.1.rest_0_), channel_id=1, source_target_pairs={{0,65},{65,0},{1,64},{64,1},{2,67},{67,2},{3,66},{66,3},{4,69},{69... | collective-permute-start | bytes 294920 | tf_op jit(solution)/shard_map/ppermute | solution.py:559
  61.8 1.9 %finish.1.home_ref = f32[128,1024]{1,0:T(8,128)S(1)} custom-call(s32[1]{0:T(128)} %bitcast.side_ref, bf16[16,128,128]{2,1,0:T(8,128)(2,1)S(1)} %all_to_all.11.att_ref, bf16[1024,1024]{1,0:T(8,128)(2,1)S(1)} %copy-done.1, bf16[128,1024]{1,0:T(8,128)(2,1)S(1)} %copy-done.2, f32[1,1024]{1,0:T(1,128)S(1)} %bitcast.10, ...), custom_call_target="tpu_custom_call" | custom-call | flops 1000 | bytes 1000 | tf_op jit(solution)/shard_map/finish/pallas_call | solution.py:448
  63.7 2.0 %collective-permute-done.7.second_ref = bf16[128,384]{1,0:T(8,128)(2,1)S(1)} collective-permute-done((bf16[128,384]{1,0:T(8,128)(2,1)S(1)}, bf16[128,384]{1,0:T(8,128)(2,1)S(1)}, u32[]{:S(2)}, u32[]{:S(2)}) %collective-permute-start.7) | collective-permute-done | bytes 98336 | tf_op jit(solution)/shard_map/ppermute | solution.py:559
  65.7 0.0 collective-permute-done.6.first_ref
  65.7 0.8 %total.1 = bf16[128,1024]{1,0:T(8,128)(2,1)} custom-call(f32[128,1024]{1,0:T(8,128)S(1)} %finish.1.home_ref, bf16[128,640]{1,0:T(8,128)(2,1)S(1)} %collective-permute-done.6.first_ref, bf16[128,384]{1,0:T(8,128)(2,1)S(1)} %collective-permute-done.7.second_ref), custom_call_target="tpu_custom_call" | custom-call | flops 1000 | bytes 1000 | tf_op jit(solution)/shard_map/total/pallas_call | solution.py:505
Async XLA Ops:
  0.0 26.1 %collective-permute-start = (bf16[1024,1024]{1,0:T(8,128)(2,1)}, bf16[1024,1024]{1,0:T(8,128)(2,1)S(1)}, u32[]{:S(2)}, u32[]{:S(2)}) collective-permute-start(bf16[1024,1024]{1,0:T(8,128)(2,1)} %in_hbm.1), channel_id=1, source_target_pairs={{0,32},{32,0},{1,33},{33,1},{2,34},{34,2},{3,35},{35,3},{4,36},{36... | collective-permute-start | bytes 6291464 | tf_op jit(solution)/shard_map/ppermute | solution.py:536
  0.0 26.1 %collective-permute-start.1 = (bf16[1024,1024]{1,0:T(8,128)(2,1)}, bf16[1024,1024]{1,0:T(8,128)(2,1)}, u32[]{:S(2)}, u32[]{:S(2)}) collective-permute-start(bf16[1024,1024]{1,0:T(8,128)(2,1)} %out_one.5), channel_id=1, source_target_pairs={{0,32},{32,0},{1,33},{33,1},{2,34},{34,2},{3,35},{35,3},{4,36},{36... | collective-permute-start | bytes 6291464 | tf_op jit(solution)/shard_map/ppermute | solution.py:537
  0.5 25.6 %copy-start.2 = (bf16[128,1024]{1,0:T(8,128)(2,1)S(1)}, bf16[128,1024]{1,0:T(8,128)(2,1)}, u32[]{:S(2)}) copy-start(bf16[128,1024]{1,0:T(8,128)(2,1)} %tok_ref.3) | copy-start | bytes 786436
  26.1 7.4 %copy-start.3 = (f32[32,16]{0,1:T(8,128)S(1)}, f32[32,16]{0,1:T(8,128)}, u32[]{:S(2)}) copy-start(f32[32,16]{0,1:T(8,128)} %param.19) | copy-start | bytes 6148
  26.2 13.7 %collective-permute-start.5 = (bf16[128,1024]{1,0:T(8,128)(2,1)S(1)}, bf16[128,1024]{1,0:T(8,128)(2,1)S(1)}, u32[]{:S(2)}, u32[]{:S(2)}) collective-permute-start(bf16[128,1024]{1,0:T(8,128)(2,1)S(1)} %get-tuple-element.37), channel_id=1, source_target_pairs={{0,65},{65,0},{1,64},{64,1},{2,67},{67,2},{3,66},{66,3},{4,69},{69... | collective-permute-start | bytes 786440 | tf_op jit(solution)/shard_map/ppermute | solution.py:548
  28.5 11.4 %collective-permute-start.2 = (bf16[768,128]{1,0:T(8,128)(2,1)S(1)}, bf16[768,128]{1,0:T(8,128)(2,1)S(1)}, u32[]{:S(2)}, u32[]{:S(2)}) collective-permute-start(bf16[768,128]{1,0:T(8,128)(2,1)S(1)} %get-tuple-element.25), channel_id=1, source_target_pairs={{0,8},{8,16},{16,24},{24,0},{1,9},{9,17},{17,25},{25,1},{2,10},{10... | collective-permute-start | bytes 589832 | tf_op jit(solution)/shard_map/ppermute | solution.py:546
  29.9 10.0 %collective-permute-start.3 = (bf16[768,128]{1,0:T(8,128)(2,1)S(1)}, bf16[768,128]{1,0:T(8,128)(2,1)S(1)}, u32[]{:S(2)}, u32[]{:S(2)}) collective-permute-start(bf16[768,128]{1,0:T(8,128)(2,1)S(1)} %get-tuple-element.26), channel_id=1, source_target_pairs={{0,24},{8,0},{16,8},{24,16},{1,25},{9,1},{17,9},{25,17},{2,26},{10... | collective-permute-start | bytes 589832 | tf_op jit(solution)/shard_map/ppermute | solution.py:547
  31.7 8.2 %collective-permute-start.4 = (bf16[512,128]{1,0:T(8,128)(2,1)S(1)}, bf16[512,128]{1,0:T(8,128)(2,1)S(1)}, u32[]{:S(2)}, u32[]{:S(2)}) collective-permute-start(bf16[512,128]{1,0:T(8,128)(2,1)S(1)} %get-tuple-element.27), channel_id=1, source_target_pairs={{0,16},{8,24},{16,0},{24,8},{1,17},{9,25},{17,1},{25,9},{2,18},{10... | collective-permute-start | bytes 393224 | tf_op jit(solution)/shard_map/ppermute | solution.py:545
  39.9 16.3 %copy-start = (bf16[1024,1024]{1,0:T(8,128)(2,1)S(1)}, bf16[1024,1024]{1,0:T(8,128)(2,1)}, u32[]{:S(2)}) copy-start(bf16[1024,1024]{1,0:T(8,128)(2,1)} %out_one.5) | copy-start | bytes 6291460
  39.9 16.3 %copy-start.1 = (bf16[1024,1024]{1,0:T(8,128)(2,1)S(1)}, bf16[1024,1024]{1,0:T(8,128)(2,1)}, u32[]{:S(2)}) copy-start(bf16[1024,1024]{1,0:T(8,128)(2,1)} %w_ref.3) | copy-start | bytes 6291460
  39.9 16.3 %copy-start.4 = (f32[1024]{0:T(1024)S(1)}, f32[1024]{0:T(1024)}, u32[]{:S(2)}) copy-start(f32[1024]{0:T(1024)} %param.23) | copy-start | bytes 12292
  58.0 7.7 %collective-permute-start.6 = (bf16[128,640]{1,0:T(8,128)(2,1)S(1)}, bf16[128,640]{1,0:T(8,128)(2,1)S(1)}, u32[]{:S(2)}, u32[]{:S(2)}) collective-permute-start(bf16[128,640]{1,0:T(8,128)(2,1)S(1)} %get-tuple-element.42), channel_id=1, source_target_pairs={{0,65},{65,0},{1,64},{64,1},{2,67},{67,2},{3,66},{66,3},{4,69},{69... | collective-permute-start | bytes 491528 | tf_op jit(solution)/shard_map/ppermute | solution.py:557
  59.8 5.9 %collective-permute-start.7 = (bf16[128,384]{1,0:T(8,128)(2,1)S(1)}, bf16[128,384]{1,0:T(8,128)(2,1)S(1)}, u32[]{:S(2)}, u32[]{:S(2)}) collective-permute-start(bf16[128,384]{1,0:T(8,128)(2,1)S(1)} %remainder.1.rest_0_), channel_id=1, source_target_pairs={{0,65},{65,0},{1,64},{64,1},{2,67},{67,2},{3,66},{66,3},{4,69},{69... | collective-permute-start | bytes 294920 | tf_op jit(solution)/shard_map/ppermute | solution.py:559

commit v14 on v13

--- a/solution.py
+++ b/solution.py
@@ -319,7 +319,7 @@
         stat_ref[step, 1:2] = row_sum
         return 0
 
-    lax.fori_loop(0, PAIRS, one, 0, unroll=PAIRS)
+    lax.fori_loop(0, PAIRS, one, 0, unroll=4)
     for copy in copies:
         copy.wait()
     for source, target in ((in_two, turned_two), (in_one, turned_one)):

time: 66.6 us -> 65.6 us (0.985)
  Pallas kernels: 19.2 us -> 18 us
    pallas_call x1, Pallas kernels: 6.37 us -> 5.18 us  [attend_own(): pl.pallas_call(own_kernel, in_specs=[SMEM_SPEC] * 4 + [VMEM_SPEC] * 7 + [...]
  transfers between devices with their start and end apart: 8 -> 8, of which waited for: 1 -> 2; matrix products, arithmetic and copies ran while one was open for 0% -> 0% of each run, Pallas kernels for 20% -> 19%
where the time goes in v14:
time: 65.6 us; the launch traced here: 65.4 us
  blocking collectives  33.5 us (51%)
  Pallas kernels  18 us (27%)
  starting transfers between devices  11.2 us (17%)
  waiting for transfers between devices  2.54 us (4%)
    all_to_all x1, blocking collectives, body(): got = lax.all_to_all(blocks, PLANE, 0, 0, tiled=True)  20.8 us
    all_to_all x1, blocking collectives, body(): att = lax.all_to_all(mixed, ('yhi',) + PLANE, 0, 0, tiled=True)  12.8 us
    pallas_call x1, Pallas kernels, attend_own(): pl.pallas_call(own_kernel, in_specs=[SMEM_SPEC] * 4 + [VMEM_SPEC] * 7 + [...  5.18 us
    pallas_call x1, Pallas kernels, project(): pl.pallas_call(project_kernel, in_specs=[SMEM_SPEC] * 3 + [HBM_SPEC] * 9,...  4.77 us
    pallas_call x1, Pallas kernels, attend_rest(): pl.pallas_call(rest_kernel, in_specs=[SMEM_SPEC] * 4 + [VMEM_SPEC] * 11,...  3.19 us
    ppermute x1, starting transfers between devices, body(): far_tokens = lax.ppermute(same, mirrored, MIRROR)  2.27 us
    ppermute x1, waiting for transfers between devices, body(): second_back = lax.ppermute(second, mirrored, MIRROR)  2.03 us
    ppermute x1, starting transfers between devices, body(): second_back = lax.ppermute(second, mirrored, MIRROR)  2.01 us
  transfers between devices with their start and end apart: 8, of which 2 were waited for; matrix products, arithmetic and copies ran while one was open for 0% of the time, Pallas kernels for 19%

profile of v14, /device:TPU:0, one launch (start us, length us, event | category | flops | bytes accessed | tf_op | source)
XLA Modules:
  0.0 65.4 jit_solution(4970423814946168556)
XLA Ops:
  0.0 0.0 collective-permute-start
  0.0 0.5 collective-permute-start.1
  0.5 0.0 copy-start.2
  0.5 4.8 %project.1 = (bf16[8,448,128]{2,1,0:T(8,128)(2,1)S(1)}, f32[384,256]{1,0:T(8,128)S(1)}, bf16[10,128,128]{2,1,0:T(8,128)(2,1)S(1)}, f32[8,8,128]{2,1,0:T(8,128)S(...) custom-call(s32[1]{0:T(128)} %bitcast.1.x_ref, s32[1]{0:T(128)} %bitcast.2.pair_ref, s32[1]{0:T(128)} %bitcast.side_ref, ...), custom_call_target="tpu_custom_call" | custom-call | flops 1000 | bytes 1000 | tf_op jit(solution)/shard_map/project/pallas_call | solution.py:172
  5.3 20.8 %all_to_all.10.got_ref = bf16[8,448,128]{2,1,0:T(8,128)(2,1)S(1)} all-to-all(bf16[8,448,128]{2,1,0:T(8,128)(2,1)S(1)} %get-tuple-element.24), channel_id=1, replica_groups=mesh['yhi'=2,'core'=2,'x'=4,'z'=4,'ylo'=2] {'z','ylo'}, dimensions={0} | all-to-all | bytes 1835008 | tf_op jit(solution)/shard_map/all_to_all | solution.py:541
  26.1 0.0 copy-start.3
  26.1 0.0 collective-permute-done.rest_0_.in_two
  26.1 0.0 collective-permute-done.1.rest_1_.out_hbm
  26.1 0.0 copy-done.2
  26.1 0.1 spread.1
  26.2 2.3 %collective-permute-start.5 = (bf16[128,1024]{1,0:T(8,128)(2,1)S(1)}, bf16[128,1024]{1,0:T(8,128)(2,1)S(1)}, u32[]{:S(2)}, u32[]{:S(2)}) collective-permute-start(bf16[128,1024]{1,0:T(8,128)(2,1)S(1)} %get-tuple-element.37), channel_id=1, source_target_pairs={{0,65},{65,0},{1,64},{64,1},{2,67},{67,2},{3,66},{66,3},{4,69},{69... | collective-permute-start | bytes 786440 | tf_op jit(solution)/shard_map/ppermute | solution.py:548
  28.5 1.5 %collective-permute-start.2 = (bf16[768,128]{1,0:T(8,128)(2,1)S(1)}, bf16[768,128]{1,0:T(8,128)(2,1)S(1)}, u32[]{:S(2)}, u32[]{:S(2)}) collective-permute-start(bf16[768,128]{1,0:T(8,128)(2,1)S(1)} %get-tuple-element.25), channel_id=1, source_target_pairs={{0,8},{8,16},{16,24},{24,0},{1,9},{9,17},{17,25},{25,1},{2,10},{10... | collective-permute-start | bytes 589832 | tf_op jit(solution)/shard_map/ppermute | solution.py:546
  29.9 1.8 %collective-permute-start.3 = (bf16[768,128]{1,0:T(8,128)(2,1)S(1)}, bf16[768,128]{1,0:T(8,128)(2,1)S(1)}, u32[]{:S(2)}, u32[]{:S(2)}) collective-permute-start(bf16[768,128]{1,0:T(8,128)(2,1)S(1)} %get-tuple-element.26), channel_id=1, source_target_pairs={{0,24},{8,0},{16,8},{24,16},{1,25},{9,1},{17,9},{25,17},{2,26},{10... | collective-permute-start | bytes 589832 | tf_op jit(solution)/shard_map/ppermute | solution.py:547
  31.7 1.8 %collective-permute-start.4 = (bf16[512,128]{1,0:T(8,128)(2,1)S(1)}, bf16[512,128]{1,0:T(8,128)(2,1)S(1)}, u32[]{:S(2)}, u32[]{:S(2)}) collective-permute-start(bf16[512,128]{1,0:T(8,128)(2,1)S(1)} %get-tuple-element.27), channel_id=1, source_target_pairs={{0,16},{8,24},{16,0},{24,8},{1,17},{9,25},{17,1},{25,9},{2,18},{10... | collective-permute-start | bytes 393224 | tf_op jit(solution)/shard_map/ppermute | solution.py:545
  33.5 0.0 copy-done.3
  33.5 5.2 %attend_own.1 = (f32[8,8,256]{2,1,0:T(8,128)S(1)}, f32[8,128,128]{2,1,0:T(8,128)S(1)}, f32[8,128,256]{2,1,0:T(8,128)S(1)}, bf16[8,256,256]{2,1,0:T(8,128)(2,1)S(...) custom-call(s32[1]{0:T(128)} %bitcast.1.x_ref, ...), custom_call_target="tpu_custom_call" | custom-call | flops 1000 | bytes 1000 | tf_op jit(solution)/shard_map/attend_own/pallas_call | solution.py:331
  38.7 0.5 collective-permute-done.4.far_ref
  39.2 0.0 collective-permute-done.2.prev_ref
  39.2 0.0 collective-permute-done.3.next_ref
  39.2 0.0 collective-permute-done.5._.tok_ref
  39.2 0.0 copy-start
  39.2 0.0 copy-start.1
  39.2 0.0 copy-start.4
  39.2 3.2 %attend_rest.1 = bf16[16,128,128]{2,1,0:T(8,128)(2,1)S(1)} custom-call(s32[1]{0:T(128)} %bitcast.1.x_ref, s32[1]{0:T(128)} %bitcast.2.pair_ref, s32[1]{0:T(128)} %bitcast.side_ref, f32[16,32]{1,0:T(8,128)S(1)} %bitcast.8, bf16[768,128]{1,0:T(8,128)(2,1)S(1)} %collective-permute-done.2.prev_ref, bf16[768,128]{1,0:T(8,128)(2,1)S(1)} %collective-permute-done.3.next_ref, ...), custom_call_target="tpu_custom_call" | custom-call | flops 1000 | bytes 1000 | tf_op jit(solution)/shard_map/attend_rest/pallas_call | solution.py:412
  42.4 12.8 %all_to_all.11.att_ref = bf16[16,128,128]{2,1,0:T(8,128)(2,1)S(1)} all-to-all(bf16[16,128,128]{2,1,0:T(8,128)(2,1)S(1)} %attend_rest.1), channel_id=1, replica_groups=mesh['yhi'=2,'core'=2,'x'=4,'z'=4,'ylo'=2] {'yhi','z','ylo'}, dimensions={0} | all-to-all | bytes 1048576 | tf_op jit(solution)/shard_map/all_to_all | solution.py:554
  55.2 0.0 copy-done
  55.2 0.0 copy-done.1
  55.2 0.0 copy-done.4
  55.2 1.7 %away.1 = (bf16[128,640]{1,0:T(8,128)(2,1)S(1)}, bf16[2,128,1024]{2,1,0:T(8,128)(2,1)S(1)}) custom-call(s32[1]{0:T(128)} %bitcast.side_ref, bf16[16,128,128]{2,1,0:T(8,128)(2,1)S(1)} %all_to_all.11.att_ref, bf16[1024,1024]{1,0:T(8,128)(2,1)S(1)} %copy-done.1, bf16[128,1024]{1,0:T(8,128)(2,1)S(1)} %collective-permute-done.5._.tok_ref, f32[1,1024]{1,0:T(1,128)S(1)} %bitcast.9, ...), custom_call_target="tpu_custom_call" | custom-call | flops 1000 | bytes 1000 | tf_op jit(solution)/shard_map/away/pallas_call | solution.py:471
  56.9 1.4 %collective-permute-start.6 = (bf16[128,640]{1,0:T(8,128)(2,1)S(1)}, bf16[128,640]{1,0:T(8,128)(2,1)S(1)}, u32[]{:S(2)}, u32[]{:S(2)}) collective-permute-start(bf16[128,640]{1,0:T(8,128)(2,1)S(1)} %get-tuple-element.42), channel_id=1, source_target_pairs={{0,65},{65,0},{1,64},{64,1},{2,67},{67,2},{3,66},{66,3},{4,69},{69... | collective-permute-start | bytes 491528 | tf_op jit(solution)/shard_map/ppermute | solution.py:557
  58.3 0.4 remainder.1.rest_0_
  58.7 2.0 %collective-permute-start.7 = (bf16[128,384]{1,0:T(8,128)(2,1)S(1)}, bf16[128,384]{1,0:T(8,128)(2,1)S(1)}, u32[]{:S(2)}, u32[]{:S(2)}) collective-permute-start(bf16[128,384]{1,0:T(8,128)(2,1)S(1)} %remainder.1.rest_0_), channel_id=1, source_target_pairs={{0,65},{65,0},{1,64},{64,1},{2,67},{67,2},{3,66},{66,3},{4,69},{69... | collective-permute-start | bytes 294920 | tf_op jit(solution)/shard_map/ppermute | solution.py:559
  60.7 1.9 %finish.1.home_ref = f32[128,1024]{1,0:T(8,128)S(1)} custom-call(s32[1]{0:T(128)} %bitcast.side_ref, bf16[16,128,128]{2,1,0:T(8,128)(2,1)S(1)} %all_to_all.11.att_ref, bf16[1024,1024]{1,0:T(8,128)(2,1)S(1)} %copy-done.1, bf16[128,1024]{1,0:T(8,128)(2,1)S(1)} %copy-done.2, f32[1,1024]{1,0:T(1,128)S(1)} %bitcast.10, ...), custom_call_target="tpu_custom_call" | custom-call | flops 1000 | bytes 1000 | tf_op jit(solution)/shard_map/finish/pallas_call | solution.py:448
  62.6 2.0 %collective-permute-done.7.second_ref = bf16[128,384]{1,0:T(8,128)(2,1)S(1)} collective-permute-done((bf16[128,384]{1,0:T(8,128)(2,1)S(1)}, bf16[128,384]{1,0:T(8,128)(2,1)S(1)}, u32[]{:S(2)}, u32[]{:S(2)}) %collective-permute-start.7) | collective-permute-done | bytes 98336 | tf_op jit(solution)/shard_map/ppermute | solution.py:559
  64.6 0.0 collective-permute-done.6.first_ref
  64.6 0.8 %total.1 = bf16[128,1024]{1,0:T(8,128)(2,1)} custom-call(f32[128,1024]{1,0:T(8,128)S(1)} %finish.1.home_ref, bf16[128,640]{1,0:T(8,128)(2,1)S(1)} %collective-permute-done.6.first_ref, bf16[128,384]{1,0:T(8,128)(2,1)S(1)} %collective-permute-done.7.second_ref), custom_call_target="tpu_custom_call" | custom-call | flops 1000 | bytes 1000 | tf_op jit(solution)/shard_map/total/pallas_call | solution.py:505
Async XLA Ops:
  0.0 26.1 %collective-permute-start = (bf16[1024,1024]{1,0:T(8,128)(2,1)}, bf16[1024,1024]{1,0:T(8,128)(2,1)S(1)}, u32[]{:S(2)}, u32[]{:S(2)}) collective-permute-start(bf16[1024,1024]{1,0:T(8,128)(2,1)} %in_hbm.1), channel_id=1, source_target_pairs={{0,32},{32,0},{1,33},{33,1},{2,34},{34,2},{3,35},{35,3},{4,36},{36... | collective-permute-start | bytes 6291464 | tf_op jit(solution)/shard_map/ppermute | solution.py:536
  0.0 26.1 %collective-permute-start.1 = (bf16[1024,1024]{1,0:T(8,128)(2,1)}, bf16[1024,1024]{1,0:T(8,128)(2,1)}, u32[]{:S(2)}, u32[]{:S(2)}) collective-permute-start(bf16[1024,1024]{1,0:T(8,128)(2,1)} %out_one.5), channel_id=1, source_target_pairs={{0,32},{32,0},{1,33},{33,1},{2,34},{34,2},{3,35},{35,3},{4,36},{36... | collective-permute-start | bytes 6291464 | tf_op jit(solution)/shard_map/ppermute | solution.py:537
  0.5 25.6 %copy-start.2 = (bf16[128,1024]{1,0:T(8,128)(2,1)S(1)}, bf16[128,1024]{1,0:T(8,128)(2,1)}, u32[]{:S(2)}) copy-start(bf16[128,1024]{1,0:T(8,128)(2,1)} %tok_ref.3) | copy-start | bytes 786436
  26.1 7.4 %copy-start.3 = (f32[32,16]{0,1:T(8,128)S(1)}, f32[32,16]{0,1:T(8,128)}, u32[]{:S(2)}) copy-start(f32[32,16]{0,1:T(8,128)} %param.19) | copy-start | bytes 6148
  26.2 13.0 %collective-permute-start.5 = (bf16[128,1024]{1,0:T(8,128)(2,1)S(1)}, bf16[128,1024]{1,0:T(8,128)(2,1)S(1)}, u32[]{:S(2)}, u32[]{:S(2)}) collective-permute-start(bf16[128,1024]{1,0:T(8,128)(2,1)S(1)} %get-tuple-element.37), channel_id=1, source_target_pairs={{0,65},{65,0},{1,64},{64,1},{2,67},{67,2},{3,66},{66,3},{4,69},{69... | collective-permute-start | bytes 786440 | tf_op jit(solution)/shard_map/ppermute | solution.py:548
  28.5 10.7 %collective-permute-start.2 = (bf16[768,128]{1,0:T(8,128)(2,1)S(1)}, bf16[768,128]{1,0:T(8,128)(2,1)S(1)}, u32[]{:S(2)}, u32[]{:S(2)}) collective-permute-start(bf16[768,128]{1,0:T(8,128)(2,1)S(1)} %get-tuple-element.25), channel_id=1, source_target_pairs={{0,8},{8,16},{16,24},{24,0},{1,9},{9,17},{17,25},{25,1},{2,10},{10... | collective-permute-start | bytes 589832 | tf_op jit(solution)/shard_map/ppermute | solution.py:546
  29.9 9.2 %collective-permute-start.3 = (bf16[768,128]{1,0:T(8,128)(2,1)S(1)}, bf16[768,128]{1,0:T(8,128)(2,1)S(1)}, u32[]{:S(2)}, u32[]{:S(2)}) collective-permute-start(bf16[768,128]{1,0:T(8,128)(2,1)S(1)} %get-tuple-element.26), channel_id=1, source_target_pairs={{0,24},{8,0},{16,8},{24,16},{1,25},{9,1},{17,9},{25,17},{2,26},{10... | collective-permute-start | bytes 589832 | tf_op jit(solution)/shard_map/ppermute | solution.py:547
  31.7 7.5 %collective-permute-start.4 = (bf16[512,128]{1,0:T(8,128)(2,1)S(1)}, bf16[512,128]{1,0:T(8,128)(2,1)S(1)}, u32[]{:S(2)}, u32[]{:S(2)}) collective-permute-start(bf16[512,128]{1,0:T(8,128)(2,1)S(1)} %get-tuple-element.27), channel_id=1, source_target_pairs={{0,16},{8,24},{16,0},{24,8},{1,17},{9,25},{17,1},{25,9},{2,18},{10... | collective-permute-start | bytes 393224 | tf_op jit(solution)/shard_map/ppermute | solution.py:545
  39.2 16.0 %copy-start = (bf16[1024,1024]{1,0:T(8,128)(2,1)S(1)}, bf16[1024,1024]{1,0:T(8,128)(2,1)}, u32[]{:S(2)}) copy-start(bf16[1024,1024]{1,0:T(8,128)(2,1)} %out_one.5) | copy-start | bytes 6291460
  39.2 16.0 %copy-start.1 = (bf16[1024,1024]{1,0:T(8,128)(2,1)S(1)}, bf16[1024,1024]{1,0:T(8,128)(2,1)}, u32[]{:S(2)}) copy-start(bf16[1024,1024]{1,0:T(8,128)(2,1)} %w_ref.3) | copy-start | bytes 6291460
  39.2 16.0 %copy-start.4 = (f32[1024]{0:T(1024)S(1)}, f32[1024]{0:T(1024)}, u32[]{:S(2)}) copy-start(f32[1024]{0:T(1024)} %param.23) | copy-start | bytes 12292
  56.9 7.7 %collective-permute-start.6 = (bf16[128,640]{1,0:T(8,128)(2,1)S(1)}, bf16[128,640]{1,0:T(8,128)(2,1)S(1)}, u32[]{:S(2)}, u32[]{:S(2)}) collective-permute-start(bf16[128,640]{1,0:T(8,128)(2,1)S(1)} %get-tuple-element.42), channel_id=1, source_target_pairs={{0,65},{65,0},{1,64},{64,1},{2,67},{67,2},{3,66},{66,3},{4,69},{69... | collective-permute-start | bytes 491528 | tf_op jit(solution)/shard_map/ppermute | solution.py:557
  58.7 5.9 %collective-permute-start.7 = (bf16[128,384]{1,0:T(8,128)(2,1)S(1)}, bf16[128,384]{1,0:T(8,128)(2,1)S(1)}, u32[]{:S(2)}, u32[]{:S(2)}) collective-permute-start(bf16[128,384]{1,0:T(8,128)(2,1)S(1)} %remainder.1.rest_0_), channel_id=1, source_target_pairs={{0,65},{65,0},{1,64},{64,1},{2,67},{67,2},{3,66},{66,3},{4,69},{69... | collective-permute-start | bytes 294920 | tf_op jit(solution)/shard_map/ppermute | solution.py:559

commit v15 on v14

--- a/solution.py
+++ b/solution.py
@@ -317,14 +317,15 @@
         acc_ref[step] = select(asked_ref, step, dot(values[...], weights[0])) + own_head(near_out)
         stat_ref[step, 0:1] = top
         stat_ref[step, 1:2] = row_sum
+        strip = pl.ds(pl.multiple_of(step * LANES, LANES), LANES)
+        turned_two[:, strip] = jnp.transpose(in_two[strip])
         return 0
 
     lax.fori_loop(0, PAIRS, one, 0, unroll=4)
     for copy in copies:
         copy.wait()
-    for source, target in ((in_two, turned_two), (in_one, turned_one)):
-        for at in range(0, D, LANES):
-            target[:, at : at + LANES] = jnp.transpose(source[at : at + LANES])
+    for at in range(0, D, LANES):
+        turned_one[:, at : at + LANES] = jnp.transpose(in_one[at : at + LANES])
 
 
 def attend_own(place, rel_bias, got, made, in_one, in_two, out_two):

time: 65.6 us -> 65.6 us (level)
  transfers between devices with their start and end apart: 8 -> 8, of which waited for: 2 -> 2; matrix products, arithmetic and copies ran while one was open for 0% -> 0% of each run, Pallas kernels for 19% -> 18%
where the time goes in v15:
time: 65.6 us; the launch traced here: 65.4 us
  blocking collectives  33.5 us (51%)
  Pallas kernels  17.5 us (27%)
  starting transfers between devices  11.2 us (17%)
  waiting for transfers between devices  2.98 us (5%)
    all_to_all x1, blocking collectives, body(): got = lax.all_to_all(blocks, PLANE, 0, 0, tiled=True)  20.8 us
    all_to_all x1, blocking collectives, body(): att = lax.all_to_all(mixed, ('yhi',) + PLANE, 0, 0, tiled=True)  12.8 us
    pallas_call x1, Pallas kernels, project(): pl.pallas_call(project_kernel, in_specs=[SMEM_SPEC] * 3 + [HBM_SPEC] * 9,...  4.77 us
    pallas_call x1, Pallas kernels, attend_own(): pl.pallas_call(own_kernel, in_specs=[SMEM_SPEC] * 4 + [VMEM_SPEC] * 7 + [...  4.74 us
    pallas_call x1, Pallas kernels, attend_rest(): pl.pallas_call(rest_kernel, in_specs=[SMEM_SPEC] * 4 + [VMEM_SPEC] * 11,...  3.19 us
    ppermute x1, starting transfers between devices, body(): far_tokens = lax.ppermute(same, mirrored, MIRROR)  2.27 us
    ppermute x1, waiting for transfers between devices, body(): second_back = lax.ppermute(second, mirrored, MIRROR)  2.03 us
    ppermute x1, starting transfers between devices, body(): second_back = lax.ppermute(second, mirrored, MIRROR)  2.01 us
  transfers between devices with their start and end apart: 8, of which 2 were waited for; matrix products, arithmetic and copies ran while one was open for 0% of the time, Pallas kernels for 18%

profile of v15, /device:TPU:0, one launch (start us, length us, event | category | flops | bytes accessed | tf_op | source)
XLA Modules:
  0.0 65.4 jit_solution(12495247181197506262)
XLA Ops:
  0.0 0.0 collective-permute-start
  0.0 0.5 collective-permute-start.1
  0.5 0.0 copy-start.2
  0.5 4.8 %project.1 = (bf16[8,448,128]{2,1,0:T(8,128)(2,1)S(1)}, f32[384,256]{1,0:T(8,128)S(1)}, bf16[10,128,128]{2,1,0:T(8,128)(2,1)S(1)}, f32[8,8,128]{2,1,0:T(8,128)S(...) custom-call(s32[1]{0:T(128)} %bitcast.1.x_ref, s32[1]{0:T(128)} %bitcast.2.pair_ref, s32[1]{0:T(128)} %bitcast.side_ref, ...), custom_call_target="tpu_custom_call" | custom-call | flops 1000 | bytes 1000 | tf_op jit(solution)/shard_map/project/pallas_call | solution.py:172
  5.3 20.8 %all_to_all.10.got_ref = bf16[8,448,128]{2,1,0:T(8,128)(2,1)S(1)} all-to-all(bf16[8,448,128]{2,1,0:T(8,128)(2,1)S(1)} %get-tuple-element.24), channel_id=1, replica_groups=mesh['yhi'=2,'core'=2,'x'=4,'z'=4,'ylo'=2] {'z','ylo'}, dimensions={0} | all-to-all | bytes 1835008 | tf_op jit(solution)/shard_map/all_to_all | solution.py:542
  26.1 0.0 copy-start.3
  26.1 0.0 collective-permute-done.rest_0_.in_two
  26.1 0.0 collective-permute-done.1.rest_1_.out_hbm
  26.1 0.0 copy-done.2
  26.1 0.1 spread.1
  26.2 2.3 %collective-permute-start.5 = (bf16[128,1024]{1,0:T(8,128)(2,1)S(1)}, bf16[128,1024]{1,0:T(8,128)(2,1)S(1)}, u32[]{:S(2)}, u32[]{:S(2)}) collective-permute-start(bf16[128,1024]{1,0:T(8,128)(2,1)S(1)} %get-tuple-element.37), channel_id=1, source_target_pairs={{0,65},{65,0},{1,64},{64,1},{2,67},{67,2},{3,66},{66,3},{4,69},{69... | collective-permute-start | bytes 786440 | tf_op jit(solution)/shard_map/ppermute | solution.py:549
  28.5 1.5 %collective-permute-start.2 = (bf16[768,128]{1,0:T(8,128)(2,1)S(1)}, bf16[768,128]{1,0:T(8,128)(2,1)S(1)}, u32[]{:S(2)}, u32[]{:S(2)}) collective-permute-start(bf16[768,128]{1,0:T(8,128)(2,1)S(1)} %get-tuple-element.25), channel_id=1, source_target_pairs={{0,8},{8,16},{16,24},{24,0},{1,9},{9,17},{17,25},{25,1},{2,10},{10... | collective-permute-start | bytes 589832 | tf_op jit(solution)/shard_map/ppermute | solution.py:547
  29.9 1.8 %collective-permute-start.3 = (bf16[768,128]{1,0:T(8,128)(2,1)S(1)}, bf16[768,128]{1,0:T(8,128)(2,1)S(1)}, u32[]{:S(2)}, u32[]{:S(2)}) collective-permute-start(bf16[768,128]{1,0:T(8,128)(2,1)S(1)} %get-tuple-element.26), channel_id=1, source_target_pairs={{0,24},{8,0},{16,8},{24,16},{1,25},{9,1},{17,9},{25,17},{2,26},{10... | collective-permute-start | bytes 589832 | tf_op jit(solution)/shard_map/ppermute | solution.py:548
  31.7 1.8 %collective-permute-start.4 = (bf16[512,128]{1,0:T(8,128)(2,1)S(1)}, bf16[512,128]{1,0:T(8,128)(2,1)S(1)}, u32[]{:S(2)}, u32[]{:S(2)}) collective-permute-start(bf16[512,128]{1,0:T(8,128)(2,1)S(1)} %get-tuple-element.27), channel_id=1, source_target_pairs={{0,16},{8,24},{16,0},{24,8},{1,17},{9,25},{17,1},{25,9},{2,18},{10... | collective-permute-start | bytes 393224 | tf_op jit(solution)/shard_map/ppermute | solution.py:546
  33.5 0.0 copy-done.3
  33.5 4.7 %attend_own.1 = (f32[8,8,256]{2,1,0:T(8,128)S(1)}, f32[8,128,128]{2,1,0:T(8,128)S(1)}, f32[8,128,256]{2,1,0:T(8,128)S(1)}, bf16[8,256,256]{2,1,0:T(8,128)(2,1)S(...) custom-call(s32[1]{0:T(128)} %bitcast.1.x_ref, ...), custom_call_target="tpu_custom_call" | custom-call | flops 1000 | bytes 1000 | tf_op jit(solution)/shard_map/attend_own/pallas_call | solution.py:332
  38.2 0.9 %collective-permute-done.4.far_ref = bf16[512,128]{1,0:T(8,128)(2,1)S(1)} collective-permute-done((bf16[512,128]{1,0:T(8,128)(2,1)S(1)}, bf16[512,128]{1,0:T(8,128)(2,1)S(1)}, u32[]{:S(2)}, u32[]{:S(2)}) %collective-permute-start.4) | collective-permute-done | bytes 131104 | tf_op jit(solution)/shard_map/ppermute | solution.py:546
  39.2 0.0 collective-permute-done.2.prev_ref
  39.2 0.0 collective-permute-done.3.next_ref
  39.2 0.0 collective-permute-done.5._.tok_ref
  39.2 0.0 copy-start
  39.2 0.0 copy-start.1
  39.2 0.0 copy-start.4
  39.2 3.2 %attend_rest.1 = bf16[16,128,128]{2,1,0:T(8,128)(2,1)S(1)} custom-call(s32[1]{0:T(128)} %bitcast.1.x_ref, s32[1]{0:T(128)} %bitcast.2.pair_ref, s32[1]{0:T(128)} %bitcast.side_ref, f32[16,32]{1,0:T(8,128)S(1)} %bitcast.8, bf16[768,128]{1,0:T(8,128)(2,1)S(1)} %collective-permute-done.2.prev_ref, bf16[768,128]{1,0:T(8,128)(2,1)S(1)} %collective-permute-done.3.next_ref, ...), custom_call_target="tpu_custom_call" | custom-call | flops 1000 | bytes 1000 | tf_op jit(solution)/shard_map/attend_rest/pallas_call | solution.py:413
  42.4 12.8 %all_to_all.11.att_ref = bf16[16,128,128]{2,1,0:T(8,128)(2,1)S(1)} all-to-all(bf16[16,128,128]{2,1,0:T(8,128)(2,1)S(1)} %attend_rest.1), channel_id=1, replica_groups=mesh['yhi'=2,'core'=2,'x'=4,'z'=4,'ylo'=2] {'yhi','z','ylo'}, dimensions={0} | all-to-all | bytes 1048576 | tf_op jit(solution)/shard_map/all_to_all | solution.py:555
  55.2 0.0 copy-done
  55.2 0.0 copy-done.1
  55.2 0.0 copy-done.4
  55.2 1.7 %away.1 = (bf16[128,640]{1,0:T(8,128)(2,1)S(1)}, bf16[2,128,1024]{2,1,0:T(8,128)(2,1)S(1)}) custom-call(s32[1]{0:T(128)} %bitcast.side_ref, bf16[16,128,128]{2,1,0:T(8,128)(2,1)S(1)} %all_to_all.11.att_ref, bf16[1024,1024]{1,0:T(8,128)(2,1)S(1)} %copy-done.1, bf16[128,1024]{1,0:T(8,128)(2,1)S(1)} %collective-permute-done.5._.tok_ref, f32[1,1024]{1,0:T(1,128)S(1)} %bitcast.9, ...), custom_call_target="tpu_custom_call" | custom-call | flops 1000 | bytes 1000 | tf_op jit(solution)/shard_map/away/pallas_call | solution.py:472
  56.9 1.4 %collective-permute-start.6 = (bf16[128,640]{1,0:T(8,128)(2,1)S(1)}, bf16[128,640]{1,0:T(8,128)(2,1)S(1)}, u32[]{:S(2)}, u32[]{:S(2)}) collective-permute-start(bf16[128,640]{1,0:T(8,128)(2,1)S(1)} %get-tuple-element.42), channel_id=1, source_target_pairs={{0,65},{65,0},{1,64},{64,1},{2,67},{67,2},{3,66},{66,3},{4,69},{69... | collective-permute-start | bytes 491528 | tf_op jit(solution)/shard_map/ppermute | solution.py:558
  58.3 0.4 remainder.1.rest_0_
  58.7 2.0 %collective-permute-start.7 = (bf16[128,384]{1,0:T(8,128)(2,1)S(1)}, bf16[128,384]{1,0:T(8,128)(2,1)S(1)}, u32[]{:S(2)}, u32[]{:S(2)}) collective-permute-start(bf16[128,384]{1,0:T(8,128)(2,1)S(1)} %remainder.1.rest_0_), channel_id=1, source_target_pairs={{0,65},{65,0},{1,64},{64,1},{2,67},{67,2},{3,66},{66,3},{4,69},{69... | collective-permute-start | bytes 294920 | tf_op jit(solution)/shard_map/ppermute | solution.py:560
  60.7 1.9 %finish.1.home_ref = f32[128,1024]{1,0:T(8,128)S(1)} custom-call(s32[1]{0:T(128)} %bitcast.side_ref, bf16[16,128,128]{2,1,0:T(8,128)(2,1)S(1)} %all_to_all.11.att_ref, bf16[1024,1024]{1,0:T(8,128)(2,1)S(1)} %copy-done.1, bf16[128,1024]{1,0:T(8,128)(2,1)S(1)} %copy-done.2, f32[1,1024]{1,0:T(1,128)S(1)} %bitcast.10, ...), custom_call_target="tpu_custom_call" | custom-call | flops 1000 | bytes 1000 | tf_op jit(solution)/shard_map/finish/pallas_call | solution.py:449
  62.6 2.0 %collective-permute-done.7.second_ref = bf16[128,384]{1,0:T(8,128)(2,1)S(1)} collective-permute-done((bf16[128,384]{1,0:T(8,128)(2,1)S(1)}, bf16[128,384]{1,0:T(8,128)(2,1)S(1)}, u32[]{:S(2)}, u32[]{:S(2)}) %collective-permute-start.7) | collective-permute-done | bytes 98336 | tf_op jit(solution)/shard_map/ppermute | solution.py:560
  64.6 0.0 collective-permute-done.6.first_ref
  64.6 0.8 %total.1 = bf16[128,1024]{1,0:T(8,128)(2,1)} custom-call(f32[128,1024]{1,0:T(8,128)S(1)} %finish.1.home_ref, bf16[128,640]{1,0:T(8,128)(2,1)S(1)} %collective-permute-done.6.first_ref, bf16[128,384]{1,0:T(8,128)(2,1)S(1)} %collective-permute-done.7.second_ref), custom_call_target="tpu_custom_call" | custom-call | flops 1000 | bytes 1000 | tf_op jit(solution)/shard_map/total/pallas_call | solution.py:506
Async XLA Ops:
  0.0 26.1 %collective-permute-start = (bf16[1024,1024]{1,0:T(8,128)(2,1)}, bf16[1024,1024]{1,0:T(8,128)(2,1)S(1)}, u32[]{:S(2)}, u32[]{:S(2)}) collective-permute-start(bf16[1024,1024]{1,0:T(8,128)(2,1)} %in_hbm.1), channel_id=1, source_target_pairs={{0,32},{32,0},{1,33},{33,1},{2,34},{34,2},{3,35},{35,3},{4,36},{36... | collective-permute-start | bytes 6291464 | tf_op jit(solution)/shard_map/ppermute | solution.py:537
  0.0 26.1 %collective-permute-start.1 = (bf16[1024,1024]{1,0:T(8,128)(2,1)}, bf16[1024,1024]{1,0:T(8,128)(2,1)}, u32[]{:S(2)}, u32[]{:S(2)}) collective-permute-start(bf16[1024,1024]{1,0:T(8,128)(2,1)} %out_one.5), channel_id=1, source_target_pairs={{0,32},{32,0},{1,33},{33,1},{2,34},{34,2},{3,35},{35,3},{4,36},{36... | collective-permute-start | bytes 6291464 | tf_op jit(solution)/shard_map/ppermute | solution.py:538
  0.5 25.6 %copy-start.2 = (bf16[128,1024]{1,0:T(8,128)(2,1)S(1)}, bf16[128,1024]{1,0:T(8,128)(2,1)}, u32[]{:S(2)}) copy-start(bf16[128,1024]{1,0:T(8,128)(2,1)} %tok_ref.3) | copy-start | bytes 786436
  26.1 7.4 %copy-start.3 = (f32[32,16]{0,1:T(8,128)S(1)}, f32[32,16]{0,1:T(8,128)}, u32[]{:S(2)}) copy-start(f32[32,16]{0,1:T(8,128)} %param.19) | copy-start | bytes 6148
  26.2 13.0 %collective-permute-start.5 = (bf16[128,1024]{1,0:T(8,128)(2,1)S(1)}, bf16[128,1024]{1,0:T(8,128)(2,1)S(1)}, u32[]{:S(2)}, u32[]{:S(2)}) collective-permute-start(bf16[128,1024]{1,0:T(8,128)(2,1)S(1)} %get-tuple-element.37), channel_id=1, source_target_pairs={{0,65},{65,0},{1,64},{64,1},{2,67},{67,2},{3,66},{66,3},{4,69},{69... | collective-permute-start | bytes 786440 | tf_op jit(solution)/shard_map/ppermute | solution.py:549
  28.5 10.7 %collective-permute-start.2 = (bf16[768,128]{1,0:T(8,128)(2,1)S(1)}, bf16[768,128]{1,0:T(8,128)(2,1)S(1)}, u32[]{:S(2)}, u32[]{:S(2)}) collective-permute-start(bf16[768,128]{1,0:T(8,128)(2,1)S(1)} %get-tuple-element.25), channel_id=1, source_target_pairs={{0,8},{8,16},{16,24},{24,0},{1,9},{9,17},{17,25},{25,1},{2,10},{10... | collective-permute-start | bytes 589832 | tf_op jit(solution)/shard_map/ppermute | solution.py:547
  29.9 9.2 %collective-permute-start.3 = (bf16[768,128]{1,0:T(8,128)(2,1)S(1)}, bf16[768,128]{1,0:T(8,128)(2,1)S(1)}, u32[]{:S(2)}, u32[]{:S(2)}) collective-permute-start(bf16[768,128]{1,0:T(8,128)(2,1)S(1)} %get-tuple-element.26), channel_id=1, source_target_pairs={{0,24},{8,0},{16,8},{24,16},{1,25},{9,1},{17,9},{25,17},{2,26},{10... | collective-permute-start | bytes 589832 | tf_op jit(solution)/shard_map/ppermute | solution.py:548
  31.7 7.5 %collective-permute-start.4 = (bf16[512,128]{1,0:T(8,128)(2,1)S(1)}, bf16[512,128]{1,0:T(8,128)(2,1)S(1)}, u32[]{:S(2)}, u32[]{:S(2)}) collective-permute-start(bf16[512,128]{1,0:T(8,128)(2,1)S(1)} %get-tuple-element.27), channel_id=1, source_target_pairs={{0,16},{8,24},{16,0},{24,8},{1,17},{9,25},{17,1},{25,9},{2,18},{10... | collective-permute-start | bytes 393224 | tf_op jit(solution)/shard_map/ppermute | solution.py:546
  39.2 16.0 %copy-start = (bf16[1024,1024]{1,0:T(8,128)(2,1)S(1)}, bf16[1024,1024]{1,0:T(8,128)(2,1)}, u32[]{:S(2)}) copy-start(bf16[1024,1024]{1,0:T(8,128)(2,1)} %out_one.5) | copy-start | bytes 6291460
  39.2 16.0 %copy-start.1 = (bf16[1024,1024]{1,0:T(8,128)(2,1)S(1)}, bf16[1024,1024]{1,0:T(8,128)(2,1)}, u32[]{:S(2)}) copy-start(bf16[1024,1024]{1,0:T(8,128)(2,1)} %w_ref.3) | copy-start | bytes 6291460
  39.2 16.0 %copy-start.4 = (f32[1024]{0:T(1024)S(1)}, f32[1024]{0:T(1024)}, u32[]{:S(2)}) copy-start(f32[1024]{0:T(1024)} %param.23) | copy-start | bytes 12292
  56.9 7.7 %collective-permute-start.6 = (bf16[128,640]{1,0:T(8,128)(2,1)S(1)}, bf16[128,640]{1,0:T(8,128)(2,1)S(1)}, u32[]{:S(2)}, u32[]{:S(2)}) collective-permute-start(bf16[128,640]{1,0:T(8,128)(2,1)S(1)} %get-tuple-element.42), channel_id=1, source_target_pairs={{0,65},{65,0},{1,64},{64,1},{2,67},{67,2},{3,66},{66,3},{4,69},{69... | collective-permute-start | bytes 491528 | tf_op jit(solution)/shard_map/ppermute | solution.py:558
  58.7 5.9 %collective-permute-start.7 = (bf16[128,384]{1,0:T(8,128)(2,1)S(1)}, bf16[128,384]{1,0:T(8,128)(2,1)S(1)}, u32[]{:S(2)}, u32[]{:S(2)}) collective-permute-start(bf16[128,384]{1,0:T(8,128)(2,1)S(1)} %remainder.1.rest_0_), channel_id=1, source_target_pairs={{0,65},{65,0},{1,64},{64,1},{2,67},{67,2},{3,66},{66,3},{4,69},{69... | collective-permute-start | bytes 294920 | tf_op jit(solution)/shard_map/ppermute | solution.py:560
